TPU v7x, 256 devices: a whole 4x4x8 slice. The times are simulated.
256 devices in a mesh: seq: 8 (over y, x_lo), tp: 32 (over z, x_hi, core).
Axes of the slice: x: 4 (x_hi: 2, x_lo: 2; x = x_hi * 2 + x_lo), y: 4, z: 8, core: 2. Of those that a mesh axis runs over, the one named last changes fastest.
Arguments:
- projected: bfloat16 [3, 8192, 8192], P(None, 'seq', 'tp'), may hold values from -6 to 6
- short_filter: float32 [3, 3, 8192], P(None, None, 'tp'), may hold values from -2.5 to 2.5
- residue: float32 [512, 16], P('tp'), may hold values from -1.5 to 1.5
- rate: float32 [512, 16], P('tp'), may hold values from 0 to 1, as said below
- out_weight: bfloat16 [8192, 8192], P('tp'), may hold values from -0.0625 to 0.0625
Outputs:
- output: bfloat16 [8192, 8192], P(('seq', 'tp'))
Inputs may be any that keep to these rules, and one draw needn't show every extreme that they name: Every rate is positive.
All inputs are finite; a program needn't handle non-finite values.
Results may differ from a plain program's by a relative error of at most 0.02.
Values may be sent and summed in bfloat16 or wider, within the bound.
No kernel may reach another device: no remote copies, remote signals or barrier semaphores. Data moves between devices by JAX's collectives and lax.ppermute only.
A program may use at most 128 MiB of HBM per device.

v0:
```python
import jax
import jax.numpy as jnp
from jax import lax
from jax.sharding import PartitionSpec as P

GROUP = 16
MODES = 16


def passed_along(value, axis, steps):
    count = lax.axis_size(axis)
    leading, last = (max(0, -steps), min(count, count - steps))
    return lax.ppermute(value, axis, [(source, source + steps) for source in range(leading, last)])


def toeplitz_from(kernel, block_len):
    group_count = kernel.shape[0]
    padded = jnp.concatenate(
        [
            jnp.zeros((group_count, block_len - 1), jnp.float32),
            kernel,
            jnp.zeros((group_count, 1), jnp.float32),
        ],
        axis=1,
    )
    tiled = jnp.tile(padded, (1, block_len))
    width = 2 * block_len - 1
    trimmed = tiled[:, : block_len * width].reshape(group_count, block_len, width)
    hankel = trimmed[:, :, block_len - 1 : width]
    return jnp.swapaxes(hankel, 1, 2)


def filter_tables(rate, residue, block_len):
    mode_weight = residue * jnp.sqrt(-jnp.expm1(-2.0 * rate))
    offsets = lax.iota(jnp.int32, block_len)
    lag_float = offsets.astype(jnp.float32)
    powers = jnp.exp(-rate[None, :, :] * lag_float[:, None, None])
    kernel = jnp.einsum("tgn,gn->gt", powers, mode_weight, precision=lax.Precision.HIGHEST)
    toeplitz = toeplitz_from(kernel, block_len)
    decay_into = jnp.exp(-rate[None, :, :] * (lag_float[:, None, None] + 1.0)) * mode_weight[None]
    decay_out = jnp.exp(-rate[None, :, :] * (block_len - 1.0 - lag_float)[:, None, None])
    block_power = jnp.exp(-rate * block_len)
    return (toeplitz, decay_into, decay_out, block_power)


def causal_conv(signal, tables, state_start):
    toeplitz, decay_into, decay_out, block_power = tables
    block_len = toeplitz.shape[1]
    row_count, group_count, group_width = signal.shape
    segments = signal.reshape(row_count // block_len, block_len, group_count, group_width)

    def advance(state_in, segment):
        within = jnp.einsum("gts,sgi->tgi", toeplitz, segment, precision=lax.Precision.HIGHEST)
        carried = jnp.einsum("tgn,gni->tgi", decay_into, state_in, precision=lax.Precision.HIGHEST)
        state_next = block_power[:, :, None] * state_in + jnp.einsum(
            "tgn,tgi->gni", decay_out, segment, precision=lax.Precision.HIGHEST
        )
        return (state_next, within + carried)

    state_end, outputs = lax.scan(advance, state_start, segments)
    return (outputs.reshape(row_count, group_count, group_width), state_end)


def local(projected, short_filter, residue, rate, out_weight):
    row_count = projected.shape[1]
    channels = projected.shape[2]
    group_count = rate.shape[0]
    prior_rows = passed_along(projected[:, -2:, :], "seq", 1)
    extended = jnp.concatenate([prior_rows, projected], axis=1).astype(jnp.float32)
    featured = (
        short_filter[:, 0, None, :] * extended[:, 2:]
        + short_filter[:, 1, None, :] * extended[:, 1 : row_count + 1]
        + short_filter[:, 2, None, :] * extended[:, 0:row_count]
    )
    signal = (featured[1] * featured[2]).reshape(row_count, group_count, GROUP)
    tables = filter_tables(rate, residue, min(256, row_count))
    local_conv, local_end = causal_conv(
        signal, tables, jnp.zeros((group_count, MODES, GROUP), jnp.float32)
    )
    device_power = jnp.exp(-rate * row_count)[:, :, None]

    def relay_state(rounds, received):
        running = device_power * received + local_end
        return passed_along(running, "seq", 1)

    incoming = lax.fori_loop(0, lax.axis_size("seq") - 1, relay_state, jnp.zeros_like(local_end))
    lag_float = lax.iota(jnp.int32, row_count).astype(jnp.float32)
    mode_weight = residue * jnp.sqrt(-jnp.expm1(-2.0 * rate))
    reach = jnp.exp(-rate[None, :, :] * (lag_float[:, None, None] + 1.0)) * mode_weight[None]
    conv = local_conv + jnp.einsum("tgn,gni->tgi", reach, incoming, precision=lax.Precision.HIGHEST)
    mixed = (featured[0] * conv.reshape(row_count, channels)).astype(jnp.bfloat16)
    summed = lax.psum_scatter(
        jnp.dot(mixed, out_weight, preferred_element_type=jnp.float32).astype(jnp.bfloat16),
        "tp",
        scatter_dimension=0,
        tiled=True,
    )
    return summed


def solution(mesh):
    placed = (
        P(None, "seq", "tp"),
        P(None, None, "tp"),
        P("tp", None),
        P("tp", None),
        P("tp", None),
    )
    return jax.shard_map(
        local, mesh=mesh, in_specs=placed, out_specs=P(("seq", "tp"), None), check_vma=False
    )
```

profile of v0, /device:TPU:1, one launch (start us, length us, event | category | flops | bytes accessed | tf_op | source)
XLA Modules:
  0.0 406.2 jit_solution(2771488180705588889)
XLA Ops:
  6.5 0.7 slice.37
  7.2 3.9 collective-permute-start.1
  11.2 0.8 fusion.40
  12.0 0.7 exponential_bitcast_fusion
  13.3 1.1 tile.4
  14.4 4.9 %copy.33 = f32[2,8,256,512]{3,1,2,0:T(8,128)S(1)} copy(f32[2,8,256,512]{3,2,1,0:T(8,128)S(1)} %bitcast.65) | data formatting | bytes 16777216
  19.3 3.8 slice.54
  23.0 11.8 %reshape.37 = f32[16,256,511]{2,1,0:T(8,128)} reshape(f32[16,130816]{1,0:T(8,128)} %slice.54) | data formatting | bytes 16744448 | tf_op jit(solution)/shard_map/reshape | solution.py:28
  34.8 5.9 %slice_bitcast_fusion = f32[16,256,256]{1,2,0:T(8,128)} fusion(f32[16,256,511]{2,1,0:T(8,128)} %reshape.37), kind=kLoop, calls=%fused_computation.25 | loop fusion | bytes 8388608 | tf_op jit(solution)/shard_map/transpose | solution.py:30
  40.7 5.5 %copy.19 = f32[16,256,256]{2,1,0:T(8,128)} copy(f32[16,256,256]{1,2,0:T(8,128)} %slice_bitcast_fusion) | data formatting | bytes 8388608
  46.5 0.9 fusion.21
  47.5 1.6 copy-done
  49.6 0.5 mul.154
  50.1 55.3 %while.26 = (s32[]{:T(128)}, f32[16,16,16]{1,2,0:T(8,128)S(1)}, f32[4,256,16,16]{1,0,3,2:T(4,128)}, f32[16,16]{1,0:T(8,128)S(1)}, f32[4,256,16,16]{1,0,3,2:T(4,1...) while((s32[]{:T(128)}, f32[16,16,16]{1,2,0:T(8,128)S(1)}, ...), condition=%wide.region_1.2_spmd.clone.clone.clone, body=%wide.region_0.1_spmd.clone.clone.clone.sunk | while | flops 226770944 | bytes 7133320 | solution.py:60
  50.4 5.7 %fusion.57 = f32[16,16,256]{2,1,0:T(8,128)S(1)} fusion(f32[16,256,256]{2,1,0:T(8,128)} %get-tuple-element.355, f32[1,256,16,16]{1,0,3,2:T(1,128)S(1)} %constant_dynamic-slice_fusion.2), kind=kOutput, calls=%fused_computation.13.clone.1 | convolution fusion | flops 201326592 | bytes 4718592 | tf_op jit(solution)/shard_map/while/body/eval_jaxpr/gts,sgi->tgi/dot_general | solution.py:53
  56.0 0.5 fusion.58
  56.8 6.5 %dynamic_update_slice.8 = f32[4,256,16,16]{1,0,3,2:T(4,128)} dynamic-update-slice(f32[4,256,16,16]{1,0,3,2:T(4,128)} %get-tuple-element.340, f32[1,256,16,16]{1,0,3,2:T(1,128)S(1)} %copy.48, s32[]{:T(128)} %get-tuple-element.338, s32[]{:T(128)} %constant.17.clone.1..sunk, s32[]{:T(128)} %constant.17.clone.1..sunk, s32[]{:T(128)} %constant.17.clone.1..sunk) | dynamic-update-slice | bytes 524292 | tf_op jit(solution)/shard_map/while/body/jit(dynamic_update_index_in_dim)/dynamic_update_slice | solution.py:60
  63.3 0.5 fusion.56
  64.1 5.7 %fusion.57 = f32[16,16,256]{2,1,0:T(8,128)S(1)} fusion(f32[16,256,256]{2,1,0:T(8,128)} %get-tuple-element.355, f32[1,256,16,16]{1,0,3,2:T(1,128)S(1)} %constant_dynamic-slice_fusion.2), kind=kOutput, calls=%fused_computation.13.clone.1 | convolution fusion | flops 201326592 | bytes 4718592 | tf_op jit(solution)/shard_map/while/body/eval_jaxpr/gts,sgi->tgi/dot_general | solution.py:53
  69.8 0.5 fusion.58
  70.6 6.5 %dynamic_update_slice.8 = f32[4,256,16,16]{1,0,3,2:T(4,128)} dynamic-update-slice(f32[4,256,16,16]{1,0,3,2:T(4,128)} %get-tuple-element.340, f32[1,256,16,16]{1,0,3,2:T(1,128)S(1)} %copy.48, s32[]{:T(128)} %get-tuple-element.338, s32[]{:T(128)} %constant.17.clone.1..sunk, s32[]{:T(128)} %constant.17.clone.1..sunk, s32[]{:T(128)} %constant.17.clone.1..sunk) | dynamic-update-slice | bytes 524292 | tf_op jit(solution)/shard_map/while/body/jit(dynamic_update_index_in_dim)/dynamic_update_slice | solution.py:60
  77.1 0.5 fusion.56
  77.9 5.7 %fusion.57 = f32[16,16,256]{2,1,0:T(8,128)S(1)} fusion(f32[16,256,256]{2,1,0:T(8,128)} %get-tuple-element.355, f32[1,256,16,16]{1,0,3,2:T(1,128)S(1)} %constant_dynamic-slice_fusion.2), kind=kOutput, calls=%fused_computation.13.clone.1 | convolution fusion | flops 201326592 | bytes 4718592 | tf_op jit(solution)/shard_map/while/body/eval_jaxpr/gts,sgi->tgi/dot_general | solution.py:53
  83.6 0.5 fusion.58
  84.3 6.5 %dynamic_update_slice.8 = f32[4,256,16,16]{1,0,3,2:T(4,128)} dynamic-update-slice(f32[4,256,16,16]{1,0,3,2:T(4,128)} %get-tuple-element.340, f32[1,256,16,16]{1,0,3,2:T(1,128)S(1)} %copy.48, s32[]{:T(128)} %get-tuple-element.338, s32[]{:T(128)} %constant.17.clone.1..sunk, s32[]{:T(128)} %constant.17.clone.1..sunk, s32[]{:T(128)} %constant.17.clone.1..sunk) | dynamic-update-slice | bytes 524292 | tf_op jit(solution)/shard_map/while/body/jit(dynamic_update_index_in_dim)/dynamic_update_slice | solution.py:60
  90.9 0.5 fusion.56
  91.6 5.7 %fusion.57 = f32[16,16,256]{2,1,0:T(8,128)S(1)} fusion(f32[16,256,256]{2,1,0:T(8,128)} %get-tuple-element.355, f32[1,256,16,16]{1,0,3,2:T(1,128)S(1)} %constant_dynamic-slice_fusion.2), kind=kOutput, calls=%fused_computation.13.clone.1 | convolution fusion | flops 201326592 | bytes 4718592 | tf_op jit(solution)/shard_map/while/body/eval_jaxpr/gts,sgi->tgi/dot_general | solution.py:53
  98.1 6.5 %dynamic_update_slice.8 = f32[4,256,16,16]{1,0,3,2:T(4,128)} dynamic-update-slice(f32[4,256,16,16]{1,0,3,2:T(4,128)} %get-tuple-element.340, f32[1,256,16,16]{1,0,3,2:T(1,128)S(1)} %copy.48, s32[]{:T(128)} %get-tuple-element.338, s32[]{:T(128)} %constant.17.clone.1..sunk, s32[]{:T(128)} %constant.17.clone.1..sunk, s32[]{:T(128)} %constant.17.clone.1..sunk) | dynamic-update-slice | bytes 524292 | tf_op jit(solution)/shard_map/while/body/jit(dynamic_update_index_in_dim)/dynamic_update_slice | solution.py:60
  104.6 0.5 fusion.56
  105.4 1.8 reshape.38
  107.2 45.8 %while.25 = (s32[]{:T(128)}, f32[16,16,16]{2,1,0:T(8,128)S(1)}, f32[16,16,1]{1,0,2:T(8,128)S(1)}, f32[16,16,16]{2,1,0:T(8,128)S(1)}, s32[]{:T(128)}) while((s32[]{:T(128)}, f32[16,16,16]{2,1,0:T(8,128)S(1)}, f32[16,16,1]{1,0,2:T(8,128)S(1)}, f32[16,16,16]{2,1,0:T(8,128)S(1)}, s32[]{:T(128)}) %tuple.56), condition=%wide.region_3.4_spmd, body=%wide.region_2.3_spmd.sunk | while | flops 8194 | bytes 115813 | solution.py:86
  107.3 3.2 collective-permute-start
  110.5 1.9 collective-permute-done
  112.6 3.8 collective-permute-start
  116.4 1.9 collective-permute-done
  118.4 4.0 collective-permute-start
  122.4 1.9 collective-permute-done
  124.4 4.7 %collective-permute-start = (f32[16,16,16]{2,1,0:T(8,128)S(1)}, f32[16,16,16]{2,1,0:T(8,128)S(1)}, u32[]{:S(2)}, u32[]{:S(2)}) collective-permute-start(f32[16,16,16]{2,1,0:T(8,128)S(1)} %multiply_add_fusion.2), channel_id=1, source_target_pairs={{0,32},{32,64},{64,96},{96,128},{128,160},{160,192},{192,224},{1,3... | collective-permute-start | bytes 49160 | tf_op jit(solution)/shard_map/while/body/eval_jaxpr/ppermute | solution.py:13
  129.1 1.9 collective-permute-done
  131.1 4.7 %collective-permute-start = (f32[16,16,16]{2,1,0:T(8,128)S(1)}, f32[16,16,16]{2,1,0:T(8,128)S(1)}, u32[]{:S(2)}, u32[]{:S(2)}) collective-permute-start(f32[16,16,16]{2,1,0:T(8,128)S(1)} %multiply_add_fusion.2), channel_id=1, source_target_pairs={{0,32},{32,64},{64,96},{96,128},{128,160},{160,192},{192,224},{1,3... | collective-permute-start | bytes 49160 | tf_op jit(solution)/shard_map/while/body/eval_jaxpr/ppermute | solution.py:13
  135.8 1.9 collective-permute-done
  137.9 4.7 %collective-permute-start = (f32[16,16,16]{2,1,0:T(8,128)S(1)}, f32[16,16,16]{2,1,0:T(8,128)S(1)}, u32[]{:S(2)}, u32[]{:S(2)}) collective-permute-start(f32[16,16,16]{2,1,0:T(8,128)S(1)} %multiply_add_fusion.2), channel_id=1, source_target_pairs={{0,32},{32,64},{64,96},{96,128},{128,160},{160,192},{192,224},{1,3... | collective-permute-start | bytes 49160 | tf_op jit(solution)/shard_map/while/body/eval_jaxpr/ppermute | solution.py:13
  142.6 2.3 collective-permute-done
  144.9 5.0 %collective-permute-start = (f32[16,16,16]{2,1,0:T(8,128)S(1)}, f32[16,16,16]{2,1,0:T(8,128)S(1)}, u32[]{:S(2)}, u32[]{:S(2)}) collective-permute-start(f32[16,16,16]{2,1,0:T(8,128)S(1)} %multiply_add_fusion.2), channel_id=1, source_target_pairs={{0,32},{32,64},{64,96},{96,128},{128,160},{160,192},{192,224},{1,3... | collective-permute-start | bytes 49160 | tf_op jit(solution)/shard_map/while/body/eval_jaxpr/ppermute | solution.py:13
  149.9 3.1 collective-permute-done
  153.0 1.2 fusion.23
  154.5 12.8 %convolution_convert_fusion = bf16[1024,8192]{1,0:T(8,128)(2,1)} fusion(bf16[256,8192]{1,0:T(8,128)(2,1)} %param.13, f32[1024,256]{1,0:T(8,128)S(1)} %copy.23, f32[3,1024,256]{2,1,0:T(8,128)} %copy-done), kind=kOutput, calls=%fused_computation.24 | convolution fusion | flops 4303880192 | bytes 23068672 | tf_op jit(solution)/shard_map/dot_general | solution.py:93
  167.3 232.0 %reduce-scatter.2.cloned.1.call-done = bf16[32,8192]{1,0:T(8,128)(2,1)} async-done(((bf16[1024,8192]{1,0:T(8,128)(2,1)}), bf16[32,8192]{1,0:T(8,128)(2,1)}) %reduce-scatter.2.cloned.1.call-update) | async-done | bytes 524304 | tf_op jit(solution)/shard_map/reduce_scatter | solution.py:92
  (41 shorter events, 5.1 us)
Async XLA Ops:
  6.5 392.8 %reduce-scatter.2.cloned.1.call-start = ((), (), s32[]{:S(2)}) async-start(), calls=%async_computation.1 | async-start | bytes 17301504 | tf_op jit(solution)/shard_map/reduce_scatter | solution.py:92
  7.2 39.0 %collective-permute-start.1 = (bf16[3,2,256]{2,1,0:T(2,128)(2,1)S(1)}, bf16[3,2,256]{2,1,0:T(2,128)(2,1)S(1)}, u32[]{:S(2)}, u32[]{:S(2)}) collective-permute-start(bf16[3,2,256]{2,1,0:T(2,128)(2,1)S(1)} %slice.37), channel_id=1, source_target_pairs={{0,32},{32,64},{64,96},{96,128},{128,160},{160,192},{192,224},{1,3... | collective-permute-start | bytes 9224 | tf_op jit(solution)/shard_map/ppermute | solution.py:13
  40.7 5.5 %copy-start.1 = (bf16[3,1024,256]{2,1,0:T(8,128)(2,1)S(1)}, bf16[3,1024,256]{2,1,0:T(8,128)(2,1)}, u32[]{:S(2)}) copy-start(bf16[3,1024,256]{2,1,0:T(8,128)(2,1)} %param.9) | copy-start | bytes 4718596
  47.5 1.6 copy-start
  107.3 5.1 %collective-permute-start = (f32[16,16,16]{2,1,0:T(8,128)S(1)}, f32[16,16,16]{2,1,0:T(8,128)S(1)}, u32[]{:S(2)}, u32[]{:S(2)}) collective-permute-start(f32[16,16,16]{2,1,0:T(8,128)S(1)} %multiply_add_fusion.2), channel_id=1, source_target_pairs={{0,32},{32,64},{64,96},{96,128},{128,160},{160,192},{192,224},{1,3... | collective-permute-start | bytes 49160 | tf_op jit(solution)/shard_map/while/body/eval_jaxpr/ppermute | solution.py:13
  112.6 5.7 %collective-permute-start = (f32[16,16,16]{2,1,0:T(8,128)S(1)}, f32[16,16,16]{2,1,0:T(8,128)S(1)}, u32[]{:S(2)}, u32[]{:S(2)}) collective-permute-start(f32[16,16,16]{2,1,0:T(8,128)S(1)} %multiply_add_fusion.2), channel_id=1, source_target_pairs={{0,32},{32,64},{64,96},{96,128},{128,160},{160,192},{192,224},{1,3... | collective-permute-start | bytes 49160 | tf_op jit(solution)/shard_map/while/body/eval_jaxpr/ppermute | solution.py:13
  118.4 6.0 %collective-permute-start = (f32[16,16,16]{2,1,0:T(8,128)S(1)}, f32[16,16,16]{2,1,0:T(8,128)S(1)}, u32[]{:S(2)}, u32[]{:S(2)}) collective-permute-start(f32[16,16,16]{2,1,0:T(8,128)S(1)} %multiply_add_fusion.2), channel_id=1, source_target_pairs={{0,32},{32,64},{64,96},{96,128},{128,160},{160,192},{192,224},{1,3... | collective-permute-start | bytes 49160 | tf_op jit(solution)/shard_map/while/body/eval_jaxpr/ppermute | solution.py:13
  124.4 6.6 %collective-permute-start = (f32[16,16,16]{2,1,0:T(8,128)S(1)}, f32[16,16,16]{2,1,0:T(8,128)S(1)}, u32[]{:S(2)}, u32[]{:S(2)}) collective-permute-start(f32[16,16,16]{2,1,0:T(8,128)S(1)} %multiply_add_fusion.2), channel_id=1, source_target_pairs={{0,32},{32,64},{64,96},{96,128},{128,160},{160,192},{192,224},{1,3... | collective-permute-start | bytes 49160 | tf_op jit(solution)/shard_map/while/body/eval_jaxpr/ppermute | solution.py:13
  131.1 6.6 %collective-permute-start = (f32[16,16,16]{2,1,0:T(8,128)S(1)}, f32[16,16,16]{2,1,0:T(8,128)S(1)}, u32[]{:S(2)}, u32[]{:S(2)}) collective-permute-start(f32[16,16,16]{2,1,0:T(8,128)S(1)} %multiply_add_fusion.2), channel_id=1, source_target_pairs={{0,32},{32,64},{64,96},{96,128},{128,160},{160,192},{192,224},{1,3... | collective-permute-start | bytes 49160 | tf_op jit(solution)/shard_map/while/body/eval_jaxpr/ppermute | solution.py:13
  137.9 7.0 %collective-permute-start = (f32[16,16,16]{2,1,0:T(8,128)S(1)}, f32[16,16,16]{2,1,0:T(8,128)S(1)}, u32[]{:S(2)}, u32[]{:S(2)}) collective-permute-start(f32[16,16,16]{2,1,0:T(8,128)S(1)} %multiply_add_fusion.2), channel_id=1, source_target_pairs={{0,32},{32,64},{64,96},{96,128},{128,160},{160,192},{192,224},{1,3... | collective-permute-start | bytes 49160 | tf_op jit(solution)/shard_map/while/body/eval_jaxpr/ppermute | solution.py:13
  144.9 8.1 %collective-permute-start = (f32[16,16,16]{2,1,0:T(8,128)S(1)}, f32[16,16,16]{2,1,0:T(8,128)S(1)}, u32[]{:S(2)}, u32[]{:S(2)}) collective-permute-start(f32[16,16,16]{2,1,0:T(8,128)S(1)} %multiply_add_fusion.2), channel_id=1, source_target_pairs={{0,32},{32,64},{64,96},{96,128},{128,160},{160,192},{192,224},{1,3... | collective-permute-start | bytes 49160 | tf_op jit(solution)/shard_map/while/body/eval_jaxpr/ppermute | solution.py:13
Sparse Core Ops, SparseCore 0:
  167.5 231.8 reduce-scatter.1
where the time goes:
time: 410 us; the launch traced here: 406 us
  waiting for transfers between devices  247 us (60%)
  local copies, waits for them, and re-layouts  67.4 us (16%)
  matrix products  40.8 us (10%)
  starting transfers between devices  33.9 us (8%)
  between operations  13.6 us (3%)
    reduce_scatter x1, waiting for transfers between devices, local(): lax.psum_scatter(jnp.dot(mixed, out_weight, preferred_element_type=jnp.fl...  232 us
    ppermute x8, starting transfers between devices, passed_along(): lax.ppermute(value, axis, [(source, source + steps) for source in range(l...  33.9 us
    dynamic_update_slice x8, local copies, waits for them, and re-layouts, causal_conv(): state_end, outputs = lax.scan(advance, state_start, segments)  27.2 us
    dot_general x4, matrix products, advance(): jnp.einsum('gts,sgi->tgi', toeplitz, segment, precision=lax.Precision.HIG...  22.7 us
    ppermute x8, waiting for transfers between devices, passed_along(): lax.ppermute(value, axis, [(source, source + steps) for source in range(l...  15 us
    dot_general x1, matrix products, local(): jnp.dot(mixed, out_weight, preferred_element_type=jnp.float32)  12.8 us
    unnamed x8, local copies, waits for them, and re-layouts  12 us
    reshape x1, local copies, waits for them, and re-layouts, toeplitz_from(): tiled[:, :block_len * width].reshape(group_count, block_len, width)  11.8 us
  transfers between devices with their start and end apart: 9, of which 8 were waited for; matrix products, arithmetic and copies ran while one was open for 9% of the time, Pallas kernels for 0%

commit v1 on v0

v1 whole, which is shorter than its diff:
```python
import jax
import jax.numpy as jnp
from jax import lax
from jax.experimental import pallas as pl
from jax.experimental.pallas import tpu as pltpu
from jax.sharding import Mesh, PartitionSpec as P

GROUP = 16
MODES = 16
CHUNK = 128
LANES = 128
BF = jnp.bfloat16
F32 = jnp.float32
VM = pl.BlockSpec(memory_space=pltpu.VMEM)
SM = pl.BlockSpec(memory_space=pltpu.SMEM)


def iota(shape, dim):
    return lax.broadcasted_iota(jnp.int32, shape, dim)


def spread(state):
    width = state.shape[1]
    groups = width // GROUP
    tall = jnp.concatenate([state] * groups, axis=0)
    shape = (groups * MODES, width)
    own = iota(shape, 0) // MODES == iota(shape, 1) // GROUP
    return jnp.where(own, tall, 0.0).astype(BF)


def conv_kernel(p_ref, halo_ref, sf_ref, rcol_ref, wcol_ref, rrow_ref, wrow_ref, rt_ref,
                y_ref, q_ref, end_ref, din_ref, table, masked):
    rows, channels = p_ref.shape[1], p_ref.shape[2]
    halves = channels // LANES
    per_half = LANES // GROUP
    groups = channels // GROUP
    rcol = rcol_ref[...]
    wcol = wcol_ref[...]
    lane = iota((groups * MODES, CHUNK), 1)
    back = jnp.where(lane == 0, 0, CHUNK - lane).astype(F32)
    taps = (wcol * jnp.exp(-rcol * back)).reshape(groups, MODES, CHUNK).sum(axis=1)
    leave = jnp.exp(-rcol * (CHUNK - 1 - lane).astype(F32)).astype(BF)
    causal = iota((CHUNK, CHUNK), 0) >= iota((CHUNK, CHUNK), 1)
    for g in range(groups):
        wide = jnp.broadcast_to(taps[g : g + 1, :], (CHUNK, CHUNK))
        turned = pltpu.roll(wide, 0, 1, stride=1, stride_axis=0)
        table[0:CHUNK, g * CHUNK : (g + 1) * CHUNK] = jnp.where(causal, turned, 0.0).astype(BF)
        table[CHUNK : CHUNK + MODES, g * CHUNK : (g + 1) * CHUNK] = leave[g * MODES : (g + 1) * MODES]
    steps = (iota((CHUNK, groups * MODES), 0) + 1).astype(F32)
    din = (wrow_ref[...] * jnp.exp(-rrow_ref[...] * steps)).astype(BF)
    din_ref[...] = din
    power = jnp.exp(-rt_ref[...] * float(CHUNK))
    group_lane = iota((CHUNK, LANES), 1) // GROUP

    def featured(i, q):
        cur = p_ref[i, q * CHUNK : (q + 1) * CHUNK, :].astype(F32)
        if q == 0:
            before = halo_ref[i].astype(F32)
        else:
            before = p_ref[i, q * CHUNK - 16 : q * CHUNK, :].astype(F32)
        ext = jnp.concatenate([before, cur], axis=0)
        skip = before.shape[0]
        one = pltpu.roll(ext, 1, 0)[skip:]
        two = pltpu.roll(ext, 2, 0)[skip:]
        return sf_ref[i, 0:1, :] * cur + sf_ref[i, 1:2, :] * one + sf_ref[i, 2:3, :] * two

    state = jnp.zeros((MODES, channels), F32)
    for pair in range(rows // (2 * CHUNK)):
        for j in range(2):
            q = 2 * pair + j
            q_ref[q * CHUNK : (q + 1) * CHUNK, :] = featured(0, q)
            signal = (featured(1, q) * featured(2, q)).astype(BF)
            for h in range(halves):
                part = signal[:, h * LANES : (h + 1) * LANES]
                for g in range(per_half):
                    masked[h, g * CHUNK : (g + 1) * CHUNK, j * LANES : (j + 1) * LANES] = jnp.where(
                        group_lane == g, part, jnp.zeros_like(part)
                    )
        span = per_half * CHUNK
        made = [
            jnp.dot(table[:, h * span : (h + 1) * span], masked[h], preferred_element_type=F32)
            for h in range(halves)
        ]
        for j in range(2):
            q = 2 * pair + j
            full = jnp.concatenate([m[:, j * LANES : (j + 1) * LANES] for m in made], axis=1)
            within = full[:CHUNK]
            if q > 0:
                within = within + jnp.dot(din, spread(state), preferred_element_type=F32)
            y_ref[q * CHUNK : (q + 1) * CHUNK, :] = within
            state = power * state + full[CHUNK:]
    end_ref[...] = state


def mix_kernel(at_ref, ends_ref, rt_ref, din_ref, y_ref, q_ref, mixed_ref):
    rows = y_ref.shape[0]
    here = at_ref[0]
    block_power = jnp.exp(-rt_ref[...] * float(rows))
    state = jnp.zeros(rt_ref.shape, F32)
    for j in range(ends_ref.shape[0]):
        state = jnp.where(j < here, block_power * state + ends_ref[j], state)
    power = jnp.exp(-rt_ref[...] * float(CHUNK))
    din = din_ref[...]
    for q in range(rows // CHUNK):
        span = slice(q * CHUNK, (q + 1) * CHUNK)
        carried = jnp.dot(din, spread(state), preferred_element_type=F32)
        mixed_ref[span, :] = (q_ref[span, :] * (y_ref[span, :] + carried)).astype(BF)
        state = power * state


def product_kernel(at_ref, a0, a1, a2, a3, w0, w1, m1, r1, r2, r3, m2, c_ref, wx):
    y, mine = at_ref[1], at_ref[2]
    piece = m1.shape[1]
    tail = m2.shape[1]

    @pl.when(pl.program_id(0) == 0)
    def _():
        for k, ref in enumerate((m1, r1, r2, r3)):
            start = pl.multiple_of(lax.rem(y - k + 4, 4) * piece, 16)
            for s in range(2):
                wx[s, pl.ds(start, piece), :] = ref[s]
        for s in range(2):
            wx[s, 4 * piece : 4 * piece + tail, :] = m2[s]

    tile = 512
    for n in range(c_ref.shape[1] // tile):
        cols = slice(n * tile, (n + 1) * tile)
        total = jnp.dot(a0[...], w0[:, cols], preferred_element_type=F32)
        total += jnp.dot(a1[...], w1[:, cols], preferred_element_type=F32)
        total += jnp.dot(a2[...], wx[0, :, cols], preferred_element_type=F32)
        total += jnp.dot(a3[...], wx[1, :, cols], preferred_element_type=F32)
        total = total.astype(BF)
        for b in range(total.shape[0] // 32):
            high, low = b // 4, b % 4
            place = pl.multiple_of((high * 4 + jnp.bitwise_xor(low, mine)) * 32, 32)
            c_ref[pl.ds(place, 32), cols] = total[b * 32 : (b + 1) * 32]


def join_kernel(at_ref, p0, p1, p2, p3, out_ref):
    mine = at_ref[2]
    width = p0.shape[1]
    for k, ref in enumerate((p0, p1, p2, p3)):
        place = pl.multiple_of(jnp.bitwise_xor(mine, k) * width, width)
        out_ref[:, pl.ds(place, width)] = ref[...]


def other_core(value):
    return lax.ppermute(value, "c", [(0, 1), (1, 0)])


def local(projected, short_filter, residue, rate, out_weight):
    rows, channels = projected.shape[1], projected.shape[2]
    groups = rate.shape[0]
    width = out_weight.shape[1] // 4
    y, xh, core = lax.axis_index("y"), lax.axis_index("xh"), lax.axis_index("c")
    seq = lax.axis_index(("y", "xl"))
    at = jnp.stack([seq, y, xh * 2 + core]).astype(jnp.int32)

    halo = lax.ppermute(projected[:, rows - 8 :, :], ("y", "xl"), [(i, i + 1) for i in range(7)])

    def columns(h, k):
        return lax.dynamic_slice(out_weight, (0, (h * 2 + k) * width), (channels, width))

    w_mine = columns(xh, core)
    o_mine = columns(1 - xh, core)
    o_other = other_core(columns(1 - xh, 1 - core))
    w_other = other_core(columns(xh, 1 - core))
    piece = 48
    mirror = [(0, 3), (3, 0), (1, 2), (2, 1)]

    def rows_of(start, size):
        return jnp.stack([lax.dynamic_slice(v, (start, 0), (size, width)) for v in (o_mine, o_other)])

    m1 = lax.ppermute(rows_of(y * piece, piece), ("xl", "xh"), mirror)
    m2 = lax.ppermute(rows_of(4 * piece, channels - 4 * piece), ("xl", "xh"), mirror)
    r1, r2, r3 = (lax.ppermute(m1, "y", [(i, (i + k) % 4) for i in range(4)]) for k in (1, 2, 3))

    weight = residue * jnp.sqrt(-jnp.expm1(-2.0 * rate))
    rt = jnp.repeat(rate.T, GROUP, axis=1)
    flat = groups * MODES
    conv, query, end, din = pl.pallas_call(
        conv_kernel,
        out_shape=(
            jax.ShapeDtypeStruct((rows, channels), F32),
            jax.ShapeDtypeStruct((rows, channels), F32),
            jax.ShapeDtypeStruct((MODES, channels), F32),
            jax.ShapeDtypeStruct((CHUNK, flat), BF),
        ),
        in_specs=[VM] * 8,
        out_specs=(VM, VM, VM, VM),
        scratch_shapes=[
            pltpu.VMEM((CHUNK + MODES, groups * CHUNK), BF),
            pltpu.VMEM((channels // LANES, LANES // GROUP * CHUNK, 2 * LANES), BF),
        ],
        cost_estimate=pl.CostEstimate(flops=2 * 10**9, bytes_accessed=4 * 2**20, transcendentals=10**5),
        name="conv",
    )(
        projected, halo, short_filter,
        rate.reshape(flat, 1), weight.reshape(flat, 1), rate.reshape(1, flat), weight.reshape(1, flat), rt,
    )
    ends = lax.all_to_all(jnp.broadcast_to(end[None], (8,) + end.shape), ("y", "xl"), 0, 0, tiled=True)
    mixed = pl.pallas_call(
        mix_kernel,
        out_shape=jax.ShapeDtypeStruct((rows, channels), BF),
        in_specs=[SM] + [VM] * 5,
        out_specs=VM,
        cost_estimate=pl.CostEstimate(flops=2 * 10**8, bytes_accessed=3 * 2**20, transcendentals=10**4),
        name="mix",
    )(at, ends, rt, din, conv, query)

    a_far = lax.ppermute(mixed, "xh", [(0, 1), (1, 0)])
    a_other = other_core(mixed)
    a_far_other = other_core(a_far)

    block = 256
    a_spec = pl.BlockSpec((block, channels), lambda i: (i, 0))

    def whole(shape):
        return pl.BlockSpec(shape, lambda i: (0,) * len(shape))

    partial = pl.pallas_call(
        product_kernel,
        out_shape=jax.ShapeDtypeStruct((rows, width), BF),
        grid=(rows // block,),
        in_specs=[SM] + [a_spec] * 4 + [whole((channels, width))] * 2 + [whole(m1.shape)] * 4 + [whole(m2.shape)],
        out_specs=pl.BlockSpec((block, width), lambda i: (i, 0)),
        scratch_shapes=[pltpu.VMEM((2, channels, width), BF)],
        cost_estimate=pl.CostEstimate(flops=4 * 10**9, bytes_accessed=10 * 2**20, transcendentals=0),
        name="product",
    )(at, mixed, a_other, a_far, a_far_other, w_mine, w_other, m1, r1, r2, r3, m2)

    summed = lax.psum_scatter(partial, "z", scatter_dimension=0, tiled=True)
    size = summed.shape[0] // 4

    def traded(k):
        pairs = [(i, i ^ k) for i in range(4)]
        return lax.ppermute(summed[k * size : (k + 1) * size], ("xh", "c"), pairs)

    return pl.pallas_call(
        join_kernel,
        out_shape=jax.ShapeDtypeStruct((size, 4 * width), BF),
        in_specs=[SM] + [VM] * 4,
        out_specs=VM,
        name="join",
    )(at, summed[:size], traded(1), traded(2), traded(3))


def solution(mesh):
    fine = Mesh(mesh.devices.reshape(4, 2, 8, 2, 2), ("y", "xl", "z", "xh", "c"))
    seq, tp = ("y", "xl"), ("z", "xh", "c")
    placed = (P(None, seq, tp), P(None, None, tp), P(tp, None), P(tp, None), P(tp, None))
    return jax.shard_map(local, mesh=fine, in_specs=placed, out_specs=P(seq + tp, None), check_vma=False)
```

time: 410 us -> 178 us (0.43)
  waiting for transfers between devices: 247 us -> 103 us
  local copies, waits for them, and re-layouts: 67.4 us -> 15.6 us
  matrix products: 40.8 us -> 0 us
  Pallas kernels: 0 us -> 19.4 us
  starting transfers between devices: 33.9 us -> 25.2 us
    reduce_scatter x1, waiting for transfers between devices: 232 us -> 55.9 us  [local(): summed = lax.psum_scatter(partial, 'z', scatter_dimension=0, tiled=True)]
    dot_general x15 -> x0, matrix products: 40.8 us -> none  [the longest x4 22.7 us: advance(): jnp.einsum('gts,sgi->tgi', toeplitz, segment, precision=lax.Precision.HIG...]
    ppermute x8 -> x14, waiting for transfers between devices: 15 us -> 42.5 us  [the longest x3 10.6 us: local(): lax.ppermute(m1, 'y', [(i, (i + k) % 4) for i in range(4)])]
    dynamic_update_slice x8 -> x0, local copies, waits for them, and re-layouts: 27.2 us -> none  [causal_conv(): state_end, outputs = lax.scan(advance, state_start, segments)]
    pallas_call x0 -> x4, Pallas kernels: none -> 19.4 us  [the longest x1 8.91 us: local(): pl.pallas_call(product_kernel, out_shape=jax.ShapeDtypeStruct((rows, widt...]
    ppermute x8 -> x14, starting transfers between devices: 33.9 us -> 20.3 us  [the longest x4 5.09 us: other_core(): return lax.ppermute(value, 'c', [(0, 1), (1, 0)])]
    reshape x3 -> x5, local copies, waits for them, and re-layouts: 13.9 us -> 3.53 us  [the longest x1 0.75 us: local(): rate.reshape(flat, 1)]
    unnamed x8 -> x28, local copies, waits for them, and re-layouts: 12 us -> 2.71 us
  transfers between devices with their start and end apart: 9 -> 16, of which waited for: 8 -> 9; matrix products, arithmetic and copies ran while one was open for 9% -> 6% of each run, Pallas kernels for 0% -> 5%
where the time goes in v1:
time: 178 us
  waiting for transfers between devices  103 us (58%)
  starting transfers between devices  25.2 us (14%)
  Pallas kernels  19.4 us (11%)
  local copies, waits for them, and re-layouts  15.6 us (9%)
  between operations  13.5 us (8%)
    reduce_scatter x1, waiting for transfers between devices, local(): summed = lax.psum_scatter(partial, 'z', scatter_dimension=0, tiled=True)  55.9 us
    ppermute x3, waiting for transfers between devices, local(): lax.ppermute(m1, 'y', [(i, (i + k) % 4) for i in range(4)])  10.6 us
    ppermute x1, waiting for transfers between devices, local(): lax.ppermute(rows_of(4 * piece, channels - 4 * piece), ('xl', 'xh'), mirror)  9.22 us
    ppermute x1, waiting for transfers between devices, local(): m1 = lax.ppermute(rows_of(y * piece, piece), ('xl', 'xh'), mirror)  9.11 us
    pallas_call x1, Pallas kernels, local(): pl.pallas_call(product_kernel, out_shape=jax.ShapeDtypeStruct((rows, widt...  8.91 us
    ppermute x1, waiting for transfers between devices, local(): a_far = lax.ppermute(mixed, 'xh', [(0, 1), (1, 0)])  7.21 us
    ppermute x3, waiting for transfers between devices, traded(): return lax.ppermute(summed[k * size:(k + 1) * size], ('xh', 'c'), pairs)  6.38 us
    pallas_call x1, Pallas kernels, local(): pl.pallas_call(conv_kernel, out_shape=(jax.ShapeDtypeStruct((rows, channe...  5.84 us
  transfers between devices with their start and end apart: 16, of which 9 were waited for; matrix products, arithmetic and copies ran while one was open for 6% of the time, Pallas kernels for 5%

profile of v1, /device:TPU:1, one launch (start us, length us, event | category | flops | bytes accessed | tf_op | source)
XLA Modules:
  0.0 177.8 jit_solution(13820192568675858362)
XLA Ops:
  6.5 0.7 slice.15
  7.3 3.9 %collective-permute-start = (bf16[3,8,256]{2,1,0:T(8,128)(2,1)S(1)}, bf16[3,8,256]{2,1,0:T(8,128)(2,1)S(1)}, u32[]{:S(2)}, u32[]{:S(2)}) collective-permute-start(bf16[3,8,256]{2,1,0:T(8,128)(2,1)S(1)} %slice.15), channel_id=1, source_target_pairs={{0,32},{32,64},{64,96},{96,128},{128,160},{160,192},{192,224},{1,3... | collective-permute-start | bytes 36872 | tf_op jit(solution)/shard_map/ppermute | solution.py:159
  11.2 3.2 %constant_dynamic-slice_fusion = (bf16[256,2048]{1,0:T(8,128)(2,1)S(1)}, bf16[256,2048]{1,0:T(8,128)(2,1)S(1)}, bf16[256,2048]{1,0:T(8,128)(2,1)}) fusion(bf16[256,8192]{1,0:T(8,128)(2,1)} %param.9, s32[]{:T(128)S(6)} %select_n.26, s32[]{:T(128)S(6)} %select_n.21, s32[]{:T(128)S(6)} %select_n.20), kind=kLoop, calls=%fused_computation.7 | loop fusion | bytes 6291468 | tf_op jit(solution)/shard_map/dynamic_slice | solution.py:162
  14.4 1.0 collective-permute-start.5
  15.4 0.7 reshape.18.rrow_ref
  16.1 0.6 reshape.19.wrow_ref
  16.7 0.7 reshape.22.wcol_ref
  17.5 0.8 reshape.21.rcol_ref
  18.2 0.1 copy.7
  18.3 0.1 broadcast_in_dim.4
  18.4 0.7 reshape.20.rt_ref
  19.1 0.6 copy-done.13
  19.7 5.8 %conv.1 = (f32[1024,256]{1,0:T(8,128)}, f32[1024,256]{1,0:T(8,128)}, f32[16,256]{1,0:T(8,128)}, bf16[128,256]{1,0:T(8,128)(2,1)}) custom-call(bf16[3,1024,256]{2,1,0:T(8,128)(2,1)} %p_ref.1, bf16[3,8,256]{2,1,0:T(8,128)(2,1)} %copy-done.13, f32[3,3,256]{2,1,0:T(4,128)} %sf_ref.1, f32[256,1]{1,0:T(8,128)} %reshape.21.rcol_ref, f32[256,1]{1,0:T(8,128)} %reshape.22.wcol_ref, ...), custom_call_target="tpu_custom_call" | custom-call | flops 2000000000 | bytes 4194304 | tf_op jit(solution)/shard_map/conv/pallas_call | solution.py:181
  25.5 1.4 broadcast_in_dim.10
  26.9 4.9 %all-to-all-start = ((f32[8,16,256]{2,1,0:T(8,128)}), f32[8,16,256]{2,1,0:T(8,128)S(1)}, u32[]{:S(2)}, u32[]{:S(2)}) async-start(f32[8,16,256]{2,1,0:T(8,128)} %broadcast_in_dim.10), calls=%async_computation | async-start | bytes 262144 | tf_op jit(solution)/shard_map/all_to_all | solution.py:201
  31.9 0.6 pad_add_fusion.at_ref
  32.5 4.9 %all-to-all-done.ends_ref = f32[8,16,256]{2,1,0:T(8,128)S(1)} async-done(((f32[8,16,256]{2,1,0:T(8,128)}), f32[8,16,256]{2,1,0:T(8,128)S(1)}, u32[]{:S(2)}, u32[]{:S(2)}) %all-to-all-start) | async-done | bytes 131104 | tf_op jit(solution)/shard_map/all_to_all | solution.py:201
  37.4 0.6 copy-done
  38.0 2.8 %mix.1.a0 = bf16[1024,256]{1,0:T(8,128)(2,1)} custom-call(s32[3]{0:T(128)} %pad_add_fusion.at_ref, f32[8,16,256]{2,1,0:T(8,128)} %copy-done, f32[16,256]{1,0:T(8,128)} %reshape.20.rt_ref, bf16[128,256]{1,0:T(8,128)(2,1)} %get-tuple-element.10.din_ref, f32[1024,256]{1,0:T(8,128)} %get-tuple-element.11.y_ref, f32[1024,256]{1,0:T(8,128)} %get-tuple-element.12.q_ref), custom_call_target="tpu_custom_call" | custom-call | flops 200000000 | bytes 3145728 | tf_op jit(solution)/shard_map/mix/pallas_call | solution.py:202
  40.8 2.7 %collective-permute-start.2 = (bf16[1024,256]{1,0:T(8,128)(2,1)}, bf16[1024,256]{1,0:T(8,128)(2,1)}, u32[]{:S(2)}, u32[]{:S(2)}) collective-permute-start(bf16[1024,256]{1,0:T(8,128)(2,1)} %mix.1.a0), channel_id=1, source_target_pairs={{0,2},{2,0},{1,3},{3,1},{4,6},{6,4},{5,7},{7,5},{8,10},{10,8},{9,1... | collective-permute-start | bytes 1572872 | tf_op jit(solution)/shard_map/ppermute | solution.py:211
  43.5 1.7 collective-permute-start.4
  45.2 1.1 dynamic-slice_bitcast_fusion.2
  46.3 1.0 dynamic-slice_bitcast_fusion
  47.3 0.1 collective-permute-start.1
  47.4 7.2 %collective-permute-done.2.a2 = bf16[1024,256]{1,0:T(8,128)(2,1)} collective-permute-done((bf16[1024,256]{1,0:T(8,128)(2,1)}, bf16[1024,256]{1,0:T(8,128)(2,1)}, u32[]{:S(2)}, u32[]{:S(2)}) %collective-permute-start.2) | collective-permute-done | bytes 524320 | tf_op jit(solution)/shard_map/ppermute | solution.py:211
  54.6 2.3 %collective-permute-start.3 = (bf16[1024,256]{1,0:T(8,128)(2,1)}, bf16[1024,256]{1,0:T(8,128)(2,1)S(1)}, u32[]{:S(2)}, u32[]{:S(2)}) collective-permute-start(bf16[1024,256]{1,0:T(8,128)(2,1)} %collective-permute-done.2.a2), channel_id=1, source_target_pairs={{0,1},{1,0},{2,3},{3,2},{4,5},{5,4},{6,7},{7,6},{8,9},{9,8},{10,11... | collective-permute-start | bytes 1572872 | tf_op jit(solution)/shard_map/ppermute | solution.py:148
  57.0 2.4 %collective-permute-start.6 = (bf16[2,48,2048]{2,1,0:T(8,128)(2,1)S(1)}, bf16[2,48,2048]{2,1,0:T(8,128)(2,1)S(1)}, u32[]{:S(2)}, u32[]{:S(2)}) collective-permute-start(bf16[2,48,2048]{2,1,0:T(8,128)(2,1)S(1)} %pad_maximum_fusion.1), channel_id=1, source_target_pairs={{0,34},{34,0},{2,32},{32,2},{1,35},{35,1},{3,33},{33,3},{4,38},{38... | collective-permute-start | bytes 1179656 | tf_op jit(solution)/shard_map/ppermute | solution.py:174
  59.4 0.1 pad_maximum_fusion
  59.5 0.5 collective-permute-start.10
  59.9 9.1 %collective-permute-done.6.m1 = bf16[2,48,2048]{2,1,0:T(8,128)(2,1)S(1)} collective-permute-done((bf16[2,48,2048]{2,1,0:T(8,128)(2,1)S(1)}, bf16[2,48,2048]{2,1,0:T(8,128)(2,1)S(1)}, u32[]{:S(2)}, u32[]{:S(2)}) %collective-permute-start.6) | collective-permute-done | bytes 393248 | tf_op jit(solution)/shard_map/ppermute | solution.py:174
  69.0 0.9 collective-permute-start.9
  69.9 1.0 collective-permute-start.8
  71.0 0.1 collective-permute-start.7
  71.1 9.2 %collective-permute-done.10.m2 = bf16[2,64,2048]{2,1,0:T(8,128)(2,1)S(1)} collective-permute-done((bf16[2,64,2048]{2,1,0:T(8,128)(2,1)S(1)}, bf16[2,64,2048]{2,1,0:T(8,128)(2,1)S(1)}, u32[]{:S(2)}, u32[]{:S(2)}) %collective-permute-start.10) | collective-permute-done | bytes 524320 | tf_op jit(solution)/shard_map/ppermute | solution.py:175
  80.3 0.3 collective-permute-done.8.r2
  80.7 10.3 %collective-permute-done.7.r1 = bf16[2,48,2048]{2,1,0:T(8,128)(2,1)S(1)} collective-permute-done((bf16[2,48,2048]{2,1,0:T(8,128)(2,1)S(1)}, bf16[2,48,2048]{2,1,0:T(8,128)(2,1)S(1)}, u32[]{:S(2)}, u32[]{:S(2)}) %collective-permute-start.7) | collective-permute-done | bytes 393248 | tf_op jit(solution)/shard_map/ppermute | solution.py:176
  90.9 0.7 copy-done.12
  91.7 8.9 %product.1 = bf16[1024,2048]{1,0:T(8,128)(2,1)} custom-call(s32[3]{0:T(128)} %pad_add_fusion.at_ref, bf16[1024,256]{1,0:T(8,128)(2,1)} %mix.1.a0, bf16[1024,256]{1,0:T(8,128)(2,1)} %copy-done.6, bf16[1024,256]{1,0:T(8,128)(2,1)} %collective-permute-done.2.a2, bf16[1024,256]{1,0:T(8,128)(2,1)} %copy-done.7, bf16[256,2048]{1,0:T(8,128)(2,1)} %get-tuple-element.15.w0, ...), custom_call_target="tpu_custom_call" | custom-call | flops 4000000000 | bytes 10485760 | tf_op jit(solution)/shard_map/product/pallas_call | solution.py:221
  100.6 55.9 %reduce-scatter.2.cloned.1.call-done = bf16[128,2048]{1,0:T(8,128)(2,1)} async-done(((bf16[1024,2048]{1,0:T(8,128)(2,1)}), bf16[128,2048]{1,0:T(8,128)(2,1)}) %reduce-scatter.2.cloned.1.call-update) | async-done | bytes 524304 | tf_op jit(solution)/shard_map/reduce_scatter | solution.py:232
  156.5 1.8 %fusion = (bf16[32,2048]{1,0:T(8,128)(2,1)S(1)}, bf16[32,2048]{1,0:T(8,128)(2,1)S(1)}, bf16[32,2048]{1,0:T(8,128)(2,1)S(1)}, bf16[32,2048]{1,0:T(8,128)(2,1)}) fusion(bf16[128,2048]{1,0:T(8,128)(2,1)} %reduce-scatter.2.cloned.1.call-done), kind=kLoop, calls=%fused_computation.11 | loop fusion | bytes 1048576 | tf_op jit(solution)/shard_map/slice | solution.py:237
  158.2 3.2 %collective-permute-start.13 = (bf16[32,2048]{1,0:T(8,128)(2,1)S(1)}, bf16[32,2048]{1,0:T(8,128)(2,1)S(1)}, u32[]{:S(2)}, u32[]{:S(2)}) collective-permute-start(bf16[32,2048]{1,0:T(8,128)(2,1)S(1)} %get-tuple-element.16), channel_id=1, source_target_pairs={{0,3},{1,2},{2,1},{3,0},{4,7},{5,6},{6,5},{7,4},{8,11},{9,10},{10,... | collective-permute-start | bytes 393224 | tf_op jit(solution)/shard_map/ppermute | solution.py:237
  161.5 0.3 collective-permute-start.12
  161.7 0.2 collective-permute-start.11
  161.9 3.8 %collective-permute-done.13.p3 = bf16[32,2048]{1,0:T(8,128)(2,1)S(1)} collective-permute-done((bf16[32,2048]{1,0:T(8,128)(2,1)S(1)}, bf16[32,2048]{1,0:T(8,128)(2,1)S(1)}, u32[]{:S(2)}, u32[]{:S(2)}) %collective-permute-start.13) | collective-permute-done | bytes 131104 | tf_op jit(solution)/shard_map/ppermute | solution.py:237
  165.7 2.6 %collective-permute-done.12.p2 = bf16[32,2048]{1,0:T(8,128)(2,1)S(1)} collective-permute-done((bf16[32,2048]{1,0:T(8,128)(2,1)S(1)}, bf16[32,2048]{1,0:T(8,128)(2,1)S(1)}, u32[]{:S(2)}, u32[]{:S(2)}) %collective-permute-start.12) | collective-permute-done | bytes 131104 | tf_op jit(solution)/shard_map/ppermute | solution.py:237
  168.3 0.6 copy-done.3
  168.9 0.1 copy-done.4
  169.0 1.9 %join.1 = bf16[32,8192]{1,0:T(8,128)(2,1)} custom-call(s32[3]{0:T(128)} %pad_add_fusion.at_ref, bf16[32,2048]{1,0:T(8,128)(2,1)} %get-tuple-element.19.p0, bf16[32,2048]{1,0:T(8,128)(2,1)} %copy-done.4, bf16[32,2048]{1,0:T(8,128)(2,1)} %copy-done.3, bf16[32,2048]{1,0:T(8,128)(2,1)} %copy-done.2), custom_call_target="tpu_custom_call" | custom-call | tf_op jit(solution)/shard_map/join/pallas_call | solution.py:239
  (36 shorter events, 0.2 us)
Async XLA Ops:
  6.5 8.8 %copy-start.1 = (f32[16,16]{1,0:T(8,128)S(1)}, f32[16,16]{1,0:T(8,128)}, u32[]{:S(2)}) copy-start(f32[16,16]{1,0:T(8,128)} %param.8) | copy-start | bytes 3076
  6.5 8.8 %copy-start.5 = (f32[16,16]{1,0:T(8,128)S(1)}, f32[16,16]{1,0:T(8,128)}, u32[]{:S(2)}) copy-start(f32[16,16]{1,0:T(8,128)} %param.7) | copy-start | bytes 3076
  7.3 11.8 %collective-permute-start = (bf16[3,8,256]{2,1,0:T(8,128)(2,1)S(1)}, bf16[3,8,256]{2,1,0:T(8,128)(2,1)S(1)}, u32[]{:S(2)}, u32[]{:S(2)}) collective-permute-start(bf16[3,8,256]{2,1,0:T(8,128)(2,1)S(1)} %slice.15), channel_id=1, source_target_pairs={{0,32},{32,64},{64,96},{96,128},{128,160},{160,192},{192,224},{1,3... | collective-permute-start | bytes 36872 | tf_op jit(solution)/shard_map/ppermute | solution.py:159
  14.4 42.5 %collective-permute-start.5 = (bf16[256,2048]{1,0:T(8,128)(2,1)S(1)}, bf16[256,2048]{1,0:T(8,128)(2,1)S(1)}, u32[]{:S(2)}, u32[]{:S(2)}) collective-permute-start(bf16[256,2048]{1,0:T(8,128)(2,1)S(1)} %get-tuple-element.13), channel_id=1, source_target_pairs={{0,1},{1,0},{2,3},{3,2},{4,5},{5,4},{6,7},{7,6},{8,9},{9,8},{10,11... | collective-permute-start | bytes 3145736 | tf_op jit(solution)/shard_map/ppermute | solution.py:148
  19.1 0.6 copy-start.13
  26.9 10.5 %all-to-all-start = ((f32[8,16,256]{2,1,0:T(8,128)}), f32[8,16,256]{2,1,0:T(8,128)S(1)}, u32[]{:S(2)}, u32[]{:S(2)}) async-start(f32[8,16,256]{2,1,0:T(8,128)} %broadcast_in_dim.10), calls=%async_computation | async-start | bytes 262144 | tf_op jit(solution)/shard_map/all_to_all | solution.py:201
  31.8 124.7 %reduce-scatter.2.cloned.1.call-start = ((), (), s32[]{:S(2)}) async-start(), calls=%async_computation.2 | async-start | bytes 4718592 | tf_op jit(solution)/shard_map/reduce_scatter | solution.py:232
  37.4 0.6 copy-start
  40.8 13.8 %collective-permute-start.2 = (bf16[1024,256]{1,0:T(8,128)(2,1)}, bf16[1024,256]{1,0:T(8,128)(2,1)}, u32[]{:S(2)}, u32[]{:S(2)}) collective-permute-start(bf16[1024,256]{1,0:T(8,128)(2,1)} %mix.1.a0), channel_id=1, source_target_pairs={{0,2},{2,0},{1,3},{3,1},{4,6},{6,4},{5,7},{7,5},{8,10},{10,8},{9,1... | collective-permute-start | bytes 1572872 | tf_op jit(solution)/shard_map/ppermute | solution.py:211
  43.5 27.4 %collective-permute-start.4 = (bf16[256,2048]{1,0:T(8,128)(2,1)S(1)}, bf16[256,2048]{1,0:T(8,128)(2,1)}, u32[]{:S(2)}, u32[]{:S(2)}) collective-permute-start(bf16[256,2048]{1,0:T(8,128)(2,1)S(1)} %get-tuple-element.14), channel_id=1, source_target_pairs={{0,1},{1,0},{2,3},{3,2},{4,5},{5,4},{6,7},{7,6},{8,9},{9,8},{10,11... | collective-permute-start | bytes 3145736 | tf_op jit(solution)/shard_map/ppermute | solution.py:148
  47.3 22.7 %collective-permute-start.1 = (bf16[1024,256]{1,0:T(8,128)(2,1)}, bf16[1024,256]{1,0:T(8,128)(2,1)S(1)}, u32[]{:S(2)}, u32[]{:S(2)}) collective-permute-start(bf16[1024,256]{1,0:T(8,128)(2,1)} %mix.1.a0), channel_id=1, source_target_pairs={{0,1},{1,0},{2,3},{3,2},{4,5},{5,4},{6,7},{7,6},{8,9},{9,8},{10,11... | collective-permute-start | bytes 1572872 | tf_op jit(solution)/shard_map/ppermute | solution.py:148
  54.6 16.5 %collective-permute-start.3 = (bf16[1024,256]{1,0:T(8,128)(2,1)}, bf16[1024,256]{1,0:T(8,128)(2,1)S(1)}, u32[]{:S(2)}, u32[]{:S(2)}) collective-permute-start(bf16[1024,256]{1,0:T(8,128)(2,1)} %collective-permute-done.2.a2), channel_id=1, source_target_pairs={{0,1},{1,0},{2,3},{3,2},{4,5},{5,4},{6,7},{7,6},{8,9},{9,8},{10,11... | collective-permute-start | bytes 1572872 | tf_op jit(solution)/shard_map/ppermute | solution.py:148
  57.0 12.0 %collective-permute-start.6 = (bf16[2,48,2048]{2,1,0:T(8,128)(2,1)S(1)}, bf16[2,48,2048]{2,1,0:T(8,128)(2,1)S(1)}, u32[]{:S(2)}, u32[]{:S(2)}) collective-permute-start(bf16[2,48,2048]{2,1,0:T(8,128)(2,1)S(1)} %pad_maximum_fusion.1), channel_id=1, source_target_pairs={{0,34},{34,0},{2,32},{32,2},{1,35},{35,1},{3,33},{33,3},{4,38},{38... | collective-permute-start | bytes 1179656 | tf_op jit(solution)/shard_map/ppermute | solution.py:174
  59.5 20.8 %collective-permute-start.10 = (bf16[2,64,2048]{2,1,0:T(8,128)(2,1)S(1)}, bf16[2,64,2048]{2,1,0:T(8,128)(2,1)S(1)}, u32[]{:S(2)}, u32[]{:S(2)}) collective-permute-start(bf16[2,64,2048]{2,1,0:T(8,128)(2,1)S(1)} %pad_maximum_fusion), channel_id=1, source_target_pairs={{0,34},{34,0},{2,32},{32,2},{1,35},{35,1},{3,33},{33,3},{4,38},{38... | collective-permute-start | bytes 1572872 | tf_op jit(solution)/shard_map/ppermute | solution.py:175
  69.0 21.9 %copy-start.9 = (bf16[2,48,2048]{2,1,0:T(8,128)(2,1)}, bf16[2,48,2048]{2,1,0:T(8,128)(2,1)S(1)}, u32[]{:S(2)}) copy-start(bf16[2,48,2048]{2,1,0:T(8,128)(2,1)S(1)} %collective-permute-done.6.m1) | copy-start | bytes 1179652
  69.0 11.2 %collective-permute-start.9 = (bf16[2,48,2048]{2,1,0:T(8,128)(2,1)S(1)}, bf16[2,48,2048]{2,1,0:T(8,128)(2,1)S(1)}, u32[]{:S(2)}, u32[]{:S(2)}) collective-permute-start(bf16[2,48,2048]{2,1,0:T(8,128)(2,1)S(1)} %collective-permute-done.6.m1), channel_id=1, source_target_pairs={{0,192},{64,0},{128,64},{192,128},{1,193},{65,1},{129,65},{193,129... | collective-permute-start | bytes 1179656 | tf_op jit(solution)/shard_map/ppermute | solution.py:176
  69.9 10.3 %copy-start.6 = (bf16[1024,256]{1,0:T(8,128)(2,1)}, bf16[1024,256]{1,0:T(8,128)(2,1)S(1)}, u32[]{:S(2)}) copy-start(bf16[1024,256]{1,0:T(8,128)(2,1)S(1)} %collective-permute-done.1.a1) | copy-start | bytes 1572868
  69.9 10.7 %collective-permute-start.8 = (bf16[2,48,2048]{2,1,0:T(8,128)(2,1)S(1)}, bf16[2,48,2048]{2,1,0:T(8,128)(2,1)S(1)}, u32[]{:S(2)}, u32[]{:S(2)}) collective-permute-start(bf16[2,48,2048]{2,1,0:T(8,128)(2,1)S(1)} %collective-permute-done.6.m1), channel_id=1, source_target_pairs={{0,128},{64,192},{128,0},{192,64},{1,129},{65,193},{129,1},{193,65... | collective-permute-start | bytes 1179656 | tf_op jit(solution)/shard_map/ppermute | solution.py:176
  71.0 19.9 %collective-permute-start.7 = (bf16[2,48,2048]{2,1,0:T(8,128)(2,1)S(1)}, bf16[2,48,2048]{2,1,0:T(8,128)(2,1)S(1)}, u32[]{:S(2)}, u32[]{:S(2)}) collective-permute-start(bf16[2,48,2048]{2,1,0:T(8,128)(2,1)S(1)} %collective-permute-done.6.m1), channel_id=1, source_target_pairs={{0,64},{64,128},{128,192},{192,0},{1,65},{65,129},{129,193},{193,1... | collective-permute-start | bytes 1179656 | tf_op jit(solution)/shard_map/ppermute | solution.py:176
  71.1 9.2 %copy-start.7 = (bf16[1024,256]{1,0:T(8,128)(2,1)}, bf16[1024,256]{1,0:T(8,128)(2,1)S(1)}, u32[]{:S(2)}) copy-start(bf16[1024,256]{1,0:T(8,128)(2,1)S(1)} %collective-permute-done.3.a3) | copy-start | bytes 1572868
  80.3 10.6 %copy-start.8 = (bf16[2,64,2048]{2,1,0:T(8,128)(2,1)}, bf16[2,64,2048]{2,1,0:T(8,128)(2,1)S(1)}, u32[]{:S(2)}) copy-start(bf16[2,64,2048]{2,1,0:T(8,128)(2,1)S(1)} %collective-permute-done.10.m2) | copy-start | bytes 1572868
  80.3 10.6 %copy-start.10 = (bf16[2,48,2048]{2,1,0:T(8,128)(2,1)}, bf16[2,48,2048]{2,1,0:T(8,128)(2,1)S(1)}, u32[]{:S(2)}) copy-start(bf16[2,48,2048]{2,1,0:T(8,128)(2,1)S(1)} %collective-permute-done.9.r3) | copy-start | bytes 1179652
  80.6 10.3 %copy-start.11 = (bf16[2,48,2048]{2,1,0:T(8,128)(2,1)}, bf16[2,48,2048]{2,1,0:T(8,128)(2,1)S(1)}, u32[]{:S(2)}) copy-start(bf16[2,48,2048]{2,1,0:T(8,128)(2,1)S(1)} %collective-permute-done.8.r2) | copy-start | bytes 1179652
  90.9 0.8 copy-start.12
  158.2 7.5 %collective-permute-start.13 = (bf16[32,2048]{1,0:T(8,128)(2,1)S(1)}, bf16[32,2048]{1,0:T(8,128)(2,1)S(1)}, u32[]{:S(2)}, u32[]{:S(2)}) collective-permute-start(bf16[32,2048]{1,0:T(8,128)(2,1)S(1)} %get-tuple-element.16), channel_id=1, source_target_pairs={{0,3},{1,2},{2,1},{3,0},{4,7},{5,6},{6,5},{7,4},{8,11},{9,10},{10,... | collective-permute-start | bytes 393224 | tf_op jit(solution)/shard_map/ppermute | solution.py:237
  161.5 6.8 %collective-permute-start.12 = (bf16[32,2048]{1,0:T(8,128)(2,1)S(1)}, bf16[32,2048]{1,0:T(8,128)(2,1)S(1)}, u32[]{:S(2)}, u32[]{:S(2)}) collective-permute-start(bf16[32,2048]{1,0:T(8,128)(2,1)S(1)} %get-tuple-element.17), channel_id=1, source_target_pairs={{0,2},{1,3},{2,0},{3,1},{4,6},{5,7},{6,4},{7,5},{8,10},{9,11},{10,... | collective-permute-start | bytes 393224 | tf_op jit(solution)/shard_map/ppermute | solution.py:237
  161.7 6.6 %collective-permute-start.11 = (bf16[32,2048]{1,0:T(8,128)(2,1)S(1)}, bf16[32,2048]{1,0:T(8,128)(2,1)S(1)}, u32[]{:S(2)}, u32[]{:S(2)}) collective-permute-start(bf16[32,2048]{1,0:T(8,128)(2,1)S(1)} %get-tuple-element.18), channel_id=1, source_target_pairs={{0,1},{1,0},{2,3},{3,2},{4,5},{5,4},{6,7},{7,6},{8,9},{9,8},{10,11... | collective-permute-start | bytes 393224 | tf_op jit(solution)/shard_map/ppermute | solution.py:237
  165.7 2.6 %copy-start.2 = (bf16[32,2048]{1,0:T(8,128)(2,1)}, bf16[32,2048]{1,0:T(8,128)(2,1)S(1)}, u32[]{:S(2)}) copy-start(bf16[32,2048]{1,0:T(8,128)(2,1)S(1)} %collective-permute-done.13.p3) | copy-start | bytes 393220
  168.3 0.7 copy-start.3
  168.3 0.7 copy-start.4
Sparse Core Ops, SparseCore 0:
  100.7 55.6 reduce-scatter.1

commit v2 on v1

v2 whole, which is shorter than its diff:
```python
import jax
import jax.numpy as jnp
from jax import lax
from jax.experimental import pallas as pl
from jax.experimental.pallas import tpu as pltpu
from jax.sharding import Mesh, PartitionSpec as P

GROUP = 16
MODES = 16
CHUNK = 128
LANES = 128
BF = jnp.bfloat16
F32 = jnp.float32
VM = pl.BlockSpec(memory_space=pltpu.VMEM)
SM = pl.BlockSpec(memory_space=pltpu.SMEM)


def iota(shape, dim):
    return lax.broadcasted_iota(jnp.int32, shape, dim)


def spread(state):
    width = state.shape[1]
    groups = width // GROUP
    tall = jnp.concatenate([state] * groups, axis=0)
    shape = (groups * MODES, width)
    own = iota(shape, 0) // MODES == iota(shape, 1) // GROUP
    return jnp.where(own, tall, 0.0).astype(BF)


def one_hot(rows, columns, row_size, column_size):
    shape = (rows, columns)
    return (iota(shape, 0) // row_size == iota(shape, 1) // column_size).astype(F32)


def exact_dot(a, b, dims):
    return lax.dot_general(a, b, (dims, ((), ())), precision=lax.Precision.HIGHEST, preferred_element_type=F32)


def by_channel(table, channels):
    return exact_dot(table, one_hot(table.shape[0], channels, 1, GROUP), ((0,), (0,)))


def by_row(table):
    flat = table.shape[0] * MODES
    wide = exact_dot(one_hot(flat, table.shape[0], MODES, 1), table, ((1,), (0,)))
    keep = iota((flat, MODES), 0) % MODES == iota((flat, MODES), 1)
    return jnp.where(keep, wide, 0.0).sum(axis=1, keepdims=True)


def by_lane(table):
    flat = table.shape[0] * MODES
    wide = exact_dot(table, one_hot(table.shape[0], flat, 1, MODES), ((0,), (0,)))
    keep = iota((MODES, flat), 1) % MODES == iota((MODES, flat), 0)
    return jnp.where(keep, wide, 0.0).sum(axis=0, keepdims=True)


def tapped(taps, cur, before):
    ext = jnp.concatenate([before, cur], axis=0)
    skip = before.shape[0]
    one = pltpu.roll(ext, 1, 0)[skip:]
    two = pltpu.roll(ext, 2, 0)[skip:]
    return taps[0:1, :] * cur + taps[1:2, :] * one + taps[2:3, :] * two


def state_kernel(k_ref, v_ref, halo_ref, sf_ref, rate_ref, x_ref, end_ref, rt_ref, tail, total, power):
    step = pl.program_id(0)
    rows, channels = k_ref.shape

    @pl.when(step == 0)
    def _():
        rt = by_channel(rate_ref[...], channels)
        rt_ref[...] = rt
        total[...] = jnp.zeros_like(total)
        for n in range(MODES):
            power[n] = jnp.broadcast_to(jnp.exp(-8.0 * rt[n : n + 1, :]), (8, channels))
        for i in range(2):
            tail[i] = halo_ref[i + 1].astype(F32)

    featured = []
    for i, ref in enumerate((k_ref, v_ref)):
        cur = ref[...].astype(F32)
        featured.append(tapped(sf_ref[i + 1], cur, tail[i]))
        tail[i] = cur[rows - 8 :]
    signal = featured[0] * featured[1]
    x_ref[...] = signal.astype(BF)
    for h in range(channels // LANES):
        lanes = slice(h * LANES, (h + 1) * LANES)
        for first in range(0, MODES, 8):
            sums = [total[n, :, lanes] for n in range(first, first + 8)]
            powers = [power[n, :, lanes] for n in range(first, first + 8)]
            for b in range(rows // 8):
                block = signal[b * 8 : (b + 1) * 8, lanes]
                sums = [s * w + block for s, w in zip(sums, powers)]
            for n in range(8):
                total[first + n, :, lanes] = sums[n]

    @pl.when(step == pl.num_programs(0) - 1)
    def _():
        rt = rt_ref[...]
        ahead = (7 - iota((8, channels), 0)).astype(F32)
        end = jnp.concatenate(
            [
                (total[n] * jnp.exp(-ahead * rt[n : n + 1, :])).sum(axis=0, keepdims=True)
                for n in range(MODES)
            ],
            axis=0,
        )
        for j in range(end_ref.shape[0]):
            end_ref[j] = end


def conv_kernel(p_ref, x_ref, halo_ref, sf_ref, rate_ref, weight_ref, rt_ref,
                y_ref, q_ref, din_ref, table, masked):
    rows, channels = x_ref.shape
    halves = channels // LANES
    per_half = LANES // GROUP
    groups = channels // GROUP
    rate, weight = rate_ref[...], weight_ref[...]
    rcol = by_row(rate)
    wcol = by_row(weight)
    lane = iota((groups * MODES, CHUNK), 1)
    back = jnp.where(lane == 0, 0, CHUNK - lane).astype(F32)
    taps = (wcol * jnp.exp(-rcol * back)).reshape(groups, MODES, CHUNK).sum(axis=1)
    leave = jnp.exp(-rcol * (CHUNK - 1 - lane).astype(F32)).astype(BF)
    causal = iota((CHUNK, CHUNK), 0) >= iota((CHUNK, CHUNK), 1)
    for g in range(groups):
        wide = jnp.broadcast_to(taps[g : g + 1, :], (CHUNK, CHUNK))
        turned = pltpu.roll(wide, 0, 1, stride=1, stride_axis=0)
        table[0:CHUNK, g * CHUNK : (g + 1) * CHUNK] = jnp.where(causal, turned, 0.0).astype(BF)
        table[CHUNK : CHUNK + MODES, g * CHUNK : (g + 1) * CHUNK] = leave[g * MODES : (g + 1) * MODES]
    steps = (iota((CHUNK, groups * MODES), 0) + 1).astype(F32)
    din = (by_lane(weight) * jnp.exp(-by_lane(rate) * steps)).astype(BF)
    din_ref[...] = din
    power = jnp.exp(-rt_ref[...] * float(CHUNK))
    group_lane = iota((CHUNK, LANES), 1) // GROUP

    state = jnp.zeros((MODES, channels), F32)
    for pair in range(rows // (2 * CHUNK)):
        for j in range(2):
            q = 2 * pair + j
            span = slice(q * CHUNK, (q + 1) * CHUNK)
            before = halo_ref[0] if q == 0 else p_ref[q * CHUNK - 16 : q * CHUNK, :]
            q_ref[span, :] = tapped(sf_ref[0], p_ref[span, :].astype(F32), before.astype(F32))
            for h in range(halves):
                part = x_ref[span, h * LANES : (h + 1) * LANES]
                for g in range(per_half):
                    masked[h, g * CHUNK : (g + 1) * CHUNK, j * LANES : (j + 1) * LANES] = jnp.where(
                        group_lane == g, part, jnp.zeros_like(part)
                    )
        depth = per_half * CHUNK
        made = [
            jnp.dot(table[:, h * depth : (h + 1) * depth], masked[h], preferred_element_type=F32)
            for h in range(halves)
        ]
        for j in range(2):
            q = 2 * pair + j
            full = jnp.concatenate([m[:, j * LANES : (j + 1) * LANES] for m in made], axis=1)
            within = full[:CHUNK]
            if q > 0:
                within = within + jnp.dot(din, spread(state), preferred_element_type=F32)
            y_ref[q * CHUNK : (q + 1) * CHUNK, :] = within
            state = power * state + full[CHUNK:]


def mix_kernel(at_ref, ends_ref, rt_ref, din_ref, y_ref, q_ref, mixed_ref):
    rows = y_ref.shape[0]
    here = at_ref[0]
    block_power = jnp.exp(-rt_ref[...] * float(rows))
    state = jnp.zeros(rt_ref.shape, F32)
    for j in range(ends_ref.shape[0]):
        state = jnp.where(j < here, block_power * state + ends_ref[j], state)
    power = jnp.exp(-rt_ref[...] * float(CHUNK))
    din = din_ref[...]
    for q in range(rows // CHUNK):
        span = slice(q * CHUNK, (q + 1) * CHUNK)
        carried = jnp.dot(din, spread(state), preferred_element_type=F32)
        mixed_ref[span, :] = (q_ref[span, :] * (y_ref[span, :] + carried)).astype(BF)
        state = power * state


def product_kernel(at_ref, a0, a1, a2, a3, w0, w1, m1, r1, r2, r3, m2, c_ref, left, right):
    y, mine = at_ref[1], at_ref[2]
    depth = w0.shape[0]
    piece, tail = m1.shape[1], m2.shape[1]

    @pl.when(pl.program_id(0) == 0)
    def _():
        for k, ref in enumerate((a0, a1, a2, a3)):
            left[:, k * depth : (k + 1) * depth] = ref[...]

    right[0:depth] = w0[...]
    right[depth : 2 * depth] = w1[...]
    for s in range(2):
        base = (2 + s) * depth
        for k, ref in enumerate((m1, r1, r2, r3)):
            start = pl.multiple_of(base + lax.rem(y - k + 4, 4) * piece, 16)
            right[pl.ds(start, piece), :] = ref[s]
        right[base + 4 * piece : base + 4 * piece + tail, :] = m2[s]
    block = 256
    for m in range(left.shape[0] // block):
        total = jnp.dot(left[m * block : (m + 1) * block, :], right[...], preferred_element_type=F32).astype(BF)
        for b in range(block // 32):
            high, low = m * (block // 128) + b // 4, b % 4
            place = pl.multiple_of((high * 4 + jnp.bitwise_xor(low, mine)) * 32, 32)
            c_ref[pl.ds(place, 32), :] = total[b * 32 : (b + 1) * 32]


def join_kernel(at_ref, p0, p1, p2, p3, out_ref):
    mine = at_ref[2]
    width = p0.shape[1]
    for k, ref in enumerate((p0, p1, p2, p3)):
        place = pl.multiple_of(jnp.bitwise_xor(mine, k) * width, width)
        out_ref[:, pl.ds(place, width)] = ref[...]


def other_core(value):
    return lax.ppermute(value, "c", [(0, 1), (1, 0)])


def local(projected, short_filter, residue, rate, out_weight):
    rows, channels = projected.shape[1], projected.shape[2]
    groups = rate.shape[0]
    width = out_weight.shape[1] // 4
    y, xh, core = lax.axis_index("y"), lax.axis_index("xh"), lax.axis_index("c")
    seq = lax.axis_index(("y", "xl"))
    at = jnp.stack([seq, y, xh * 2 + core]).astype(jnp.int32)

    halo = lax.ppermute(projected[:, rows - 8 :, :], ("y", "xl"), [(i, i + 1) for i in range(7)])

    def columns(h, k):
        return lax.dynamic_slice(out_weight, (0, (h * 2 + k) * width), (channels, width))

    w_mine = columns(xh, core)
    o_mine = columns(1 - xh, core)
    o_other = other_core(columns(1 - xh, 1 - core))
    w_other = other_core(columns(xh, 1 - core))
    piece = 48
    mirror = [(0, 3), (3, 0), (1, 2), (2, 1)]

    def rows_of(start, size):
        return jnp.stack([lax.dynamic_slice(v, (start, 0), (size, width)) for v in (o_mine, o_other)])

    m1 = lax.ppermute(rows_of(y * piece, piece), ("xl", "xh"), mirror)
    m2 = lax.ppermute(rows_of(4 * piece, channels - 4 * piece), ("xl", "xh"), mirror)

    weight = residue * jnp.sqrt(-jnp.expm1(-2.0 * rate))
    flat = groups * MODES
    span = 256
    once = {"pipeline_mode": pl.Buffered(1)}

    def whole(shape):
        return pl.BlockSpec(shape, lambda i: (0,) * len(shape))

    def third(k):
        return pl.BlockSpec((None, span, channels), lambda i: (k, i, 0))

    signal, end, rt = pl.pallas_call(
        state_kernel,
        out_shape=(
            pltpu.HBM((rows, channels), BF),
            jax.ShapeDtypeStruct((8, MODES, channels), F32),
            jax.ShapeDtypeStruct((MODES, channels), F32),
        ),
        grid=(rows // span,),
        in_specs=[third(1), third(2), whole(halo.shape), whole(short_filter.shape), whole(rate.shape)],
        out_specs=(
            pl.BlockSpec((span, channels), lambda i: (i, 0)),
            whole((8, MODES, channels)),
            whole((MODES, channels)),
        ),
        scratch_shapes=[
            pltpu.VMEM((2, 8, channels), F32),
            pltpu.VMEM((MODES, 8, channels), F32),
            pltpu.VMEM((MODES, 8, channels), F32),
        ],
        compiler_params=pltpu.CompilerParams(vmem_limit_bytes=12 * 2**20),
        cost_estimate=pl.CostEstimate(flops=2 * 10**7, bytes_accessed=6 * 2**20, transcendentals=10**4),
        name="state",
    )(projected, projected, halo, short_filter, rate)
    ends = lax.all_to_all(end, ("y", "xl"), 0, 0, tiled=True)
    conv, query, din = pl.pallas_call(
        conv_kernel,
        out_shape=(
            pltpu.HBM((rows, channels), F32),
            pltpu.HBM((rows, channels), F32),
            jax.ShapeDtypeStruct((CHUNK, flat), BF),
        ),
        grid=(1,),
        in_specs=[
            pl.BlockSpec((None, rows, channels), lambda i: (0, 0, 0)),
            whole((rows, channels)), whole(halo.shape), whole(short_filter.shape),
            whole(rate.shape), whole(rate.shape), whole(rt.shape),
        ],
        out_specs=(whole((rows, channels)), whole((rows, channels)), whole((CHUNK, flat))),
        scratch_shapes=[
            pltpu.VMEM((CHUNK + MODES, groups * CHUNK), BF),
            pltpu.VMEM((channels // LANES, LANES // GROUP * CHUNK, 2 * LANES), BF),
        ],
        compiler_params=pltpu.CompilerParams(vmem_limit_bytes=20 * 2**20),
        cost_estimate=pl.CostEstimate(flops=4 * 10**9, bytes_accessed=12 * 2**20, transcendentals=10**5),
        name="conv",
    )(projected, signal, halo, short_filter, rate, weight, rt)
    ends, m1 = lax.optimization_barrier((ends, m1))
    mixed = pl.pallas_call(
        mix_kernel,
        out_shape=jax.ShapeDtypeStruct((rows, channels), BF),
        in_specs=[SM] + [VM] * 5,
        out_specs=VM,
        compiler_params=pltpu.CompilerParams(vmem_limit_bytes=12 * 2**20),
        cost_estimate=pl.CostEstimate(flops=2 * 10**8, bytes_accessed=5 * 2**20, transcendentals=10**4),
        name="mix",
    )(at, ends, rt, din, conv, query)

    r1, r2, r3 = (lax.ppermute(m1, "y", [(i, (i + k) % 4) for i in range(4)]) for k in (1, 2, 3))
    a_far = lax.ppermute(mixed, "xh", [(0, 1), (1, 0)])
    a_other = other_core(mixed)
    a_far, m2, r1, r2, r3 = lax.optimization_barrier((a_far, m2, r1, r2, r3))
    a_far_other = other_core(a_far)

    tile = 512

    def strip(shape):
        return pl.BlockSpec(shape[:-1] + (tile,), lambda i: (0,) * (len(shape) - 1) + (i,))

    partial = pl.pallas_call(
        product_kernel,
        out_shape=pltpu.HBM((rows, width), BF),
        grid=(width // tile,),
        in_specs=[SM]
        + [pl.BlockSpec((rows, channels), lambda i: (0, 0), **once)] * 4
        + [strip((channels, width))] * 2
        + [strip(m1.shape)] * 4
        + [strip(m2.shape)],
        out_specs=strip((rows, width)),
        scratch_shapes=[pltpu.VMEM((rows, 4 * channels), BF), pltpu.VMEM((4 * channels, tile), BF)],
        compiler_params=pltpu.CompilerParams(vmem_limit_bytes=28 * 2**20),
        cost_estimate=pl.CostEstimate(flops=4 * 10**9, bytes_accessed=10 * 2**20, transcendentals=0),
        name="product",
    )(at, mixed, a_other, a_far, a_far_other, w_mine, w_other, m1, r1, r2, r3, m2)

    summed = lax.psum_scatter(partial, "z", scatter_dimension=0, tiled=True)
    size = summed.shape[0] // 4

    def traded(k):
        pairs = [(i, i ^ k) for i in range(4)]
        return lax.ppermute(summed[k * size : (k + 1) * size], ("xh", "c"), pairs)

    return pl.pallas_call(
        join_kernel,
        out_shape=jax.ShapeDtypeStruct((size, 4 * width), BF),
        in_specs=[SM] + [VM] * 4,
        out_specs=VM,
        compiler_params=pltpu.CompilerParams(vmem_limit_bytes=4 * 2**20),
        name="join",
    )(at, summed[:size], traded(1), traded(2), traded(3))


def solution(mesh):
    fine = Mesh(mesh.devices.reshape(4, 2, 8, 2, 2), ("y", "xl", "z", "xh", "c"))
    seq, tp = ("y", "xl"), ("z", "xh", "c")
    placed = (P(None, seq, tp), P(None, None, tp), P(tp, None), P(tp, None), P(tp, None))
    return jax.shard_map(local, mesh=fine, in_specs=placed, out_specs=P(seq + tp, None), check_vma=False)
```

time: 178 us -> 160 us (0.90)
  waiting for transfers between devices: 103 us -> 85.7 us
  starting transfers between devices: 25.2 us -> 28.6 us
  local copies, waits for them, and re-layouts: 15.6 us -> 12.3 us
  Pallas kernels: 19.4 us -> 17.3 us
    ppermute x1, waiting for transfers between devices: 9.11 us -> 1.78 us  [local(): m1 = lax.ppermute(rows_of(y * piece, piece), ('xl', 'xh'), mirror)]
    ppermute x1, waiting for transfers between devices: 7.21 us -> 0.01 us  [local(): a_far = lax.ppermute(mixed, 'xh', [(0, 1), (1, 0)])]
    all_to_all x1, waiting for transfers between devices: 4.87 us -> 0.01 us  [local(): ends = lax.all_to_all(end, ('y', 'xl'), 0, 0, tiled=True)]
    ppermute x4, starting transfers between devices: 5.09 us -> 9.77 us  [other_core(): return lax.ppermute(value, 'c', [(0, 1), (1, 0)])]
    reshape x5 -> x0, local copies, waits for them, and re-layouts: 3.53 us -> none  [the longest x1 0.75 us: local(): rate.reshape(flat, 1)]
    ppermute x1, starting transfers between devices: 3.93 us -> 1.37 us  [local(): lax.ppermute(projected[:, rows - 8:, :], ('y', 'xl'), [(i, i + 1) for i i...]
    ppermute x3, starting transfers between devices: 1.99 us -> 4.42 us  [local(): lax.ppermute(m1, 'y', [(i, (i + k) % 4) for i in range(4)])]
    ppermute x3, waiting for transfers between devices: 10.6 us -> 8.59 us  [local(): lax.ppermute(m1, 'y', [(i, (i + k) % 4) for i in range(4)])]
  transfers between devices with their start and end apart: 16 -> 16, of which waited for: 9 -> 8; matrix products, arithmetic and copies ran while one was open for 6% -> 4% of each run, Pallas kernels for 5% -> 5%
where the time goes in v2:
time: 160 us; the launch traced here: 159 us
  waiting for transfers between devices  85.7 us (54%)
  starting transfers between devices  28.6 us (18%)
  Pallas kernels  17.3 us (11%)
  between operations  13.5 us (8%)
  local copies, waits for them, and re-layouts  12.3 us (8%)
  other arithmetic  1.72 us (1%)
    reduce_scatter x1, waiting for transfers between devices, local(): summed = lax.psum_scatter(partial, 'z', scatter_dimension=0, tiled=True)  56.3 us
    ppermute x1, waiting for transfers between devices, local(): lax.ppermute(rows_of(4 * piece, channels - 4 * piece), ('xl', 'xh'), mirror)  11.1 us
    ppermute x4, starting transfers between devices, other_core(): return lax.ppermute(value, 'c', [(0, 1), (1, 0)])  9.77 us
    ppermute x3, waiting for transfers between devices, local(): lax.ppermute(m1, 'y', [(i, (i + k) % 4) for i in range(4)])  8.59 us
    pallas_call x1, Pallas kernels, local(): pl.pallas_call(product_kernel, out_shape=pltpu.HBM((rows, width), BF), gr...  7.57 us
    ppermute x3, waiting for transfers between devices, traded(): return lax.ppermute(summed[k * size:(k + 1) * size], ('xh', 'c'), pairs)  6.3 us
    all_to_all x1, starting transfers between devices, local(): ends = lax.all_to_all(end, ('y', 'xl'), 0, 0, tiled=True)  4.88 us
    ppermute x3, starting transfers between devices, local(): lax.ppermute(m1, 'y', [(i, (i + k) % 4) for i in range(4)])  4.42 us
  transfers between devices with their start and end apart: 16, of which 8 were waited for; matrix products, arithmetic and copies ran while one was open for 4% of the time, Pallas kernels for 5%

profile of v2, /device:TPU:1, one launch (start us, length us, event | category | flops | bytes accessed | tf_op | source)
XLA Modules:
  0.0 159.1 jit_solution(10264747286323757148)
XLA Ops:
  6.5 3.7 %constant_dynamic-slice_fusion = (bf16[256,2048]{1,0:T(8,128)(2,1)}, bf16[256,2048]{1,0:T(8,128)(2,1)}, bf16[256,2048]{1,0:T(8,128)(2,1)S(1)}) fusion(bf16[256,8192]{1,0:T(8,128)(2,1)} %param.9, s32[]{:T(128)S(6)} %select_n.26, s32[]{:T(128)S(6)} %select_n.24, s32[]{:T(128)S(6)} %select_n.25), kind=kLoop, calls=%fused_computation.7 | loop fusion | bytes 6291468 | tf_op jit(solution)/shard_map/dynamic_slice | solution.py:232
  10.3 3.2 %collective-permute-start.1 = (bf16[256,2048]{1,0:T(8,128)(2,1)}, bf16[256,2048]{1,0:T(8,128)(2,1)}, u32[]{:S(2)}, u32[]{:S(2)}) collective-permute-start(bf16[256,2048]{1,0:T(8,128)(2,1)} %get-tuple-element.32), channel_id=1, source_target_pairs={{0,1},{1,0},{2,3},{3,2},{4,5},{5,4},{6,7},{7,6},{8,9},{9,8},{10,11... | collective-permute-start | bytes 3145736 | tf_op jit(solution)/shard_map/ppermute | solution.py:218
  13.5 1.4 collective-permute-start
  15.0 1.1 dynamic-slice_bitcast_fusion.2
  16.1 1.0 dynamic-slice_bitcast_fusion
  17.0 0.1 pad_add_fusion.at_ref
  17.1 0.0 collective-permute-done.halo_ref
  17.1 3.3 %state.1 = (bf16[1024,256]{1,0:T(8,128)(2,1)}, f32[8,16,256]{2,1,0:T(8,128)}, f32[16,256]{1,0:T(8,128)S(1)}) custom-call(bf16[3,1024,256]{2,1,0:T(8,128)(2,1)S(1)} %copy-done, bf16[3,1024,256]{2,1,0:T(8,128)(2,1)S(1)} %copy-done, bf16[3,8,256]{2,1,0:T(8,128)(2,1)S(1)} %collective-permute-done.halo_ref, f32[3,3,256]{2,1,0:T(4,128)S(1)} %copy-done.4, ...), custom_call_target="tpu_custom_call" | custom-call | flops 20000000 | bytes 6291456 | tf_op jit(solution)/shard_map/state/pallas_call | solution.py:258
  20.4 4.9 %all-to-all-start = ((f32[8,16,256]{2,1,0:T(8,128)}), f32[8,16,256]{2,1,0:T(8,128)S(1)}, u32[]{:S(2)}, u32[]{:S(2)}) async-start(f32[8,16,256]{2,1,0:T(8,128)} %get-tuple-element.18), calls=%async_computation | async-start | bytes 262144 | tf_op jit(solution)/shard_map/all_to_all | solution.py:281
  25.3 0.0 reduce-scatter.2.cloned.1.call-start
  25.3 0.0 collective-permute-done.1
  25.3 0.9 dynamic-slice_bitcast_fusion.1
  26.3 0.8 pad_maximum_fusion.1
  27.1 3.0 %collective-permute-start.2 = (bf16[2,48,2048]{2,1,0:T(8,128)(2,1)}, bf16[2,48,2048]{2,1,0:T(8,128)(2,1)}, u32[]{:S(2)}, u32[]{:S(2)}) collective-permute-start(bf16[2,48,2048]{2,1,0:T(8,128)(2,1)} %pad_maximum_fusion.1), channel_id=1, source_target_pairs={{0,34},{34,0},{2,32},{32,2},{1,35},{35,1},{3,33},{33,3},{4,38},{38... | collective-permute-start | bytes 1179656 | tf_op jit(solution)/shard_map/ppermute | solution.py:244
  30.0 1.0 slice_bitcast_fusion
  31.0 0.8 pad_maximum_fusion
  31.9 0.0 collective-permute-start.5
  31.9 1.0 copy-done.5
  32.9 4.1 %conv.1 = (f32[1024,256]{1,0:T(8,128)}, f32[1024,256]{1,0:T(8,128)}, bf16[128,256]{1,0:T(8,128)(2,1)S(1)}) custom-call(bf16[3,1024,256]{2,1,0:T(8,128)(2,1)S(1)} %copy-done, bf16[1024,256]{1,0:T(8,128)(2,1)S(1)} %copy-done.5, bf16[3,8,256]{2,1,0:T(8,128)(2,1)S(1)} %collective-permute-done.halo_ref, f32[3,3,256]{2,1,0:T(4,128)S(1)} %copy-done.4, ...), custom_call_target="tpu_custom_call" | custom-call | flops 4000000000 | bytes 12582912 | tf_op jit(solution)/shard_map/conv/pallas_call | solution.py:282
  37.0 0.0 all-to-all-done.ends_ref
  37.0 1.8 %collective-permute-done.2.m1 = bf16[2,48,2048]{2,1,0:T(8,128)(2,1)} collective-permute-done((bf16[2,48,2048]{2,1,0:T(8,128)(2,1)}, bf16[2,48,2048]{2,1,0:T(8,128)(2,1)}, u32[]{:S(2)}, u32[]{:S(2)}) %collective-permute-start.2) | collective-permute-done | bytes 393248 | tf_op jit(solution)/shard_map/ppermute | solution.py:244
  38.8 1.2 copy-done.1
  40.0 1.2 copy-done.2
  41.3 0.9 mix.1.a0
  42.2 1.3 collective-permute-start.4
  43.5 3.1 %collective-permute-start.10 = (bf16[256,2048]{1,0:T(8,128)(2,1)}, bf16[256,2048]{1,0:T(8,128)(2,1)S(1)}, u32[]{:S(2)}, u32[]{:S(2)}) collective-permute-start(bf16[256,2048]{1,0:T(8,128)(2,1)} %get-tuple-element.31), channel_id=1, source_target_pairs={{0,1},{1,0},{2,3},{3,2},{4,5},{5,4},{6,7},{7,6},{8,9},{9,8},{10,11... | collective-permute-start | bytes 3145736 | tf_op jit(solution)/shard_map/ppermute | solution.py:218
  46.6 2.9 %collective-permute-start.8 = (bf16[2,48,2048]{2,1,0:T(8,128)(2,1)}, bf16[2,48,2048]{2,1,0:T(8,128)(2,1)S(1)}, u32[]{:S(2)}, u32[]{:S(2)}) collective-permute-start(bf16[2,48,2048]{2,1,0:T(8,128)(2,1)} %collective-permute-done.2.m1), channel_id=1, source_target_pairs={{0,192},{64,0},{128,64},{192,128},{1,193},{65,1},{129,65},{193,129... | collective-permute-start | bytes 1179656 | tf_op jit(solution)/shard_map/ppermute | solution.py:315
  49.5 0.6 collective-permute-start.7
  50.1 11.1 %collective-permute-done.5.m2 = bf16[2,64,2048]{2,1,0:T(8,128)(2,1)S(1)} collective-permute-done((bf16[2,64,2048]{2,1,0:T(8,128)(2,1)}, bf16[2,64,2048]{2,1,0:T(8,128)(2,1)S(1)}, u32[]{:S(2)}, u32[]{:S(2)}) %collective-permute-start.5) | collective-permute-done | bytes 524320 | tf_op jit(solution)/shard_map/ppermute | solution.py:245
  61.2 0.9 collective-permute-start.6
  62.1 4.6 %collective-permute-done.8.r3 = bf16[2,48,2048]{2,1,0:T(8,128)(2,1)S(1)} collective-permute-done((bf16[2,48,2048]{2,1,0:T(8,128)(2,1)}, bf16[2,48,2048]{2,1,0:T(8,128)(2,1)S(1)}, u32[]{:S(2)}, u32[]{:S(2)}) %collective-permute-start.8) | collective-permute-done | bytes 393248 | tf_op jit(solution)/shard_map/ppermute | solution.py:315
  66.7 0.9 collective-permute-start.3
  67.6 4.0 %collective-permute-done.6.r1 = bf16[2,48,2048]{2,1,0:T(8,128)(2,1)S(1)} collective-permute-done((bf16[2,48,2048]{2,1,0:T(8,128)(2,1)}, bf16[2,48,2048]{2,1,0:T(8,128)(2,1)S(1)}, u32[]{:S(2)}, u32[]{:S(2)}) %collective-permute-start.6) | collective-permute-done | bytes 393248 | tf_op jit(solution)/shard_map/ppermute | solution.py:315
  71.6 0.0 collective-permute-done.4.a2
  71.6 2.5 %collective-permute-start.9 = (bf16[1024,256]{1,0:T(8,128)(2,1)S(1)}, bf16[1024,256]{1,0:T(8,128)(2,1)S(1)}, u32[]{:S(2)}, u32[]{:S(2)}) collective-permute-start(bf16[1024,256]{1,0:T(8,128)(2,1)S(1)} %collective-permute-done.4.a2), channel_id=1, source_target_pairs={{0,1},{1,0},{2,3},{3,2},{4,5},{5,4},{6,7},{7,6},{8,9},{9,8},{10,11... | collective-permute-start | bytes 1572872 | tf_op jit(solution)/shard_map/ppermute | solution.py:218
  74.1 0.0 collective-permute-done.10.w1
  74.1 1.5 collective-permute-done.9.a3
  75.7 7.6 %product.1 = bf16[1024,2048]{1,0:T(8,128)(2,1)} custom-call(s32[3]{0:T(128)S(1)} %pad_add_fusion.at_ref, bf16[1024,256]{1,0:T(8,128)(2,1)S(1)} %mix.1.a0, bf16[1024,256]{1,0:T(8,128)(2,1)S(1)} %collective-permute-done.3.a1, bf16[1024,256]{1,0:T(8,128)(2,1)S(1)} %collective-permute-done.4.a2, bf16[1024,256]{1,0:T(8,128)(2,1)S(1)} %collective-permute-done.9.a3, ...), custom_call_target="tpu_custom_call" | custom-call | flops 4000000000 | bytes 10485760 | tf_op jit(solution)/shard_map/product/pallas_call | solution.py:326
  83.3 0.0 reduce-scatter.2.cloned.1.call-update
  83.3 56.3 %reduce-scatter.2.cloned.1.call-done = bf16[128,2048]{1,0:T(8,128)(2,1)} async-done(((bf16[1024,2048]{1,0:T(8,128)(2,1)}), bf16[128,2048]{1,0:T(8,128)(2,1)}) %reduce-scatter.2.cloned.1.call-update) | async-done | bytes 524304 | tf_op jit(solution)/shard_map/reduce_scatter | solution.py:342
  139.6 1.1 fusion
  140.7 3.3 %collective-permute-start.13 = (bf16[32,2048]{1,0:T(8,128)(2,1)S(1)}, bf16[32,2048]{1,0:T(8,128)(2,1)S(1)}, u32[]{:S(2)}, u32[]{:S(2)}) collective-permute-start(bf16[32,2048]{1,0:T(8,128)(2,1)S(1)} %get-tuple-element.34), channel_id=1, source_target_pairs={{0,3},{1,2},{2,1},{3,0},{4,7},{5,6},{6,5},{7,4},{8,11},{9,10},{10,... | collective-permute-start | bytes 393224 | tf_op jit(solution)/shard_map/ppermute | solution.py:347
  144.0 0.3 collective-permute-start.12
  144.3 0.2 collective-permute-start.11
  144.5 3.7 %collective-permute-done.13.p3 = bf16[32,2048]{1,0:T(8,128)(2,1)S(1)} collective-permute-done((bf16[32,2048]{1,0:T(8,128)(2,1)S(1)}, bf16[32,2048]{1,0:T(8,128)(2,1)S(1)}, u32[]{:S(2)}, u32[]{:S(2)}) %collective-permute-start.13) | collective-permute-done | bytes 131104 | tf_op jit(solution)/shard_map/ppermute | solution.py:347
  148.3 2.6 %collective-permute-done.12.p2 = bf16[32,2048]{1,0:T(8,128)(2,1)S(1)} collective-permute-done((bf16[32,2048]{1,0:T(8,128)(2,1)S(1)}, bf16[32,2048]{1,0:T(8,128)(2,1)S(1)}, u32[]{:S(2)}, u32[]{:S(2)}) %collective-permute-start.12) | collective-permute-done | bytes 131104 | tf_op jit(solution)/shard_map/ppermute | solution.py:347
  150.8 0.0 collective-permute-done.11.p1
  150.8 1.4 join.1
  (15 shorter events, 0.0 us)
Async XLA Ops:
  6.5 7.0 %copy-start = (bf16[3,1024,256]{2,1,0:T(8,128)(2,1)S(1)}, bf16[3,1024,256]{2,1,0:T(8,128)(2,1)}, u32[]{:S(2)}) copy-start(bf16[3,1024,256]{2,1,0:T(8,128)(2,1)} %p_ref.1) | copy-start | bytes 4718596
  6.5 8.4 %copy-start.3 = (f32[16,16]{1,0:T(8,128)S(1)}, f32[16,16]{1,0:T(8,128)}, u32[]{:S(2)}) copy-start(f32[16,16]{1,0:T(8,128)} %rate_ref.3) | copy-start | bytes 3076
  6.5 8.4 %copy-start.6 = (f32[16,16]{1,0:T(8,128)S(1)}, f32[16,16]{1,0:T(8,128)}, u32[]{:S(2)}) copy-start(f32[16,16]{1,0:T(8,128)} %param.7) | copy-start | bytes 3076
  6.5 10.6 %copy-start.4 = (f32[3,3,256]{2,1,0:T(4,128)S(1)}, f32[3,3,256]{2,1,0:T(4,128)}, u32[]{:S(2)}) copy-start(f32[3,3,256]{2,1,0:T(4,128)} %sf_ref.3) | copy-start | bytes 27652
  10.3 15.0 %collective-permute-start.1 = (bf16[256,2048]{1,0:T(8,128)(2,1)}, bf16[256,2048]{1,0:T(8,128)(2,1)}, u32[]{:S(2)}, u32[]{:S(2)}) collective-permute-start(bf16[256,2048]{1,0:T(8,128)(2,1)} %get-tuple-element.32), channel_id=1, source_target_pairs={{0,1},{1,0},{2,3},{3,2},{4,5},{5,4},{6,7},{7,6},{8,9},{9,8},{10,11... | collective-permute-start | bytes 3145736 | tf_op jit(solution)/shard_map/ppermute | solution.py:218
  13.5 3.6 %collective-permute-start = (bf16[3,8,256]{2,1,0:T(8,128)(2,1)S(1)}, bf16[3,8,256]{2,1,0:T(8,128)(2,1)S(1)}, u32[]{:S(2)}, u32[]{:S(2)}) collective-permute-start(bf16[3,8,256]{2,1,0:T(8,128)(2,1)S(1)} %slice.15), channel_id=1, source_target_pairs={{0,32},{32,64},{64,96},{96,128},{128,160},{160,192},{192,224},{1,3... | collective-permute-start | bytes 36872 | tf_op jit(solution)/shard_map/ppermute | solution.py:229
  20.4 16.7 %all-to-all-start = ((f32[8,16,256]{2,1,0:T(8,128)}), f32[8,16,256]{2,1,0:T(8,128)S(1)}, u32[]{:S(2)}, u32[]{:S(2)}) async-start(f32[8,16,256]{2,1,0:T(8,128)} %get-tuple-element.18), calls=%async_computation | async-start | bytes 262144 | tf_op jit(solution)/shard_map/all_to_all | solution.py:281
  25.3 114.3 %reduce-scatter.2.cloned.1.call-start = ((), (), s32[]{:S(2)}) async-start(), calls=%async_computation.2 | async-start | bytes 4718592 | tf_op jit(solution)/shard_map/reduce_scatter | solution.py:342
  27.1 11.8 %collective-permute-start.2 = (bf16[2,48,2048]{2,1,0:T(8,128)(2,1)}, bf16[2,48,2048]{2,1,0:T(8,128)(2,1)}, u32[]{:S(2)}, u32[]{:S(2)}) collective-permute-start(bf16[2,48,2048]{2,1,0:T(8,128)(2,1)} %pad_maximum_fusion.1), channel_id=1, source_target_pairs={{0,34},{34,0},{2,32},{32,2},{1,35},{35,1},{3,33},{33,3},{4,38},{38... | collective-permute-start | bytes 1179656 | tf_op jit(solution)/shard_map/ppermute | solution.py:244
  31.9 29.3 %collective-permute-start.5 = (bf16[2,64,2048]{2,1,0:T(8,128)(2,1)}, bf16[2,64,2048]{2,1,0:T(8,128)(2,1)S(1)}, u32[]{:S(2)}, u32[]{:S(2)}) collective-permute-start(bf16[2,64,2048]{2,1,0:T(8,128)(2,1)} %pad_maximum_fusion), channel_id=1, source_target_pairs={{0,34},{34,0},{2,32},{32,2},{1,35},{35,1},{3,33},{33,3},{4,38},{38... | collective-permute-start | bytes 1572872 | tf_op jit(solution)/shard_map/ppermute | solution.py:245
  31.9 1.0 copy-start.5
  38.8 1.2 copy-start.1
  40.0 1.2 copy-start.2
  42.2 29.4 %collective-permute-start.4 = (bf16[1024,256]{1,0:T(8,128)(2,1)S(1)}, bf16[1024,256]{1,0:T(8,128)(2,1)S(1)}, u32[]{:S(2)}, u32[]{:S(2)}) collective-permute-start(bf16[1024,256]{1,0:T(8,128)(2,1)S(1)} %mix.1.a0), channel_id=1, source_target_pairs={{0,2},{2,0},{1,3},{3,1},{4,6},{6,4},{5,7},{7,5},{8,10},{10,8},{9,1... | collective-permute-start | bytes 1572872 | tf_op jit(solution)/shard_map/ppermute | solution.py:316
  43.5 30.6 %collective-permute-start.10 = (bf16[256,2048]{1,0:T(8,128)(2,1)}, bf16[256,2048]{1,0:T(8,128)(2,1)S(1)}, u32[]{:S(2)}, u32[]{:S(2)}) collective-permute-start(bf16[256,2048]{1,0:T(8,128)(2,1)} %get-tuple-element.31), channel_id=1, source_target_pairs={{0,1},{1,0},{2,3},{3,2},{4,5},{5,4},{6,7},{7,6},{8,9},{9,8},{10,11... | collective-permute-start | bytes 3145736 | tf_op jit(solution)/shard_map/ppermute | solution.py:218
  46.6 20.1 %collective-permute-start.8 = (bf16[2,48,2048]{2,1,0:T(8,128)(2,1)}, bf16[2,48,2048]{2,1,0:T(8,128)(2,1)S(1)}, u32[]{:S(2)}, u32[]{:S(2)}) collective-permute-start(bf16[2,48,2048]{2,1,0:T(8,128)(2,1)} %collective-permute-done.2.m1), channel_id=1, source_target_pairs={{0,192},{64,0},{128,64},{192,128},{1,193},{65,1},{129,65},{193,129... | collective-permute-start | bytes 1179656 | tf_op jit(solution)/shard_map/ppermute | solution.py:315
  49.5 18.1 %collective-permute-start.7 = (bf16[2,48,2048]{2,1,0:T(8,128)(2,1)}, bf16[2,48,2048]{2,1,0:T(8,128)(2,1)S(1)}, u32[]{:S(2)}, u32[]{:S(2)}) collective-permute-start(bf16[2,48,2048]{2,1,0:T(8,128)(2,1)} %collective-permute-done.2.m1), channel_id=1, source_target_pairs={{0,128},{64,192},{128,0},{192,64},{1,129},{65,193},{129,1},{193,65... | collective-permute-start | bytes 1179656 | tf_op jit(solution)/shard_map/ppermute | solution.py:315
  61.2 10.4 %collective-permute-start.6 = (bf16[2,48,2048]{2,1,0:T(8,128)(2,1)}, bf16[2,48,2048]{2,1,0:T(8,128)(2,1)S(1)}, u32[]{:S(2)}, u32[]{:S(2)}) collective-permute-start(bf16[2,48,2048]{2,1,0:T(8,128)(2,1)} %collective-permute-done.2.m1), channel_id=1, source_target_pairs={{0,64},{64,128},{128,192},{192,0},{1,65},{65,129},{129,193},{193,1... | collective-permute-start | bytes 1179656 | tf_op jit(solution)/shard_map/ppermute | solution.py:315
  66.7 7.5 %collective-permute-start.3 = (bf16[1024,256]{1,0:T(8,128)(2,1)S(1)}, bf16[1024,256]{1,0:T(8,128)(2,1)S(1)}, u32[]{:S(2)}, u32[]{:S(2)}) collective-permute-start(bf16[1024,256]{1,0:T(8,128)(2,1)S(1)} %mix.1.a0), channel_id=1, source_target_pairs={{0,1},{1,0},{2,3},{3,2},{4,5},{5,4},{6,7},{7,6},{8,9},{9,8},{10,11... | collective-permute-start | bytes 1572872 | tf_op jit(solution)/shard_map/ppermute | solution.py:218
  71.6 4.1 %collective-permute-start.9 = (bf16[1024,256]{1,0:T(8,128)(2,1)S(1)}, bf16[1024,256]{1,0:T(8,128)(2,1)S(1)}, u32[]{:S(2)}, u32[]{:S(2)}) collective-permute-start(bf16[1024,256]{1,0:T(8,128)(2,1)S(1)} %collective-permute-done.4.a2), channel_id=1, source_target_pairs={{0,1},{1,0},{2,3},{3,2},{4,5},{5,4},{6,7},{7,6},{8,9},{9,8},{10,11... | collective-permute-start | bytes 1572872 | tf_op jit(solution)/shard_map/ppermute | solution.py:218
  140.7 7.5 %collective-permute-start.13 = (bf16[32,2048]{1,0:T(8,128)(2,1)S(1)}, bf16[32,2048]{1,0:T(8,128)(2,1)S(1)}, u32[]{:S(2)}, u32[]{:S(2)}) collective-permute-start(bf16[32,2048]{1,0:T(8,128)(2,1)S(1)} %get-tuple-element.34), channel_id=1, source_target_pairs={{0,3},{1,2},{2,1},{3,0},{4,7},{5,6},{6,5},{7,4},{8,11},{9,10},{10,... | collective-permute-start | bytes 393224 | tf_op jit(solution)/shard_map/ppermute | solution.py:347
  144.0 6.8 %collective-permute-start.12 = (bf16[32,2048]{1,0:T(8,128)(2,1)S(1)}, bf16[32,2048]{1,0:T(8,128)(2,1)S(1)}, u32[]{:S(2)}, u32[]{:S(2)}) collective-permute-start(bf16[32,2048]{1,0:T(8,128)(2,1)S(1)} %get-tuple-element.35), channel_id=1, source_target_pairs={{0,2},{1,3},{2,0},{3,1},{4,6},{5,7},{6,4},{7,5},{8,10},{9,11},{10,... | collective-permute-start | bytes 393224 | tf_op jit(solution)/shard_map/ppermute | solution.py:347
  144.3 6.5 %collective-permute-start.11 = (bf16[32,2048]{1,0:T(8,128)(2,1)S(1)}, bf16[32,2048]{1,0:T(8,128)(2,1)S(1)}, u32[]{:S(2)}, u32[]{:S(2)}) collective-permute-start(bf16[32,2048]{1,0:T(8,128)(2,1)S(1)} %get-tuple-element.36), channel_id=1, source_target_pairs={{0,1},{1,0},{2,3},{3,2},{4,5},{5,4},{6,7},{7,6},{8,9},{9,8},{10,11... | collective-permute-start | bytes 393224 | tf_op jit(solution)/shard_map/ppermute | solution.py:347
Sparse Core Ops, SparseCore 0:
  83.4 56.1 reduce-scatter.1

commit v3 on v2

--- a/solution.py
+++ b/solution.py
@@ -163,26 +163,34 @@
             state = power * state + full[CHUNK:]
 
 
-def mix_kernel(at_ref, ends_ref, rt_ref, din_ref, y_ref, q_ref, mixed_ref):
+def mix_kernel(at_ref, ends_ref, rt_ref, din_ref, y_ref, q_ref, mixed_ref, carried_state):
     rows = y_ref.shape[0]
-    here = at_ref[0]
-    block_power = jnp.exp(-rt_ref[...] * float(rows))
-    state = jnp.zeros(rt_ref.shape, F32)
-    for j in range(ends_ref.shape[0]):
-        state = jnp.where(j < here, block_power * state + ends_ref[j], state)
-    power = jnp.exp(-rt_ref[...] * float(CHUNK))
+    rt = rt_ref[...]
+
+    @pl.when(pl.program_id(0) == 0)
+    def _():
+        here = at_ref[0]
+        block_power = jnp.exp(-rt * float(rows * pl.num_programs(0)))
+        state = jnp.zeros(rt.shape, F32)
+        for j in range(ends_ref.shape[0]):
+            state = jnp.where(j < here, block_power * state + ends_ref[j], state)
+        carried_state[...] = state
+
+    state = carried_state[...]
+    power = jnp.exp(-rt * float(CHUNK))
     din = din_ref[...]
     for q in range(rows // CHUNK):
         span = slice(q * CHUNK, (q + 1) * CHUNK)
         carried = jnp.dot(din, spread(state), preferred_element_type=F32)
         mixed_ref[span, :] = (q_ref[span, :] * (y_ref[span, :] + carried)).astype(BF)
         state = power * state
-
-
-def product_kernel(at_ref, a0, a1, a2, a3, w0, w1, m1, r1, r2, r3, m2, c_ref, left, right):
+    carried_state[...] = state
+
+
+def product_kernel(at_ref, a0, a1, a2, a3, w0, w1, m1, r1, r2, r3, m2, f1, c_ref, left, right):
     y, mine = at_ref[1], at_ref[2]
     depth = w0.shape[0]
-    piece, tail = m1.shape[1], m2.shape[1]
+    piece, tail = m1.shape[0], m2.shape[0]
 
     @pl.when(pl.program_id(0) == 0)
     def _():
@@ -191,12 +199,14 @@
 
     right[0:depth] = w0[...]
     right[depth : 2 * depth] = w1[...]
-    for s in range(2):
-        base = (2 + s) * depth
-        for k, ref in enumerate((m1, r1, r2, r3)):
-            start = pl.multiple_of(base + lax.rem(y - k + 4, 4) * piece, 16)
-            right[pl.ds(start, piece), :] = ref[s]
-        right[base + 4 * piece : base + 4 * piece + tail, :] = m2[s]
+    for k, ref in enumerate((m1, r1, r2, r3)):
+        shift = lax.rem(y - k + 4, 4) * piece
+        start = pl.multiple_of(2 * depth + shift, 16)
+        right[pl.ds(start, piece), :] = ref[...]
+        start = pl.multiple_of(3 * depth + shift, 16)
+        right[pl.ds(start, piece), :] = f1[k * piece : (k + 1) * piece]
+    right[3 * depth - tail : 3 * depth] = m2[...]
+    right[4 * depth - tail : 4 * depth] = f1[4 * piece :]
     block = 256
     for m in range(left.shape[0] // block):
         total = jnp.dot(left[m * block : (m + 1) * block, :], right[...], preferred_element_type=F32).astype(BF)
@@ -224,25 +234,20 @@
     width = out_weight.shape[1] // 4
     y, xh, core = lax.axis_index("y"), lax.axis_index("xh"), lax.axis_index("c")
     seq = lax.axis_index(("y", "xl"))
-    at = jnp.stack([seq, y, xh * 2 + core]).astype(jnp.int32)
+    at = jnp.stack([seq, y, xh * 2 + core, core]).astype(jnp.int32)
 
     halo = lax.ppermute(projected[:, rows - 8 :, :], ("y", "xl"), [(i, i + 1) for i in range(7)])
 
-    def columns(h, k):
-        return lax.dynamic_slice(out_weight, (0, (h * 2 + k) * width), (channels, width))
-
-    w_mine = columns(xh, core)
-    o_mine = columns(1 - xh, core)
-    o_other = other_core(columns(1 - xh, 1 - core))
-    w_other = other_core(columns(xh, 1 - core))
     piece = 48
+    half = 2 * width
     mirror = [(0, 3), (3, 0), (1, 2), (2, 1)]
 
-    def rows_of(start, size):
-        return jnp.stack([lax.dynamic_slice(v, (start, 0), (size, width)) for v in (o_mine, o_other)])
-
-    m1 = lax.ppermute(rows_of(y * piece, piece), ("xl", "xh"), mirror)
-    m2 = lax.ppermute(rows_of(4 * piece, channels - 4 * piece), ("xl", "xh"), mirror)
+    def weight_rows(start, size):
+        return lax.dynamic_slice(out_weight, (start, (1 - xh) * half), (size, half))
+
+    m1 = lax.ppermute(weight_rows(y * piece, piece), ("xl", "xh"), mirror)
+    m2 = lax.ppermute(weight_rows(4 * piece, channels - 4 * piece), ("xl", "xh"), mirror)
+    w_other = other_core(lax.dynamic_slice(out_weight, (0, (xh * 2 + 1 - core) * width), (channels, width)))
 
     weight = residue * jnp.sqrt(-jnp.expm1(-2.0 * rate))
     flat = groups * MODES
@@ -278,6 +283,7 @@
         cost_estimate=pl.CostEstimate(flops=2 * 10**7, bytes_accessed=6 * 2**20, transcendentals=10**4),
         name="state",
     )(projected, projected, halo, short_filter, rate)
+    signal, m1 = lax.optimization_barrier((signal, m1))
     ends = lax.all_to_all(end, ("y", "xl"), 0, 0, tiled=True)
     conv, query, din = pl.pallas_call(
         conv_kernel,
@@ -297,47 +303,60 @@
             pltpu.VMEM((CHUNK + MODES, groups * CHUNK), BF),
             pltpu.VMEM((channels // LANES, LANES // GROUP * CHUNK, 2 * LANES), BF),
         ],
-        compiler_params=pltpu.CompilerParams(vmem_limit_bytes=20 * 2**20),
         cost_estimate=pl.CostEstimate(flops=4 * 10**9, bytes_accessed=12 * 2**20, transcendentals=10**5),
         name="conv",
     )(projected, signal, halo, short_filter, rate, weight, rt)
-    ends, m1 = lax.optimization_barrier((ends, m1))
+    r1, r2, r3 = (lax.ppermute(m1, "y", [(i, (i + k) % 4) for i in range(4)]) for k in (1, 2, 3))
+    ends, r1, r3, m2 = lax.optimization_barrier((ends, r1, r3, m2))
     mixed = pl.pallas_call(
         mix_kernel,
         out_shape=jax.ShapeDtypeStruct((rows, channels), BF),
-        in_specs=[SM] + [VM] * 5,
-        out_specs=VM,
-        compiler_params=pltpu.CompilerParams(vmem_limit_bytes=12 * 2**20),
+        grid=(rows // span,),
+        in_specs=[
+            SM, whole(ends.shape), whole(rt.shape), whole(din.shape),
+            pl.BlockSpec((span, channels), lambda i: (i, 0)),
+            pl.BlockSpec((span, channels), lambda i: (i, 0)),
+        ],
+        out_specs=pl.BlockSpec((span, channels), lambda i: (i, 0)),
+        scratch_shapes=[pltpu.VMEM((MODES, channels), F32)],
         cost_estimate=pl.CostEstimate(flops=2 * 10**8, bytes_accessed=5 * 2**20, transcendentals=10**4),
         name="mix",
     )(at, ends, rt, din, conv, query)
 
-    r1, r2, r3 = (lax.ppermute(m1, "y", [(i, (i + k) % 4) for i in range(4)]) for k in (1, 2, 3))
     a_far = lax.ppermute(mixed, "xh", [(0, 1), (1, 0)])
     a_other = other_core(mixed)
-    a_far, m2, r1, r2, r3 = lax.optimization_barrier((a_far, m2, r1, r2, r3))
     a_far_other = other_core(a_far)
+    given = jnp.concatenate(
+        [lax.dynamic_slice(v, (0, (1 - core) * width), (v.shape[0], width)) for v in (m1, r1, r2, r3, m2)], axis=0
+    )
+    f_other = other_core(given)
 
     tile = 512
+    strips = width // tile
 
     def strip(shape):
-        return pl.BlockSpec(shape[:-1] + (tile,), lambda i: (0,) * (len(shape) - 1) + (i,))
+        return pl.BlockSpec(shape[:-1] + (tile,), lambda i, at_ref: (0, i))
+
+    def half_strip(shape):
+        return pl.BlockSpec(shape[:-1] + (tile,), lambda i, at_ref: (0, at_ref[3] * strips + i))
 
     partial = pl.pallas_call(
         product_kernel,
         out_shape=pltpu.HBM((rows, width), BF),
-        grid=(width // tile,),
-        in_specs=[SM]
-        + [pl.BlockSpec((rows, channels), lambda i: (0, 0), **once)] * 4
-        + [strip((channels, width))] * 2
-        + [strip(m1.shape)] * 4
-        + [strip(m2.shape)],
-        out_specs=strip((rows, width)),
-        scratch_shapes=[pltpu.VMEM((rows, 4 * channels), BF), pltpu.VMEM((4 * channels, tile), BF)],
+        grid_spec=pltpu.PrefetchScalarGridSpec(
+            num_scalar_prefetch=1,
+            grid=(strips,),
+            in_specs=[pl.BlockSpec((rows, channels), lambda i, at_ref: (0, 0), **once)] * 4
+            + [pl.BlockSpec((channels, tile), lambda i, at_ref: (0, at_ref[2] * strips + i)), strip(w_other.shape)]
+            + [half_strip(m1.shape)] * 4
+            + [half_strip(m2.shape), strip(f_other.shape)],
+            out_specs=strip((rows, width)),
+            scratch_shapes=[pltpu.VMEM((rows, 4 * channels), BF), pltpu.VMEM((4 * channels, tile), BF)],
+        ),
         compiler_params=pltpu.CompilerParams(vmem_limit_bytes=28 * 2**20),
         cost_estimate=pl.CostEstimate(flops=4 * 10**9, bytes_accessed=10 * 2**20, transcendentals=0),
         name="product",
-    )(at, mixed, a_other, a_far, a_far_other, w_mine, w_other, m1, r1, r2, r3, m2)
+    )(at, mixed, a_other, a_far, a_far_other, pltpu.with_memory_space_constraint(out_weight, pltpu.HBM), w_other, m1, r1, r2, r3, m2, f_other)
 
     summed = lax.psum_scatter(partial, "z", scatter_dimension=0, tiled=True)
     size = summed.shape[0] // 4

time: 160 us -> 165 us (1.031)
  Pallas kernels: 17.3 us -> 22.1 us
  starting transfers between devices: 28.6 us -> 25.7 us
  local copies, waits for them, and re-layouts: 12.3 us -> 15.1 us
    ppermute x2, waiting for transfers between devices: 12.9 us -> 0.01 us  [the longest x1 0.01 us: local(): lax.ppermute(weight_rows(4 * piece, channels - 4 * piece), ('xl', 'xh'),...]
    ppermute x1, waiting for transfers between devices: 0.01 us -> 8.58 us  [local(): a_far = lax.ppermute(mixed, 'xh', [(0, 1), (1, 0)])]
    ppermute x4, starting transfers between devices: 9.77 us -> 3.07 us  [other_core(): return lax.ppermute(value, 'c', [(0, 1), (1, 0)])]
    another operation x4 -> x0, local copies, waits for them, and re-layouts: 3.98 us -> none  [rows_of(): jnp.stack([lax.dynamic_slice(v, (start, 0), (size, width)) for v in (o_mi...]
    ppermute x3, waiting for transfers between devices: 8.59 us -> 12.1 us  [local(): lax.ppermute(m1, 'y', [(i, (i + k) % 4) for i in range(4)])]
    pallas_call x1, Pallas kernels: 0.9 us -> 3.94 us  [local(): pl.pallas_call(mix_kernel, out_shape=jax.ShapeDtypeStruct((rows, channels...]
    ppermute x1, starting transfers between devices: 1.37 us -> 3.93 us  [local(): lax.ppermute(projected[:, rows - 8:, :], ('y', 'xl'), [(i, i + 1) for i i...]
    unnamed x14 -> x20, local copies, waits for them, and re-layouts: 3.5 us -> 5.8 us
  transfers between devices with their start and end apart: 16 -> 16, of which waited for: 8 -> 7; matrix products, arithmetic and copies ran while one was open for 4% -> 7% of each run, Pallas kernels for 5% -> 8%
where the time goes in v3:
time: 165 us; the launch traced here: 164 us
  waiting for transfers between devices  85.5 us (52%)
  starting transfers between devices  25.7 us (16%)
  Pallas kernels  22.1 us (13%)
  local copies, waits for them, and re-layouts  15.1 us (9%)
  between operations  13.5 us (8%)
  other arithmetic  2 us (1%)
    reduce_scatter x1, waiting for transfers between devices, local(): summed = lax.psum_scatter(partial, 'z', scatter_dimension=0, tiled=True)  57 us
    ppermute x3, waiting for transfers between devices, local(): lax.ppermute(m1, 'y', [(i, (i + k) % 4) for i in range(4)])  12.1 us
    ppermute x1, waiting for transfers between devices, local(): a_far = lax.ppermute(mixed, 'xh', [(0, 1), (1, 0)])  8.58 us
    pallas_call x1, Pallas kernels, local(): pl.pallas_call(product_kernel, out_shape=pltpu.HBM((rows, width), BF), gr...  8.25 us
    ppermute x3, waiting for transfers between devices, traded(): return lax.ppermute(summed[k * size:(k + 1) * size], ('xh', 'c'), pairs)  6.3 us
    unnamed x20, local copies, waits for them, and re-layouts  5.8 us
    pallas_call x1, Pallas kernels, local(): pl.pallas_call(conv_kernel, out_shape=(pltpu.HBM((rows, channels), F32),...  5.29 us
    ppermute x3, starting transfers between devices, local(): lax.ppermute(m1, 'y', [(i, (i + k) % 4) for i in range(4)])  4.47 us
  transfers between devices with their start and end apart: 16, of which 7 were waited for; matrix products, arithmetic and copies ran while one was open for 7% of the time, Pallas kernels for 8%

profile of v3, /device:TPU:1, one launch (start us, length us, event | category | flops | bytes accessed | tf_op | source)
XLA Modules:
  0.0 163.9 jit_solution(4682409856339328959)
XLA Ops:
  6.5 1.4 slice.15
  8.0 3.9 %collective-permute-start = (bf16[3,8,256]{2,1,0:T(8,128)(2,1)}, bf16[3,8,256]{2,1,0:T(8,128)(2,1)S(1)}, u32[]{:S(2)}, u32[]{:S(2)}) collective-permute-start(bf16[3,8,256]{2,1,0:T(8,128)(2,1)} %slice.15), channel_id=1, source_target_pairs={{0,32},{32,64},{64,96},{96,128},{128,160},{160,192},{192,224},{1,3... | collective-permute-start | bytes 36872 | tf_op jit(solution)/shard_map/ppermute | solution.py:239
  11.9 1.8 %dynamic_slice.24 = bf16[48,4096]{1,0:T(8,128)(2,1)} dynamic-slice(bf16[256,8192]{1,0:T(8,128)(2,1)} %w0.1, s32[]{:T(128)S(6)} %select_n.8, s32[]{:T(128)S(6)} %select_n.18), dynamic_slice_sizes={48,4096} | dynamic-slice | bytes 786436 | tf_op jit(solution)/shard_map/dynamic_slice | solution.py:246
  13.7 2.8 %collective-permute-start.1 = (bf16[48,4096]{1,0:T(8,128)(2,1)}, bf16[48,4096]{1,0:T(8,128)(2,1)S(1)}, u32[]{:S(2)}, u32[]{:S(2)}) collective-permute-start(bf16[48,4096]{1,0:T(8,128)(2,1)} %dynamic_slice.24), channel_id=1, source_target_pairs={{0,34},{34,0},{2,32},{32,2},{1,35},{35,1},{3,33},{33,3},{4,38},{38... | collective-permute-start | bytes 1179656 | tf_op jit(solution)/shard_map/ppermute | solution.py:248
  16.5 1.9 %constant_dynamic-slice_fusion.1 = bf16[64,4096]{1,0:T(8,128)(2,1)} fusion(bf16[256,8192]{1,0:T(8,128)(2,1)} %w0.1, s32[]{:T(128)S(6)} %select_n.18), kind=kLoop, calls=%fused_computation.8 | loop fusion | bytes 1048580 | tf_op jit(solution)/shard_map/dynamic_slice | solution.py:246
  18.4 0.0 collective-permute-start.4
  18.4 2.3 %constant_dynamic-slice_fusion = bf16[256,2048]{1,0:T(8,128)(2,1)} fusion(bf16[256,8192]{1,0:T(8,128)(2,1)} %w0.1, s32[]{:T(128)S(6)} %select_n.19), kind=kLoop, calls=%fused_computation.6 | loop fusion | bytes 2097156 | tf_op jit(solution)/shard_map/dynamic_slice | solution.py:250
  20.7 1.4 collective-permute-start.8
  22.1 1.3 sqrt_multiply_fusion.weight_ref
  23.4 0.7 pad_add_fusion.at_ref
  24.1 0.0 collective-permute-done.halo_ref
  24.1 0.7 copy-done.2
  24.8 0.7 copy-done.4
  25.5 3.3 %state.1 = (bf16[1024,256]{1,0:T(8,128)(2,1)}, f32[8,16,256]{2,1,0:T(8,128)}, f32[16,256]{1,0:T(8,128)S(1)}) custom-call(bf16[3,1024,256]{2,1,0:T(8,128)(2,1)S(1)} %copy-done, bf16[3,1024,256]{2,1,0:T(8,128)(2,1)S(1)} %copy-done, bf16[3,8,256]{2,1,0:T(8,128)(2,1)S(1)} %collective-permute-done.halo_ref, f32[3,3,256]{2,1,0:T(4,128)S(1)} %copy-done.4, ...), custom_call_target="tpu_custom_call" | custom-call | flops 20000000 | bytes 6291456 | tf_op jit(solution)/shard_map/state/pallas_call | solution.py:263
  28.8 0.6 copy-done.3
  29.4 4.2 %all-to-all-start = ((f32[8,16,256]{2,1,0:T(8,128)}), f32[8,16,256]{2,1,0:T(8,128)S(1)}, u32[]{:S(2)}, u32[]{:S(2)}) async-start(f32[8,16,256]{2,1,0:T(8,128)} %get-tuple-element.17), calls=%async_computation | async-start | bytes 262144 | tf_op jit(solution)/shard_map/all_to_all | solution.py:287
  33.6 0.0 reduce-scatter.2.cloned.1.call-start
  33.6 3.0 %collective-permute-start.9 = (bf16[48,4096]{1,0:T(8,128)(2,1)S(1)}, bf16[48,4096]{1,0:T(8,128)(2,1)S(1)}, u32[]{:S(2)}, u32[]{:S(2)}) collective-permute-start(bf16[48,4096]{1,0:T(8,128)(2,1)S(1)} %collective-permute-done.1.m1), channel_id=1, source_target_pairs={{0,128},{64,192},{128,0},{192,64},{1,129},{65,193},{129,1},{193,65... | collective-permute-start | bytes 1179656 | tf_op jit(solution)/shard_map/ppermute | solution.py:309
  36.6 0.9 collective-permute-start.3
  37.5 0.6 collective-permute-start.2
  38.1 5.3 %conv.1 = (f32[1024,256]{1,0:T(8,128)}, f32[1024,256]{1,0:T(8,128)}, bf16[128,256]{1,0:T(8,128)(2,1)}) custom-call(bf16[3,1024,256]{2,1,0:T(8,128)(2,1)} %p_ref.1, bf16[1024,256]{1,0:T(8,128)(2,1)} %get-tuple-element.22.x_ref, bf16[3,8,256]{2,1,0:T(8,128)(2,1)} %copy-done.5, f32[3,3,256]{2,1,0:T(4,128)} %sf_ref.3, f32[16,16]{1,0:T(8,128)} %rate_ref.3, ...), custom_call_target="tpu_custom_call" | custom-call | flops 4000000000 | bytes 12582912 | tf_op jit(solution)/shard_map/conv/pallas_call | solution.py:288
  43.4 0.7 dynamic-slice_dynamic-update-slice_fusion.4
  44.1 0.0 all-to-all-done.ends_ref
  44.1 0.0 collective-permute-done.4.m2
  44.1 10.6 %collective-permute-done.3.r3 = bf16[48,4096]{1,0:T(8,128)(2,1)S(1)} collective-permute-done((bf16[48,4096]{1,0:T(8,128)(2,1)S(1)}, bf16[48,4096]{1,0:T(8,128)(2,1)S(1)}, u32[]{:S(2)}, u32[]{:S(2)}) %collective-permute-start.3) | collective-permute-done | bytes 393248 | tf_op jit(solution)/shard_map/ppermute | solution.py:309
  54.7 1.5 collective-permute-done.2.r1
  56.2 3.9 %mix.1.a0 = bf16[1024,256]{1,0:T(8,128)(2,1)} custom-call(s32[4]{0:T(128)} %pad_add_fusion.at_ref, f32[8,16,256]{2,1,0:T(8,128)} %copy-done.7, f32[16,256]{1,0:T(8,128)} %copy-done.3, bf16[128,256]{1,0:T(8,128)(2,1)} %get-tuple-element.23.din_ref, f32[1024,256]{1,0:T(8,128)} %get-tuple-element.24.y_ref, f32[1024,256]{1,0:T(8,128)} %get-tuple-element.25.q_ref), custom_call_target="tpu_custom_call" | custom-call | flops 200000000 | bytes 5242880 | tf_op jit(solution)/shard_map/mix/pallas_call | solution.py:311
  60.1 3.4 %collective-permute-start.6 = (bf16[1024,256]{1,0:T(8,128)(2,1)}, bf16[1024,256]{1,0:T(8,128)(2,1)S(1)}, u32[]{:S(2)}, u32[]{:S(2)}) collective-permute-start(bf16[1024,256]{1,0:T(8,128)(2,1)} %mix.1.a0), channel_id=1, source_target_pairs={{0,2},{2,0},{1,3},{3,1},{4,6},{6,4},{5,7},{7,5},{8,10},{10,8},{9,1... | collective-permute-start | bytes 1572872 | tf_op jit(solution)/shard_map/ppermute | solution.py:326
  63.6 0.7 dynamic-slice_dynamic-update-slice_fusion.3
  64.3 0.7 dynamic-slice_dynamic-update-slice_fusion.2
  65.0 0.7 dynamic-slice_dynamic-update-slice_fusion.1
  65.6 0.7 dynamic-slice_dynamic-update-slice_fusion
  66.4 0.7 collective-permute-start.10
  67.1 0.0 collective-permute-start.5
  67.1 8.6 %collective-permute-done.6.a2 = bf16[1024,256]{1,0:T(8,128)(2,1)S(1)} collective-permute-done((bf16[1024,256]{1,0:T(8,128)(2,1)}, bf16[1024,256]{1,0:T(8,128)(2,1)S(1)}, u32[]{:S(2)}, u32[]{:S(2)}) %collective-permute-start.6) | collective-permute-done | bytes 524320 | tf_op jit(solution)/shard_map/ppermute | solution.py:326
  75.7 1.0 collective-permute-start.7
  76.7 1.5 collective-permute-done.7.a3
  78.2 1.0 copy-done.1
  79.2 8.3 %product.1 = bf16[1024,2048]{1,0:T(8,128)(2,1)} custom-call(s32[4]{0:T(128)S(1)} %copy-done.6, bf16[1024,256]{1,0:T(8,128)(2,1)S(1)} %copy-done.1, bf16[1024,256]{1,0:T(8,128)(2,1)S(1)} %collective-permute-done.5.a1, bf16[1024,256]{1,0:T(8,128)(2,1)S(1)} %collective-permute-done.6.a2, bf16[1024,256]{1,0:T(8,128)(2,1)S(1)} %collective-permute-done.7.a3, ...), custom_call_target="tpu_custom_call" | custom-call | flops 4000000000 | bytes 10485760 | tf_op jit(solution)/shard_map/product/pallas_call | solution.py:343
  87.5 0.0 reduce-scatter.2.cloned.1.call-update
  87.5 57.0 %reduce-scatter.2.cloned.1.call-done = bf16[128,2048]{1,0:T(8,128)(2,1)} async-done(((bf16[1024,2048]{1,0:T(8,128)(2,1)}), bf16[128,2048]{1,0:T(8,128)(2,1)}) %reduce-scatter.2.cloned.1.call-update) | async-done | bytes 524304 | tf_op jit(solution)/shard_map/reduce_scatter | solution.py:361
  144.5 1.1 fusion
  145.6 3.3 %collective-permute-start.13 = (bf16[32,2048]{1,0:T(8,128)(2,1)S(1)}, bf16[32,2048]{1,0:T(8,128)(2,1)S(1)}, u32[]{:S(2)}, u32[]{:S(2)}) collective-permute-start(bf16[32,2048]{1,0:T(8,128)(2,1)S(1)} %get-tuple-element.29), channel_id=1, source_target_pairs={{0,3},{1,2},{2,1},{3,0},{4,7},{5,6},{6,5},{7,4},{8,11},{9,10},{10,... | collective-permute-start | bytes 393224 | tf_op jit(solution)/shard_map/ppermute | solution.py:366
  148.9 0.3 collective-permute-start.12
  149.2 0.2 collective-permute-start.11
  149.4 3.7 %collective-permute-done.13.p3 = bf16[32,2048]{1,0:T(8,128)(2,1)S(1)} collective-permute-done((bf16[32,2048]{1,0:T(8,128)(2,1)S(1)}, bf16[32,2048]{1,0:T(8,128)(2,1)S(1)}, u32[]{:S(2)}, u32[]{:S(2)}) %collective-permute-start.13) | collective-permute-done | bytes 131104 | tf_op jit(solution)/shard_map/ppermute | solution.py:366
  153.1 2.6 %collective-permute-done.12.p2 = bf16[32,2048]{1,0:T(8,128)(2,1)S(1)} collective-permute-done((bf16[32,2048]{1,0:T(8,128)(2,1)S(1)}, bf16[32,2048]{1,0:T(8,128)(2,1)S(1)}, u32[]{:S(2)}, u32[]{:S(2)}) %collective-permute-start.12) | collective-permute-done | bytes 131104 | tf_op jit(solution)/shard_map/ppermute | solution.py:366
  155.7 1.4 join.1
  (18 shorter events, 0.0 us)
Async XLA Ops:
  6.5 17.6 %copy-start = (bf16[3,1024,256]{2,1,0:T(8,128)(2,1)S(1)}, bf16[3,1024,256]{2,1,0:T(8,128)(2,1)}, u32[]{:S(2)}) copy-start(bf16[3,1024,256]{2,1,0:T(8,128)(2,1)} %p_ref.1) | copy-start | bytes 4718596
  8.0 16.1 %collective-permute-start = (bf16[3,8,256]{2,1,0:T(8,128)(2,1)}, bf16[3,8,256]{2,1,0:T(8,128)(2,1)S(1)}, u32[]{:S(2)}, u32[]{:S(2)}) collective-permute-start(bf16[3,8,256]{2,1,0:T(8,128)(2,1)} %slice.15), channel_id=1, source_target_pairs={{0,32},{32,64},{64,96},{96,128},{128,160},{160,192},{192,224},{1,3... | collective-permute-start | bytes 36872 | tf_op jit(solution)/shard_map/ppermute | solution.py:239
  13.7 19.9 %collective-permute-start.1 = (bf16[48,4096]{1,0:T(8,128)(2,1)}, bf16[48,4096]{1,0:T(8,128)(2,1)S(1)}, u32[]{:S(2)}, u32[]{:S(2)}) collective-permute-start(bf16[48,4096]{1,0:T(8,128)(2,1)} %dynamic_slice.24), channel_id=1, source_target_pairs={{0,34},{34,0},{2,32},{32,2},{1,35},{35,1},{3,33},{33,3},{4,38},{38... | collective-permute-start | bytes 1179656 | tf_op jit(solution)/shard_map/ppermute | solution.py:248
  18.4 25.7 %collective-permute-start.4 = (bf16[64,4096]{1,0:T(8,128)(2,1)}, bf16[64,4096]{1,0:T(8,128)(2,1)S(1)}, u32[]{:S(2)}, u32[]{:S(2)}) collective-permute-start(bf16[64,4096]{1,0:T(8,128)(2,1)} %constant_dynamic-slice_fusion.1), channel_id=1, source_target_pairs={{0,34},{34,0},{2,32},{32,2},{1,35},{35,1},{3,33},{33,3},{4,38},{38... | collective-permute-start | bytes 1572872 | tf_op jit(solution)/shard_map/ppermute | solution.py:249
  20.7 55.9 %collective-permute-start.8 = (bf16[256,2048]{1,0:T(8,128)(2,1)}, bf16[256,2048]{1,0:T(8,128)(2,1)S(1)}, u32[]{:S(2)}, u32[]{:S(2)}) collective-permute-start(bf16[256,2048]{1,0:T(8,128)(2,1)} %constant_dynamic-slice_fusion), channel_id=1, source_target_pairs={{0,1},{1,0},{2,3},{3,2},{4,5},{5,4},{6,7},{7,6},{8,9},{9,8},{10,11... | collective-permute-start | bytes 3145736 | tf_op jit(solution)/shard_map/ppermute | solution.py:228
  24.1 0.7 copy-start.2
  24.8 0.7 copy-start.4
  25.5 12.6 %copy-start.5 = (bf16[3,8,256]{2,1,0:T(8,128)(2,1)}, bf16[3,8,256]{2,1,0:T(8,128)(2,1)S(1)}, u32[]{:S(2)}) copy-start(bf16[3,8,256]{2,1,0:T(8,128)(2,1)S(1)} %collective-permute-done.halo_ref) | copy-start | bytes 36868
  28.8 0.6 copy-start.3
  29.4 14.7 %all-to-all-start = ((f32[8,16,256]{2,1,0:T(8,128)}), f32[8,16,256]{2,1,0:T(8,128)S(1)}, u32[]{:S(2)}, u32[]{:S(2)}) async-start(f32[8,16,256]{2,1,0:T(8,128)} %get-tuple-element.17), calls=%async_computation | async-start | bytes 262144 | tf_op jit(solution)/shard_map/all_to_all | solution.py:287
  33.6 110.9 %reduce-scatter.2.cloned.1.call-start = ((), (), s32[]{:S(2)}) async-start(), calls=%async_computation.2 | async-start | bytes 4718592 | tf_op jit(solution)/shard_map/reduce_scatter | solution.py:361
  33.6 30.6 %collective-permute-start.9 = (bf16[48,4096]{1,0:T(8,128)(2,1)S(1)}, bf16[48,4096]{1,0:T(8,128)(2,1)S(1)}, u32[]{:S(2)}, u32[]{:S(2)}) collective-permute-start(bf16[48,4096]{1,0:T(8,128)(2,1)S(1)} %collective-permute-done.1.m1), channel_id=1, source_target_pairs={{0,128},{64,192},{128,0},{192,64},{1,129},{65,193},{129,1},{193,65... | collective-permute-start | bytes 1179656 | tf_op jit(solution)/shard_map/ppermute | solution.py:309
  36.6 18.1 %collective-permute-start.3 = (bf16[48,4096]{1,0:T(8,128)(2,1)S(1)}, bf16[48,4096]{1,0:T(8,128)(2,1)S(1)}, u32[]{:S(2)}, u32[]{:S(2)}) collective-permute-start(bf16[48,4096]{1,0:T(8,128)(2,1)S(1)} %collective-permute-done.1.m1), channel_id=1, source_target_pairs={{0,192},{64,0},{128,64},{192,128},{1,193},{65,1},{129,65},{193,129... | collective-permute-start | bytes 1179656 | tf_op jit(solution)/shard_map/ppermute | solution.py:309
  37.5 18.7 %collective-permute-start.2 = (bf16[48,4096]{1,0:T(8,128)(2,1)S(1)}, bf16[48,4096]{1,0:T(8,128)(2,1)S(1)}, u32[]{:S(2)}, u32[]{:S(2)}) collective-permute-start(bf16[48,4096]{1,0:T(8,128)(2,1)S(1)} %collective-permute-done.1.m1), channel_id=1, source_target_pairs={{0,64},{64,128},{128,192},{192,0},{1,65},{65,129},{129,193},{193,1... | collective-permute-start | bytes 1179656 | tf_op jit(solution)/shard_map/ppermute | solution.py:309
  43.4 34.8 %copy-start.6 = (s32[4]{0:T(128)S(1)}, s32[4]{0:T(128)}, u32[]{:S(2)}) copy-start(s32[4]{0:T(128)} %pad_add_fusion.at_ref) | copy-start | bytes 52
  44.1 12.1 %copy-start.7 = (f32[8,16,256]{2,1,0:T(8,128)}, f32[8,16,256]{2,1,0:T(8,128)S(1)}, u32[]{:S(2)}) copy-start(f32[8,16,256]{2,1,0:T(8,128)S(1)} %all-to-all-done.ends_ref) | copy-start | bytes 393220
  60.1 15.5 %collective-permute-start.6 = (bf16[1024,256]{1,0:T(8,128)(2,1)}, bf16[1024,256]{1,0:T(8,128)(2,1)S(1)}, u32[]{:S(2)}, u32[]{:S(2)}) collective-permute-start(bf16[1024,256]{1,0:T(8,128)(2,1)} %mix.1.a0), channel_id=1, source_target_pairs={{0,2},{2,0},{1,3},{3,1},{4,6},{6,4},{5,7},{7,5},{8,10},{10,8},{9,1... | collective-permute-start | bytes 1572872 | tf_op jit(solution)/shard_map/ppermute | solution.py:326
  66.4 10.3 %collective-permute-start.10 = (bf16[256,2048]{1,0:T(8,128)(2,1)}, bf16[256,2048]{1,0:T(8,128)(2,1)S(1)}, u32[]{:S(2)}, u32[]{:S(2)}) collective-permute-start(bf16[256,2048]{1,0:T(8,128)(2,1)} %dynamic-slice_dynamic-update-slice_fusion), channel_id=1, source_target_pairs={{0,1},{1,0},{2,3},{3,2},{4,5},{5,4},{6,7},{7,6},{8,9},{9,8},{10,11... | collective-permute-start | bytes 3145736 | tf_op jit(solution)/shard_map/ppermute | solution.py:228
  67.1 9.6 %collective-permute-start.5 = (bf16[1024,256]{1,0:T(8,128)(2,1)}, bf16[1024,256]{1,0:T(8,128)(2,1)S(1)}, u32[]{:S(2)}, u32[]{:S(2)}) collective-permute-start(bf16[1024,256]{1,0:T(8,128)(2,1)} %mix.1.a0), channel_id=1, source_target_pairs={{0,1},{1,0},{2,3},{3,2},{4,5},{5,4},{6,7},{7,6},{8,9},{9,8},{10,11... | collective-permute-start | bytes 1572872 | tf_op jit(solution)/shard_map/ppermute | solution.py:228
  75.7 2.5 %collective-permute-start.7 = (bf16[1024,256]{1,0:T(8,128)(2,1)S(1)}, bf16[1024,256]{1,0:T(8,128)(2,1)S(1)}, u32[]{:S(2)}, u32[]{:S(2)}) collective-permute-start(bf16[1024,256]{1,0:T(8,128)(2,1)S(1)} %collective-permute-done.6.a2), channel_id=1, source_target_pairs={{0,1},{1,0},{2,3},{3,2},{4,5},{5,4},{6,7},{7,6},{8,9},{9,8},{10,11... | collective-permute-start | bytes 1572872 | tf_op jit(solution)/shard_map/ppermute | solution.py:228
  78.2 1.0 copy-start.1
  145.6 7.5 %collective-permute-start.13 = (bf16[32,2048]{1,0:T(8,128)(2,1)S(1)}, bf16[32,2048]{1,0:T(8,128)(2,1)S(1)}, u32[]{:S(2)}, u32[]{:S(2)}) collective-permute-start(bf16[32,2048]{1,0:T(8,128)(2,1)S(1)} %get-tuple-element.29), channel_id=1, source_target_pairs={{0,3},{1,2},{2,1},{3,0},{4,7},{5,6},{6,5},{7,4},{8,11},{9,10},{10,... | collective-permute-start | bytes 393224 | tf_op jit(solution)/shard_map/ppermute | solution.py:366
  148.9 6.8 %collective-permute-start.12 = (bf16[32,2048]{1,0:T(8,128)(2,1)S(1)}, bf16[32,2048]{1,0:T(8,128)(2,1)S(1)}, u32[]{:S(2)}, u32[]{:S(2)}) collective-permute-start(bf16[32,2048]{1,0:T(8,128)(2,1)S(1)} %get-tuple-element.30), channel_id=1, source_target_pairs={{0,2},{1,3},{2,0},{3,1},{4,6},{5,7},{6,4},{7,5},{8,10},{9,11},{10,... | collective-permute-start | bytes 393224 | tf_op jit(solution)/shard_map/ppermute | solution.py:366
  149.2 6.5 %collective-permute-start.11 = (bf16[32,2048]{1,0:T(8,128)(2,1)S(1)}, bf16[32,2048]{1,0:T(8,128)(2,1)S(1)}, u32[]{:S(2)}, u32[]{:S(2)}) collective-permute-start(bf16[32,2048]{1,0:T(8,128)(2,1)S(1)} %get-tuple-element.31), channel_id=1, source_target_pairs={{0,1},{1,0},{2,3},{3,2},{4,5},{5,4},{6,7},{7,6},{8,9},{9,8},{10,11... | collective-permute-start | bytes 393224 | tf_op jit(solution)/shard_map/ppermute | solution.py:366
Sparse Core Ops, SparseCore 0:
  87.6 56.8 reduce-scatter.1

commit v4 on v3

--- a/solution.py
+++ b/solution.py
@@ -141,7 +141,7 @@
             q = 2 * pair + j
             span = slice(q * CHUNK, (q + 1) * CHUNK)
             before = halo_ref[0] if q == 0 else p_ref[q * CHUNK - 16 : q * CHUNK, :]
-            q_ref[span, :] = tapped(sf_ref[0], p_ref[span, :].astype(F32), before.astype(F32))
+            q_ref[span, :] = tapped(sf_ref[0], p_ref[span, :].astype(F32), before.astype(F32)).astype(BF)
             for h in range(halves):
                 part = x_ref[span, h * LANES : (h + 1) * LANES]
                 for g in range(per_half):
@@ -159,32 +159,25 @@
             within = full[:CHUNK]
             if q > 0:
                 within = within + jnp.dot(din, spread(state), preferred_element_type=F32)
-            y_ref[q * CHUNK : (q + 1) * CHUNK, :] = within
+            y_ref[q * CHUNK : (q + 1) * CHUNK, :] = within.astype(BF)
             state = power * state + full[CHUNK:]
 
 
-def mix_kernel(at_ref, ends_ref, rt_ref, din_ref, y_ref, q_ref, mixed_ref, carried_state):
+def mix_kernel(at_ref, ends_ref, rt_ref, din_ref, y_ref, q_ref, mixed_ref):
     rows = y_ref.shape[0]
+    here = at_ref[0]
     rt = rt_ref[...]
-
-    @pl.when(pl.program_id(0) == 0)
-    def _():
-        here = at_ref[0]
-        block_power = jnp.exp(-rt * float(rows * pl.num_programs(0)))
-        state = jnp.zeros(rt.shape, F32)
-        for j in range(ends_ref.shape[0]):
-            state = jnp.where(j < here, block_power * state + ends_ref[j], state)
-        carried_state[...] = state
-
-    state = carried_state[...]
+    block_power = jnp.exp(-rt * float(rows))
+    state = jnp.zeros(rt.shape, F32)
+    for j in range(ends_ref.shape[0]):
+        state = jnp.where(j < here, block_power * state + ends_ref[j], state)
     power = jnp.exp(-rt * float(CHUNK))
     din = din_ref[...]
     for q in range(rows // CHUNK):
         span = slice(q * CHUNK, (q + 1) * CHUNK)
         carried = jnp.dot(din, spread(state), preferred_element_type=F32)
-        mixed_ref[span, :] = (q_ref[span, :] * (y_ref[span, :] + carried)).astype(BF)
+        mixed_ref[span, :] = (q_ref[span, :].astype(F32) * (y_ref[span, :].astype(F32) + carried)).astype(BF)
         state = power * state
-    carried_state[...] = state
 
 
 def product_kernel(at_ref, a0, a1, a2, a3, w0, w1, m1, r1, r2, r3, m2, f1, c_ref, left, right):
@@ -234,22 +227,18 @@
     width = out_weight.shape[1] // 4
     y, xh, core = lax.axis_index("y"), lax.axis_index("xh"), lax.axis_index("c")
     seq = lax.axis_index(("y", "xl"))
-    at = jnp.stack([seq, y, xh * 2 + core, core]).astype(jnp.int32)
-
     halo = lax.ppermute(projected[:, rows - 8 :, :], ("y", "xl"), [(i, i + 1) for i in range(7)])
 
     piece = 48
     half = 2 * width
     mirror = [(0, 3), (3, 0), (1, 2), (2, 1)]
 
-    def weight_rows(start, size):
-        return lax.dynamic_slice(out_weight, (start, (1 - xh) * half), (size, half))
-
-    m1 = lax.ppermute(weight_rows(y * piece, piece), ("xl", "xh"), mirror)
-    m2 = lax.ppermute(weight_rows(4 * piece, channels - 4 * piece), ("xl", "xh"), mirror)
-    w_other = other_core(lax.dynamic_slice(out_weight, (0, (xh * 2 + 1 - core) * width), (channels, width)))
-
-    weight = residue * jnp.sqrt(-jnp.expm1(-2.0 * rate))
+    def mirrored_rows(start, size, xh):
+        rows_there = lax.dynamic_slice(out_weight, (start, (1 - xh) * half), (size, half))
+        return lax.ppermute(rows_there, ("xl", "xh"), mirror)
+
+    m1 = mirrored_rows(y * piece, piece, xh)
+
     flat = groups * MODES
     span = 256
     once = {"pipeline_mode": pl.Buffered(1)}
@@ -263,7 +252,7 @@
     signal, end, rt = pl.pallas_call(
         state_kernel,
         out_shape=(
-            pltpu.HBM((rows, channels), BF),
+            jax.ShapeDtypeStruct((rows, channels), BF),
             jax.ShapeDtypeStruct((8, MODES, channels), F32),
             jax.ShapeDtypeStruct((MODES, channels), F32),
         ),
@@ -280,16 +269,22 @@
             pltpu.VMEM((MODES, 8, channels), F32),
         ],
         compiler_params=pltpu.CompilerParams(vmem_limit_bytes=12 * 2**20),
-        cost_estimate=pl.CostEstimate(flops=2 * 10**7, bytes_accessed=6 * 2**20, transcendentals=10**4),
+        cost_estimate=pl.CostEstimate(flops=10**6, bytes_accessed=2**16, transcendentals=0),
         name="state",
     )(projected, projected, halo, short_filter, rate)
-    signal, m1 = lax.optimization_barrier((signal, m1))
+    end, xh_late, core_late, residue_late = lax.optimization_barrier((end, xh, core, residue))
+    at = jnp.stack([seq, y, xh_late * 2 + core_late, core_late]).astype(jnp.int32)
+    m2 = mirrored_rows(4 * piece, channels - 4 * piece, xh_late)
+    w_other = other_core(
+        lax.dynamic_slice(out_weight, (0, (xh_late * 2 + 1 - core_late) * width), (channels, width))
+    )
+    weight = residue_late * jnp.sqrt(-jnp.expm1(-2.0 * rate))
     ends = lax.all_to_all(end, ("y", "xl"), 0, 0, tiled=True)
     conv, query, din = pl.pallas_call(
         conv_kernel,
         out_shape=(
-            pltpu.HBM((rows, channels), F32),
-            pltpu.HBM((rows, channels), F32),
+            jax.ShapeDtypeStruct((rows, channels), BF),
+            jax.ShapeDtypeStruct((rows, channels), BF),
             jax.ShapeDtypeStruct((CHUNK, flat), BF),
         ),
         grid=(1,),
@@ -303,23 +298,19 @@
             pltpu.VMEM((CHUNK + MODES, groups * CHUNK), BF),
             pltpu.VMEM((channels // LANES, LANES // GROUP * CHUNK, 2 * LANES), BF),
         ],
-        cost_estimate=pl.CostEstimate(flops=4 * 10**9, bytes_accessed=12 * 2**20, transcendentals=10**5),
+        compiler_params=pltpu.CompilerParams(vmem_limit_bytes=16 * 2**20),
+        cost_estimate=pl.CostEstimate(flops=10**6, bytes_accessed=2**16, transcendentals=0),
         name="conv",
     )(projected, signal, halo, short_filter, rate, weight, rt)
     r1, r2, r3 = (lax.ppermute(m1, "y", [(i, (i + k) % 4) for i in range(4)]) for k in (1, 2, 3))
-    ends, r1, r3, m2 = lax.optimization_barrier((ends, r1, r3, m2))
+    ends, r1, r3 = lax.optimization_barrier((ends, r1, r3))
     mixed = pl.pallas_call(
         mix_kernel,
         out_shape=jax.ShapeDtypeStruct((rows, channels), BF),
-        grid=(rows // span,),
-        in_specs=[
-            SM, whole(ends.shape), whole(rt.shape), whole(din.shape),
-            pl.BlockSpec((span, channels), lambda i: (i, 0)),
-            pl.BlockSpec((span, channels), lambda i: (i, 0)),
-        ],
-        out_specs=pl.BlockSpec((span, channels), lambda i: (i, 0)),
-        scratch_shapes=[pltpu.VMEM((MODES, channels), F32)],
-        cost_estimate=pl.CostEstimate(flops=2 * 10**8, bytes_accessed=5 * 2**20, transcendentals=10**4),
+        in_specs=[SM] + [VM] * 5,
+        out_specs=VM,
+        compiler_params=pltpu.CompilerParams(vmem_limit_bytes=10 * 2**20),
+        cost_estimate=pl.CostEstimate(flops=10**6, bytes_accessed=2**16, transcendentals=0),
         name="mix",
     )(at, ends, rt, din, conv, query)
 

time: 165 us -> 149 us (0.903)
  waiting for transfers between devices: 85.5 us -> 70.4 us
  starting transfers between devices: 25.7 us -> 33.4 us
  Pallas kernels: 22.1 us -> 16.7 us
  other arithmetic: 2 us -> 0.1 us
    ppermute x1, waiting for transfers between devices: 8.58 us -> 0.01 us  [local(): a_far = lax.ppermute(mixed, 'xh', [(0, 1), (1, 0)])]
    ppermute x4, starting transfers between devices: 3.07 us -> 11.6 us  [other_core(): return lax.ppermute(value, 'c', [(0, 1), (1, 0)])]
    ppermute x3, waiting for transfers between devices: 12.1 us -> 6.37 us  [local(): lax.ppermute(m1, 'y', [(i, (i + k) % 4) for i in range(4)])]
    pallas_call x1, Pallas kernels: 3.94 us -> 0.91 us  [local(): pl.pallas_call(mix_kernel, out_shape=jax.ShapeDtypeStruct((rows, channels...]
    pallas_call x2, Pallas kernels: 8.55 us -> 6.11 us  [the longest x1 3.16 us: local(): pl.pallas_call(conv_kernel, out_shape=(jax.ShapeDtypeStruct((rows, channe...]
    ppermute x1, starting transfers between devices: 3.43 us -> 1.18 us  [local(): a_far = lax.ppermute(mixed, 'xh', [(0, 1), (1, 0)])]
    unnamed x20 -> x18, local copies, waits for them, and re-layouts: 5.8 us -> 5.7 us
  transfers between devices with their start and end apart: 16 -> 16, of which waited for: 7 -> 5; matrix products, arithmetic and copies ran while one was open for 7% -> 6% of each run, Pallas kernels for 8% -> 5%
where the time goes in v4:
time: 149 us; the launch traced here: 148 us
  waiting for transfers between devices  70.4 us (47%)
  starting transfers between devices  33.4 us (22%)
  Pallas kernels  16.7 us (11%)
  local copies, waits for them, and re-layouts  13.8 us (9%)
  between operations  13.5 us (9%)
    reduce_scatter x1, waiting for transfers between devices, local(): summed = lax.psum_scatter(partial, 'z', scatter_dimension=0, tiled=True)  56.1 us
    ppermute x4, starting transfers between devices, other_core(): return lax.ppermute(value, 'c', [(0, 1), (1, 0)])  11.6 us
    pallas_call x1, Pallas kernels, local(): pl.pallas_call(product_kernel, out_shape=pltpu.HBM((rows, width), BF), gr...  8.35 us
    ppermute x3, waiting for transfers between devices, local(): lax.ppermute(m1, 'y', [(i, (i + k) % 4) for i in range(4)])  6.37 us
    ppermute x3, waiting for transfers between devices, traded(): return lax.ppermute(summed[k * size:(k + 1) * size], ('xh', 'c'), pairs)  6.33 us
    unnamed x18, local copies, waits for them, and re-layouts  5.7 us
    ppermute x3, starting transfers between devices, local(): lax.ppermute(m1, 'y', [(i, (i + k) % 4) for i in range(4)])  4.54 us
    ppermute x2, starting transfers between devices, mirrored_rows(): return lax.ppermute(rows_there, ('xl', 'xh'), mirror)  4.44 us
  transfers between devices with their start and end apart: 16, of which 5 were waited for; matrix products, arithmetic and copies ran while one was open for 6% of the time, Pallas kernels for 5%

profile of v4, /device:TPU:1, one launch (start us, length us, event | category | flops | bytes accessed | tf_op | source)
XLA Modules:
  0.0 147.9 jit_solution(7026470024934974521)
XLA Ops:
  6.5 0.7 slice.15
  7.3 3.9 %collective-permute-start = (bf16[3,8,256]{2,1,0:T(8,128)(2,1)S(1)}, bf16[3,8,256]{2,1,0:T(8,128)(2,1)S(1)}, u32[]{:S(2)}, u32[]{:S(2)}) collective-permute-start(bf16[3,8,256]{2,1,0:T(8,128)(2,1)S(1)} %slice.15), channel_id=1, source_target_pairs={{0,32},{32,64},{64,96},{96,128},{128,160},{160,192},{192,224},{1,3... | collective-permute-start | bytes 36872 | tf_op jit(solution)/shard_map/ppermute | solution.py:230
  11.2 1.0 dynamic_slice.24
  12.3 2.9 %collective-permute-start.1 = (bf16[48,4096]{1,0:T(8,128)(2,1)S(1)}, bf16[48,4096]{1,0:T(8,128)(2,1)}, u32[]{:S(2)}, u32[]{:S(2)}) collective-permute-start(bf16[48,4096]{1,0:T(8,128)(2,1)S(1)} %dynamic_slice.24), channel_id=1, source_target_pairs={{0,34},{34,0},{2,32},{32,2},{1,35},{35,1},{3,33},{33,3},{4,38},{38... | collective-permute-start | bytes 1179656 | tf_op jit(solution)/shard_map/ppermute | solution.py:238
  15.2 0.0 collective-permute-done.halo_ref
  15.2 1.4 copy-done
  16.6 0.7 copy-done.2
  17.3 0.7 copy-done.4
  18.0 3.0 %state.1 = (bf16[1024,256]{1,0:T(8,128)(2,1)S(1)}, f32[8,16,256]{2,1,0:T(8,128)}, f32[16,256]{1,0:T(8,128)S(1)}) custom-call(bf16[3,1024,256]{2,1,0:T(8,128)(2,1)S(1)} %copy-done, bf16[3,1024,256]{2,1,0:T(8,128)(2,1)S(1)} %copy-done, bf16[3,8,256]{2,1,0:T(8,128)(2,1)S(1)} %collective-permute-done.halo_ref, f32[3,3,256]{2,1,0:T(4,128)S(1)} %copy-done.4, ...), custom_call_target="tpu_custom_call" | custom-call | flops 1000000 | bytes 65536 | tf_op jit(solution)/shard_map/state/pallas_call | solution.py:252
  21.0 3.9 %all-to-all-start = ((f32[8,16,256]{2,1,0:T(8,128)}), f32[8,16,256]{2,1,0:T(8,128)S(1)}, u32[]{:S(2)}, u32[]{:S(2)}) async-start(f32[8,16,256]{2,1,0:T(8,128)} %get-tuple-element.21), calls=%async_computation | async-start | bytes 262144 | tf_op jit(solution)/shard_map/all_to_all | solution.py:282
  24.9 0.0 reduce-scatter.2.cloned.1.call-start
  24.9 1.9 %constant_dynamic-slice_fusion.1 = bf16[64,4096]{1,0:T(8,128)(2,1)} fusion(bf16[256,8192]{1,0:T(8,128)(2,1)} %w0.1, s32[]{:T(128)S(6)} %select_n.22), kind=kLoop, calls=%fused_computation.8 | loop fusion | bytes 1048580 | tf_op jit(solution)/shard_map/dynamic_slice | solution.py:237
  26.8 1.5 %collective-permute-start.9 = (bf16[64,4096]{1,0:T(8,128)(2,1)}, bf16[64,4096]{1,0:T(8,128)(2,1)}, u32[]{:S(2)}, u32[]{:S(2)}) collective-permute-start(bf16[64,4096]{1,0:T(8,128)(2,1)} %constant_dynamic-slice_fusion.1), channel_id=1, source_target_pairs={{0,34},{34,0},{2,32},{32,2},{1,35},{35,1},{3,33},{33,3},{4,38},{38... | collective-permute-start | bytes 1572872 | tf_op jit(solution)/shard_map/ppermute | solution.py:238
  28.3 0.0 collective-permute-done.1.m1
  28.3 2.5 %collective-permute-start.3 = (bf16[48,4096]{1,0:T(8,128)(2,1)}, bf16[48,4096]{1,0:T(8,128)(2,1)}, u32[]{:S(2)}, u32[]{:S(2)}) collective-permute-start(bf16[48,4096]{1,0:T(8,128)(2,1)} %collective-permute-done.1.m1), channel_id=1, source_target_pairs={{0,192},{64,0},{128,64},{192,128},{1,193},{65,1},{129,65},{193,129... | collective-permute-start | bytes 1179656 | tf_op jit(solution)/shard_map/ppermute | solution.py:305
  30.8 0.0 collective-permute-start.2
  30.8 2.4 %constant_dynamic-slice_fusion = bf16[256,2048]{1,0:T(8,128)(2,1)} fusion(bf16[256,8192]{1,0:T(8,128)(2,1)} %w0.1, s32[]{:T(128)S(6)} %select_n.21), kind=kLoop, calls=%fused_computation.6 | loop fusion | bytes 2097156 | tf_op jit(solution)/shard_map/dynamic_slice | solution.py:279
  33.2 2.9 %collective-permute-start.7 = (bf16[256,2048]{1,0:T(8,128)(2,1)}, bf16[256,2048]{1,0:T(8,128)(2,1)}, u32[]{:S(2)}, u32[]{:S(2)}) collective-permute-start(bf16[256,2048]{1,0:T(8,128)(2,1)} %constant_dynamic-slice_fusion), channel_id=1, source_target_pairs={{0,1},{1,0},{2,3},{3,2},{4,5},{5,4},{6,7},{7,6},{8,9},{9,8},{10,11... | collective-permute-start | bytes 3145736 | tf_op jit(solution)/shard_map/ppermute | solution.py:221
  36.1 3.2 %conv.1 = (bf16[1024,256]{1,0:T(8,128)(2,1)S(1)}, bf16[1024,256]{1,0:T(8,128)(2,1)S(1)}, bf16[128,256]{1,0:T(8,128)(2,1)S(1)}) custom-call(bf16[3,1024,256]{2,1,0:T(8,128)(2,1)S(1)} %copy-done.1, bf16[1024,256]{1,0:T(8,128)(2,1)S(1)} %get-tuple-element.24.x_ref, bf16[3,8,256]{2,1,0:T(8,128)(2,1)S(1)} %collective-permute-done.halo_ref, ...), custom_call_target="tpu_custom_call" | custom-call | flops 1000000 | bytes 65536 | tf_op jit(solution)/shard_map/conv/pallas_call | solution.py:283
  39.3 0.1 pad_add_fusion.at_ref
  39.4 2.1 %collective-permute-start.8 = (bf16[48,4096]{1,0:T(8,128)(2,1)}, bf16[48,4096]{1,0:T(8,128)(2,1)S(1)}, u32[]{:S(2)}, u32[]{:S(2)}) collective-permute-start(bf16[48,4096]{1,0:T(8,128)(2,1)} %collective-permute-done.1.m1), channel_id=1, source_target_pairs={{0,128},{64,192},{128,0},{192,64},{1,129},{65,193},{129,1},{193,65... | collective-permute-start | bytes 1179656 | tf_op jit(solution)/shard_map/ppermute | solution.py:305
  41.4 1.0 dynamic-slice_dynamic-update-slice_fusion.4
  42.4 0.0 collective-permute-done.2.r1
  42.4 0.9 mix.1.a0
  43.3 1.2 collective-permute-start.5
  44.5 0.9 dynamic-slice_dynamic-update-slice_fusion.3
  45.5 6.4 %collective-permute-done.8.r2 = bf16[48,4096]{1,0:T(8,128)(2,1)S(1)} collective-permute-done((bf16[48,4096]{1,0:T(8,128)(2,1)}, bf16[48,4096]{1,0:T(8,128)(2,1)S(1)}, u32[]{:S(2)}, u32[]{:S(2)}) %collective-permute-start.8) | collective-permute-done | bytes 393248 | tf_op jit(solution)/shard_map/ppermute | solution.py:305
  51.9 0.9 dynamic-slice_dynamic-update-slice_fusion.1
  52.8 0.0 collective-permute-done.9.m2
  52.8 1.0 dynamic-slice_dynamic-update-slice_fusion
  53.8 4.5 %collective-permute-start.10 = (bf16[256,2048]{1,0:T(8,128)(2,1)S(1)}, bf16[256,2048]{1,0:T(8,128)(2,1)S(1)}, u32[]{:S(2)}, u32[]{:S(2)}) collective-permute-start(bf16[256,2048]{1,0:T(8,128)(2,1)S(1)} %dynamic-slice_dynamic-update-slice_fusion), channel_id=1, source_target_pairs={{0,1},{1,0},{2,3},{3,2},{4,5},{5,4},{6,7},{7,6},{8,9},{9,8},{10,11... | collective-permute-start | bytes 3145736 | tf_op jit(solution)/shard_map/ppermute | solution.py:221
  58.3 0.1 collective-permute-start.4
  58.4 0.0 collective-permute-done.5.a2
  58.4 4.0 %collective-permute-start.6 = (bf16[1024,256]{1,0:T(8,128)(2,1)S(1)}, bf16[1024,256]{1,0:T(8,128)(2,1)S(1)}, u32[]{:S(2)}, u32[]{:S(2)}) collective-permute-start(bf16[1024,256]{1,0:T(8,128)(2,1)S(1)} %collective-permute-done.5.a2), channel_id=1, source_target_pairs={{0,1},{1,0},{2,3},{3,2},{4,5},{5,4},{6,7},{7,6},{8,9},{9,8},{10,11... | collective-permute-start | bytes 1572872 | tf_op jit(solution)/shard_map/ppermute | solution.py:221
  62.4 0.0 collective-permute-done.7.w1
  62.4 1.5 %collective-permute-done.6.a3 = bf16[1024,256]{1,0:T(8,128)(2,1)S(1)} collective-permute-done((bf16[1024,256]{1,0:T(8,128)(2,1)S(1)}, bf16[1024,256]{1,0:T(8,128)(2,1)S(1)}, u32[]{:S(2)}, u32[]{:S(2)}) %collective-permute-start.6) | collective-permute-done | bytes 524320 | tf_op jit(solution)/shard_map/ppermute | solution.py:221
  63.9 0.0 collective-permute-done.10.f1
  63.9 8.3 %product.1 = bf16[1024,2048]{1,0:T(8,128)(2,1)} custom-call(s32[4]{0:T(128)S(1)} %pad_add_fusion.at_ref, bf16[1024,256]{1,0:T(8,128)(2,1)S(1)} %mix.1.a0, bf16[1024,256]{1,0:T(8,128)(2,1)S(1)} %collective-permute-done.4.a1, bf16[1024,256]{1,0:T(8,128)(2,1)S(1)} %collective-permute-done.5.a2, bf16[1024,256]{1,0:T(8,128)(2,1)S(1)} %collective-permute-done.6.a3, ...), custom_call_target="tpu_custom_call" | custom-call | flops 4000000000 | bytes 10485760 | tf_op jit(solution)/shard_map/product/pallas_call | solution.py:334
  72.3 0.0 reduce-scatter.2.cloned.1.call-update
  72.3 56.1 %reduce-scatter.2.cloned.1.call-done = bf16[128,2048]{1,0:T(8,128)(2,1)} async-done(((bf16[1024,2048]{1,0:T(8,128)(2,1)}), bf16[128,2048]{1,0:T(8,128)(2,1)}) %reduce-scatter.2.cloned.1.call-update) | async-done | bytes 524304 | tf_op jit(solution)/shard_map/reduce_scatter | solution.py:352
  128.5 1.1 fusion
  129.6 3.3 %collective-permute-start.13 = (bf16[32,2048]{1,0:T(8,128)(2,1)S(1)}, bf16[32,2048]{1,0:T(8,128)(2,1)S(1)}, u32[]{:S(2)}, u32[]{:S(2)}) collective-permute-start(bf16[32,2048]{1,0:T(8,128)(2,1)S(1)} %get-tuple-element.31), channel_id=1, source_target_pairs={{0,3},{1,2},{2,1},{3,0},{4,7},{5,6},{6,5},{7,4},{8,11},{9,10},{10,... | collective-permute-start | bytes 393224 | tf_op jit(solution)/shard_map/ppermute | solution.py:357
  132.9 0.3 collective-permute-start.12
  133.2 0.2 collective-permute-start.11
  133.4 3.8 %collective-permute-done.13.p3 = bf16[32,2048]{1,0:T(8,128)(2,1)S(1)} collective-permute-done((bf16[32,2048]{1,0:T(8,128)(2,1)S(1)}, bf16[32,2048]{1,0:T(8,128)(2,1)S(1)}, u32[]{:S(2)}, u32[]{:S(2)}) %collective-permute-start.13) | collective-permute-done | bytes 131104 | tf_op jit(solution)/shard_map/ppermute | solution.py:357
  137.1 2.6 %collective-permute-done.12.p2 = bf16[32,2048]{1,0:T(8,128)(2,1)S(1)} collective-permute-done((bf16[32,2048]{1,0:T(8,128)(2,1)S(1)}, bf16[32,2048]{1,0:T(8,128)(2,1)S(1)}, u32[]{:S(2)}, u32[]{:S(2)}) %collective-permute-start.12) | collective-permute-done | bytes 131104 | tf_op jit(solution)/shard_map/ppermute | solution.py:357
  139.7 0.0 collective-permute-done.11.p1
  139.7 1.4 join.1
  (16 shorter events, 0.1 us)
Async XLA Ops:
  6.5 21.8 %copy-start.3 = (f32[16,16]{1,0:T(8,128)S(1)}, f32[16,16]{1,0:T(8,128)}, u32[]{:S(2)}) copy-start(f32[16,16]{1,0:T(8,128)} %rate_ref.3) | copy-start | bytes 3076
  6.5 29.6 %copy-start.5 = (f32[3,3,256]{2,1,0:T(4,128)S(1)}, f32[3,3,256]{2,1,0:T(4,128)}, u32[]{:S(2)}) copy-start(f32[3,3,256]{2,1,0:T(4,128)} %sf_ref.3) | copy-start | bytes 27652
  6.5 21.8 %copy-start.6 = (f32[16,16]{1,0:T(8,128)S(1)}, f32[16,16]{1,0:T(8,128)}, u32[]{:S(2)}) copy-start(f32[16,16]{1,0:T(8,128)} %param.7) | copy-start | bytes 3076
  7.3 7.9 %collective-permute-start = (bf16[3,8,256]{2,1,0:T(8,128)(2,1)S(1)}, bf16[3,8,256]{2,1,0:T(8,128)(2,1)S(1)}, u32[]{:S(2)}, u32[]{:S(2)}) collective-permute-start(bf16[3,8,256]{2,1,0:T(8,128)(2,1)S(1)} %slice.15), channel_id=1, source_target_pairs={{0,32},{32,64},{64,96},{96,128},{128,160},{160,192},{192,224},{1,3... | collective-permute-start | bytes 36872 | tf_op jit(solution)/shard_map/ppermute | solution.py:230
  12.3 16.1 %collective-permute-start.1 = (bf16[48,4096]{1,0:T(8,128)(2,1)S(1)}, bf16[48,4096]{1,0:T(8,128)(2,1)}, u32[]{:S(2)}, u32[]{:S(2)}) collective-permute-start(bf16[48,4096]{1,0:T(8,128)(2,1)S(1)} %dynamic_slice.24), channel_id=1, source_target_pairs={{0,34},{34,0},{2,32},{32,2},{1,35},{35,1},{3,33},{33,3},{4,38},{38... | collective-permute-start | bytes 1179656 | tf_op jit(solution)/shard_map/ppermute | solution.py:238
  15.2 1.4 copy-start
  16.6 0.7 copy-start.2
  17.3 0.7 copy-start.4
  18.0 18.1 %copy-start.1 = (bf16[3,1024,256]{2,1,0:T(8,128)(2,1)S(1)}, bf16[3,1024,256]{2,1,0:T(8,128)(2,1)}, u32[]{:S(2)}) copy-start(bf16[3,1024,256]{2,1,0:T(8,128)(2,1)} %p_ref.1) | copy-start | bytes 4718596
  21.0 21.4 %all-to-all-start = ((f32[8,16,256]{2,1,0:T(8,128)}), f32[8,16,256]{2,1,0:T(8,128)S(1)}, u32[]{:S(2)}, u32[]{:S(2)}) async-start(f32[8,16,256]{2,1,0:T(8,128)} %get-tuple-element.21), calls=%async_computation | async-start | bytes 262144 | tf_op jit(solution)/shard_map/all_to_all | solution.py:282
  24.9 103.6 %reduce-scatter.2.cloned.1.call-start = ((), (), s32[]{:S(2)}) async-start(), calls=%async_computation.2 | async-start | bytes 4718592 | tf_op jit(solution)/shard_map/reduce_scatter | solution.py:352
  26.8 26.0 %collective-permute-start.9 = (bf16[64,4096]{1,0:T(8,128)(2,1)}, bf16[64,4096]{1,0:T(8,128)(2,1)}, u32[]{:S(2)}, u32[]{:S(2)}) collective-permute-start(bf16[64,4096]{1,0:T(8,128)(2,1)} %constant_dynamic-slice_fusion.1), channel_id=1, source_target_pairs={{0,34},{34,0},{2,32},{32,2},{1,35},{35,1},{3,33},{33,3},{4,38},{38... | collective-permute-start | bytes 1572872 | tf_op jit(solution)/shard_map/ppermute | solution.py:238
  28.3 14.1 %collective-permute-start.3 = (bf16[48,4096]{1,0:T(8,128)(2,1)}, bf16[48,4096]{1,0:T(8,128)(2,1)}, u32[]{:S(2)}, u32[]{:S(2)}) collective-permute-start(bf16[48,4096]{1,0:T(8,128)(2,1)} %collective-permute-done.1.m1), channel_id=1, source_target_pairs={{0,192},{64,0},{128,64},{192,128},{1,193},{65,1},{129,65},{193,129... | collective-permute-start | bytes 1179656 | tf_op jit(solution)/shard_map/ppermute | solution.py:305
  30.8 11.6 %collective-permute-start.2 = (bf16[48,4096]{1,0:T(8,128)(2,1)}, bf16[48,4096]{1,0:T(8,128)(2,1)}, u32[]{:S(2)}, u32[]{:S(2)}) collective-permute-start(bf16[48,4096]{1,0:T(8,128)(2,1)} %collective-permute-done.1.m1), channel_id=1, source_target_pairs={{0,64},{64,128},{128,192},{192,0},{1,65},{65,129},{129,193},{193,1... | collective-permute-start | bytes 1179656 | tf_op jit(solution)/shard_map/ppermute | solution.py:305
  33.2 29.3 %collective-permute-start.7 = (bf16[256,2048]{1,0:T(8,128)(2,1)}, bf16[256,2048]{1,0:T(8,128)(2,1)}, u32[]{:S(2)}, u32[]{:S(2)}) collective-permute-start(bf16[256,2048]{1,0:T(8,128)(2,1)} %constant_dynamic-slice_fusion), channel_id=1, source_target_pairs={{0,1},{1,0},{2,3},{3,2},{4,5},{5,4},{6,7},{7,6},{8,9},{9,8},{10,11... | collective-permute-start | bytes 3145736 | tf_op jit(solution)/shard_map/ppermute | solution.py:221
  39.4 12.5 %collective-permute-start.8 = (bf16[48,4096]{1,0:T(8,128)(2,1)}, bf16[48,4096]{1,0:T(8,128)(2,1)S(1)}, u32[]{:S(2)}, u32[]{:S(2)}) collective-permute-start(bf16[48,4096]{1,0:T(8,128)(2,1)} %collective-permute-done.1.m1), channel_id=1, source_target_pairs={{0,128},{64,192},{128,0},{192,64},{1,129},{65,193},{129,1},{193,65... | collective-permute-start | bytes 1179656 | tf_op jit(solution)/shard_map/ppermute | solution.py:305
  43.3 15.0 %collective-permute-start.5 = (bf16[1024,256]{1,0:T(8,128)(2,1)S(1)}, bf16[1024,256]{1,0:T(8,128)(2,1)S(1)}, u32[]{:S(2)}, u32[]{:S(2)}) collective-permute-start(bf16[1024,256]{1,0:T(8,128)(2,1)S(1)} %mix.1.a0), channel_id=1, source_target_pairs={{0,2},{2,0},{1,3},{3,1},{4,6},{6,4},{5,7},{7,5},{8,10},{10,8},{9,1... | collective-permute-start | bytes 1572872 | tf_op jit(solution)/shard_map/ppermute | solution.py:317
  53.8 10.2 %collective-permute-start.10 = (bf16[256,2048]{1,0:T(8,128)(2,1)S(1)}, bf16[256,2048]{1,0:T(8,128)(2,1)S(1)}, u32[]{:S(2)}, u32[]{:S(2)}) collective-permute-start(bf16[256,2048]{1,0:T(8,128)(2,1)S(1)} %dynamic-slice_dynamic-update-slice_fusion), channel_id=1, source_target_pairs={{0,1},{1,0},{2,3},{3,2},{4,5},{5,4},{6,7},{7,6},{8,9},{9,8},{10,11... | collective-permute-start | bytes 3145736 | tf_op jit(solution)/shard_map/ppermute | solution.py:221
  58.3 4.2 %collective-permute-start.4 = (bf16[1024,256]{1,0:T(8,128)(2,1)S(1)}, bf16[1024,256]{1,0:T(8,128)(2,1)S(1)}, u32[]{:S(2)}, u32[]{:S(2)}) collective-permute-start(bf16[1024,256]{1,0:T(8,128)(2,1)S(1)} %mix.1.a0), channel_id=1, source_target_pairs={{0,1},{1,0},{2,3},{3,2},{4,5},{5,4},{6,7},{7,6},{8,9},{9,8},{10,11... | collective-permute-start | bytes 1572872 | tf_op jit(solution)/shard_map/ppermute | solution.py:221
  58.4 5.6 %collective-permute-start.6 = (bf16[1024,256]{1,0:T(8,128)(2,1)S(1)}, bf16[1024,256]{1,0:T(8,128)(2,1)S(1)}, u32[]{:S(2)}, u32[]{:S(2)}) collective-permute-start(bf16[1024,256]{1,0:T(8,128)(2,1)S(1)} %collective-permute-done.5.a2), channel_id=1, source_target_pairs={{0,1},{1,0},{2,3},{3,2},{4,5},{5,4},{6,7},{7,6},{8,9},{9,8},{10,11... | collective-permute-start | bytes 1572872 | tf_op jit(solution)/shard_map/ppermute | solution.py:221
  129.6 7.6 %collective-permute-start.13 = (bf16[32,2048]{1,0:T(8,128)(2,1)S(1)}, bf16[32,2048]{1,0:T(8,128)(2,1)S(1)}, u32[]{:S(2)}, u32[]{:S(2)}) collective-permute-start(bf16[32,2048]{1,0:T(8,128)(2,1)S(1)} %get-tuple-element.31), channel_id=1, source_target_pairs={{0,3},{1,2},{2,1},{3,0},{4,7},{5,6},{6,5},{7,4},{8,11},{9,10},{10,... | collective-permute-start | bytes 393224 | tf_op jit(solution)/shard_map/ppermute | solution.py:357
  132.9 6.8 %collective-permute-start.12 = (bf16[32,2048]{1,0:T(8,128)(2,1)S(1)}, bf16[32,2048]{1,0:T(8,128)(2,1)S(1)}, u32[]{:S(2)}, u32[]{:S(2)}) collective-permute-start(bf16[32,2048]{1,0:T(8,128)(2,1)S(1)} %get-tuple-element.32), channel_id=1, source_target_pairs={{0,2},{1,3},{2,0},{3,1},{4,6},{5,7},{6,4},{7,5},{8,10},{9,11},{10,... | collective-permute-start | bytes 393224 | tf_op jit(solution)/shard_map/ppermute | solution.py:357
  133.2 6.5 %collective-permute-start.11 = (bf16[32,2048]{1,0:T(8,128)(2,1)S(1)}, bf16[32,2048]{1,0:T(8,128)(2,1)S(1)}, u32[]{:S(2)}, u32[]{:S(2)}) collective-permute-start(bf16[32,2048]{1,0:T(8,128)(2,1)S(1)} %get-tuple-element.33), channel_id=1, source_target_pairs={{0,1},{1,0},{2,3},{3,2},{4,5},{5,4},{6,7},{7,6},{8,9},{9,8},{10,11... | collective-permute-start | bytes 393224 | tf_op jit(solution)/shard_map/ppermute | solution.py:357
Sparse Core Ops, SparseCore 0:
  72.4 55.9 reduce-scatter.1

commit v5 on v4

--- a/solution.py
+++ b/solution.py
@@ -180,10 +180,10 @@
         state = power * state
 
 
-def product_kernel(at_ref, a0, a1, a2, a3, w0, w1, m1, r1, r2, r3, m2, f1, c_ref, left, right):
-    y, mine = at_ref[1], at_ref[2]
+def product_kernel(at_ref, a0, a1, a2, a3, w0, w1, f0, f1, f2, g0, g1, g2, c_ref, left, right):
+    parity, mine = at_ref[1], at_ref[2]
     depth = w0.shape[0]
-    piece, tail = m1.shape[0], m2.shape[0]
+    size, quarter = f0.shape[0], f1.shape[0]
 
     @pl.when(pl.program_id(0) == 0)
     def _():
@@ -192,14 +192,13 @@
 
     right[0:depth] = w0[...]
     right[depth : 2 * depth] = w1[...]
-    for k, ref in enumerate((m1, r1, r2, r3)):
-        shift = lax.rem(y - k + 4, 4) * piece
-        start = pl.multiple_of(2 * depth + shift, 16)
-        right[pl.ds(start, piece), :] = ref[...]
-        start = pl.multiple_of(3 * depth + shift, 16)
-        right[pl.ds(start, piece), :] = f1[k * piece : (k + 1) * piece]
-    right[3 * depth - tail : 3 * depth] = m2[...]
-    right[4 * depth - tail : 4 * depth] = f1[4 * piece :]
+    for s, refs in enumerate(((f0, f1, f2), (g0, g1, g2))):
+        base = (2 + s) * depth
+        near = pl.multiple_of(base + parity * size, 64)
+        far = pl.multiple_of(base + (1 - parity) * size, 64)
+        right[pl.ds(near, size), :] = refs[0][...]
+        right[pl.ds(far, quarter), :] = refs[1][...]
+        right[pl.ds(pl.multiple_of(far + quarter, 64), quarter), :] = refs[2][...]
     block = 256
     for m in range(left.shape[0] // block):
         total = jnp.dot(left[m * block : (m + 1) * block, :], right[...], preferred_element_type=F32).astype(BF)
@@ -217,6 +216,10 @@
         out_ref[:, pl.ds(place, width)] = ref[...]
 
 
+def far(value):
+    return pltpu.with_memory_space_constraint(value, pltpu.HBM)
+
+
 def other_core(value):
     return lax.ppermute(value, "c", [(0, 1), (1, 0)])
 
@@ -229,15 +232,13 @@
     seq = lax.axis_index(("y", "xl"))
     halo = lax.ppermute(projected[:, rows - 8 :, :], ("y", "xl"), [(i, i + 1) for i in range(7)])
 
-    piece = 48
+    size = channels // 2
     half = 2 * width
+    parity = lax.rem(y, 2)
     mirror = [(0, 3), (3, 0), (1, 2), (2, 1)]
-
-    def mirrored_rows(start, size, xh):
-        rows_there = lax.dynamic_slice(out_weight, (start, (1 - xh) * half), (size, half))
-        return lax.ppermute(rows_there, ("xl", "xh"), mirror)
-
-    m1 = mirrored_rows(y * piece, piece, xh)
+    fetched = lax.ppermute(
+        lax.dynamic_slice(out_weight, (parity * size, (1 - xh) * half), (size, half)), ("xl", "xh"), mirror
+    )
 
     flat = groups * MODES
     span = 256
@@ -271,13 +272,9 @@
         compiler_params=pltpu.CompilerParams(vmem_limit_bytes=12 * 2**20),
         cost_estimate=pl.CostEstimate(flops=10**6, bytes_accessed=2**16, transcendentals=0),
         name="state",
-    )(projected, projected, halo, short_filter, rate)
+    )(far(projected), far(projected), halo, far(short_filter), far(rate))
     end, xh_late, core_late, residue_late = lax.optimization_barrier((end, xh, core, residue))
-    at = jnp.stack([seq, y, xh_late * 2 + core_late, core_late]).astype(jnp.int32)
-    m2 = mirrored_rows(4 * piece, channels - 4 * piece, xh_late)
-    w_other = other_core(
-        lax.dynamic_slice(out_weight, (0, (xh_late * 2 + 1 - core_late) * width), (channels, width))
-    )
+    at = jnp.stack([seq, parity, xh_late * 2 + core_late, core_late]).astype(jnp.int32)
     weight = residue_late * jnp.sqrt(-jnp.expm1(-2.0 * rate))
     ends = lax.all_to_all(end, ("y", "xl"), 0, 0, tiled=True)
     conv, query, din = pl.pallas_call(
@@ -301,9 +298,7 @@
         compiler_params=pltpu.CompilerParams(vmem_limit_bytes=16 * 2**20),
         cost_estimate=pl.CostEstimate(flops=10**6, bytes_accessed=2**16, transcendentals=0),
         name="conv",
-    )(projected, signal, halo, short_filter, rate, weight, rt)
-    r1, r2, r3 = (lax.ppermute(m1, "y", [(i, (i + k) % 4) for i in range(4)]) for k in (1, 2, 3))
-    ends, r1, r3 = lax.optimization_barrier((ends, r1, r3))
+    )(far(projected), signal, halo, far(short_filter), far(rate), weight, rt)
     mixed = pl.pallas_call(
         mix_kernel,
         out_shape=jax.ShapeDtypeStruct((rows, channels), BF),
@@ -317,10 +312,19 @@
     a_far = lax.ppermute(mixed, "xh", [(0, 1), (1, 0)])
     a_other = other_core(mixed)
     a_far_other = other_core(a_far)
-    given = jnp.concatenate(
-        [lax.dynamic_slice(v, (0, (1 - core) * width), (v.shape[0], width)) for v in (m1, r1, r2, r3, m2)], axis=0
+    core_last, _ = lax.optimization_barrier((core, mixed))
+    zero = jnp.minimum(core_last, 0)
+    quarter = size // 2
+    above, below = (lax.dynamic_slice(fetched, (zero + k * quarter, 0), (quarter, half)) for k in (0, 1))
+    above = lax.ppermute(above, "y", [(i, (i + 1) % 4) for i in range(4)])
+    below = lax.ppermute(below, "y", [(i, (i - 1) % 4) for i in range(4)])
+    w_other = other_core(
+        lax.dynamic_slice(out_weight, (0, (xh * 2 + 1 - core_last) * width), (channels, width))
     )
-    f_other = other_core(given)
+    g0, g1, g2 = (
+        other_core(lax.dynamic_slice(v, (0, (1 - core) * width), (v.shape[0], width)))
+        for v in (fetched, above, below)
+    )
 
     tile = 512
     strips = width // tile
@@ -339,15 +343,16 @@
             grid=(strips,),
             in_specs=[pl.BlockSpec((rows, channels), lambda i, at_ref: (0, 0), **once)] * 4
             + [pl.BlockSpec((channels, tile), lambda i, at_ref: (0, at_ref[2] * strips + i)), strip(w_other.shape)]
-            + [half_strip(m1.shape)] * 4
-            + [half_strip(m2.shape), strip(f_other.shape)],
+            + [half_strip(v.shape) for v in (fetched, above, below)]
+            + [strip(v.shape) for v in (g0, g1, g2)],
             out_specs=strip((rows, width)),
             scratch_shapes=[pltpu.VMEM((rows, 4 * channels), BF), pltpu.VMEM((4 * channels, tile), BF)],
         ),
         compiler_params=pltpu.CompilerParams(vmem_limit_bytes=28 * 2**20),
         cost_estimate=pl.CostEstimate(flops=4 * 10**9, bytes_accessed=10 * 2**20, transcendentals=0),
         name="product",
-    )(at, mixed, a_other, a_far, a_far_other, pltpu.with_memory_space_constraint(out_weight, pltpu.HBM), w_other, m1, r1, r2, r3, m2, f_other)
+    )(at, mixed, a_other, a_far, a_far_other, far(out_weight), w_other,
+      fetched, above, below, g0, g1, g2)
 
     summed = lax.psum_scatter(partial, "z", scatter_dimension=0, tiled=True)
     size = summed.shape[0] // 4

time: 149 us -> 156 us (1.047)
  waiting for transfers between devices: 70.4 us -> 76.5 us
  local copies, waits for them, and re-layouts: 13.8 us -> 7.87 us
  starting transfers between devices: 33.4 us -> 37.7 us
  Pallas kernels: 16.7 us -> 19.4 us
    ppermute x4 -> x6, starting transfers between devices: 11.6 us -> 17.7 us  [other_core(): return lax.ppermute(value, 'c', [(0, 1), (1, 0)])]
    unnamed x18 -> x4, local copies, waits for them, and re-layouts: 5.7 us -> 0.01 us
    ppermute x5 -> x3, waiting for transfers between devices: 6.38 us -> 10.7 us  [the longest x1 10.3 us: local(): above = lax.ppermute(above, 'y', [(i, (i + 1) % 4) for i in range(4)])]
    all_to_all x1, starting transfers between devices: 3.9 us -> 7.15 us  [local(): ends = lax.all_to_all(end, ('y', 'xl'), 0, 0, tiled=True)]
    ppermute x5 -> x3, starting transfers between devices: 8.97 us -> 6.87 us  [the longest x1 3.56 us: local(): below = lax.ppermute(below, 'y', [(i, (i - 1) % 4) for i in range(4)])]
    ppermute x1, starting transfers between devices: 3.93 us -> 1.84 us  [local(): lax.ppermute(projected[:, rows - 8:, :], ('y', 'xl'), [(i, i + 1) for i i...]
    dynamic_slice x3 -> x6, local copies, waits for them, and re-layouts: 5.25 us -> 6.02 us  [the longest x1 2.34 us: local(): lax.dynamic_slice(out_weight, (parity * size, (1 - xh) * half), (size, ha...]
  transfers between devices with their start and end apart: 16 -> 16, of which waited for: 5 -> 9; matrix products, arithmetic and copies ran while one was open for 6% -> 3% of each run, Pallas kernels for 5% -> 6%
where the time goes in v5:
time: 156 us; the launch traced here: 155 us
  waiting for transfers between devices  76.5 us (49%)
  starting transfers between devices  37.7 us (24%)
  Pallas kernels  19.4 us (12%)
  between operations  13.6 us (9%)
  local copies, waits for them, and re-layouts  7.87 us (5%)
    reduce_scatter x1, waiting for transfers between devices, local(): summed = lax.psum_scatter(partial, 'z', scatter_dimension=0, tiled=True)  56 us
    ppermute x6, starting transfers between devices, other_core(): return lax.ppermute(value, 'c', [(0, 1), (1, 0)])  17.7 us
    ppermute x1, waiting for transfers between devices, local(): above = lax.ppermute(above, 'y', [(i, (i + 1) % 4) for i in range(4)])  10.3 us
    pallas_call x1, Pallas kernels, local(): pl.pallas_call(product_kernel, out_shape=pltpu.HBM((rows, width), BF), gr...  8.49 us
    all_to_all x1, starting transfers between devices, local(): ends = lax.all_to_all(end, ('y', 'xl'), 0, 0, tiled=True)  7.15 us
    ppermute x3, waiting for transfers between devices, traded(): return lax.ppermute(summed[k * size:(k + 1) * size], ('xh', 'c'), pairs)  6.33 us
    pallas_call x1, Pallas kernels, local(): pl.pallas_call(state_kernel, out_shape=(jax.ShapeDtypeStruct((rows, chann...  4.45 us
    pallas_call x1, Pallas kernels, local(): pl.pallas_call(conv_kernel, out_shape=(jax.ShapeDtypeStruct((rows, channe...  4.22 us
  transfers between devices with their start and end apart: 16, of which 9 were waited for; matrix products, arithmetic and copies ran while one was open for 3% of the time, Pallas kernels for 6%

profile of v5, /device:TPU:1, one launch (start us, length us, event | category | flops | bytes accessed | tf_op | source)
XLA Modules:
  0.0 155.1 jit_solution(11848638321380560402)
XLA Ops:
  6.5 0.0 copy-start
  6.5 0.0 copy-start.1
  6.5 2.3 %dynamic_slice.22 = bf16[128,4096]{1,0:T(8,128)(2,1)} dynamic-slice(bf16[256,8192]{1,0:T(8,128)(2,1)} %w0.1, s32[]{:T(128)S(6)} %select_n.21, s32[]{:T(128)S(6)} %select_n.22), dynamic_slice_sizes={128,4096} | dynamic-slice | bytes 2097156 | tf_op jit(solution)/shard_map/dynamic_slice | solution.py:240
  8.9 3.3 %collective-permute-start.5 = (bf16[128,4096]{1,0:T(8,128)(2,1)}, bf16[128,4096]{1,0:T(8,128)(2,1)S(1)}, u32[]{:S(2)}, u32[]{:S(2)}) collective-permute-start(bf16[128,4096]{1,0:T(8,128)(2,1)} %dynamic_slice.22), channel_id=1, source_target_pairs={{0,34},{34,0},{2,32},{32,2},{1,35},{35,1},{3,33},{33,3},{4,38},{38... | collective-permute-start | bytes 3145736 | tf_op jit(solution)/shard_map/ppermute | solution.py:239
  12.2 0.7 slice.15
  12.9 1.8 %collective-permute-start = (bf16[3,8,256]{2,1,0:T(8,128)(2,1)S(1)}, bf16[3,8,256]{2,1,0:T(8,128)(2,1)S(1)}, u32[]{:S(2)}, u32[]{:S(2)}) collective-permute-start(bf16[3,8,256]{2,1,0:T(8,128)(2,1)S(1)} %slice.15), channel_id=1, source_target_pairs={{0,32},{32,64},{64,96},{96,128},{128,160},{160,192},{192,224},{1,3... | collective-permute-start | bytes 36872 | tf_op jit(solution)/shard_map/ppermute | solution.py:233
  14.8 0.8 collective-permute-done.halo_ref
  15.6 4.4 %state.1 = (bf16[1024,256]{1,0:T(8,128)(2,1)S(1)}, f32[8,16,256]{2,1,0:T(8,128)}, f32[16,256]{1,0:T(8,128)S(1)}) custom-call(bf16[3,1024,256]{2,1,0:T(8,128)(2,1)} %p_ref.1, bf16[3,1024,256]{2,1,0:T(8,128)(2,1)} %p_ref.1, bf16[3,8,256]{2,1,0:T(8,128)(2,1)S(1)} %collective-permute-done.halo_ref, f32[3,3,256]{2,1,0:T(4,128)} %sf_ref.3, f32[16,16]{1,0:T(8,128)} %rate_ref.3), custom_call_target="tpu_custom_call" | custom-call | flops 1000000 | bytes 65536 | tf_op jit(solution)/shard_map/state/pallas_call | solution.py:253
  20.0 7.2 %all-to-all-start = ((f32[8,16,256]{2,1,0:T(8,128)}), f32[8,16,256]{2,1,0:T(8,128)S(1)}, u32[]{:S(2)}, u32[]{:S(2)}) async-start(f32[8,16,256]{2,1,0:T(8,128)} %get-tuple-element.19), calls=%async_computation | async-start | bytes 262144 | tf_op jit(solution)/shard_map/all_to_all | solution.py:279
  27.2 0.0 reduce-scatter.2.cloned.1.call-start
  27.2 0.0 copy-done
  27.2 0.0 copy-done.1
  27.3 4.2 %conv.1 = (bf16[1024,256]{1,0:T(8,128)(2,1)S(1)}, bf16[1024,256]{1,0:T(8,128)(2,1)S(1)}, bf16[128,256]{1,0:T(8,128)(2,1)S(1)}) custom-call(bf16[3,1024,256]{2,1,0:T(8,128)(2,1)} %p_ref.1, bf16[1024,256]{1,0:T(8,128)(2,1)S(1)} %get-tuple-element.21.x_ref, bf16[3,8,256]{2,1,0:T(8,128)(2,1)S(1)} %collective-permute-done.halo_ref, f32[3,3,256]{2,1,0:T(4,128)} %sf_ref.3, ...), custom_call_target="tpu_custom_call" | custom-call | flops 1000000 | bytes 65536 | tf_op jit(solution)/shard_map/conv/pallas_call | solution.py:280
  31.5 0.1 pad_add_fusion.at_ref
  31.6 1.1 all-to-all-done.ends_ref
  32.7 0.9 mix.1.a0
  33.6 0.3 collective-permute-start.2
  33.9 0.4 collective-permute-done.5.f0
  34.3 1.3 constant_dynamic-slice_fusion.3
  35.6 3.6 %collective-permute-start.7 = (bf16[64,4096]{1,0:T(8,128)(2,1)}, bf16[64,4096]{1,0:T(8,128)(2,1)S(1)}, u32[]{:S(2)}, u32[]{:S(2)}) collective-permute-start(bf16[64,4096]{1,0:T(8,128)(2,1)} %get-tuple-element.27), channel_id=1, source_target_pairs={{0,192},{64,0},{128,64},{192,128},{1,193},{65,1},{129,65},{193,129... | collective-permute-start | bytes 1572872 | tf_op jit(solution)/shard_map/ppermute | solution.py:320
  39.2 2.3 %constant_dynamic-slice_fusion.5 = bf16[256,2048]{1,0:T(8,128)(2,1)} fusion(bf16[256,8192]{1,0:T(8,128)(2,1)} %w0.1, s32[]{:T(128)S(6)} %select_n.20), kind=kLoop, calls=%fused_computation.6 | loop fusion | bytes 2097156 | tf_op jit(solution)/shard_map/dynamic_slice | solution.py:322
  41.5 12.2 %collective-permute-start.4 = (bf16[256,2048]{1,0:T(8,128)(2,1)}, bf16[256,2048]{1,0:T(8,128)(2,1)}, u32[]{:S(2)}, u32[]{:S(2)}) collective-permute-start(bf16[256,2048]{1,0:T(8,128)(2,1)} %constant_dynamic-slice_fusion.5), channel_id=1, source_target_pairs={{0,1},{1,0},{2,3},{3,2},{4,5},{5,4},{6,7},{7,6},{8,9},{9,8},{10,11... | collective-permute-start | bytes 3145736 | tf_op jit(solution)/shard_map/ppermute | solution.py:224
  53.7 0.0 collective-permute-start.6
  53.7 0.0 collective-permute-start.1
  53.7 0.0 collective-permute-done.2.a2
  53.8 0.5 collective-permute-start.3
  54.3 0.0 collective-permute-done.7.f2
  54.3 4.1 %collective-permute-start.8 = (bf16[128,2048]{1,0:T(8,128)(2,1)S(1)}, bf16[128,2048]{1,0:T(8,128)(2,1)S(1)}, u32[]{:S(2)}, u32[]{:S(2)}) collective-permute-start(bf16[128,2048]{1,0:T(8,128)(2,1)S(1)} %constant_dynamic-slice_fusion.2), channel_id=1, source_target_pairs={{0,1},{1,0},{2,3},{3,2},{4,5},{5,4},{6,7},{7,6},{8,9},{9,8},{10,11... | collective-permute-start | bytes 1572872 | tf_op jit(solution)/shard_map/ppermute | solution.py:224
  58.4 10.3 %collective-permute-done.6.f1 = bf16[64,4096]{1,0:T(8,128)(2,1)S(1)} collective-permute-done((bf16[64,4096]{1,0:T(8,128)(2,1)}, bf16[64,4096]{1,0:T(8,128)(2,1)S(1)}, u32[]{:S(2)}, u32[]{:S(2)}) %collective-permute-start.6) | collective-permute-done | bytes 524320 | tf_op jit(solution)/shard_map/ppermute | solution.py:319
  68.7 0.8 collective-permute-start.10
  69.5 0.0 collective-permute-done.1.a1
  69.5 0.1 collective-permute-start.9
  69.6 0.0 collective-permute-done.3.a3
  69.6 0.0 collective-permute-done.4.w1
  69.7 0.0 collective-permute-done.8.g0
  69.7 1.0 collective-permute-done.10.g2
  70.7 0.5 collective-permute-done.9.g1
  71.2 8.5 %product.1 = bf16[1024,2048]{1,0:T(8,128)(2,1)} custom-call(s32[4]{0:T(128)S(1)} %pad_add_fusion.at_ref, bf16[1024,256]{1,0:T(8,128)(2,1)S(1)} %mix.1.a0, bf16[1024,256]{1,0:T(8,128)(2,1)S(1)} %collective-permute-done.1.a1, bf16[1024,256]{1,0:T(8,128)(2,1)S(1)} %collective-permute-done.2.a2, bf16[1024,256]{1,0:T(8,128)(2,1)S(1)} %collective-permute-done.3.a3, ...), custom_call_target="tpu_custom_call" | custom-call | flops 4000000000 | bytes 10485760 | tf_op jit(solution)/shard_map/product/pallas_call | solution.py:338
  79.6 0.0 reduce-scatter.2.cloned.1.call-update
  79.7 56.0 %reduce-scatter.2.cloned.1.call-done = bf16[128,2048]{1,0:T(8,128)(2,1)} async-done(((bf16[1024,2048]{1,0:T(8,128)(2,1)}), bf16[128,2048]{1,0:T(8,128)(2,1)}) %reduce-scatter.2.cloned.1.call-update) | async-done | bytes 524304 | tf_op jit(solution)/shard_map/reduce_scatter | solution.py:357
  135.7 1.1 fusion
  136.8 3.3 %collective-permute-start.13 = (bf16[32,2048]{1,0:T(8,128)(2,1)S(1)}, bf16[32,2048]{1,0:T(8,128)(2,1)S(1)}, u32[]{:S(2)}, u32[]{:S(2)}) collective-permute-start(bf16[32,2048]{1,0:T(8,128)(2,1)S(1)} %get-tuple-element.29), channel_id=1, source_target_pairs={{0,3},{1,2},{2,1},{3,0},{4,7},{5,6},{6,5},{7,4},{8,11},{9,10},{10,... | collective-permute-start | bytes 393224 | tf_op jit(solution)/shard_map/ppermute | solution.py:362
  140.1 0.3 collective-permute-start.12
  140.4 0.2 collective-permute-start.11
  140.6 3.8 %collective-permute-done.13.p3 = bf16[32,2048]{1,0:T(8,128)(2,1)S(1)} collective-permute-done((bf16[32,2048]{1,0:T(8,128)(2,1)S(1)}, bf16[32,2048]{1,0:T(8,128)(2,1)S(1)}, u32[]{:S(2)}, u32[]{:S(2)}) %collective-permute-start.13) | collective-permute-done | bytes 131104 | tf_op jit(solution)/shard_map/ppermute | solution.py:362
  144.3 2.6 %collective-permute-done.12.p2 = bf16[32,2048]{1,0:T(8,128)(2,1)S(1)} collective-permute-done((bf16[32,2048]{1,0:T(8,128)(2,1)S(1)}, bf16[32,2048]{1,0:T(8,128)(2,1)S(1)}, u32[]{:S(2)}, u32[]{:S(2)}) %collective-permute-start.12) | collective-permute-done | bytes 131104 | tf_op jit(solution)/shard_map/ppermute | solution.py:362
  146.9 0.0 collective-permute-done.11.p1
  146.9 1.4 join.1
  (4 shorter events, 0.1 us)
Async XLA Ops:
  6.5 20.7 %copy-start = (f32[16,16]{1,0:T(8,128)S(1)}, f32[16,16]{1,0:T(8,128)}, u32[]{:S(2)}) copy-start(f32[16,16]{1,0:T(8,128)} %rate_ref.3) | copy-start | bytes 3076
  6.5 20.7 %copy-start.1 = (f32[16,16]{1,0:T(8,128)S(1)}, f32[16,16]{1,0:T(8,128)}, u32[]{:S(2)}) copy-start(f32[16,16]{1,0:T(8,128)} %param.7) | copy-start | bytes 3076
  8.9 25.5 %collective-permute-start.5 = (bf16[128,4096]{1,0:T(8,128)(2,1)}, bf16[128,4096]{1,0:T(8,128)(2,1)S(1)}, u32[]{:S(2)}, u32[]{:S(2)}) collective-permute-start(bf16[128,4096]{1,0:T(8,128)(2,1)} %dynamic_slice.22), channel_id=1, source_target_pairs={{0,34},{34,0},{2,32},{32,2},{1,35},{35,1},{3,33},{33,3},{4,38},{38... | collective-permute-start | bytes 3145736 | tf_op jit(solution)/shard_map/ppermute | solution.py:239
  12.9 2.7 %collective-permute-start = (bf16[3,8,256]{2,1,0:T(8,128)(2,1)S(1)}, bf16[3,8,256]{2,1,0:T(8,128)(2,1)S(1)}, u32[]{:S(2)}, u32[]{:S(2)}) collective-permute-start(bf16[3,8,256]{2,1,0:T(8,128)(2,1)S(1)} %slice.15), channel_id=1, source_target_pairs={{0,32},{32,64},{64,96},{96,128},{128,160},{160,192},{192,224},{1,3... | collective-permute-start | bytes 36872 | tf_op jit(solution)/shard_map/ppermute | solution.py:233
  20.0 12.7 %all-to-all-start = ((f32[8,16,256]{2,1,0:T(8,128)}), f32[8,16,256]{2,1,0:T(8,128)S(1)}, u32[]{:S(2)}, u32[]{:S(2)}) async-start(f32[8,16,256]{2,1,0:T(8,128)} %get-tuple-element.19), calls=%async_computation | async-start | bytes 262144 | tf_op jit(solution)/shard_map/all_to_all | solution.py:279
  27.2 108.5 %reduce-scatter.2.cloned.1.call-start = ((), (), s32[]{:S(2)}) async-start(), calls=%async_computation.2 | async-start | bytes 4718592 | tf_op jit(solution)/shard_map/reduce_scatter | solution.py:357
  33.6 20.1 %collective-permute-start.2 = (bf16[1024,256]{1,0:T(8,128)(2,1)S(1)}, bf16[1024,256]{1,0:T(8,128)(2,1)S(1)}, u32[]{:S(2)}, u32[]{:S(2)}) collective-permute-start(bf16[1024,256]{1,0:T(8,128)(2,1)S(1)} %mix.1.a0), channel_id=1, source_target_pairs={{0,2},{2,0},{1,3},{3,1},{4,6},{6,4},{5,7},{7,5},{8,10},{10,8},{9,1... | collective-permute-start | bytes 1572872 | tf_op jit(solution)/shard_map/ppermute | solution.py:312
  35.6 18.7 %collective-permute-start.7 = (bf16[64,4096]{1,0:T(8,128)(2,1)}, bf16[64,4096]{1,0:T(8,128)(2,1)S(1)}, u32[]{:S(2)}, u32[]{:S(2)}) collective-permute-start(bf16[64,4096]{1,0:T(8,128)(2,1)} %get-tuple-element.27), channel_id=1, source_target_pairs={{0,192},{64,0},{128,64},{192,128},{1,193},{65,1},{129,65},{193,129... | collective-permute-start | bytes 1572872 | tf_op jit(solution)/shard_map/ppermute | solution.py:320
  41.5 28.1 %collective-permute-start.4 = (bf16[256,2048]{1,0:T(8,128)(2,1)}, bf16[256,2048]{1,0:T(8,128)(2,1)}, u32[]{:S(2)}, u32[]{:S(2)}) collective-permute-start(bf16[256,2048]{1,0:T(8,128)(2,1)} %constant_dynamic-slice_fusion.5), channel_id=1, source_target_pairs={{0,1},{1,0},{2,3},{3,2},{4,5},{5,4},{6,7},{7,6},{8,9},{9,8},{10,11... | collective-permute-start | bytes 3145736 | tf_op jit(solution)/shard_map/ppermute | solution.py:224
  53.7 15.0 %collective-permute-start.6 = (bf16[64,4096]{1,0:T(8,128)(2,1)}, bf16[64,4096]{1,0:T(8,128)(2,1)S(1)}, u32[]{:S(2)}, u32[]{:S(2)}) collective-permute-start(bf16[64,4096]{1,0:T(8,128)(2,1)} %get-tuple-element.28), channel_id=1, source_target_pairs={{0,64},{64,128},{128,192},{192,0},{1,65},{65,129},{129,193},{193,1... | collective-permute-start | bytes 1572872 | tf_op jit(solution)/shard_map/ppermute | solution.py:319
  53.7 15.8 %collective-permute-start.1 = (bf16[1024,256]{1,0:T(8,128)(2,1)S(1)}, bf16[1024,256]{1,0:T(8,128)(2,1)S(1)}, u32[]{:S(2)}, u32[]{:S(2)}) collective-permute-start(bf16[1024,256]{1,0:T(8,128)(2,1)S(1)} %mix.1.a0), channel_id=1, source_target_pairs={{0,1},{1,0},{2,3},{3,2},{4,5},{5,4},{6,7},{7,6},{8,9},{9,8},{10,11... | collective-permute-start | bytes 1572872 | tf_op jit(solution)/shard_map/ppermute | solution.py:224
  53.8 15.9 %collective-permute-start.3 = (bf16[1024,256]{1,0:T(8,128)(2,1)S(1)}, bf16[1024,256]{1,0:T(8,128)(2,1)S(1)}, u32[]{:S(2)}, u32[]{:S(2)}) collective-permute-start(bf16[1024,256]{1,0:T(8,128)(2,1)S(1)} %collective-permute-done.2.a2), channel_id=1, source_target_pairs={{0,1},{1,0},{2,3},{3,2},{4,5},{5,4},{6,7},{7,6},{8,9},{9,8},{10,11... | collective-permute-start | bytes 1572872 | tf_op jit(solution)/shard_map/ppermute | solution.py:224
  54.3 15.3 %collective-permute-start.8 = (bf16[128,2048]{1,0:T(8,128)(2,1)S(1)}, bf16[128,2048]{1,0:T(8,128)(2,1)S(1)}, u32[]{:S(2)}, u32[]{:S(2)}) collective-permute-start(bf16[128,2048]{1,0:T(8,128)(2,1)S(1)} %constant_dynamic-slice_fusion.2), channel_id=1, source_target_pairs={{0,1},{1,0},{2,3},{3,2},{4,5},{5,4},{6,7},{7,6},{8,9},{9,8},{10,11... | collective-permute-start | bytes 1572872 | tf_op jit(solution)/shard_map/ppermute | solution.py:224
  68.7 1.9 %collective-permute-start.10 = (bf16[64,2048]{1,0:T(8,128)(2,1)S(1)}, bf16[64,2048]{1,0:T(8,128)(2,1)S(1)}, u32[]{:S(2)}, u32[]{:S(2)}) collective-permute-start(bf16[64,2048]{1,0:T(8,128)(2,1)S(1)} %constant_dynamic-slice_fusion), channel_id=1, source_target_pairs={{0,1},{1,0},{2,3},{3,2},{4,5},{5,4},{6,7},{7,6},{8,9},{9,8},{10,11... | collective-permute-start | bytes 786440 | tf_op jit(solution)/shard_map/ppermute | solution.py:224
  69.5 1.6 %collective-permute-start.9 = (bf16[64,2048]{1,0:T(8,128)(2,1)S(1)}, bf16[64,2048]{1,0:T(8,128)(2,1)S(1)}, u32[]{:S(2)}, u32[]{:S(2)}) collective-permute-start(bf16[64,2048]{1,0:T(8,128)(2,1)S(1)} %constant_dynamic-slice_fusion.1), channel_id=1, source_target_pairs={{0,1},{1,0},{2,3},{3,2},{4,5},{5,4},{6,7},{7,6},{8,9},{9,8},{10,11... | collective-permute-start | bytes 786440 | tf_op jit(solution)/shard_map/ppermute | solution.py:224
  136.8 7.5 %collective-permute-start.13 = (bf16[32,2048]{1,0:T(8,128)(2,1)S(1)}, bf16[32,2048]{1,0:T(8,128)(2,1)S(1)}, u32[]{:S(2)}, u32[]{:S(2)}) collective-permute-start(bf16[32,2048]{1,0:T(8,128)(2,1)S(1)} %get-tuple-element.29), channel_id=1, source_target_pairs={{0,3},{1,2},{2,1},{3,0},{4,7},{5,6},{6,5},{7,4},{8,11},{9,10},{10,... | collective-permute-start | bytes 393224 | tf_op jit(solution)/shard_map/ppermute | solution.py:362
  140.1 6.8 %collective-permute-start.12 = (bf16[32,2048]{1,0:T(8,128)(2,1)S(1)}, bf16[32,2048]{1,0:T(8,128)(2,1)S(1)}, u32[]{:S(2)}, u32[]{:S(2)}) collective-permute-start(bf16[32,2048]{1,0:T(8,128)(2,1)S(1)} %get-tuple-element.30), channel_id=1, source_target_pairs={{0,2},{1,3},{2,0},{3,1},{4,6},{5,7},{6,4},{7,5},{8,10},{9,11},{10,... | collective-permute-start | bytes 393224 | tf_op jit(solution)/shard_map/ppermute | solution.py:362
  140.4 6.6 %collective-permute-start.11 = (bf16[32,2048]{1,0:T(8,128)(2,1)S(1)}, bf16[32,2048]{1,0:T(8,128)(2,1)S(1)}, u32[]{:S(2)}, u32[]{:S(2)}) collective-permute-start(bf16[32,2048]{1,0:T(8,128)(2,1)S(1)} %get-tuple-element.31), channel_id=1, source_target_pairs={{0,1},{1,0},{2,3},{3,2},{4,5},{5,4},{6,7},{7,6},{8,9},{9,8},{10,11... | collective-permute-start | bytes 393224 | tf_op jit(solution)/shard_map/ppermute | solution.py:362
Sparse Core Ops, SparseCore 0:
  79.8 55.8 reduce-scatter.1

commit v6 on v4

--- a/solution.py
+++ b/solution.py
@@ -180,29 +180,44 @@
         state = power * state
 
 
-def product_kernel(at_ref, a0, a1, a2, a3, w0, w1, m1, r1, r2, r3, m2, f1, c_ref, left, right):
-    y, mine = at_ref[1], at_ref[2]
-    depth = w0.shape[0]
-    piece, tail = m1.shape[0], m2.shape[0]
+def side_by_side(left, refs):
+    depth = refs[0].shape[1]
 
     @pl.when(pl.program_id(0) == 0)
     def _():
-        for k, ref in enumerate((a0, a1, a2, a3)):
+        for k, ref in enumerate(refs):
             left[:, k * depth : (k + 1) * depth] = ref[...]
 
+
+def near_kernel(at_ref, a0, a1, w0, w1, c_ref, left, right):
+    depth = w0.shape[0]
+    side_by_side(left, (a0, a1))
     right[0:depth] = w0[...]
     right[depth : 2 * depth] = w1[...]
-    for k, ref in enumerate((m1, r1, r2, r3)):
-        shift = lax.rem(y - k + 4, 4) * piece
-        start = pl.multiple_of(2 * depth + shift, 16)
-        right[pl.ds(start, piece), :] = ref[...]
-        start = pl.multiple_of(3 * depth + shift, 16)
-        right[pl.ds(start, piece), :] = f1[k * piece : (k + 1) * piece]
-    right[3 * depth - tail : 3 * depth] = m2[...]
-    right[4 * depth - tail : 4 * depth] = f1[4 * piece :]
     block = 256
     for m in range(left.shape[0] // block):
-        total = jnp.dot(left[m * block : (m + 1) * block, :], right[...], preferred_element_type=F32).astype(BF)
+        span = slice(m * block, (m + 1) * block)
+        c_ref[span, :] = jnp.dot(left[span, :], right[...], preferred_element_type=F32).astype(BF)
+
+
+def far_kernel(at_ref, a2, a3, f0, f1, f2, f3, g013, g2, near_ref, c_ref, left, right):
+    y, mine = at_ref[1], at_ref[2]
+    size = f0.shape[0]
+    depth = right.shape[0] // 2
+    tail = depth - 4 * size
+    side_by_side(left, (a2, a3))
+    for k, ref in enumerate((f0, f1, f2, f3)):
+        owner = lax.rem(y - k + 4, 4) * size
+        right[pl.ds(pl.multiple_of(owner, 16), size), :] = ref[0:size]
+        passed = g2[0:size] if k == 2 else g013[(0, 1, 0, 2)[k] * size : ((0, 1, 0, 2)[k] + 1) * size]
+        right[pl.ds(pl.multiple_of(depth + owner, 16), size), :] = passed
+    right[4 * size : depth] = f2[size : size + tail]
+    right[depth + 4 * size : 2 * depth] = g2[size : size + tail]
+    block = 256
+    for m in range(left.shape[0] // block):
+        span = slice(m * block, (m + 1) * block)
+        total = jnp.dot(left[span, :], right[...], preferred_element_type=F32)
+        total = (total + near_ref[span, :].astype(F32)).astype(BF)
         for b in range(block // 32):
             high, low = m * (block // 128) + b // 4, b % 4
             place = pl.multiple_of((high * 4 + jnp.bitwise_xor(low, mine)) * 32, 32)
@@ -217,6 +232,10 @@
         out_ref[:, pl.ds(place, width)] = ref[...]
 
 
+def far(value):
+    return pltpu.with_memory_space_constraint(value, pltpu.HBM)
+
+
 def other_core(value):
     return lax.ppermute(value, "c", [(0, 1), (1, 0)])
 
@@ -227,17 +246,19 @@
     width = out_weight.shape[1] // 4
     y, xh, core = lax.axis_index("y"), lax.axis_index("xh"), lax.axis_index("c")
     seq = lax.axis_index(("y", "xl"))
-    halo = lax.ppermute(projected[:, rows - 8 :, :], ("y", "xl"), [(i, i + 1) for i in range(7)])
-
-    piece = 48
+    edge = projected[:, rows - 8 :, :]
+    edge, y_then = lax.optimization_barrier((edge, y))
+    halo = lax.ppermute(edge, ("y", "xl"), [(i, i + 1) for i in range(7)])
+
+    size = 48
+    tail = channels - 4 * size
     half = 2 * width
     mirror = [(0, 3), (3, 0), (1, 2), (2, 1)]
 
-    def mirrored_rows(start, size, xh):
-        rows_there = lax.dynamic_slice(out_weight, (start, (1 - xh) * half), (size, half))
-        return lax.ppermute(rows_there, ("xl", "xh"), mirror)
-
-    m1 = mirrored_rows(y * piece, piece, xh)
+    def there(source, start, count):
+        return lax.dynamic_slice(source, (start, (1 - xh) * half), (count, half))
+
+    f0 = lax.ppermute(there(out_weight, y_then * size, size), ("xl", "xh"), mirror)
 
     flat = groups * MODES
     span = 256
@@ -252,7 +273,7 @@
     signal, end, rt = pl.pallas_call(
         state_kernel,
         out_shape=(
-            jax.ShapeDtypeStruct((rows, channels), BF),
+            pltpu.HBM((rows, channels), BF),
             jax.ShapeDtypeStruct((8, MODES, channels), F32),
             jax.ShapeDtypeStruct((MODES, channels), F32),
         ),
@@ -271,20 +292,23 @@
         compiler_params=pltpu.CompilerParams(vmem_limit_bytes=12 * 2**20),
         cost_estimate=pl.CostEstimate(flops=10**6, bytes_accessed=2**16, transcendentals=0),
         name="state",
-    )(projected, projected, halo, short_filter, rate)
-    end, xh_late, core_late, residue_late = lax.optimization_barrier((end, xh, core, residue))
+    )(far(projected), far(projected), halo, far(short_filter), far(rate))
+    end, xh_late, core_late, residue_late, weight_late = lax.optimization_barrier((end, xh, core, residue, out_weight))
+    f2 = jnp.concatenate(
+        [there(weight_late, lax.rem(y + 2, 4) * size, size), there(weight_late, 4 * size, tail)], axis=0
+    )
+    f2 = lax.ppermute(f2, ("xl", "xh"), mirror)
+    w_other = other_core(
+        lax.dynamic_slice(weight_late, (0, (xh_late * 2 + 1 - core_late) * width), (channels, width))
+    )
     at = jnp.stack([seq, y, xh_late * 2 + core_late, core_late]).astype(jnp.int32)
-    m2 = mirrored_rows(4 * piece, channels - 4 * piece, xh_late)
-    w_other = other_core(
-        lax.dynamic_slice(out_weight, (0, (xh_late * 2 + 1 - core_late) * width), (channels, width))
-    )
     weight = residue_late * jnp.sqrt(-jnp.expm1(-2.0 * rate))
     ends = lax.all_to_all(end, ("y", "xl"), 0, 0, tiled=True)
     conv, query, din = pl.pallas_call(
         conv_kernel,
         out_shape=(
-            jax.ShapeDtypeStruct((rows, channels), BF),
-            jax.ShapeDtypeStruct((rows, channels), BF),
+            pltpu.HBM((rows, channels), BF),
+            pltpu.HBM((rows, channels), BF),
             jax.ShapeDtypeStruct((CHUNK, flat), BF),
         ),
         grid=(1,),
@@ -301,9 +325,10 @@
         compiler_params=pltpu.CompilerParams(vmem_limit_bytes=16 * 2**20),
         cost_estimate=pl.CostEstimate(flops=10**6, bytes_accessed=2**16, transcendentals=0),
         name="conv",
-    )(projected, signal, halo, short_filter, rate, weight, rt)
-    r1, r2, r3 = (lax.ppermute(m1, "y", [(i, (i + k) % 4) for i in range(4)]) for k in (1, 2, 3))
-    ends, r1, r3 = lax.optimization_barrier((ends, r1, r3))
+    )(far(projected), far(signal), halo, far(short_filter), far(rate), weight, rt)
+    f1 = lax.ppermute(f0, "y", [(i, (i + 1) % 4) for i in range(4)])
+    f3 = lax.ppermute(f0, "y", [(i, (i - 1) % 4) for i in range(4)])
+    ends, f1, f3 = lax.optimization_barrier((ends, f1, f3))
     mixed = pl.pallas_call(
         mix_kernel,
         out_shape=jax.ShapeDtypeStruct((rows, channels), BF),
@@ -312,15 +337,16 @@
         compiler_params=pltpu.CompilerParams(vmem_limit_bytes=10 * 2**20),
         cost_estimate=pl.CostEstimate(flops=10**6, bytes_accessed=2**16, transcendentals=0),
         name="mix",
-    )(at, ends, rt, din, conv, query)
+    )(at, ends, rt, din, far(conv), far(query))
 
     a_far = lax.ppermute(mixed, "xh", [(0, 1), (1, 0)])
     a_other = other_core(mixed)
-    a_far_other = other_core(a_far)
-    given = jnp.concatenate(
-        [lax.dynamic_slice(v, (0, (1 - core) * width), (v.shape[0], width)) for v in (m1, r1, r2, r3, m2)], axis=0
-    )
-    f_other = other_core(given)
+    def given(parts):
+        return other_core(
+            jnp.concatenate([lax.dynamic_slice(v, (0, (1 - core) * width), (v.shape[0], width)) for v in parts], axis=0)
+        )
+
+    g013, g2 = given((f0, f1, f3)), given((f2,))
 
     tile = 512
     strips = width // tile
@@ -331,23 +357,41 @@
     def half_strip(shape):
         return pl.BlockSpec(shape[:-1] + (tile,), lambda i, at_ref: (0, at_ref[3] * strips + i))
 
+    left_specs = [pl.BlockSpec((rows, channels), lambda i, at_ref: (0, 0), **once)] * 2
+    near = pl.pallas_call(
+        near_kernel,
+        out_shape=jax.ShapeDtypeStruct((rows, width), BF),
+        grid_spec=pltpu.PrefetchScalarGridSpec(
+            num_scalar_prefetch=1,
+            grid=(strips,),
+            in_specs=left_specs
+            + [pl.BlockSpec((channels, tile), lambda i, at_ref: (0, at_ref[2] * strips + i)), strip(w_other.shape)],
+            out_specs=strip((rows, width)),
+            scratch_shapes=[pltpu.VMEM((rows, 2 * channels), BF), pltpu.VMEM((2 * channels, tile), BF)],
+        ),
+        compiler_params=pltpu.CompilerParams(vmem_limit_bytes=16 * 2**20),
+        cost_estimate=pl.CostEstimate(flops=2 * 10**9, bytes_accessed=6 * 2**20, transcendentals=0),
+        name="near",
+    )(at, mixed, a_other, far(out_weight), w_other)
+    a_far, near = lax.optimization_barrier((a_far, near))
+    a_far_other = other_core(a_far)
     partial = pl.pallas_call(
-        product_kernel,
+        far_kernel,
         out_shape=pltpu.HBM((rows, width), BF),
         grid_spec=pltpu.PrefetchScalarGridSpec(
             num_scalar_prefetch=1,
             grid=(strips,),
-            in_specs=[pl.BlockSpec((rows, channels), lambda i, at_ref: (0, 0), **once)] * 4
-            + [pl.BlockSpec((channels, tile), lambda i, at_ref: (0, at_ref[2] * strips + i)), strip(w_other.shape)]
-            + [half_strip(m1.shape)] * 4
-            + [half_strip(m2.shape), strip(f_other.shape)],
+            in_specs=left_specs
+            + [half_strip(v.shape) for v in (f0, f1, f2, f3)]
+            + [strip(g013.shape), strip(g2.shape)]
+            + [strip((rows, width))],
             out_specs=strip((rows, width)),
-            scratch_shapes=[pltpu.VMEM((rows, 4 * channels), BF), pltpu.VMEM((4 * channels, tile), BF)],
+            scratch_shapes=[pltpu.VMEM((rows, 2 * channels), BF), pltpu.VMEM((2 * channels, tile), BF)],
         ),
-        compiler_params=pltpu.CompilerParams(vmem_limit_bytes=28 * 2**20),
-        cost_estimate=pl.CostEstimate(flops=4 * 10**9, bytes_accessed=10 * 2**20, transcendentals=0),
-        name="product",
-    )(at, mixed, a_other, a_far, a_far_other, pltpu.with_memory_space_constraint(out_weight, pltpu.HBM), w_other, m1, r1, r2, r3, m2, f_other)
+        compiler_params=pltpu.CompilerParams(vmem_limit_bytes=20 * 2**20),
+        cost_estimate=pl.CostEstimate(flops=2 * 10**9, bytes_accessed=10 * 2**20, transcendentals=0),
+        name="far",
+    )(at, a_far, a_far_other, f0, f1, f2, f3, g013, g2, near)
 
     summed = lax.psum_scatter(partial, "z", scatter_dimension=0, tiled=True)
     size = summed.shape[0] // 4

time: 149 us -> 152 us (1.020)
  waiting for transfers between devices: 70.4 us -> 81.1 us
  local copies, waits for them, and re-layouts: 13.8 us -> 6.41 us
  starting transfers between devices: 33.4 us -> 26.7 us
  Pallas kernels: 16.7 us -> 23.1 us
    ppermute x1, waiting for transfers between devices: 0.01 us -> 7.77 us  [local(): a_far = lax.ppermute(mixed, 'xh', [(0, 1), (1, 0)])]
    ppermute x4 -> x5, starting transfers between devices: 11.6 us -> 5.21 us  [other_core(): return lax.ppermute(value, 'c', [(0, 1), (1, 0)])]
    unnamed x18 -> x4, local copies, waits for them, and re-layouts: 5.7 us -> 0.01 us
    pallas_call x3 -> x4, Pallas kernels: 14.5 us -> 20.1 us  [the longest x1 5.44 us: local(): pl.pallas_call(far_kernel, out_shape=pltpu.HBM((rows, width), BF), grid_s...]
    ppermute x6 -> x5, waiting for transfers between devices: 6.38 us -> 8.43 us  [the longest x1 4.95 us: local(): f2 = lax.ppermute(f2, ('xl', 'xh'), mirror)]
    ppermute x6 -> x5, starting transfers between devices: 12.9 us -> 11.8 us  [the longest x1 3.93 us: local(): halo = lax.ppermute(edge, ('y', 'xl'), [(i, i + 1) for i in range(7)])]
    dynamic_slice x3 -> x8, local copies, waits for them, and re-layouts: 5.25 us -> 4.57 us  [the longest x1 2.38 us: local(): lax.dynamic_slice(weight_late, (0, (xh_late * 2 + 1 - core_late) * width)...]
  transfers between devices with their start and end apart: 16 -> 16, of which waited for: 5 -> 8; matrix products, arithmetic and copies ran while one was open for 6% -> 4% of each run, Pallas kernels for 5% -> 11%
where the time goes in v6:
time: 152 us
  waiting for transfers between devices  81.1 us (53%)
  starting transfers between devices  26.7 us (18%)
  Pallas kernels  23.1 us (15%)
  between operations  13.5 us (9%)
  local copies, waits for them, and re-layouts  6.41 us (4%)
    reduce_scatter x1, waiting for transfers between devices, local(): summed = lax.psum_scatter(partial, 'z', scatter_dimension=0, tiled=True)  57.1 us
    ppermute x1, waiting for transfers between devices, local(): a_far = lax.ppermute(mixed, 'xh', [(0, 1), (1, 0)])  7.77 us
    ppermute x3, waiting for transfers between devices, traded(): return lax.ppermute(summed[k * size:(k + 1) * size], ('xh', 'c'), pairs)  6.34 us
    pallas_call x1, Pallas kernels, local(): pl.pallas_call(far_kernel, out_shape=pltpu.HBM((rows, width), BF), grid_s...  5.44 us
    ppermute x5, starting transfers between devices, other_core(): return lax.ppermute(value, 'c', [(0, 1), (1, 0)])  5.21 us
    pallas_call x1, Pallas kernels, local(): pl.pallas_call(conv_kernel, out_shape=(pltpu.HBM((rows, channels), BF), p...  5.06 us
    pallas_call x1, Pallas kernels, local(): pl.pallas_call(near_kernel, out_shape=jax.ShapeDtypeStruct((rows, width),...  4.95 us
    ppermute x1, waiting for transfers between devices, local(): f2 = lax.ppermute(f2, ('xl', 'xh'), mirror)  4.95 us
  transfers between devices with their start and end apart: 16, of which 8 were waited for; matrix products, arithmetic and copies ran while one was open for 4% of the time, Pallas kernels for 11%

profile of v6, /device:TPU:1, one launch (start us, length us, event | category | flops | bytes accessed | tf_op | source)
XLA Modules:
  0.0 151.9 jit_solution(12006175976050641040)
XLA Ops:
  6.5 0.7 slice.15
  7.2 3.9 %collective-permute-start = (bf16[3,8,256]{2,1,0:T(8,128)(2,1)S(1)}, bf16[3,8,256]{2,1,0:T(8,128)(2,1)S(1)}, u32[]{:S(2)}, u32[]{:S(2)}) collective-permute-start(bf16[3,8,256]{2,1,0:T(8,128)(2,1)S(1)} %slice.15), channel_id=1, source_target_pairs={{0,32},{32,64},{64,96},{96,128},{128,160},{160,192},{192,224},{1,3... | collective-permute-start | bytes 36872 | tf_op jit(solution)/shard_map/ppermute | solution.py:251
  11.2 1.0 dynamic_slice.24
  12.2 2.9 %collective-permute-start.1 = (bf16[48,4096]{1,0:T(8,128)(2,1)S(1)}, bf16[48,4096]{1,0:T(8,128)(2,1)S(1)}, u32[]{:S(2)}, u32[]{:S(2)}) collective-permute-start(bf16[48,4096]{1,0:T(8,128)(2,1)S(1)} %dynamic_slice.24), channel_id=1, source_target_pairs={{0,34},{34,0},{2,32},{32,2},{1,35},{35,1},{3,33},{33,3},{4,38},{38... | collective-permute-start | bytes 1179656 | tf_op jit(solution)/shard_map/ppermute | solution.py:261
  15.1 0.0 collective-permute-done.halo_ref
  15.1 4.7 %state.1 = (bf16[1024,256]{1,0:T(8,128)(2,1)}, f32[8,16,256]{2,1,0:T(8,128)}, f32[16,256]{1,0:T(8,128)S(1)}) custom-call(bf16[3,1024,256]{2,1,0:T(8,128)(2,1)} %p_ref.1, bf16[3,1024,256]{2,1,0:T(8,128)(2,1)} %p_ref.1, bf16[3,8,256]{2,1,0:T(8,128)(2,1)S(1)} %collective-permute-done.halo_ref, f32[3,3,256]{2,1,0:T(4,128)} %sf_ref.3, f32[16,16]{1,0:T(8,128)} %rate_ref.3), custom_call_target="tpu_custom_call" | custom-call | flops 1000000 | bytes 65536 | tf_op jit(solution)/shard_map/state/pallas_call | solution.py:273
  19.8 3.9 %all-to-all-start = ((f32[8,16,256]{2,1,0:T(8,128)}), f32[8,16,256]{2,1,0:T(8,128)S(1)}, u32[]{:S(2)}, u32[]{:S(2)}) async-start(f32[8,16,256]{2,1,0:T(8,128)} %get-tuple-element.27), calls=%async_computation | async-start | bytes 262144 | tf_op jit(solution)/shard_map/all_to_all | solution.py:306
  23.7 0.0 reduce-scatter.2.cloned.1.call-start
  23.8 0.0 dynamic-slice-start
  23.8 2.4 %constant_dynamic-slice_fusion.4 = bf16[256,2048]{1,0:T(8,128)(2,1)} fusion(bf16[256,8192]{1,0:T(8,128)(2,1)} %w0.1, s32[]{:T(128)S(6)} %select_n.22), kind=kLoop, calls=%fused_computation.7 | loop fusion | bytes 2097156 | tf_op jit(solution)/shard_map/dynamic_slice | solution.py:302
  26.2 1.5 collective-permute-start.6
  27.7 1.1 constant_dynamic-slice_fusion.5
  28.8 0.0 collective-permute-done.1.f0
  28.8 3.0 %collective-permute-start.3 = (bf16[48,4096]{1,0:T(8,128)(2,1)S(1)}, bf16[48,4096]{1,0:T(8,128)(2,1)S(1)}, u32[]{:S(2)}, u32[]{:S(2)}) collective-permute-start(bf16[48,4096]{1,0:T(8,128)(2,1)S(1)} %collective-permute-done.1.f0), channel_id=1, source_target_pairs={{0,192},{64,0},{128,64},{192,128},{1,193},{65,1},{129,65},{193,129... | collective-permute-start | bytes 1179656 | tf_op jit(solution)/shard_map/ppermute | solution.py:330
  31.8 0.0 collective-permute-start.2
  31.8 0.0 dynamic-slice-done
  31.8 1.0 pad_maximum_fusion
  32.8 2.0 %collective-permute-start.8 = (bf16[112,4096]{1,0:T(8,128)(2,1)}, bf16[112,4096]{1,0:T(8,128)(2,1)S(1)}, u32[]{:S(2)}, u32[]{:S(2)}) collective-permute-start(bf16[112,4096]{1,0:T(8,128)(2,1)} %pad_maximum_fusion), channel_id=1, source_target_pairs={{0,34},{34,0},{2,32},{32,2},{1,35},{35,1},{3,33},{33,3},{4,38},{38... | collective-permute-start | bytes 2752520 | tf_op jit(solution)/shard_map/ppermute | solution.py:300
  34.8 0.1 pad_add_fusion.at_ref
  34.8 5.1 %conv.1 = (bf16[1024,256]{1,0:T(8,128)(2,1)}, bf16[1024,256]{1,0:T(8,128)(2,1)}, bf16[128,256]{1,0:T(8,128)(2,1)S(1)}) custom-call(bf16[3,1024,256]{2,1,0:T(8,128)(2,1)} %p_ref.1, bf16[1024,256]{1,0:T(8,128)(2,1)} %get-tuple-element.31.x_ref, bf16[3,8,256]{2,1,0:T(8,128)(2,1)S(1)} %collective-permute-done.halo_ref, f32[3,3,256]{2,1,0:T(4,128)} %sf_ref.3, ...), custom_call_target="tpu_custom_call" | custom-call | flops 1000000 | bytes 65536 | tf_op jit(solution)/shard_map/conv/pallas_call | solution.py:307
  39.9 0.0 all-to-all-done.ends_ref
  39.9 0.4 collective-permute-done.3.f3
  40.3 3.1 %collective-permute-done.2.f1 = bf16[48,4096]{1,0:T(8,128)(2,1)S(1)} collective-permute-done((bf16[48,4096]{1,0:T(8,128)(2,1)S(1)}, bf16[48,4096]{1,0:T(8,128)(2,1)S(1)}, u32[]{:S(2)}, u32[]{:S(2)}) %collective-permute-start.2) | collective-permute-done | bytes 393248 | tf_op jit(solution)/shard_map/ppermute | solution.py:329
  43.4 1.6 %mix.1.a0 = bf16[1024,256]{1,0:T(8,128)(2,1)S(1)} custom-call(s32[4]{0:T(128)S(1)} %pad_add_fusion.at_ref, f32[8,16,256]{2,1,0:T(8,128)S(1)} %all-to-all-done.ends_ref, f32[16,256]{1,0:T(8,128)S(1)} %get-tuple-element.30.rt_ref, bf16[128,256]{1,0:T(8,128)(2,1)S(1)} %get-tuple-element.33.din_ref, bf16[1024,256]{1,0:T(8,128)(2,1)} %get-tuple-element.34.y_ref, ...), custom_call_target="tpu_custom_call" | custom-call | flops 1000000 | bytes 65536 | tf_op jit(solution)/shard_map/mix/pallas_call | solution.py:332
  45.0 1.2 collective-permute-start.5
  46.2 1.9 %collective-permute-start.4 = (bf16[1024,256]{1,0:T(8,128)(2,1)S(1)}, bf16[1024,256]{1,0:T(8,128)(2,1)S(1)}, u32[]{:S(2)}, u32[]{:S(2)}) collective-permute-start(bf16[1024,256]{1,0:T(8,128)(2,1)S(1)} %mix.1.a0), channel_id=1, source_target_pairs={{0,2},{2,0},{1,3},{3,1},{4,6},{6,4},{5,7},{7,5},{8,10},{10,8},{9,1... | collective-permute-start | bytes 1572872 | tf_op jit(solution)/shard_map/ppermute | solution.py:342
  48.2 0.4 collective-permute-start.9
  48.6 0.0 collective-permute-done.6.w1
  48.6 0.0 collective-permute-done.5.a1
  48.6 5.0 %near.1.near_ref = bf16[1024,2048]{1,0:T(8,128)(2,1)S(1)} custom-call(s32[4]{0:T(128)S(1)} %pad_add_fusion.at_ref, bf16[1024,256]{1,0:T(8,128)(2,1)S(1)} %mix.1.a0, bf16[1024,256]{1,0:T(8,128)(2,1)S(1)} %collective-permute-done.5.a1, bf16[256,8192]{1,0:T(8,128)(2,1)} %w0.1, bf16[256,2048]{1,0:T(8,128)(2,1)S(1)} %collective-permute-done.6.w1), custom_call_target="tpu_custom_call" | custom-call | flops 2000000000 | bytes 6291456 | tf_op jit(solution)/shard_map/near/pallas_call | solution.py:361
  53.6 7.8 %collective-permute-done.4.a2 = bf16[1024,256]{1,0:T(8,128)(2,1)S(1)} collective-permute-done((bf16[1024,256]{1,0:T(8,128)(2,1)S(1)}, bf16[1024,256]{1,0:T(8,128)(2,1)S(1)}, u32[]{:S(2)}, u32[]{:S(2)}) %collective-permute-start.4) | collective-permute-done | bytes 524320 | tf_op jit(solution)/shard_map/ppermute | solution.py:342
  61.4 0.9 collective-permute-start.7
  62.2 5.0 %collective-permute-done.8.f2 = bf16[112,4096]{1,0:T(8,128)(2,1)S(1)} collective-permute-done((bf16[112,4096]{1,0:T(8,128)(2,1)}, bf16[112,4096]{1,0:T(8,128)(2,1)S(1)}, u32[]{:S(2)}, u32[]{:S(2)}) %collective-permute-start.8) | collective-permute-done | bytes 917536 | tf_op jit(solution)/shard_map/ppermute | solution.py:300
  67.2 1.2 collective-permute-start.10
  68.4 0.0 collective-permute-done.9.g013
  68.4 1.4 collective-permute-done.10.g2
  69.9 0.0 collective-permute-done.7.a3
  69.9 5.4 %far.1 = bf16[1024,2048]{1,0:T(8,128)(2,1)} custom-call(s32[4]{0:T(128)S(1)} %pad_add_fusion.at_ref, bf16[1024,256]{1,0:T(8,128)(2,1)S(1)} %collective-permute-done.4.a2, bf16[1024,256]{1,0:T(8,128)(2,1)S(1)} %collective-permute-done.7.a3, bf16[48,4096]{1,0:T(8,128)(2,1)S(1)} %collective-permute-done.1.f0, bf16[48,4096]{1,0:T(8,128)(2,1)S(1)} %collective-permute-done.2.f1, ...), custom_call_target="tpu_custom_call" | custom-call | flops 2000000000 | bytes 10485760 | tf_op jit(solution)/shard_map/far/pallas_call | solution.py:378
  75.3 0.0 reduce-scatter.2.cloned.1.call-update
  75.3 57.1 %reduce-scatter.2.cloned.1.call-done = bf16[128,2048]{1,0:T(8,128)(2,1)} async-done(((bf16[1024,2048]{1,0:T(8,128)(2,1)}), bf16[128,2048]{1,0:T(8,128)(2,1)}) %reduce-scatter.2.cloned.1.call-update) | async-done | bytes 524304 | tf_op jit(solution)/shard_map/reduce_scatter | solution.py:396
  132.4 1.1 fusion
  133.5 3.3 %collective-permute-start.13 = (bf16[32,2048]{1,0:T(8,128)(2,1)S(1)}, bf16[32,2048]{1,0:T(8,128)(2,1)S(1)}, u32[]{:S(2)}, u32[]{:S(2)}) collective-permute-start(bf16[32,2048]{1,0:T(8,128)(2,1)S(1)} %get-tuple-element.41), channel_id=1, source_target_pairs={{0,3},{1,2},{2,1},{3,0},{4,7},{5,6},{6,5},{7,4},{8,11},{9,10},{10,... | collective-permute-start | bytes 393224 | tf_op jit(solution)/shard_map/ppermute | solution.py:401
  136.8 0.3 collective-permute-start.12
  137.1 0.2 collective-permute-start.11
  137.3 3.8 %collective-permute-done.13.p3 = bf16[32,2048]{1,0:T(8,128)(2,1)S(1)} collective-permute-done((bf16[32,2048]{1,0:T(8,128)(2,1)S(1)}, bf16[32,2048]{1,0:T(8,128)(2,1)S(1)}, u32[]{:S(2)}, u32[]{:S(2)}) %collective-permute-start.13) | collective-permute-done | bytes 131104 | tf_op jit(solution)/shard_map/ppermute | solution.py:401
  141.1 2.6 %collective-permute-done.12.p2 = bf16[32,2048]{1,0:T(8,128)(2,1)S(1)} collective-permute-done((bf16[32,2048]{1,0:T(8,128)(2,1)S(1)}, bf16[32,2048]{1,0:T(8,128)(2,1)S(1)}, u32[]{:S(2)}, u32[]{:S(2)}) %collective-permute-start.12) | collective-permute-done | bytes 131104 | tf_op jit(solution)/shard_map/ppermute | solution.py:401
  143.7 0.0 collective-permute-done.11.p1
  143.7 1.4 join.1
  (9 shorter events, 0.1 us)
Async XLA Ops:
  7.2 7.9 %collective-permute-start = (bf16[3,8,256]{2,1,0:T(8,128)(2,1)S(1)}, bf16[3,8,256]{2,1,0:T(8,128)(2,1)S(1)}, u32[]{:S(2)}, u32[]{:S(2)}) collective-permute-start(bf16[3,8,256]{2,1,0:T(8,128)(2,1)S(1)} %slice.15), channel_id=1, source_target_pairs={{0,32},{32,64},{64,96},{96,128},{128,160},{160,192},{192,224},{1,3... | collective-permute-start | bytes 36872 | tf_op jit(solution)/shard_map/ppermute | solution.py:251
  12.2 16.6 %collective-permute-start.1 = (bf16[48,4096]{1,0:T(8,128)(2,1)S(1)}, bf16[48,4096]{1,0:T(8,128)(2,1)S(1)}, u32[]{:S(2)}, u32[]{:S(2)}) collective-permute-start(bf16[48,4096]{1,0:T(8,128)(2,1)S(1)} %dynamic_slice.24), channel_id=1, source_target_pairs={{0,34},{34,0},{2,32},{32,2},{1,35},{35,1},{3,33},{33,3},{4,38},{38... | collective-permute-start | bytes 1179656 | tf_op jit(solution)/shard_map/ppermute | solution.py:261
  19.8 20.1 %all-to-all-start = ((f32[8,16,256]{2,1,0:T(8,128)}), f32[8,16,256]{2,1,0:T(8,128)S(1)}, u32[]{:S(2)}, u32[]{:S(2)}) async-start(f32[8,16,256]{2,1,0:T(8,128)} %get-tuple-element.27), calls=%async_computation | async-start | bytes 262144 | tf_op jit(solution)/shard_map/all_to_all | solution.py:306
  23.7 108.7 %reduce-scatter.2.cloned.1.call-start = ((), (), s32[]{:S(2)}) async-start(), calls=%async_computation.2 | async-start | bytes 4718592 | tf_op jit(solution)/shard_map/reduce_scatter | solution.py:396
  23.8 8.0 %dynamic-slice-start = ((bf16[256,8192]{1,0:T(8,128)(2,1)}, s32[]{:T(128)}, s32[]{:T(128)}), bf16[48,4096]{1,0:T(8,128)(2,1)S(1)}, s32[]{:S(2)}) async-start(bf16[256,8192]{1,0:T(8,128)(2,1)} %w0.1, s32[]{:T(128)} %select_n.23, s32[]{:T(128)} %select_n.21), calls=%async_computation.3 | async-start | bytes 786944 | tf_op jit(solution)/shard_map/dynamic_slice | solution.py:259
  26.2 6.6 %copy-start = (f32[16,16]{1,0:T(8,128)S(1)}, f32[16,16]{1,0:T(8,128)}, u32[]{:S(2)}) copy-start(f32[16,16]{1,0:T(8,128)} %rate_ref.3) | copy-start | bytes 3076
  26.2 6.6 %copy-start.1 = (f32[16,16]{1,0:T(8,128)S(1)}, f32[16,16]{1,0:T(8,128)}, u32[]{:S(2)}) copy-start(f32[16,16]{1,0:T(8,128)} %param.7) | copy-start | bytes 3076
  26.2 22.4 %collective-permute-start.6 = (bf16[256,2048]{1,0:T(8,128)(2,1)}, bf16[256,2048]{1,0:T(8,128)(2,1)S(1)}, u32[]{:S(2)}, u32[]{:S(2)}) collective-permute-start(bf16[256,2048]{1,0:T(8,128)(2,1)} %constant_dynamic-slice_fusion.4), channel_id=1, source_target_pairs={{0,1},{1,0},{2,3},{3,2},{4,5},{5,4},{6,7},{7,6},{8,9},{9,8},{10,11... | collective-permute-start | bytes 3145736 | tf_op jit(solution)/shard_map/ppermute | solution.py:240
  28.8 11.5 %collective-permute-start.3 = (bf16[48,4096]{1,0:T(8,128)(2,1)S(1)}, bf16[48,4096]{1,0:T(8,128)(2,1)S(1)}, u32[]{:S(2)}, u32[]{:S(2)}) collective-permute-start(bf16[48,4096]{1,0:T(8,128)(2,1)S(1)} %collective-permute-done.1.f0), channel_id=1, source_target_pairs={{0,192},{64,0},{128,64},{192,128},{1,193},{65,1},{129,65},{193,129... | collective-permute-start | bytes 1179656 | tf_op jit(solution)/shard_map/ppermute | solution.py:330
  31.8 11.6 %collective-permute-start.2 = (bf16[48,4096]{1,0:T(8,128)(2,1)S(1)}, bf16[48,4096]{1,0:T(8,128)(2,1)S(1)}, u32[]{:S(2)}, u32[]{:S(2)}) collective-permute-start(bf16[48,4096]{1,0:T(8,128)(2,1)S(1)} %collective-permute-done.1.f0), channel_id=1, source_target_pairs={{0,64},{64,128},{128,192},{192,0},{1,65},{65,129},{129,193},{193,1... | collective-permute-start | bytes 1179656 | tf_op jit(solution)/shard_map/ppermute | solution.py:329
  32.8 34.4 %collective-permute-start.8 = (bf16[112,4096]{1,0:T(8,128)(2,1)}, bf16[112,4096]{1,0:T(8,128)(2,1)S(1)}, u32[]{:S(2)}, u32[]{:S(2)}) collective-permute-start(bf16[112,4096]{1,0:T(8,128)(2,1)} %pad_maximum_fusion), channel_id=1, source_target_pairs={{0,34},{34,0},{2,32},{32,2},{1,35},{35,1},{3,33},{33,3},{4,38},{38... | collective-permute-start | bytes 2752520 | tf_op jit(solution)/shard_map/ppermute | solution.py:300
  45.0 3.7 %collective-permute-start.5 = (bf16[1024,256]{1,0:T(8,128)(2,1)S(1)}, bf16[1024,256]{1,0:T(8,128)(2,1)S(1)}, u32[]{:S(2)}, u32[]{:S(2)}) collective-permute-start(bf16[1024,256]{1,0:T(8,128)(2,1)S(1)} %mix.1.a0), channel_id=1, source_target_pairs={{0,1},{1,0},{2,3},{3,2},{4,5},{5,4},{6,7},{7,6},{8,9},{9,8},{10,11... | collective-permute-start | bytes 1572872 | tf_op jit(solution)/shard_map/ppermute | solution.py:240
  46.2 15.2 %collective-permute-start.4 = (bf16[1024,256]{1,0:T(8,128)(2,1)S(1)}, bf16[1024,256]{1,0:T(8,128)(2,1)S(1)}, u32[]{:S(2)}, u32[]{:S(2)}) collective-permute-start(bf16[1024,256]{1,0:T(8,128)(2,1)S(1)} %mix.1.a0), channel_id=1, source_target_pairs={{0,2},{2,0},{1,3},{3,1},{4,6},{6,4},{5,7},{7,5},{8,10},{10,8},{9,1... | collective-permute-start | bytes 1572872 | tf_op jit(solution)/shard_map/ppermute | solution.py:342
  48.2 20.2 %collective-permute-start.9 = (bf16[144,2048]{1,0:T(8,128)(2,1)S(1)}, bf16[144,2048]{1,0:T(8,128)(2,1)S(1)}, u32[]{:S(2)}, u32[]{:S(2)}) collective-permute-start(bf16[144,2048]{1,0:T(8,128)(2,1)S(1)} %pad_maximum_fusion.1), channel_id=1, source_target_pairs={{0,1},{1,0},{2,3},{3,2},{4,5},{5,4},{6,7},{7,6},{8,9},{9,8},{10,11... | collective-permute-start | bytes 1769480 | tf_op jit(solution)/shard_map/ppermute | solution.py:240
  61.4 8.5 %collective-permute-start.7 = (bf16[1024,256]{1,0:T(8,128)(2,1)S(1)}, bf16[1024,256]{1,0:T(8,128)(2,1)S(1)}, u32[]{:S(2)}, u32[]{:S(2)}) collective-permute-start(bf16[1024,256]{1,0:T(8,128)(2,1)S(1)} %collective-permute-done.4.a2), channel_id=1, source_target_pairs={{0,1},{1,0},{2,3},{3,2},{4,5},{5,4},{6,7},{7,6},{8,9},{9,8},{10,11... | collective-permute-start | bytes 1572872 | tf_op jit(solution)/shard_map/ppermute | solution.py:240
  67.2 2.7 %collective-permute-start.10 = (bf16[112,2048]{1,0:T(8,128)(2,1)S(1)}, bf16[112,2048]{1,0:T(8,128)(2,1)S(1)}, u32[]{:S(2)}, u32[]{:S(2)}) collective-permute-start(bf16[112,2048]{1,0:T(8,128)(2,1)S(1)} %constant_dynamic-slice_fusion), channel_id=1, source_target_pairs={{0,1},{1,0},{2,3},{3,2},{4,5},{5,4},{6,7},{7,6},{8,9},{9,8},{10,11... | collective-permute-start | bytes 1376264 | tf_op jit(solution)/shard_map/ppermute | solution.py:240
  133.5 7.6 %collective-permute-start.13 = (bf16[32,2048]{1,0:T(8,128)(2,1)S(1)}, bf16[32,2048]{1,0:T(8,128)(2,1)S(1)}, u32[]{:S(2)}, u32[]{:S(2)}) collective-permute-start(bf16[32,2048]{1,0:T(8,128)(2,1)S(1)} %get-tuple-element.41), channel_id=1, source_target_pairs={{0,3},{1,2},{2,1},{3,0},{4,7},{5,6},{6,5},{7,4},{8,11},{9,10},{10,... | collective-permute-start | bytes 393224 | tf_op jit(solution)/shard_map/ppermute | solution.py:401
  136.8 6.8 %collective-permute-start.12 = (bf16[32,2048]{1,0:T(8,128)(2,1)S(1)}, bf16[32,2048]{1,0:T(8,128)(2,1)S(1)}, u32[]{:S(2)}, u32[]{:S(2)}) collective-permute-start(bf16[32,2048]{1,0:T(8,128)(2,1)S(1)} %get-tuple-element.42), channel_id=1, source_target_pairs={{0,2},{1,3},{2,0},{3,1},{4,6},{5,7},{6,4},{7,5},{8,10},{9,11},{10,... | collective-permute-start | bytes 393224 | tf_op jit(solution)/shard_map/ppermute | solution.py:401
  137.1 6.6 %collective-permute-start.11 = (bf16[32,2048]{1,0:T(8,128)(2,1)S(1)}, bf16[32,2048]{1,0:T(8,128)(2,1)S(1)}, u32[]{:S(2)}, u32[]{:S(2)}) collective-permute-start(bf16[32,2048]{1,0:T(8,128)(2,1)S(1)} %get-tuple-element.43), channel_id=1, source_target_pairs={{0,1},{1,0},{2,3},{3,2},{4,5},{5,4},{6,7},{7,6},{8,9},{9,8},{10,11... | collective-permute-start | bytes 393224 | tf_op jit(solution)/shard_map/ppermute | solution.py:401
Sparse Core Ops, SparseCore 0:
  75.5 56.8 reduce-scatter.1

commit v7 on v6

--- a/solution.py
+++ b/solution.py
@@ -200,7 +200,7 @@
         c_ref[span, :] = jnp.dot(left[span, :], right[...], preferred_element_type=F32).astype(BF)
 
 
-def far_kernel(at_ref, a2, a3, f0, f1, f2, f3, g013, g2, near_ref, c_ref, left, right):
+def far_kernel(at_ref, a2, a3, f0, f1, f2, f3, rest, g013, g2, near_ref, c_ref, left, right):
     y, mine = at_ref[1], at_ref[2]
     size = f0.shape[0]
     depth = right.shape[0] // 2
@@ -211,8 +211,8 @@
         right[pl.ds(pl.multiple_of(owner, 16), size), :] = ref[0:size]
         passed = g2[0:size] if k == 2 else g013[(0, 1, 0, 2)[k] * size : ((0, 1, 0, 2)[k] + 1) * size]
         right[pl.ds(pl.multiple_of(depth + owner, 16), size), :] = passed
-    right[4 * size : depth] = f2[size : size + tail]
-    right[depth + 4 * size : 2 * depth] = g2[size : size + tail]
+    right[4 * size : depth] = rest[...]
+    right[depth + 4 * size : 2 * depth] = g013[3 * size : 3 * size + tail]
     block = 256
     for m in range(left.shape[0] // block):
         span = slice(m * block, (m + 1) * block)
@@ -259,6 +259,7 @@
         return lax.dynamic_slice(source, (start, (1 - xh) * half), (count, half))
 
     f0 = lax.ppermute(there(out_weight, y_then * size, size), ("xl", "xh"), mirror)
+    rest = lax.ppermute(there(out_weight, 4 * size, tail), ("xl", "xh"), mirror)
 
     flat = groups * MODES
     span = 256
@@ -293,15 +294,8 @@
         cost_estimate=pl.CostEstimate(flops=10**6, bytes_accessed=2**16, transcendentals=0),
         name="state",
     )(far(projected), far(projected), halo, far(short_filter), far(rate))
-    end, xh_late, core_late, residue_late, weight_late = lax.optimization_barrier((end, xh, core, residue, out_weight))
-    f2 = jnp.concatenate(
-        [there(weight_late, lax.rem(y + 2, 4) * size, size), there(weight_late, 4 * size, tail)], axis=0
-    )
-    f2 = lax.ppermute(f2, ("xl", "xh"), mirror)
-    w_other = other_core(
-        lax.dynamic_slice(weight_late, (0, (xh_late * 2 + 1 - core_late) * width), (channels, width))
-    )
-    at = jnp.stack([seq, y, xh_late * 2 + core_late, core_late]).astype(jnp.int32)
+    end, residue_late, core_late = lax.optimization_barrier((end, residue, core))
+    at = jnp.stack([seq, y, xh * 2 + core, core]).astype(jnp.int32)
     weight = residue_late * jnp.sqrt(-jnp.expm1(-2.0 * rate))
     ends = lax.all_to_all(end, ("y", "xl"), 0, 0, tiled=True)
     conv, query, din = pl.pallas_call(
@@ -323,12 +317,16 @@
             pltpu.VMEM((channels // LANES, LANES // GROUP * CHUNK, 2 * LANES), BF),
         ],
         compiler_params=pltpu.CompilerParams(vmem_limit_bytes=16 * 2**20),
-        cost_estimate=pl.CostEstimate(flops=10**6, bytes_accessed=2**16, transcendentals=0),
+        cost_estimate=pl.CostEstimate(flops=6 * 10**9, bytes_accessed=2**16, transcendentals=0),
         name="conv",
     )(far(projected), far(signal), halo, far(short_filter), far(rate), weight, rt)
     f1 = lax.ppermute(f0, "y", [(i, (i + 1) % 4) for i in range(4)])
     f3 = lax.ppermute(f0, "y", [(i, (i - 1) % 4) for i in range(4)])
-    ends, f1, f3 = lax.optimization_barrier((ends, f1, f3))
+    ends, f1, f3, rest, f0_late = lax.optimization_barrier((ends, f1, f3, rest, f0))
+    f2 = lax.ppermute(f0_late, "y", [(i, (i + 2) % 4) for i in range(4)])
+    w_other = other_core(
+        lax.dynamic_slice(out_weight, (0, (xh * 2 + 1 - core_late) * width), (channels, width))
+    )
     mixed = pl.pallas_call(
         mix_kernel,
         out_shape=jax.ShapeDtypeStruct((rows, channels), BF),
@@ -346,7 +344,7 @@
             jnp.concatenate([lax.dynamic_slice(v, (0, (1 - core) * width), (v.shape[0], width)) for v in parts], axis=0)
         )
 
-    g013, g2 = given((f0, f1, f3)), given((f2,))
+    g013, g2 = given((f0_late, f1, f3, rest)), given((f2,))
 
     tile = 512
     strips = width // tile
@@ -382,7 +380,7 @@
             num_scalar_prefetch=1,
             grid=(strips,),
             in_specs=left_specs
-            + [half_strip(v.shape) for v in (f0, f1, f2, f3)]
+            + [half_strip(v.shape) for v in (f0, f1, f2, f3, rest)]
             + [strip(g013.shape), strip(g2.shape)]
             + [strip((rows, width))],
             out_specs=strip((rows, width)),
@@ -391,7 +389,7 @@
         compiler_params=pltpu.CompilerParams(vmem_limit_bytes=20 * 2**20),
         cost_estimate=pl.CostEstimate(flops=2 * 10**9, bytes_accessed=10 * 2**20, transcendentals=0),
         name="far",
-    )(at, a_far, a_far_other, f0, f1, f2, f3, g013, g2, near)
+    )(at, a_far, a_far_other, f0_late, f1, f2, f3, rest, g013, g2, near)
 
     summed = lax.psum_scatter(partial, "z", scatter_dimension=0, tiled=True)
     size = summed.shape[0] // 4

time: 152 us -> 146 us (0.961)
  waiting for transfers between devices: 81.1 us -> 76 us
    ppermute x1 -> x2, waiting for transfers between devices: 4.95 us -> 0.01 us  [the longest x1 0.01 us: local(): rest = lax.ppermute(there(out_weight, 4 * size, tail), ('xl', 'xh'), mirror)]
    ppermute x1, waiting for transfers between devices: 0.38 us -> 3.47 us  [local(): f3 = lax.ppermute(f0, 'y', [(i, (i - 1) % 4) for i in range(4)])]
    ppermute x1 -> x2, starting transfers between devices: 1.95 us -> 0.11 us  [the longest x1 0.11 us: local(): rest = lax.ppermute(there(out_weight, 4 * size, tail), ('xl', 'xh'), mirror)]
    reduce_scatter x1, waiting for transfers between devices: 57.1 us -> 55.4 us  [local(): summed = lax.psum_scatter(partial, 'z', scatter_dimension=0, tiled=True)]
  transfers between devices with their start and end apart: 16 -> 17, of which waited for: 8 -> 7; matrix products, arithmetic and copies ran while one was open for 4% -> 3% of each run, Pallas kernels for 11% -> 11%
where the time goes in v7:
time: 146 us
  waiting for transfers between devices  76 us (52%)
  starting transfers between devices  26.4 us (18%)
  Pallas kernels  23.1 us (16%)
  between operations  13.5 us (9%)
  local copies, waits for them, and re-layouts  6.38 us (4%)
    reduce_scatter x1, waiting for transfers between devices, local(): summed = lax.psum_scatter(partial, 'z', scatter_dimension=0, tiled=True)  55.4 us
    ppermute x1, waiting for transfers between devices, local(): a_far = lax.ppermute(mixed, 'xh', [(0, 1), (1, 0)])  6.57 us
    ppermute x3, waiting for transfers between devices, traded(): return lax.ppermute(summed[k * size:(k + 1) * size], ('xh', 'c'), pairs)  6.33 us
    pallas_call x1, Pallas kernels, local(): pl.pallas_call(far_kernel, out_shape=pltpu.HBM((rows, width), BF), grid_s...  5.48 us
    ppermute x5, starting transfers between devices, other_core(): return lax.ppermute(value, 'c', [(0, 1), (1, 0)])  5.19 us
    pallas_call x1, Pallas kernels, local(): pl.pallas_call(conv_kernel, out_shape=(pltpu.HBM((rows, channels), BF), p...  5.06 us
    pallas_call x1, Pallas kernels, local(): pl.pallas_call(near_kernel, out_shape=jax.ShapeDtypeStruct((rows, width),...  4.96 us
    pallas_call x1, Pallas kernels, local(): pl.pallas_call(state_kernel, out_shape=(pltpu.HBM((rows, channels), BF),...  4.67 us
  transfers between devices with their start and end apart: 17, of which 7 were waited for; matrix products, arithmetic and copies ran while one was open for 3% of the time, Pallas kernels for 11%

profile of v7, /device:TPU:1, one launch (start us, length us, event | category | flops | bytes accessed | tf_op | source)
XLA Modules:
  0.0 145.6 jit_solution(1612804055338123141)
XLA Ops:
  6.5 0.7 slice.15
  7.2 3.9 %collective-permute-start = (bf16[3,8,256]{2,1,0:T(8,128)(2,1)S(1)}, bf16[3,8,256]{2,1,0:T(8,128)(2,1)S(1)}, u32[]{:S(2)}, u32[]{:S(2)}) collective-permute-start(bf16[3,8,256]{2,1,0:T(8,128)(2,1)S(1)} %slice.15), channel_id=1, source_target_pairs={{0,32},{32,64},{64,96},{96,128},{128,160},{160,192},{192,224},{1,3... | collective-permute-start | bytes 36872 | tf_op jit(solution)/shard_map/ppermute | solution.py:251
  11.2 1.0 dynamic_slice.24
  12.2 2.9 %collective-permute-start.1 = (bf16[48,4096]{1,0:T(8,128)(2,1)S(1)}, bf16[48,4096]{1,0:T(8,128)(2,1)S(1)}, u32[]{:S(2)}, u32[]{:S(2)}) collective-permute-start(bf16[48,4096]{1,0:T(8,128)(2,1)S(1)} %dynamic_slice.24), channel_id=1, source_target_pairs={{0,34},{34,0},{2,32},{32,2},{1,35},{35,1},{3,33},{33,3},{4,38},{38... | collective-permute-start | bytes 1179656 | tf_op jit(solution)/shard_map/ppermute | solution.py:261
  15.1 1.1 constant_dynamic-slice_fusion.6
  16.2 0.1 collective-permute-start.4
  16.3 0.1 pad_add_fusion.at_ref
  16.4 0.0 collective-permute-done.halo_ref
  16.4 4.7 %state.1 = (bf16[1024,256]{1,0:T(8,128)(2,1)}, f32[8,16,256]{2,1,0:T(8,128)}, f32[16,256]{1,0:T(8,128)S(1)}) custom-call(bf16[3,1024,256]{2,1,0:T(8,128)(2,1)} %p_ref.1, bf16[3,1024,256]{2,1,0:T(8,128)(2,1)} %p_ref.1, bf16[3,8,256]{2,1,0:T(8,128)(2,1)S(1)} %collective-permute-done.halo_ref, f32[3,3,256]{2,1,0:T(4,128)} %sf_ref.3, f32[16,16]{1,0:T(8,128)} %rate_ref.3), custom_call_target="tpu_custom_call" | custom-call | flops 1000000 | bytes 65536 | tf_op jit(solution)/shard_map/state/pallas_call | solution.py:274
  21.1 0.0 copy-start.1
  21.1 4.0 %all-to-all-start = ((f32[8,16,256]{2,1,0:T(8,128)}), f32[8,16,256]{2,1,0:T(8,128)S(1)}, u32[]{:S(2)}, u32[]{:S(2)}) async-start(f32[8,16,256]{2,1,0:T(8,128)} %get-tuple-element.25), calls=%async_computation | async-start | bytes 262144 | tf_op jit(solution)/shard_map/all_to_all | solution.py:300
  25.1 0.0 reduce-scatter.2.cloned.1.call-start
  25.2 2.3 %constant_dynamic-slice_fusion.5 = bf16[256,2048]{1,0:T(8,128)(2,1)} fusion(bf16[256,8192]{1,0:T(8,128)(2,1)} %w0.1, s32[]{:T(128)S(6)} %select_n.19), kind=kLoop, calls=%fused_computation.7 | loop fusion | bytes 2097156 | tf_op jit(solution)/shard_map/dynamic_slice | solution.py:328
  27.5 1.8 %collective-permute-start.7 = (bf16[256,2048]{1,0:T(8,128)(2,1)}, bf16[256,2048]{1,0:T(8,128)(2,1)S(1)}, u32[]{:S(2)}, u32[]{:S(2)}) collective-permute-start(bf16[256,2048]{1,0:T(8,128)(2,1)} %constant_dynamic-slice_fusion.5), channel_id=1, source_target_pairs={{0,1},{1,0},{2,3},{3,2},{4,5},{5,4},{6,7},{7,6},{8,9},{9,8},{10,11... | collective-permute-start | bytes 3145736 | tf_op jit(solution)/shard_map/ppermute | solution.py:240
  29.3 0.0 collective-permute-done.1.f0
  29.4 3.0 %collective-permute-start.3 = (bf16[48,4096]{1,0:T(8,128)(2,1)S(1)}, bf16[48,4096]{1,0:T(8,128)(2,1)S(1)}, u32[]{:S(2)}, u32[]{:S(2)}) collective-permute-start(bf16[48,4096]{1,0:T(8,128)(2,1)S(1)} %collective-permute-done.1.f0), channel_id=1, source_target_pairs={{0,192},{64,0},{128,64},{192,128},{1,193},{65,1},{129,65},{193,129... | collective-permute-start | bytes 1179656 | tf_op jit(solution)/shard_map/ppermute | solution.py:324
  32.3 0.0 collective-permute-start.2
  32.3 5.1 %conv.1 = (bf16[1024,256]{1,0:T(8,128)(2,1)}, bf16[1024,256]{1,0:T(8,128)(2,1)}, bf16[128,256]{1,0:T(8,128)(2,1)S(1)}) custom-call(bf16[3,1024,256]{2,1,0:T(8,128)(2,1)} %p_ref.1, bf16[1024,256]{1,0:T(8,128)(2,1)} %get-tuple-element.29.x_ref, bf16[3,8,256]{2,1,0:T(8,128)(2,1)S(1)} %collective-permute-done.halo_ref, f32[3,3,256]{2,1,0:T(4,128)} %sf_ref.3, ...), custom_call_target="tpu_custom_call" | custom-call | flops 6000000000 | bytes 65536 | tf_op jit(solution)/shard_map/conv/pallas_call | solution.py:301
  37.4 0.0 all-to-all-done.ends_ref
  37.4 0.0 collective-permute-done.4.rest
  37.4 3.5 %collective-permute-done.3.f3 = bf16[48,4096]{1,0:T(8,128)(2,1)S(1)} collective-permute-done((bf16[48,4096]{1,0:T(8,128)(2,1)S(1)}, bf16[48,4096]{1,0:T(8,128)(2,1)S(1)}, u32[]{:S(2)}, u32[]{:S(2)}) %collective-permute-start.3) | collective-permute-done | bytes 393248 | tf_op jit(solution)/shard_map/ppermute | solution.py:324
  40.9 3.1 %collective-permute-done.2.f1 = bf16[48,4096]{1,0:T(8,128)(2,1)S(1)} collective-permute-done((bf16[48,4096]{1,0:T(8,128)(2,1)S(1)}, bf16[48,4096]{1,0:T(8,128)(2,1)S(1)}, u32[]{:S(2)}, u32[]{:S(2)}) %collective-permute-start.2) | collective-permute-done | bytes 393248 | tf_op jit(solution)/shard_map/ppermute | solution.py:323
  44.0 1.6 %mix.1.a0 = bf16[1024,256]{1,0:T(8,128)(2,1)S(1)} custom-call(s32[4]{0:T(128)S(1)} %pad_add_fusion.at_ref, f32[8,16,256]{2,1,0:T(8,128)S(1)} %all-to-all-done.ends_ref, f32[16,256]{1,0:T(8,128)S(1)} %get-tuple-element.28.rt_ref, bf16[128,256]{1,0:T(8,128)(2,1)S(1)} %get-tuple-element.31.din_ref, bf16[1024,256]{1,0:T(8,128)(2,1)} %get-tuple-element.32.y_ref, ...), custom_call_target="tpu_custom_call" | custom-call | flops 1000000 | bytes 65536 | tf_op jit(solution)/shard_map/mix/pallas_call | solution.py:330
  45.6 1.2 collective-permute-start.6
  46.7 3.4 %collective-permute-start.5 = (bf16[1024,256]{1,0:T(8,128)(2,1)S(1)}, bf16[1024,256]{1,0:T(8,128)(2,1)S(1)}, u32[]{:S(2)}, u32[]{:S(2)}) collective-permute-start(bf16[1024,256]{1,0:T(8,128)(2,1)S(1)} %mix.1.a0), channel_id=1, source_target_pairs={{0,2},{2,0},{1,3},{3,1},{4,6},{6,4},{5,7},{7,5},{8,10},{10,8},{9,1... | collective-permute-start | bytes 1572872 | tf_op jit(solution)/shard_map/ppermute | solution.py:340
  50.3 0.1 pad_maximum_fusion
  50.4 0.4 collective-permute-start.10
  50.8 0.0 collective-permute-start.9
  50.8 0.0 collective-permute-done.7.w1
  50.8 0.0 collective-permute-done.6.a1
  50.8 5.0 %near.1.near_ref = bf16[1024,2048]{1,0:T(8,128)(2,1)S(1)} custom-call(s32[4]{0:T(128)S(1)} %pad_add_fusion.at_ref, bf16[1024,256]{1,0:T(8,128)(2,1)S(1)} %mix.1.a0, bf16[1024,256]{1,0:T(8,128)(2,1)S(1)} %collective-permute-done.6.a1, bf16[256,8192]{1,0:T(8,128)(2,1)} %w0.1, bf16[256,2048]{1,0:T(8,128)(2,1)S(1)} %collective-permute-done.7.w1), custom_call_target="tpu_custom_call" | custom-call | flops 2000000000 | bytes 6291456 | tf_op jit(solution)/shard_map/near/pallas_call | solution.py:359
  55.8 6.6 %collective-permute-done.5.a2 = bf16[1024,256]{1,0:T(8,128)(2,1)S(1)} collective-permute-done((bf16[1024,256]{1,0:T(8,128)(2,1)S(1)}, bf16[1024,256]{1,0:T(8,128)(2,1)S(1)}, u32[]{:S(2)}, u32[]{:S(2)}) %collective-permute-start.5) | collective-permute-done | bytes 524320 | tf_op jit(solution)/shard_map/ppermute | solution.py:340
  62.4 0.7 collective-permute-start.8
  63.1 0.0 collective-permute-done.9.f2
  63.1 1.1 collective-permute-start.11
  64.1 1.1 collective-permute-done.11.g2
  65.2 0.0 collective-permute-done.10.g013
  65.2 5.5 %far.1 = bf16[1024,2048]{1,0:T(8,128)(2,1)} custom-call(s32[4]{0:T(128)S(1)} %pad_add_fusion.at_ref, bf16[1024,256]{1,0:T(8,128)(2,1)S(1)} %collective-permute-done.5.a2, bf16[1024,256]{1,0:T(8,128)(2,1)S(1)} %collective-permute-done.8.a3, bf16[48,4096]{1,0:T(8,128)(2,1)S(1)} %collective-permute-done.1.f0, bf16[48,4096]{1,0:T(8,128)(2,1)S(1)} %collective-permute-done.2.f1, ...), custom_call_target="tpu_custom_call" | custom-call | flops 2000000000 | bytes 10485760 | tf_op jit(solution)/shard_map/far/pallas_call | solution.py:376
  70.7 0.0 reduce-scatter.2.cloned.1.call-update
  70.7 55.4 %reduce-scatter.2.cloned.1.call-done = bf16[128,2048]{1,0:T(8,128)(2,1)} async-done(((bf16[1024,2048]{1,0:T(8,128)(2,1)}), bf16[128,2048]{1,0:T(8,128)(2,1)}) %reduce-scatter.2.cloned.1.call-update) | async-done | bytes 524304 | tf_op jit(solution)/shard_map/reduce_scatter | solution.py:394
  126.2 1.1 fusion
  127.3 3.3 %collective-permute-start.14 = (bf16[32,2048]{1,0:T(8,128)(2,1)S(1)}, bf16[32,2048]{1,0:T(8,128)(2,1)S(1)}, u32[]{:S(2)}, u32[]{:S(2)}) collective-permute-start(bf16[32,2048]{1,0:T(8,128)(2,1)S(1)} %get-tuple-element.41), channel_id=1, source_target_pairs={{0,3},{1,2},{2,1},{3,0},{4,7},{5,6},{6,5},{7,4},{8,11},{9,10},{10,... | collective-permute-start | bytes 393224 | tf_op jit(solution)/shard_map/ppermute | solution.py:399
  130.6 0.3 collective-permute-start.13
  130.9 0.2 collective-permute-start.12
  131.1 3.8 %collective-permute-done.14.p3 = bf16[32,2048]{1,0:T(8,128)(2,1)S(1)} collective-permute-done((bf16[32,2048]{1,0:T(8,128)(2,1)S(1)}, bf16[32,2048]{1,0:T(8,128)(2,1)S(1)}, u32[]{:S(2)}, u32[]{:S(2)}) %collective-permute-start.14) | collective-permute-done | bytes 131104 | tf_op jit(solution)/shard_map/ppermute | solution.py:399
  134.8 2.6 %collective-permute-done.13.p2 = bf16[32,2048]{1,0:T(8,128)(2,1)S(1)} collective-permute-done((bf16[32,2048]{1,0:T(8,128)(2,1)S(1)}, bf16[32,2048]{1,0:T(8,128)(2,1)S(1)}, u32[]{:S(2)}, u32[]{:S(2)}) %collective-permute-start.13) | collective-permute-done | bytes 131104 | tf_op jit(solution)/shard_map/ppermute | solution.py:399
  137.4 0.0 collective-permute-done.12.p1
  137.4 1.4 join.1
  (9 shorter events, 0.1 us)
Async XLA Ops:
  7.2 9.2 %collective-permute-start = (bf16[3,8,256]{2,1,0:T(8,128)(2,1)S(1)}, bf16[3,8,256]{2,1,0:T(8,128)(2,1)S(1)}, u32[]{:S(2)}, u32[]{:S(2)}) collective-permute-start(bf16[3,8,256]{2,1,0:T(8,128)(2,1)S(1)} %slice.15), channel_id=1, source_target_pairs={{0,32},{32,64},{64,96},{96,128},{128,160},{160,192},{192,224},{1,3... | collective-permute-start | bytes 36872 | tf_op jit(solution)/shard_map/ppermute | solution.py:251
  12.2 17.1 %collective-permute-start.1 = (bf16[48,4096]{1,0:T(8,128)(2,1)S(1)}, bf16[48,4096]{1,0:T(8,128)(2,1)S(1)}, u32[]{:S(2)}, u32[]{:S(2)}) collective-permute-start(bf16[48,4096]{1,0:T(8,128)(2,1)S(1)} %dynamic_slice.24), channel_id=1, source_target_pairs={{0,34},{34,0},{2,32},{32,2},{1,35},{35,1},{3,33},{33,3},{4,38},{38... | collective-permute-start | bytes 1179656 | tf_op jit(solution)/shard_map/ppermute | solution.py:261
  16.2 21.2 %collective-permute-start.4 = (bf16[64,4096]{1,0:T(8,128)(2,1)S(1)}, bf16[64,4096]{1,0:T(8,128)(2,1)S(1)}, u32[]{:S(2)}, u32[]{:S(2)}) collective-permute-start(bf16[64,4096]{1,0:T(8,128)(2,1)S(1)} %constant_dynamic-slice_fusion.6), channel_id=1, source_target_pairs={{0,34},{34,0},{2,32},{32,2},{1,35},{35,1},{3,33},{33,3},{4,38},{38... | collective-permute-start | bytes 1572872 | tf_op jit(solution)/shard_map/ppermute | solution.py:262
  21.1 8.2 %copy-start = (f32[16,16]{1,0:T(8,128)S(1)}, f32[16,16]{1,0:T(8,128)}, u32[]{:S(2)}) copy-start(f32[16,16]{1,0:T(8,128)} %rate_ref.3) | copy-start | bytes 3076
  21.1 8.2 %copy-start.1 = (f32[16,16]{1,0:T(8,128)S(1)}, f32[16,16]{1,0:T(8,128)}, u32[]{:S(2)}) copy-start(f32[16,16]{1,0:T(8,128)} %param.7) | copy-start | bytes 3076
  21.1 16.3 %all-to-all-start = ((f32[8,16,256]{2,1,0:T(8,128)}), f32[8,16,256]{2,1,0:T(8,128)S(1)}, u32[]{:S(2)}, u32[]{:S(2)}) async-start(f32[8,16,256]{2,1,0:T(8,128)} %get-tuple-element.25), calls=%async_computation | async-start | bytes 262144 | tf_op jit(solution)/shard_map/all_to_all | solution.py:300
  25.1 101.0 %reduce-scatter.2.cloned.1.call-start = ((), (), s32[]{:S(2)}) async-start(), calls=%async_computation.2 | async-start | bytes 4718592 | tf_op jit(solution)/shard_map/reduce_scatter | solution.py:394
  27.5 23.3 %collective-permute-start.7 = (bf16[256,2048]{1,0:T(8,128)(2,1)}, bf16[256,2048]{1,0:T(8,128)(2,1)S(1)}, u32[]{:S(2)}, u32[]{:S(2)}) collective-permute-start(bf16[256,2048]{1,0:T(8,128)(2,1)} %constant_dynamic-slice_fusion.5), channel_id=1, source_target_pairs={{0,1},{1,0},{2,3},{3,2},{4,5},{5,4},{6,7},{7,6},{8,9},{9,8},{10,11... | collective-permute-start | bytes 3145736 | tf_op jit(solution)/shard_map/ppermute | solution.py:240
  29.4 11.5 %collective-permute-start.3 = (bf16[48,4096]{1,0:T(8,128)(2,1)S(1)}, bf16[48,4096]{1,0:T(8,128)(2,1)S(1)}, u32[]{:S(2)}, u32[]{:S(2)}) collective-permute-start(bf16[48,4096]{1,0:T(8,128)(2,1)S(1)} %collective-permute-done.1.f0), channel_id=1, source_target_pairs={{0,192},{64,0},{128,64},{192,128},{1,193},{65,1},{129,65},{193,129... | collective-permute-start | bytes 1179656 | tf_op jit(solution)/shard_map/ppermute | solution.py:324
  32.3 11.6 %collective-permute-start.2 = (bf16[48,4096]{1,0:T(8,128)(2,1)S(1)}, bf16[48,4096]{1,0:T(8,128)(2,1)S(1)}, u32[]{:S(2)}, u32[]{:S(2)}) collective-permute-start(bf16[48,4096]{1,0:T(8,128)(2,1)S(1)} %collective-permute-done.1.f0), channel_id=1, source_target_pairs={{0,64},{64,128},{128,192},{192,0},{1,65},{65,129},{129,193},{193,1... | collective-permute-start | bytes 1179656 | tf_op jit(solution)/shard_map/ppermute | solution.py:323
  45.6 5.3 %collective-permute-start.6 = (bf16[1024,256]{1,0:T(8,128)(2,1)S(1)}, bf16[1024,256]{1,0:T(8,128)(2,1)S(1)}, u32[]{:S(2)}, u32[]{:S(2)}) collective-permute-start(bf16[1024,256]{1,0:T(8,128)(2,1)S(1)} %mix.1.a0), channel_id=1, source_target_pairs={{0,1},{1,0},{2,3},{3,2},{4,5},{5,4},{6,7},{7,6},{8,9},{9,8},{10,11... | collective-permute-start | bytes 1572872 | tf_op jit(solution)/shard_map/ppermute | solution.py:240
  46.7 15.6 %collective-permute-start.5 = (bf16[1024,256]{1,0:T(8,128)(2,1)S(1)}, bf16[1024,256]{1,0:T(8,128)(2,1)S(1)}, u32[]{:S(2)}, u32[]{:S(2)}) collective-permute-start(bf16[1024,256]{1,0:T(8,128)(2,1)S(1)} %mix.1.a0), channel_id=1, source_target_pairs={{0,2},{2,0},{1,3},{3,1},{4,6},{6,4},{5,7},{7,5},{8,10},{10,8},{9,1... | collective-permute-start | bytes 1572872 | tf_op jit(solution)/shard_map/ppermute | solution.py:340
  50.4 14.8 %collective-permute-start.10 = (bf16[208,2048]{1,0:T(8,128)(2,1)S(1)}, bf16[208,2048]{1,0:T(8,128)(2,1)S(1)}, u32[]{:S(2)}, u32[]{:S(2)}) collective-permute-start(bf16[208,2048]{1,0:T(8,128)(2,1)S(1)} %pad_maximum_fusion), channel_id=1, source_target_pairs={{0,1},{1,0},{2,3},{3,2},{4,5},{5,4},{6,7},{7,6},{8,9},{9,8},{10,11... | collective-permute-start | bytes 2555912 | tf_op jit(solution)/shard_map/ppermute | solution.py:240
  50.8 12.2 %collective-permute-start.9 = (bf16[48,4096]{1,0:T(8,128)(2,1)S(1)}, bf16[48,4096]{1,0:T(8,128)(2,1)S(1)}, u32[]{:S(2)}, u32[]{:S(2)}) collective-permute-start(bf16[48,4096]{1,0:T(8,128)(2,1)S(1)} %collective-permute-done.1.f0), channel_id=1, source_target_pairs={{0,128},{64,192},{128,0},{192,64},{1,129},{65,193},{129,1},{193,65... | collective-permute-start | bytes 1179656 | tf_op jit(solution)/shard_map/ppermute | solution.py:326
  62.4 2.8 %collective-permute-start.8 = (bf16[1024,256]{1,0:T(8,128)(2,1)S(1)}, bf16[1024,256]{1,0:T(8,128)(2,1)S(1)}, u32[]{:S(2)}, u32[]{:S(2)}) collective-permute-start(bf16[1024,256]{1,0:T(8,128)(2,1)S(1)} %collective-permute-done.5.a2), channel_id=1, source_target_pairs={{0,1},{1,0},{2,3},{3,2},{4,5},{5,4},{6,7},{7,6},{8,9},{9,8},{10,11... | collective-permute-start | bytes 1572872 | tf_op jit(solution)/shard_map/ppermute | solution.py:240
  63.1 2.1 %collective-permute-start.11 = (bf16[48,2048]{1,0:T(8,128)(2,1)S(1)}, bf16[48,2048]{1,0:T(8,128)(2,1)S(1)}, u32[]{:S(2)}, u32[]{:S(2)}) collective-permute-start(bf16[48,2048]{1,0:T(8,128)(2,1)S(1)} %constant_dynamic-slice_fusion), channel_id=1, source_target_pairs={{0,1},{1,0},{2,3},{3,2},{4,5},{5,4},{6,7},{7,6},{8,9},{9,8},{10,11... | collective-permute-start | bytes 589832 | tf_op jit(solution)/shard_map/ppermute | solution.py:240
  127.3 7.5 %collective-permute-start.14 = (bf16[32,2048]{1,0:T(8,128)(2,1)S(1)}, bf16[32,2048]{1,0:T(8,128)(2,1)S(1)}, u32[]{:S(2)}, u32[]{:S(2)}) collective-permute-start(bf16[32,2048]{1,0:T(8,128)(2,1)S(1)} %get-tuple-element.41), channel_id=1, source_target_pairs={{0,3},{1,2},{2,1},{3,0},{4,7},{5,6},{6,5},{7,4},{8,11},{9,10},{10,... | collective-permute-start | bytes 393224 | tf_op jit(solution)/shard_map/ppermute | solution.py:399
  130.6 6.8 %collective-permute-start.13 = (bf16[32,2048]{1,0:T(8,128)(2,1)S(1)}, bf16[32,2048]{1,0:T(8,128)(2,1)S(1)}, u32[]{:S(2)}, u32[]{:S(2)}) collective-permute-start(bf16[32,2048]{1,0:T(8,128)(2,1)S(1)} %get-tuple-element.42), channel_id=1, source_target_pairs={{0,2},{1,3},{2,0},{3,1},{4,6},{5,7},{6,4},{7,5},{8,10},{9,11},{10,... | collective-permute-start | bytes 393224 | tf_op jit(solution)/shard_map/ppermute | solution.py:399
  130.9 6.6 %collective-permute-start.12 = (bf16[32,2048]{1,0:T(8,128)(2,1)S(1)}, bf16[32,2048]{1,0:T(8,128)(2,1)S(1)}, u32[]{:S(2)}, u32[]{:S(2)}) collective-permute-start(bf16[32,2048]{1,0:T(8,128)(2,1)S(1)} %get-tuple-element.43), channel_id=1, source_target_pairs={{0,1},{1,0},{2,3},{3,2},{4,5},{5,4},{6,7},{7,6},{8,9},{9,8},{10,11... | collective-permute-start | bytes 393224 | tf_op jit(solution)/shard_map/ppermute | solution.py:399
Sparse Core Ops, SparseCore 0:
  70.8 55.2 reduce-scatter.1

commit v8 on v7

--- a/solution.py
+++ b/solution.py
@@ -294,7 +294,7 @@
         cost_estimate=pl.CostEstimate(flops=10**6, bytes_accessed=2**16, transcendentals=0),
         name="state",
     )(far(projected), far(projected), halo, far(short_filter), far(rate))
-    end, residue_late, core_late = lax.optimization_barrier((end, residue, core))
+    end, residue_late = lax.optimization_barrier((end, residue))
     at = jnp.stack([seq, y, xh * 2 + core, core]).astype(jnp.int32)
     weight = residue_late * jnp.sqrt(-jnp.expm1(-2.0 * rate))
     ends = lax.all_to_all(end, ("y", "xl"), 0, 0, tiled=True)
@@ -324,9 +324,6 @@
     f3 = lax.ppermute(f0, "y", [(i, (i - 1) % 4) for i in range(4)])
     ends, f1, f3, rest, f0_late = lax.optimization_barrier((ends, f1, f3, rest, f0))
     f2 = lax.ppermute(f0_late, "y", [(i, (i + 2) % 4) for i in range(4)])
-    w_other = other_core(
-        lax.dynamic_slice(out_weight, (0, (xh * 2 + 1 - core_late) * width), (channels, width))
-    )
     mixed = pl.pallas_call(
         mix_kernel,
         out_shape=jax.ShapeDtypeStruct((rows, channels), BF),
@@ -339,6 +336,10 @@
 
     a_far = lax.ppermute(mixed, "xh", [(0, 1), (1, 0)])
     a_other = other_core(mixed)
+    a_other, core_late = lax.optimization_barrier((a_other, core))
+    w_other = other_core(
+        lax.dynamic_slice(out_weight, (0, (xh * 2 + 1 - core_late) * width), (channels, width))
+    )
     def given(parts):
         return other_core(
             jnp.concatenate([lax.dynamic_slice(v, (0, (1 - core) * width), (v.shape[0], width)) for v in parts], axis=0)
@@ -371,7 +372,7 @@
         cost_estimate=pl.CostEstimate(flops=2 * 10**9, bytes_accessed=6 * 2**20, transcendentals=0),
         name="near",
     )(at, mixed, a_other, far(out_weight), w_other)
-    a_far, near = lax.optimization_barrier((a_far, near))
+    a_far, near, g2 = lax.optimization_barrier((a_far, near, g2))
     a_far_other = other_core(a_far)
     partial = pl.pallas_call(
         far_kernel,

time: 146 us -> 145 us (level)
    ppermute x1, waiting for transfers between devices: 0.01 us -> 9.64 us  [local(): f2 = lax.ppermute(f0_late, 'y', [(i, (i + 2) % 4) for i in range(4)])]
    ppermute x1, waiting for transfers between devices: 6.57 us -> 0.01 us  [local(): a_far = lax.ppermute(mixed, 'xh', [(0, 1), (1, 0)])]
    reduce_scatter x1, waiting for transfers between devices: 55.4 us -> 53 us  [local(): summed = lax.psum_scatter(partial, 'z', scatter_dimension=0, tiled=True)]
    ppermute x1, waiting for transfers between devices: 3.47 us -> 1.12 us  [local(): f3 = lax.ppermute(f0, 'y', [(i, (i - 1) % 4) for i in range(4)])]
    ppermute x1, waiting for transfers between devices: 0.01 us -> 1.79 us  [local(): rest = lax.ppermute(there(out_weight, 4 * size, tail), ('xl', 'xh'), mirror)]
  transfers between devices with their start and end apart: 17 -> 17, of which waited for: 7 -> 8; matrix products, arithmetic and copies ran while one was open for 3% -> 3% of each run, Pallas kernels for 11% -> 10%
where the time goes in v8:
time: 145 us
  waiting for transfers between devices  76.4 us (53%)
  starting transfers between devices  26.1 us (18%)
  Pallas kernels  23.3 us (16%)
  between operations  13.6 us (9%)
  local copies, waits for them, and re-layouts  5.37 us (4%)
    reduce_scatter x1, waiting for transfers between devices, local(): summed = lax.psum_scatter(partial, 'z', scatter_dimension=0, tiled=True)  53 us
    ppermute x1, waiting for transfers between devices, local(): f2 = lax.ppermute(f0_late, 'y', [(i, (i + 2) % 4) for i in range(4)])  9.64 us
    ppermute x3, waiting for transfers between devices, traded(): return lax.ppermute(summed[k * size:(k + 1) * size], ('xh', 'c'), pairs)  6.34 us
    pallas_call x1, Pallas kernels, local(): pl.pallas_call(far_kernel, out_shape=pltpu.HBM((rows, width), BF), grid_s...  5.48 us
    pallas_call x1, Pallas kernels, local(): pl.pallas_call(near_kernel, out_shape=jax.ShapeDtypeStruct((rows, width),...  5.16 us
    ppermute x5, starting transfers between devices, other_core(): return lax.ppermute(value, 'c', [(0, 1), (1, 0)])  5.1 us
    pallas_call x1, Pallas kernels, local(): pl.pallas_call(conv_kernel, out_shape=(pltpu.HBM((rows, channels), BF), p...  5.04 us
    pallas_call x1, Pallas kernels, local(): pl.pallas_call(state_kernel, out_shape=(pltpu.HBM((rows, channels), BF),...  4.68 us
  transfers between devices with their start and end apart: 17, of which 8 were waited for; matrix products, arithmetic and copies ran while one was open for 3% of the time, Pallas kernels for 10%

profile of v8, /device:TPU:1, one launch (start us, length us, event | category | flops | bytes accessed | tf_op | source)
XLA Modules:
  0.0 144.8 jit_solution(8378645876357162259)
XLA Ops:
  6.5 0.7 slice.15
  7.2 3.9 %collective-permute-start = (bf16[3,8,256]{2,1,0:T(8,128)(2,1)S(1)}, bf16[3,8,256]{2,1,0:T(8,128)(2,1)S(1)}, u32[]{:S(2)}, u32[]{:S(2)}) collective-permute-start(bf16[3,8,256]{2,1,0:T(8,128)(2,1)S(1)} %slice.15), channel_id=1, source_target_pairs={{0,32},{32,64},{64,96},{96,128},{128,160},{160,192},{192,224},{1,3... | collective-permute-start | bytes 36872 | tf_op jit(solution)/shard_map/ppermute | solution.py:251
  11.2 1.0 dynamic_slice.24
  12.2 2.9 %collective-permute-start.1 = (bf16[48,4096]{1,0:T(8,128)(2,1)S(1)}, bf16[48,4096]{1,0:T(8,128)(2,1)S(1)}, u32[]{:S(2)}, u32[]{:S(2)}) collective-permute-start(bf16[48,4096]{1,0:T(8,128)(2,1)S(1)} %dynamic_slice.24), channel_id=1, source_target_pairs={{0,34},{34,0},{2,32},{32,2},{1,35},{35,1},{3,33},{33,3},{4,38},{38... | collective-permute-start | bytes 1179656 | tf_op jit(solution)/shard_map/ppermute | solution.py:261
  15.1 1.1 constant_dynamic-slice_fusion.6
  16.2 0.1 collective-permute-start.4
  16.3 0.1 pad_add_fusion.at_ref
  16.4 0.0 collective-permute-done.halo_ref
  16.4 4.7 %state.1 = (bf16[1024,256]{1,0:T(8,128)(2,1)}, f32[8,16,256]{2,1,0:T(8,128)}, f32[16,256]{1,0:T(8,128)S(1)}) custom-call(bf16[3,1024,256]{2,1,0:T(8,128)(2,1)} %p_ref.1, bf16[3,1024,256]{2,1,0:T(8,128)(2,1)} %p_ref.1, bf16[3,8,256]{2,1,0:T(8,128)(2,1)S(1)} %collective-permute-done.halo_ref, f32[3,3,256]{2,1,0:T(4,128)} %sf_ref.3, f32[16,16]{1,0:T(8,128)} %rate_ref.3), custom_call_target="tpu_custom_call" | custom-call | flops 1000000 | bytes 65536 | tf_op jit(solution)/shard_map/state/pallas_call | solution.py:274
  21.1 4.0 %all-to-all-start = ((f32[8,16,256]{2,1,0:T(8,128)}), f32[8,16,256]{2,1,0:T(8,128)S(1)}, u32[]{:S(2)}, u32[]{:S(2)}) async-start(f32[8,16,256]{2,1,0:T(8,128)} %get-tuple-element.27), calls=%async_computation | async-start | bytes 262144 | tf_op jit(solution)/shard_map/all_to_all | solution.py:300
  25.1 0.0 reduce-scatter.2.cloned.1.call-start
  25.2 0.0 collective-permute-done.1.f0
  25.2 2.7 %collective-permute-start.3 = (bf16[48,4096]{1,0:T(8,128)(2,1)S(1)}, bf16[48,4096]{1,0:T(8,128)(2,1)S(1)}, u32[]{:S(2)}, u32[]{:S(2)}) collective-permute-start(bf16[48,4096]{1,0:T(8,128)(2,1)S(1)} %collective-permute-done.1.f0), channel_id=1, source_target_pairs={{0,192},{64,0},{128,64},{192,128},{1,193},{65,1},{129,65},{193,129... | collective-permute-start | bytes 1179656 | tf_op jit(solution)/shard_map/ppermute | solution.py:324
  27.9 0.0 collective-permute-start.2
  27.9 5.0 %conv.1 = (bf16[1024,256]{1,0:T(8,128)(2,1)}, bf16[1024,256]{1,0:T(8,128)(2,1)}, bf16[128,256]{1,0:T(8,128)(2,1)S(1)}) custom-call(bf16[3,1024,256]{2,1,0:T(8,128)(2,1)} %p_ref.1, bf16[1024,256]{1,0:T(8,128)(2,1)} %get-tuple-element.31.x_ref, bf16[3,8,256]{2,1,0:T(8,128)(2,1)S(1)} %collective-permute-done.halo_ref, f32[3,3,256]{2,1,0:T(4,128)} %sf_ref.3, ...), custom_call_target="tpu_custom_call" | custom-call | flops 6000000000 | bytes 65536 | tf_op jit(solution)/shard_map/conv/pallas_call | solution.py:301
  33.0 0.0 all-to-all-done.ends_ref
  33.0 1.8 %collective-permute-done.4.rest = bf16[64,4096]{1,0:T(8,128)(2,1)S(1)} collective-permute-done((bf16[64,4096]{1,0:T(8,128)(2,1)S(1)}, bf16[64,4096]{1,0:T(8,128)(2,1)S(1)}, u32[]{:S(2)}, u32[]{:S(2)}) %collective-permute-start.4) | collective-permute-done | bytes 524320 | tf_op jit(solution)/shard_map/ppermute | solution.py:262
  34.8 1.1 collective-permute-done.3.f3
  35.9 2.5 %collective-permute-done.2.f1 = bf16[48,4096]{1,0:T(8,128)(2,1)S(1)} collective-permute-done((bf16[48,4096]{1,0:T(8,128)(2,1)S(1)}, bf16[48,4096]{1,0:T(8,128)(2,1)S(1)}, u32[]{:S(2)}, u32[]{:S(2)}) %collective-permute-start.2) | collective-permute-done | bytes 393248 | tf_op jit(solution)/shard_map/ppermute | solution.py:323
  38.4 1.6 %mix.1.a0 = bf16[1024,256]{1,0:T(8,128)(2,1)S(1)} custom-call(s32[4]{0:T(128)S(1)} %pad_add_fusion.at_ref, f32[8,16,256]{2,1,0:T(8,128)S(1)} %all-to-all-done.ends_ref, f32[16,256]{1,0:T(8,128)S(1)} %get-tuple-element.30.rt_ref, bf16[128,256]{1,0:T(8,128)(2,1)S(1)} %get-tuple-element.33.din_ref, bf16[1024,256]{1,0:T(8,128)(2,1)} %get-tuple-element.34.y_ref, ...), custom_call_target="tpu_custom_call" | custom-call | flops 1000000 | bytes 65536 | tf_op jit(solution)/shard_map/mix/pallas_call | solution.py:327
  40.0 2.9 %collective-permute-start.6 = (bf16[1024,256]{1,0:T(8,128)(2,1)S(1)}, bf16[1024,256]{1,0:T(8,128)(2,1)}, u32[]{:S(2)}, u32[]{:S(2)}) collective-permute-start(bf16[1024,256]{1,0:T(8,128)(2,1)S(1)} %mix.1.a0), channel_id=1, source_target_pairs={{0,1},{1,0},{2,3},{3,2},{4,5},{5,4},{6,7},{7,6},{8,9},{9,8},{10,11... | collective-permute-start | bytes 1572872 | tf_op jit(solution)/shard_map/ppermute | solution.py:240
  42.9 3.5 %collective-permute-start.5 = (bf16[1024,256]{1,0:T(8,128)(2,1)S(1)}, bf16[1024,256]{1,0:T(8,128)(2,1)S(1)}, u32[]{:S(2)}, u32[]{:S(2)}) collective-permute-start(bf16[1024,256]{1,0:T(8,128)(2,1)S(1)} %mix.1.a0), channel_id=1, source_target_pairs={{0,2},{2,0},{1,3},{3,1},{4,6},{6,4},{5,7},{7,5},{8,10},{10,8},{9,1... | collective-permute-start | bytes 1572872 | tf_op jit(solution)/shard_map/ppermute | solution.py:337
  46.3 0.0 collective-permute-start.8
  46.3 0.0 collective-permute-done.6.a1
  46.3 1.3 constant_dynamic-slice_fusion.5
  47.7 0.4 collective-permute-start.7
  48.2 0.1 pad_maximum_fusion
  48.3 0.2 collective-permute-start.11
  48.5 9.6 %collective-permute-done.8.f2 = bf16[48,4096]{1,0:T(8,128)(2,1)S(1)} collective-permute-done((bf16[48,4096]{1,0:T(8,128)(2,1)S(1)}, bf16[48,4096]{1,0:T(8,128)(2,1)S(1)}, u32[]{:S(2)}, u32[]{:S(2)}) %collective-permute-start.8) | collective-permute-done | bytes 393248 | tf_op jit(solution)/shard_map/ppermute | solution.py:326
  58.2 1.3 collective-permute-start.9
  59.5 0.0 collective-permute-done.7.w1
  59.5 5.2 %near.1.near_ref = bf16[1024,2048]{1,0:T(8,128)(2,1)S(1)} custom-call(s32[4]{0:T(128)S(1)} %pad_add_fusion.at_ref, bf16[1024,256]{1,0:T(8,128)(2,1)S(1)} %mix.1.a0, bf16[1024,256]{1,0:T(8,128)(2,1)} %collective-permute-done.6.a1, bf16[256,8192]{1,0:T(8,128)(2,1)} %w0.1, bf16[256,2048]{1,0:T(8,128)(2,1)S(1)} %collective-permute-done.7.w1), custom_call_target="tpu_custom_call" | custom-call | flops 2000000000 | bytes 6291456 | tf_op jit(solution)/shard_map/near/pallas_call | solution.py:360
  64.6 0.0 collective-permute-done.5.a2
  64.6 0.0 collective-permute-done.9.g2
  64.7 0.3 collective-permute-start.10
  65.0 0.0 collective-permute-done.11.g013
  65.0 1.9 %collective-permute-done.10.a3 = bf16[1024,256]{1,0:T(8,128)(2,1)S(1)} collective-permute-done((bf16[1024,256]{1,0:T(8,128)(2,1)S(1)}, bf16[1024,256]{1,0:T(8,128)(2,1)S(1)}, u32[]{:S(2)}, u32[]{:S(2)}) %collective-permute-start.10) | collective-permute-done | bytes 524320 | tf_op jit(solution)/shard_map/ppermute | solution.py:240
  66.8 5.5 %far.1 = bf16[1024,2048]{1,0:T(8,128)(2,1)} custom-call(s32[4]{0:T(128)S(1)} %pad_add_fusion.at_ref, bf16[1024,256]{1,0:T(8,128)(2,1)S(1)} %collective-permute-done.5.a2, bf16[1024,256]{1,0:T(8,128)(2,1)S(1)} %collective-permute-done.10.a3, bf16[48,4096]{1,0:T(8,128)(2,1)S(1)} %collective-permute-done.1.f0, bf16[48,4096]{1,0:T(8,128)(2,1)S(1)} %collective-permute-done.2.f1, ...), custom_call_target="tpu_custom_call" | custom-call | flops 2000000000 | bytes 10485760 | tf_op jit(solution)/shard_map/far/pallas_call | solution.py:377
  72.3 0.0 reduce-scatter.2.cloned.1.call-update
  72.3 53.0 %reduce-scatter.2.cloned.1.call-done = bf16[128,2048]{1,0:T(8,128)(2,1)} async-done(((bf16[1024,2048]{1,0:T(8,128)(2,1)}), bf16[128,2048]{1,0:T(8,128)(2,1)}) %reduce-scatter.2.cloned.1.call-update) | async-done | bytes 524304 | tf_op jit(solution)/shard_map/reduce_scatter | solution.py:395
  125.3 1.1 fusion
  126.5 3.3 %collective-permute-start.14 = (bf16[32,2048]{1,0:T(8,128)(2,1)S(1)}, bf16[32,2048]{1,0:T(8,128)(2,1)S(1)}, u32[]{:S(2)}, u32[]{:S(2)}) collective-permute-start(bf16[32,2048]{1,0:T(8,128)(2,1)S(1)} %get-tuple-element.45), channel_id=1, source_target_pairs={{0,3},{1,2},{2,1},{3,0},{4,7},{5,6},{6,5},{7,4},{8,11},{9,10},{10,... | collective-permute-start | bytes 393224 | tf_op jit(solution)/shard_map/ppermute | solution.py:400
  129.8 0.3 collective-permute-start.13
  130.1 0.2 collective-permute-start.12
  130.3 3.8 %collective-permute-done.14.p3 = bf16[32,2048]{1,0:T(8,128)(2,1)S(1)} collective-permute-done((bf16[32,2048]{1,0:T(8,128)(2,1)S(1)}, bf16[32,2048]{1,0:T(8,128)(2,1)S(1)}, u32[]{:S(2)}, u32[]{:S(2)}) %collective-permute-start.14) | collective-permute-done | bytes 131104 | tf_op jit(solution)/shard_map/ppermute | solution.py:400
  134.1 2.6 %collective-permute-done.13.p2 = bf16[32,2048]{1,0:T(8,128)(2,1)S(1)} collective-permute-done((bf16[32,2048]{1,0:T(8,128)(2,1)S(1)}, bf16[32,2048]{1,0:T(8,128)(2,1)S(1)}, u32[]{:S(2)}, u32[]{:S(2)}) %collective-permute-start.13) | collective-permute-done | bytes 131104 | tf_op jit(solution)/shard_map/ppermute | solution.py:400
  136.6 0.0 collective-permute-done.12.p1
  136.6 1.4 join.1
  (9 shorter events, 0.1 us)
Async XLA Ops:
  7.2 9.2 %collective-permute-start = (bf16[3,8,256]{2,1,0:T(8,128)(2,1)S(1)}, bf16[3,8,256]{2,1,0:T(8,128)(2,1)S(1)}, u32[]{:S(2)}, u32[]{:S(2)}) collective-permute-start(bf16[3,8,256]{2,1,0:T(8,128)(2,1)S(1)} %slice.15), channel_id=1, source_target_pairs={{0,32},{32,64},{64,96},{96,128},{128,160},{160,192},{192,224},{1,3... | collective-permute-start | bytes 36872 | tf_op jit(solution)/shard_map/ppermute | solution.py:251
  12.2 13.0 %collective-permute-start.1 = (bf16[48,4096]{1,0:T(8,128)(2,1)S(1)}, bf16[48,4096]{1,0:T(8,128)(2,1)S(1)}, u32[]{:S(2)}, u32[]{:S(2)}) collective-permute-start(bf16[48,4096]{1,0:T(8,128)(2,1)S(1)} %dynamic_slice.24), channel_id=1, source_target_pairs={{0,34},{34,0},{2,32},{32,2},{1,35},{35,1},{3,33},{33,3},{4,38},{38... | collective-permute-start | bytes 1179656 | tf_op jit(solution)/shard_map/ppermute | solution.py:261
  16.2 18.5 %collective-permute-start.4 = (bf16[64,4096]{1,0:T(8,128)(2,1)S(1)}, bf16[64,4096]{1,0:T(8,128)(2,1)S(1)}, u32[]{:S(2)}, u32[]{:S(2)}) collective-permute-start(bf16[64,4096]{1,0:T(8,128)(2,1)S(1)} %constant_dynamic-slice_fusion.6), channel_id=1, source_target_pairs={{0,34},{34,0},{2,32},{32,2},{1,35},{35,1},{3,33},{33,3},{4,38},{38... | collective-permute-start | bytes 1572872 | tf_op jit(solution)/shard_map/ppermute | solution.py:262
  16.4 8.8 %copy-start = (f32[16,16]{1,0:T(8,128)S(1)}, f32[16,16]{1,0:T(8,128)}, u32[]{:S(2)}) copy-start(f32[16,16]{1,0:T(8,128)} %rate_ref.3) | copy-start | bytes 3076
  16.4 8.8 %copy-start.1 = (f32[16,16]{1,0:T(8,128)S(1)}, f32[16,16]{1,0:T(8,128)}, u32[]{:S(2)}) copy-start(f32[16,16]{1,0:T(8,128)} %param.7) | copy-start | bytes 3076
  21.1 11.9 %all-to-all-start = ((f32[8,16,256]{2,1,0:T(8,128)}), f32[8,16,256]{2,1,0:T(8,128)S(1)}, u32[]{:S(2)}, u32[]{:S(2)}) async-start(f32[8,16,256]{2,1,0:T(8,128)} %get-tuple-element.27), calls=%async_computation | async-start | bytes 262144 | tf_op jit(solution)/shard_map/all_to_all | solution.py:300
  25.1 100.2 %reduce-scatter.2.cloned.1.call-start = ((), (), s32[]{:S(2)}) async-start(), calls=%async_computation.2 | async-start | bytes 4718592 | tf_op jit(solution)/shard_map/reduce_scatter | solution.py:395
  25.2 10.7 %collective-permute-start.3 = (bf16[48,4096]{1,0:T(8,128)(2,1)S(1)}, bf16[48,4096]{1,0:T(8,128)(2,1)S(1)}, u32[]{:S(2)}, u32[]{:S(2)}) collective-permute-start(bf16[48,4096]{1,0:T(8,128)(2,1)S(1)} %collective-permute-done.1.f0), channel_id=1, source_target_pairs={{0,192},{64,0},{128,64},{192,128},{1,193},{65,1},{129,65},{193,129... | collective-permute-start | bytes 1179656 | tf_op jit(solution)/shard_map/ppermute | solution.py:324
  27.9 10.5 %collective-permute-start.2 = (bf16[48,4096]{1,0:T(8,128)(2,1)S(1)}, bf16[48,4096]{1,0:T(8,128)(2,1)S(1)}, u32[]{:S(2)}, u32[]{:S(2)}) collective-permute-start(bf16[48,4096]{1,0:T(8,128)(2,1)S(1)} %collective-permute-done.1.f0), channel_id=1, source_target_pairs={{0,64},{64,128},{128,192},{192,0},{1,65},{65,129},{129,193},{193,1... | collective-permute-start | bytes 1179656 | tf_op jit(solution)/shard_map/ppermute | solution.py:323
  40.0 6.3 %collective-permute-start.6 = (bf16[1024,256]{1,0:T(8,128)(2,1)S(1)}, bf16[1024,256]{1,0:T(8,128)(2,1)}, u32[]{:S(2)}, u32[]{:S(2)}) collective-permute-start(bf16[1024,256]{1,0:T(8,128)(2,1)S(1)} %mix.1.a0), channel_id=1, source_target_pairs={{0,1},{1,0},{2,3},{3,2},{4,5},{5,4},{6,7},{7,6},{8,9},{9,8},{10,11... | collective-permute-start | bytes 1572872 | tf_op jit(solution)/shard_map/ppermute | solution.py:240
  42.9 21.8 %collective-permute-start.5 = (bf16[1024,256]{1,0:T(8,128)(2,1)S(1)}, bf16[1024,256]{1,0:T(8,128)(2,1)S(1)}, u32[]{:S(2)}, u32[]{:S(2)}) collective-permute-start(bf16[1024,256]{1,0:T(8,128)(2,1)S(1)} %mix.1.a0), channel_id=1, source_target_pairs={{0,2},{2,0},{1,3},{3,1},{4,6},{6,4},{5,7},{7,5},{8,10},{10,8},{9,1... | collective-permute-start | bytes 1572872 | tf_op jit(solution)/shard_map/ppermute | solution.py:337
  46.3 11.8 %collective-permute-start.8 = (bf16[48,4096]{1,0:T(8,128)(2,1)S(1)}, bf16[48,4096]{1,0:T(8,128)(2,1)S(1)}, u32[]{:S(2)}, u32[]{:S(2)}) collective-permute-start(bf16[48,4096]{1,0:T(8,128)(2,1)S(1)} %collective-permute-done.1.f0), channel_id=1, source_target_pairs={{0,128},{64,192},{128,0},{192,64},{1,129},{65,193},{129,1},{193,65... | collective-permute-start | bytes 1179656 | tf_op jit(solution)/shard_map/ppermute | solution.py:326
  47.7 11.8 %collective-permute-start.7 = (bf16[256,2048]{1,0:T(8,128)(2,1)S(1)}, bf16[256,2048]{1,0:T(8,128)(2,1)S(1)}, u32[]{:S(2)}, u32[]{:S(2)}) collective-permute-start(bf16[256,2048]{1,0:T(8,128)(2,1)S(1)} %constant_dynamic-slice_fusion.5), channel_id=1, source_target_pairs={{0,1},{1,0},{2,3},{3,2},{4,5},{5,4},{6,7},{7,6},{8,9},{9,8},{10,11... | collective-permute-start | bytes 3145736 | tf_op jit(solution)/shard_map/ppermute | solution.py:240
  48.3 16.7 %collective-permute-start.11 = (bf16[208,2048]{1,0:T(8,128)(2,1)S(1)}, bf16[208,2048]{1,0:T(8,128)(2,1)S(1)}, u32[]{:S(2)}, u32[]{:S(2)}) collective-permute-start(bf16[208,2048]{1,0:T(8,128)(2,1)S(1)} %pad_maximum_fusion), channel_id=1, source_target_pairs={{0,1},{1,0},{2,3},{3,2},{4,5},{5,4},{6,7},{7,6},{8,9},{9,8},{10,11... | collective-permute-start | bytes 2555912 | tf_op jit(solution)/shard_map/ppermute | solution.py:240
  58.2 6.5 %collective-permute-start.9 = (bf16[48,2048]{1,0:T(8,128)(2,1)S(1)}, bf16[48,2048]{1,0:T(8,128)(2,1)S(1)}, u32[]{:S(2)}, u32[]{:S(2)}) collective-permute-start(bf16[48,2048]{1,0:T(8,128)(2,1)S(1)} %constant_dynamic-slice_fusion.4), channel_id=1, source_target_pairs={{0,1},{1,0},{2,3},{3,2},{4,5},{5,4},{6,7},{7,6},{8,9},{9,8},{10,11... | collective-permute-start | bytes 589832 | tf_op jit(solution)/shard_map/ppermute | solution.py:240
  64.7 2.2 %collective-permute-start.10 = (bf16[1024,256]{1,0:T(8,128)(2,1)S(1)}, bf16[1024,256]{1,0:T(8,128)(2,1)S(1)}, u32[]{:S(2)}, u32[]{:S(2)}) collective-permute-start(bf16[1024,256]{1,0:T(8,128)(2,1)S(1)} %collective-permute-done.5.a2), channel_id=1, source_target_pairs={{0,1},{1,0},{2,3},{3,2},{4,5},{5,4},{6,7},{7,6},{8,9},{9,8},{10,11... | collective-permute-start | bytes 1572872 | tf_op jit(solution)/shard_map/ppermute | solution.py:240
  126.5 7.6 %collective-permute-start.14 = (bf16[32,2048]{1,0:T(8,128)(2,1)S(1)}, bf16[32,2048]{1,0:T(8,128)(2,1)S(1)}, u32[]{:S(2)}, u32[]{:S(2)}) collective-permute-start(bf16[32,2048]{1,0:T(8,128)(2,1)S(1)} %get-tuple-element.45), channel_id=1, source_target_pairs={{0,3},{1,2},{2,1},{3,0},{4,7},{5,6},{6,5},{7,4},{8,11},{9,10},{10,... | collective-permute-start | bytes 393224 | tf_op jit(solution)/shard_map/ppermute | solution.py:400
  129.8 6.8 %collective-permute-start.13 = (bf16[32,2048]{1,0:T(8,128)(2,1)S(1)}, bf16[32,2048]{1,0:T(8,128)(2,1)S(1)}, u32[]{:S(2)}, u32[]{:S(2)}) collective-permute-start(bf16[32,2048]{1,0:T(8,128)(2,1)S(1)} %get-tuple-element.46), channel_id=1, source_target_pairs={{0,2},{1,3},{2,0},{3,1},{4,6},{5,7},{6,4},{7,5},{8,10},{9,11},{10,... | collective-permute-start | bytes 393224 | tf_op jit(solution)/shard_map/ppermute | solution.py:400
  130.1 6.6 %collective-permute-start.12 = (bf16[32,2048]{1,0:T(8,128)(2,1)S(1)}, bf16[32,2048]{1,0:T(8,128)(2,1)S(1)}, u32[]{:S(2)}, u32[]{:S(2)}) collective-permute-start(bf16[32,2048]{1,0:T(8,128)(2,1)S(1)} %get-tuple-element.47), channel_id=1, source_target_pairs={{0,1},{1,0},{2,3},{3,2},{4,5},{5,4},{6,7},{7,6},{8,9},{9,8},{10,11... | collective-permute-start | bytes 393224 | tf_op jit(solution)/shard_map/ppermute | solution.py:400
Sparse Core Ops, SparseCore 0:
  72.5 52.8 reduce-scatter.1

commit v9 on v8

--- a/solution.py
+++ b/solution.py
@@ -345,7 +345,7 @@
             jnp.concatenate([lax.dynamic_slice(v, (0, (1 - core) * width), (v.shape[0], width)) for v in parts], axis=0)
         )
 
-    g013, g2 = given((f0_late, f1, f3, rest)), given((f2,))
+    g013 = given((f0_late, f1, f3, rest))
 
     tile = 512
     strips = width // tile
@@ -372,7 +372,8 @@
         cost_estimate=pl.CostEstimate(flops=2 * 10**9, bytes_accessed=6 * 2**20, transcendentals=0),
         name="near",
     )(at, mixed, a_other, far(out_weight), w_other)
-    a_far, near, g2 = lax.optimization_barrier((a_far, near, g2))
+    a_far, near, f2 = lax.optimization_barrier((a_far, near, f2))
+    g2 = given((f2,))
     a_far_other = other_core(a_far)
     partial = pl.pallas_call(
         far_kernel,

time: 145 us -> 142 us (0.979)
  waiting for transfers between devices: 76.4 us -> 73.7 us
    ppermute x1, waiting for transfers between devices: 9.64 us -> 2.59 us  [local(): f2 = lax.ppermute(f0_late, 'y', [(i, (i + 2) % 4) for i in range(4)])]
    reduce_scatter x1, waiting for transfers between devices: 53 us -> 55.6 us  [local(): summed = lax.psum_scatter(partial, 'z', scatter_dimension=0, tiled=True)]
    ppermute x5, waiting for transfers between devices: 1.89 us -> 3.4 us  [other_core(): return lax.ppermute(value, 'c', [(0, 1), (1, 0)])]
  transfers between devices with their start and end apart: 17 -> 17, of which waited for: 8 -> 10; matrix products, arithmetic and copies ran while one was open for 3% -> 3% of each run, Pallas kernels for 10% -> 10%
where the time goes in v9:
time: 142 us
  waiting for transfers between devices  73.7 us (52%)
  starting transfers between devices  25.7 us (18%)
  Pallas kernels  23.3 us (16%)
  between operations  13.6 us (10%)
  local copies, waits for them, and re-layouts  5.37 us (4%)
    reduce_scatter x1, waiting for transfers between devices, local(): summed = lax.psum_scatter(partial, 'z', scatter_dimension=0, tiled=True)  55.6 us
    ppermute x3, waiting for transfers between devices, traded(): return lax.ppermute(summed[k * size:(k + 1) * size], ('xh', 'c'), pairs)  6.31 us
    pallas_call x1, Pallas kernels, local(): pl.pallas_call(far_kernel, out_shape=pltpu.HBM((rows, width), BF), grid_s...  5.48 us
    pallas_call x1, Pallas kernels, local(): pl.pallas_call(near_kernel, out_shape=jax.ShapeDtypeStruct((rows, width),...  5.16 us
    pallas_call x1, Pallas kernels, local(): pl.pallas_call(conv_kernel, out_shape=(pltpu.HBM((rows, channels), BF), p...  5.04 us
    ppermute x5, starting transfers between devices, other_core(): return lax.ppermute(value, 'c', [(0, 1), (1, 0)])  4.69 us
    pallas_call x1, Pallas kernels, local(): pl.pallas_call(state_kernel, out_shape=(pltpu.HBM((rows, channels), BF),...  4.68 us
    all_to_all x1, starting transfers between devices, local(): ends = lax.all_to_all(end, ('y', 'xl'), 0, 0, tiled=True)  4.02 us
  transfers between devices with their start and end apart: 17, of which 10 were waited for; matrix products, arithmetic and copies ran while one was open for 3% of the time, Pallas kernels for 10%

profile of v9, /device:TPU:1, one launch (start us, length us, event | category | flops | bytes accessed | tf_op | source)
XLA Modules:
  0.0 141.8 jit_solution(349779983439509915)
XLA Ops:
  6.5 0.7 slice.15
  7.2 3.9 %collective-permute-start = (bf16[3,8,256]{2,1,0:T(8,128)(2,1)S(1)}, bf16[3,8,256]{2,1,0:T(8,128)(2,1)S(1)}, u32[]{:S(2)}, u32[]{:S(2)}) collective-permute-start(bf16[3,8,256]{2,1,0:T(8,128)(2,1)S(1)} %slice.15), channel_id=1, source_target_pairs={{0,32},{32,64},{64,96},{96,128},{128,160},{160,192},{192,224},{1,3... | collective-permute-start | bytes 36872 | tf_op jit(solution)/shard_map/ppermute | solution.py:251
  11.2 1.0 dynamic_slice.24
  12.2 2.9 %collective-permute-start.1 = (bf16[48,4096]{1,0:T(8,128)(2,1)S(1)}, bf16[48,4096]{1,0:T(8,128)(2,1)S(1)}, u32[]{:S(2)}, u32[]{:S(2)}) collective-permute-start(bf16[48,4096]{1,0:T(8,128)(2,1)S(1)} %dynamic_slice.24), channel_id=1, source_target_pairs={{0,34},{34,0},{2,32},{32,2},{1,35},{35,1},{3,33},{33,3},{4,38},{38... | collective-permute-start | bytes 1179656 | tf_op jit(solution)/shard_map/ppermute | solution.py:261
  15.1 1.1 constant_dynamic-slice_fusion.6
  16.2 0.1 collective-permute-start.4
  16.3 0.1 pad_add_fusion.at_ref
  16.4 0.0 collective-permute-done.halo_ref
  16.4 4.7 %state.1 = (bf16[1024,256]{1,0:T(8,128)(2,1)}, f32[8,16,256]{2,1,0:T(8,128)}, f32[16,256]{1,0:T(8,128)S(1)}) custom-call(bf16[3,1024,256]{2,1,0:T(8,128)(2,1)} %p_ref.1, bf16[3,1024,256]{2,1,0:T(8,128)(2,1)} %p_ref.1, bf16[3,8,256]{2,1,0:T(8,128)(2,1)S(1)} %collective-permute-done.halo_ref, f32[3,3,256]{2,1,0:T(4,128)} %sf_ref.3, f32[16,16]{1,0:T(8,128)} %rate_ref.3), custom_call_target="tpu_custom_call" | custom-call | flops 1000000 | bytes 65536 | tf_op jit(solution)/shard_map/state/pallas_call | solution.py:274
  21.1 4.0 %all-to-all-start = ((f32[8,16,256]{2,1,0:T(8,128)}), f32[8,16,256]{2,1,0:T(8,128)S(1)}, u32[]{:S(2)}, u32[]{:S(2)}) async-start(f32[8,16,256]{2,1,0:T(8,128)} %get-tuple-element.27), calls=%async_computation | async-start | bytes 262144 | tf_op jit(solution)/shard_map/all_to_all | solution.py:300
  25.1 0.0 reduce-scatter.2.cloned.1.call-start
  25.2 0.0 collective-permute-done.1.f0
  25.2 2.7 %collective-permute-start.3 = (bf16[48,4096]{1,0:T(8,128)(2,1)S(1)}, bf16[48,4096]{1,0:T(8,128)(2,1)S(1)}, u32[]{:S(2)}, u32[]{:S(2)}) collective-permute-start(bf16[48,4096]{1,0:T(8,128)(2,1)S(1)} %collective-permute-done.1.f0), channel_id=1, source_target_pairs={{0,192},{64,0},{128,64},{192,128},{1,193},{65,1},{129,65},{193,129... | collective-permute-start | bytes 1179656 | tf_op jit(solution)/shard_map/ppermute | solution.py:324
  27.9 0.0 collective-permute-start.2
  27.9 5.0 %conv.1 = (bf16[1024,256]{1,0:T(8,128)(2,1)}, bf16[1024,256]{1,0:T(8,128)(2,1)}, bf16[128,256]{1,0:T(8,128)(2,1)S(1)}) custom-call(bf16[3,1024,256]{2,1,0:T(8,128)(2,1)} %p_ref.1, bf16[1024,256]{1,0:T(8,128)(2,1)} %get-tuple-element.31.x_ref, bf16[3,8,256]{2,1,0:T(8,128)(2,1)S(1)} %collective-permute-done.halo_ref, f32[3,3,256]{2,1,0:T(4,128)} %sf_ref.3, ...), custom_call_target="tpu_custom_call" | custom-call | flops 6000000000 | bytes 65536 | tf_op jit(solution)/shard_map/conv/pallas_call | solution.py:301
  33.0 0.0 all-to-all-done.ends_ref
  33.0 1.8 %collective-permute-done.4.rest = bf16[64,4096]{1,0:T(8,128)(2,1)S(1)} collective-permute-done((bf16[64,4096]{1,0:T(8,128)(2,1)S(1)}, bf16[64,4096]{1,0:T(8,128)(2,1)S(1)}, u32[]{:S(2)}, u32[]{:S(2)}) %collective-permute-start.4) | collective-permute-done | bytes 524320 | tf_op jit(solution)/shard_map/ppermute | solution.py:262
  34.8 1.1 collective-permute-done.3.f3
  35.9 2.5 %collective-permute-done.2.f1 = bf16[48,4096]{1,0:T(8,128)(2,1)S(1)} collective-permute-done((bf16[48,4096]{1,0:T(8,128)(2,1)S(1)}, bf16[48,4096]{1,0:T(8,128)(2,1)S(1)}, u32[]{:S(2)}, u32[]{:S(2)}) %collective-permute-start.2) | collective-permute-done | bytes 393248 | tf_op jit(solution)/shard_map/ppermute | solution.py:323
  38.4 1.6 %mix.1.a0 = bf16[1024,256]{1,0:T(8,128)(2,1)S(1)} custom-call(s32[4]{0:T(128)S(1)} %pad_add_fusion.at_ref, f32[8,16,256]{2,1,0:T(8,128)S(1)} %all-to-all-done.ends_ref, f32[16,256]{1,0:T(8,128)S(1)} %get-tuple-element.30.rt_ref, bf16[128,256]{1,0:T(8,128)(2,1)S(1)} %get-tuple-element.33.din_ref, bf16[1024,256]{1,0:T(8,128)(2,1)} %get-tuple-element.34.y_ref, ...), custom_call_target="tpu_custom_call" | custom-call | flops 1000000 | bytes 65536 | tf_op jit(solution)/shard_map/mix/pallas_call | solution.py:327
  40.0 2.9 %collective-permute-start.6 = (bf16[1024,256]{1,0:T(8,128)(2,1)S(1)}, bf16[1024,256]{1,0:T(8,128)(2,1)}, u32[]{:S(2)}, u32[]{:S(2)}) collective-permute-start(bf16[1024,256]{1,0:T(8,128)(2,1)S(1)} %mix.1.a0), channel_id=1, source_target_pairs={{0,1},{1,0},{2,3},{3,2},{4,5},{5,4},{6,7},{7,6},{8,9},{9,8},{10,11... | collective-permute-start | bytes 1572872 | tf_op jit(solution)/shard_map/ppermute | solution.py:240
  42.9 3.5 %collective-permute-start.5 = (bf16[1024,256]{1,0:T(8,128)(2,1)S(1)}, bf16[1024,256]{1,0:T(8,128)(2,1)S(1)}, u32[]{:S(2)}, u32[]{:S(2)}) collective-permute-start(bf16[1024,256]{1,0:T(8,128)(2,1)S(1)} %mix.1.a0), channel_id=1, source_target_pairs={{0,2},{2,0},{1,3},{3,1},{4,6},{6,4},{5,7},{7,5},{8,10},{10,8},{9,1... | collective-permute-start | bytes 1572872 | tf_op jit(solution)/shard_map/ppermute | solution.py:337
  46.3 0.0 collective-permute-start.8
  46.3 0.0 collective-permute-done.6.a1
  46.3 1.3 constant_dynamic-slice_fusion.5
  47.7 0.4 collective-permute-start.7
  48.2 0.1 pad_maximum_fusion
  48.3 0.2 collective-permute-start.10
  48.5 1.9 %collective-permute-done.7.w1 = bf16[256,2048]{1,0:T(8,128)(2,1)S(1)} collective-permute-done((bf16[256,2048]{1,0:T(8,128)(2,1)S(1)}, bf16[256,2048]{1,0:T(8,128)(2,1)S(1)}, u32[]{:S(2)}, u32[]{:S(2)}) %collective-permute-start.7) | collective-permute-done | bytes 1048608 | tf_op jit(solution)/shard_map/ppermute | solution.py:240
  50.4 5.2 %near.1.near_ref = bf16[1024,2048]{1,0:T(8,128)(2,1)S(1)} custom-call(s32[4]{0:T(128)S(1)} %pad_add_fusion.at_ref, bf16[1024,256]{1,0:T(8,128)(2,1)S(1)} %mix.1.a0, bf16[1024,256]{1,0:T(8,128)(2,1)} %collective-permute-done.6.a1, bf16[256,8192]{1,0:T(8,128)(2,1)} %w0.1, bf16[256,2048]{1,0:T(8,128)(2,1)S(1)} %collective-permute-done.7.w1), custom_call_target="tpu_custom_call" | custom-call | flops 2000000000 | bytes 6291456 | tf_op jit(solution)/shard_map/near/pallas_call | solution.py:360
  55.6 2.6 %collective-permute-done.8.f2 = bf16[48,4096]{1,0:T(8,128)(2,1)S(1)} collective-permute-done((bf16[48,4096]{1,0:T(8,128)(2,1)S(1)}, bf16[48,4096]{1,0:T(8,128)(2,1)S(1)}, u32[]{:S(2)}, u32[]{:S(2)}) %collective-permute-start.8) | collective-permute-done | bytes 393248 | tf_op jit(solution)/shard_map/ppermute | solution.py:326
  58.2 0.3 collective-permute-done.5.a2
  58.5 0.9 collective-permute-start.9
  59.4 0.3 collective-permute-start.11
  59.7 0.0 collective-permute-done.10.g013
  59.7 1.5 %collective-permute-done.11.g2 = bf16[48,2048]{1,0:T(8,128)(2,1)S(1)} collective-permute-done((bf16[48,2048]{1,0:T(8,128)(2,1)S(1)}, bf16[48,2048]{1,0:T(8,128)(2,1)S(1)}, u32[]{:S(2)}, u32[]{:S(2)}) %collective-permute-start.11) | collective-permute-done | bytes 196640 | tf_op jit(solution)/shard_map/ppermute | solution.py:240
  61.2 0.0 collective-permute-done.9.a3
  61.2 5.5 %far.1 = bf16[1024,2048]{1,0:T(8,128)(2,1)} custom-call(s32[4]{0:T(128)S(1)} %pad_add_fusion.at_ref, bf16[1024,256]{1,0:T(8,128)(2,1)S(1)} %collective-permute-done.5.a2, bf16[1024,256]{1,0:T(8,128)(2,1)S(1)} %collective-permute-done.9.a3, bf16[48,4096]{1,0:T(8,128)(2,1)S(1)} %collective-permute-done.1.f0, bf16[48,4096]{1,0:T(8,128)(2,1)S(1)} %collective-permute-done.2.f1, ...), custom_call_target="tpu_custom_call" | custom-call | flops 2000000000 | bytes 10485760 | tf_op jit(solution)/shard_map/far/pallas_call | solution.py:378
  66.7 0.0 reduce-scatter.2.cloned.1.call-update
  66.7 55.6 %reduce-scatter.2.cloned.1.call-done = bf16[128,2048]{1,0:T(8,128)(2,1)} async-done(((bf16[1024,2048]{1,0:T(8,128)(2,1)}), bf16[128,2048]{1,0:T(8,128)(2,1)}) %reduce-scatter.2.cloned.1.call-update) | async-done | bytes 524304 | tf_op jit(solution)/shard_map/reduce_scatter | solution.py:396
  122.3 1.1 fusion
  123.4 3.3 %collective-permute-start.14 = (bf16[32,2048]{1,0:T(8,128)(2,1)S(1)}, bf16[32,2048]{1,0:T(8,128)(2,1)S(1)}, u32[]{:S(2)}, u32[]{:S(2)}) collective-permute-start(bf16[32,2048]{1,0:T(8,128)(2,1)S(1)} %get-tuple-element.45), channel_id=1, source_target_pairs={{0,3},{1,2},{2,1},{3,0},{4,7},{5,6},{6,5},{7,4},{8,11},{9,10},{10,... | collective-permute-start | bytes 393224 | tf_op jit(solution)/shard_map/ppermute | solution.py:401
  126.7 0.3 collective-permute-start.13
  127.0 0.2 collective-permute-start.12
  127.2 3.8 %collective-permute-done.14.p3 = bf16[32,2048]{1,0:T(8,128)(2,1)S(1)} collective-permute-done((bf16[32,2048]{1,0:T(8,128)(2,1)S(1)}, bf16[32,2048]{1,0:T(8,128)(2,1)S(1)}, u32[]{:S(2)}, u32[]{:S(2)}) %collective-permute-start.14) | collective-permute-done | bytes 131104 | tf_op jit(solution)/shard_map/ppermute | solution.py:401
  131.0 2.5 %collective-permute-done.13.p2 = bf16[32,2048]{1,0:T(8,128)(2,1)S(1)} collective-permute-done((bf16[32,2048]{1,0:T(8,128)(2,1)S(1)}, bf16[32,2048]{1,0:T(8,128)(2,1)S(1)}, u32[]{:S(2)}, u32[]{:S(2)}) %collective-permute-start.13) | collective-permute-done | bytes 131104 | tf_op jit(solution)/shard_map/ppermute | solution.py:401
  133.5 0.0 collective-permute-done.12.p1
  133.5 1.4 join.1
  (9 shorter events, 0.1 us)
Async XLA Ops:
  7.2 9.2 %collective-permute-start = (bf16[3,8,256]{2,1,0:T(8,128)(2,1)S(1)}, bf16[3,8,256]{2,1,0:T(8,128)(2,1)S(1)}, u32[]{:S(2)}, u32[]{:S(2)}) collective-permute-start(bf16[3,8,256]{2,1,0:T(8,128)(2,1)S(1)} %slice.15), channel_id=1, source_target_pairs={{0,32},{32,64},{64,96},{96,128},{128,160},{160,192},{192,224},{1,3... | collective-permute-start | bytes 36872 | tf_op jit(solution)/shard_map/ppermute | solution.py:251
  12.2 13.0 %collective-permute-start.1 = (bf16[48,4096]{1,0:T(8,128)(2,1)S(1)}, bf16[48,4096]{1,0:T(8,128)(2,1)S(1)}, u32[]{:S(2)}, u32[]{:S(2)}) collective-permute-start(bf16[48,4096]{1,0:T(8,128)(2,1)S(1)} %dynamic_slice.24), channel_id=1, source_target_pairs={{0,34},{34,0},{2,32},{32,2},{1,35},{35,1},{3,33},{33,3},{4,38},{38... | collective-permute-start | bytes 1179656 | tf_op jit(solution)/shard_map/ppermute | solution.py:261
  16.2 18.5 %collective-permute-start.4 = (bf16[64,4096]{1,0:T(8,128)(2,1)S(1)}, bf16[64,4096]{1,0:T(8,128)(2,1)S(1)}, u32[]{:S(2)}, u32[]{:S(2)}) collective-permute-start(bf16[64,4096]{1,0:T(8,128)(2,1)S(1)} %constant_dynamic-slice_fusion.6), channel_id=1, source_target_pairs={{0,34},{34,0},{2,32},{32,2},{1,35},{35,1},{3,33},{33,3},{4,38},{38... | collective-permute-start | bytes 1572872 | tf_op jit(solution)/shard_map/ppermute | solution.py:262
  16.4 8.8 %copy-start = (f32[16,16]{1,0:T(8,128)S(1)}, f32[16,16]{1,0:T(8,128)}, u32[]{:S(2)}) copy-start(f32[16,16]{1,0:T(8,128)} %rate_ref.3) | copy-start | bytes 3076
  16.4 8.8 %copy-start.1 = (f32[16,16]{1,0:T(8,128)S(1)}, f32[16,16]{1,0:T(8,128)}, u32[]{:S(2)}) copy-start(f32[16,16]{1,0:T(8,128)} %param.7) | copy-start | bytes 3076
  21.1 11.9 %all-to-all-start = ((f32[8,16,256]{2,1,0:T(8,128)}), f32[8,16,256]{2,1,0:T(8,128)S(1)}, u32[]{:S(2)}, u32[]{:S(2)}) async-start(f32[8,16,256]{2,1,0:T(8,128)} %get-tuple-element.27), calls=%async_computation | async-start | bytes 262144 | tf_op jit(solution)/shard_map/all_to_all | solution.py:300
  25.1 97.2 %reduce-scatter.2.cloned.1.call-start = ((), (), s32[]{:S(2)}) async-start(), calls=%async_computation.2 | async-start | bytes 4718592 | tf_op jit(solution)/shard_map/reduce_scatter | solution.py:396
  25.2 10.7 %collective-permute-start.3 = (bf16[48,4096]{1,0:T(8,128)(2,1)S(1)}, bf16[48,4096]{1,0:T(8,128)(2,1)S(1)}, u32[]{:S(2)}, u32[]{:S(2)}) collective-permute-start(bf16[48,4096]{1,0:T(8,128)(2,1)S(1)} %collective-permute-done.1.f0), channel_id=1, source_target_pairs={{0,192},{64,0},{128,64},{192,128},{1,193},{65,1},{129,65},{193,129... | collective-permute-start | bytes 1179656 | tf_op jit(solution)/shard_map/ppermute | solution.py:324
  27.9 10.5 %collective-permute-start.2 = (bf16[48,4096]{1,0:T(8,128)(2,1)S(1)}, bf16[48,4096]{1,0:T(8,128)(2,1)S(1)}, u32[]{:S(2)}, u32[]{:S(2)}) collective-permute-start(bf16[48,4096]{1,0:T(8,128)(2,1)S(1)} %collective-permute-done.1.f0), channel_id=1, source_target_pairs={{0,64},{64,128},{128,192},{192,0},{1,65},{65,129},{129,193},{193,1... | collective-permute-start | bytes 1179656 | tf_op jit(solution)/shard_map/ppermute | solution.py:323
  40.0 6.3 %collective-permute-start.6 = (bf16[1024,256]{1,0:T(8,128)(2,1)S(1)}, bf16[1024,256]{1,0:T(8,128)(2,1)}, u32[]{:S(2)}, u32[]{:S(2)}) collective-permute-start(bf16[1024,256]{1,0:T(8,128)(2,1)S(1)} %mix.1.a0), channel_id=1, source_target_pairs={{0,1},{1,0},{2,3},{3,2},{4,5},{5,4},{6,7},{7,6},{8,9},{9,8},{10,11... | collective-permute-start | bytes 1572872 | tf_op jit(solution)/shard_map/ppermute | solution.py:240
  42.9 15.6 %collective-permute-start.5 = (bf16[1024,256]{1,0:T(8,128)(2,1)S(1)}, bf16[1024,256]{1,0:T(8,128)(2,1)S(1)}, u32[]{:S(2)}, u32[]{:S(2)}) collective-permute-start(bf16[1024,256]{1,0:T(8,128)(2,1)S(1)} %mix.1.a0), channel_id=1, source_target_pairs={{0,2},{2,0},{1,3},{3,1},{4,6},{6,4},{5,7},{7,5},{8,10},{10,8},{9,1... | collective-permute-start | bytes 1572872 | tf_op jit(solution)/shard_map/ppermute | solution.py:337
  46.3 11.8 %collective-permute-start.8 = (bf16[48,4096]{1,0:T(8,128)(2,1)S(1)}, bf16[48,4096]{1,0:T(8,128)(2,1)S(1)}, u32[]{:S(2)}, u32[]{:S(2)}) collective-permute-start(bf16[48,4096]{1,0:T(8,128)(2,1)S(1)} %collective-permute-done.1.f0), channel_id=1, source_target_pairs={{0,128},{64,192},{128,0},{192,64},{1,129},{65,193},{129,1},{193,65... | collective-permute-start | bytes 1179656 | tf_op jit(solution)/shard_map/ppermute | solution.py:326
  47.7 2.7 %collective-permute-start.7 = (bf16[256,2048]{1,0:T(8,128)(2,1)S(1)}, bf16[256,2048]{1,0:T(8,128)(2,1)S(1)}, u32[]{:S(2)}, u32[]{:S(2)}) collective-permute-start(bf16[256,2048]{1,0:T(8,128)(2,1)S(1)} %constant_dynamic-slice_fusion.5), channel_id=1, source_target_pairs={{0,1},{1,0},{2,3},{3,2},{4,5},{5,4},{6,7},{7,6},{8,9},{9,8},{10,11... | collective-permute-start | bytes 3145736 | tf_op jit(solution)/shard_map/ppermute | solution.py:240
  48.3 11.4 %collective-permute-start.10 = (bf16[208,2048]{1,0:T(8,128)(2,1)S(1)}, bf16[208,2048]{1,0:T(8,128)(2,1)S(1)}, u32[]{:S(2)}, u32[]{:S(2)}) collective-permute-start(bf16[208,2048]{1,0:T(8,128)(2,1)S(1)} %pad_maximum_fusion), channel_id=1, source_target_pairs={{0,1},{1,0},{2,3},{3,2},{4,5},{5,4},{6,7},{7,6},{8,9},{9,8},{10,11... | collective-permute-start | bytes 2555912 | tf_op jit(solution)/shard_map/ppermute | solution.py:240
  58.5 2.7 %collective-permute-start.9 = (bf16[1024,256]{1,0:T(8,128)(2,1)S(1)}, bf16[1024,256]{1,0:T(8,128)(2,1)S(1)}, u32[]{:S(2)}, u32[]{:S(2)}) collective-permute-start(bf16[1024,256]{1,0:T(8,128)(2,1)S(1)} %collective-permute-done.5.a2), channel_id=1, source_target_pairs={{0,1},{1,0},{2,3},{3,2},{4,5},{5,4},{6,7},{7,6},{8,9},{9,8},{10,11... | collective-permute-start | bytes 1572872 | tf_op jit(solution)/shard_map/ppermute | solution.py:240
  59.4 1.8 %collective-permute-start.11 = (bf16[48,2048]{1,0:T(8,128)(2,1)S(1)}, bf16[48,2048]{1,0:T(8,128)(2,1)S(1)}, u32[]{:S(2)}, u32[]{:S(2)}) collective-permute-start(bf16[48,2048]{1,0:T(8,128)(2,1)S(1)} %constant_dynamic-slice_fusion), channel_id=1, source_target_pairs={{0,1},{1,0},{2,3},{3,2},{4,5},{5,4},{6,7},{7,6},{8,9},{9,8},{10,11... | collective-permute-start | bytes 589832 | tf_op jit(solution)/shard_map/ppermute | solution.py:240
  123.4 7.6 %collective-permute-start.14 = (bf16[32,2048]{1,0:T(8,128)(2,1)S(1)}, bf16[32,2048]{1,0:T(8,128)(2,1)S(1)}, u32[]{:S(2)}, u32[]{:S(2)}) collective-permute-start(bf16[32,2048]{1,0:T(8,128)(2,1)S(1)} %get-tuple-element.45), channel_id=1, source_target_pairs={{0,3},{1,2},{2,1},{3,0},{4,7},{5,6},{6,5},{7,4},{8,11},{9,10},{10,... | collective-permute-start | bytes 393224 | tf_op jit(solution)/shard_map/ppermute | solution.py:401
  126.7 6.8 %collective-permute-start.13 = (bf16[32,2048]{1,0:T(8,128)(2,1)S(1)}, bf16[32,2048]{1,0:T(8,128)(2,1)S(1)}, u32[]{:S(2)}, u32[]{:S(2)}) collective-permute-start(bf16[32,2048]{1,0:T(8,128)(2,1)S(1)} %get-tuple-element.46), channel_id=1, source_target_pairs={{0,2},{1,3},{2,0},{3,1},{4,6},{5,7},{6,4},{7,5},{8,10},{9,11},{10,... | collective-permute-start | bytes 393224 | tf_op jit(solution)/shard_map/ppermute | solution.py:401
  127.0 6.5 %collective-permute-start.12 = (bf16[32,2048]{1,0:T(8,128)(2,1)S(1)}, bf16[32,2048]{1,0:T(8,128)(2,1)S(1)}, u32[]{:S(2)}, u32[]{:S(2)}) collective-permute-start(bf16[32,2048]{1,0:T(8,128)(2,1)S(1)} %get-tuple-element.47), channel_id=1, source_target_pairs={{0,1},{1,0},{2,3},{3,2},{4,5},{5,4},{6,7},{7,6},{8,9},{9,8},{10,11... | collective-permute-start | bytes 393224 | tf_op jit(solution)/shard_map/ppermute | solution.py:401
Sparse Core Ops, SparseCore 0:
  66.8 55.4 reduce-scatter.1

commit v10 on v9

--- a/solution.py
+++ b/solution.py
@@ -335,17 +335,17 @@
     )(at, ends, rt, din, far(conv), far(query))
 
     a_far = lax.ppermute(mixed, "xh", [(0, 1), (1, 0)])
-    a_other = other_core(mixed)
-    a_other, core_late = lax.optimization_barrier((a_other, core))
-    w_other = other_core(
-        lax.dynamic_slice(out_weight, (0, (xh * 2 + 1 - core_late) * width), (channels, width))
-    )
     def given(parts):
-        return other_core(
-            jnp.concatenate([lax.dynamic_slice(v, (0, (1 - core) * width), (v.shape[0], width)) for v in parts], axis=0)
+        return jnp.concatenate(
+            [lax.dynamic_slice(v, (0, (1 - core) * width), (v.shape[0], width)) for v in parts], axis=0
         )
 
-    g013 = given((f0_late, f1, f3, rest))
+    _, core_late = lax.optimization_barrier((mixed, core))
+    w_given = lax.dynamic_slice(out_weight, (0, (xh * 2 + 1 - core_late) * width), (channels, width))
+    w_given, mixed_late = lax.optimization_barrier((w_given, mixed))
+    a_other = other_core(mixed_late)
+    w_other = other_core(w_given)
+    g013 = other_core(given((f0_late, f1, f3, rest)))
 
     tile = 512
     strips = width // tile
@@ -373,7 +373,7 @@
         name="near",
     )(at, mixed, a_other, far(out_weight), w_other)
     a_far, near, f2 = lax.optimization_barrier((a_far, near, f2))
-    g2 = given((f2,))
+    g2 = other_core(given((f2,)))
     a_far_other = other_core(a_far)
     partial = pl.pallas_call(
         far_kernel,

time: 142 us -> 140 us (0.986)
  waiting for transfers between devices: 73.7 us -> 71.7 us
    ppermute x1, waiting for transfers between devices: 2.59 us -> 0.01 us  [local(): f2 = lax.ppermute(f0_late, 'y', [(i, (i + 2) % 4) for i in range(4)])]
  transfers between devices with their start and end apart: 17 -> 17, of which waited for: 10 -> 9; matrix products, arithmetic and copies ran while one was open for 3% -> 3% of each run, Pallas kernels for 10% -> 11%
where the time goes in v10:
time: 140 us; the launch traced here: 139 us
  waiting for transfers between devices  71.7 us (51%)
  starting transfers between devices  25.6 us (18%)
  Pallas kernels  23.1 us (16%)
  between operations  13.6 us (10%)
  local copies, waits for them, and re-layouts  5.36 us (4%)
    reduce_scatter x1, waiting for transfers between devices, local(): summed = lax.psum_scatter(partial, 'z', scatter_dimension=0, tiled=True)  56.1 us
    ppermute x3, waiting for transfers between devices, traded(): return lax.ppermute(summed[k * size:(k + 1) * size], ('xh', 'c'), pairs)  6.35 us
    pallas_call x1, Pallas kernels, local(): pl.pallas_call(far_kernel, out_shape=pltpu.HBM((rows, width), BF), grid_s...  5.48 us
    pallas_call x1, Pallas kernels, local(): pl.pallas_call(conv_kernel, out_shape=(pltpu.HBM((rows, channels), BF), p...  5.04 us
    pallas_call x1, Pallas kernels, local(): pl.pallas_call(near_kernel, out_shape=jax.ShapeDtypeStruct((rows, width),...  4.95 us
    pallas_call x1, Pallas kernels, local(): pl.pallas_call(state_kernel, out_shape=(pltpu.HBM((rows, channels), BF),...  4.68 us
    ppermute x5, starting transfers between devices, other_core(): return lax.ppermute(value, 'c', [(0, 1), (1, 0)])  4.51 us
    all_to_all x1, starting transfers between devices, local(): ends = lax.all_to_all(end, ('y', 'xl'), 0, 0, tiled=True)  4.01 us
  transfers between devices with their start and end apart: 17, of which 9 were waited for; matrix products, arithmetic and copies ran while one was open for 3% of the time, Pallas kernels for 11%

profile of v10, /device:TPU:1, one launch (start us, length us, event | category | flops | bytes accessed | tf_op | source)
XLA Modules:
  0.0 139.5 jit_solution(9188134754671578374)
XLA Ops:
  6.5 0.7 slice.15
  7.2 3.9 %collective-permute-start = (bf16[3,8,256]{2,1,0:T(8,128)(2,1)S(1)}, bf16[3,8,256]{2,1,0:T(8,128)(2,1)S(1)}, u32[]{:S(2)}, u32[]{:S(2)}) collective-permute-start(bf16[3,8,256]{2,1,0:T(8,128)(2,1)S(1)} %slice.15), channel_id=1, source_target_pairs={{0,32},{32,64},{64,96},{96,128},{128,160},{160,192},{192,224},{1,3... | collective-permute-start | bytes 36872 | tf_op jit(solution)/shard_map/ppermute | solution.py:251
  11.2 1.0 dynamic_slice.24
  12.2 2.9 %collective-permute-start.1 = (bf16[48,4096]{1,0:T(8,128)(2,1)S(1)}, bf16[48,4096]{1,0:T(8,128)(2,1)S(1)}, u32[]{:S(2)}, u32[]{:S(2)}) collective-permute-start(bf16[48,4096]{1,0:T(8,128)(2,1)S(1)} %dynamic_slice.24), channel_id=1, source_target_pairs={{0,34},{34,0},{2,32},{32,2},{1,35},{35,1},{3,33},{33,3},{4,38},{38... | collective-permute-start | bytes 1179656 | tf_op jit(solution)/shard_map/ppermute | solution.py:261
  15.1 1.1 constant_dynamic-slice_fusion.6
  16.2 0.1 collective-permute-start.4
  16.3 0.1 pad_add_fusion.at_ref
  16.4 0.0 collective-permute-done.halo_ref
  16.4 4.7 %state.1 = (bf16[1024,256]{1,0:T(8,128)(2,1)}, f32[8,16,256]{2,1,0:T(8,128)}, f32[16,256]{1,0:T(8,128)S(1)}) custom-call(bf16[3,1024,256]{2,1,0:T(8,128)(2,1)} %p_ref.1, bf16[3,1024,256]{2,1,0:T(8,128)(2,1)} %p_ref.1, bf16[3,8,256]{2,1,0:T(8,128)(2,1)S(1)} %collective-permute-done.halo_ref, f32[3,3,256]{2,1,0:T(4,128)} %sf_ref.3, f32[16,16]{1,0:T(8,128)} %rate_ref.3), custom_call_target="tpu_custom_call" | custom-call | flops 1000000 | bytes 65536 | tf_op jit(solution)/shard_map/state/pallas_call | solution.py:274
  21.1 4.0 %all-to-all-start = ((f32[8,16,256]{2,1,0:T(8,128)}), f32[8,16,256]{2,1,0:T(8,128)S(1)}, u32[]{:S(2)}, u32[]{:S(2)}) async-start(f32[8,16,256]{2,1,0:T(8,128)} %get-tuple-element.28), calls=%async_computation | async-start | bytes 262144 | tf_op jit(solution)/shard_map/all_to_all | solution.py:300
  25.1 0.0 reduce-scatter.2.cloned.1.call-start
  25.2 0.0 collective-permute-done.1.f0
  25.2 2.7 %collective-permute-start.3 = (bf16[48,4096]{1,0:T(8,128)(2,1)S(1)}, bf16[48,4096]{1,0:T(8,128)(2,1)S(1)}, u32[]{:S(2)}, u32[]{:S(2)}) collective-permute-start(bf16[48,4096]{1,0:T(8,128)(2,1)S(1)} %collective-permute-done.1.f0), channel_id=1, source_target_pairs={{0,192},{64,0},{128,64},{192,128},{1,193},{65,1},{129,65},{193,129... | collective-permute-start | bytes 1179656 | tf_op jit(solution)/shard_map/ppermute | solution.py:324
  27.9 0.0 collective-permute-start.2
  27.9 5.0 %conv.1 = (bf16[1024,256]{1,0:T(8,128)(2,1)}, bf16[1024,256]{1,0:T(8,128)(2,1)}, bf16[128,256]{1,0:T(8,128)(2,1)S(1)}) custom-call(bf16[3,1024,256]{2,1,0:T(8,128)(2,1)} %p_ref.1, bf16[1024,256]{1,0:T(8,128)(2,1)} %get-tuple-element.32.x_ref, bf16[3,8,256]{2,1,0:T(8,128)(2,1)S(1)} %collective-permute-done.halo_ref, f32[3,3,256]{2,1,0:T(4,128)} %sf_ref.3, ...), custom_call_target="tpu_custom_call" | custom-call | flops 6000000000 | bytes 65536 | tf_op jit(solution)/shard_map/conv/pallas_call | solution.py:301
  33.0 0.0 all-to-all-done.ends_ref
  33.0 1.8 %collective-permute-done.4.rest = bf16[64,4096]{1,0:T(8,128)(2,1)S(1)} collective-permute-done((bf16[64,4096]{1,0:T(8,128)(2,1)S(1)}, bf16[64,4096]{1,0:T(8,128)(2,1)S(1)}, u32[]{:S(2)}, u32[]{:S(2)}) %collective-permute-start.4) | collective-permute-done | bytes 524320 | tf_op jit(solution)/shard_map/ppermute | solution.py:262
  34.8 1.1 collective-permute-done.3.f3
  35.9 2.5 %collective-permute-done.2.f1 = bf16[48,4096]{1,0:T(8,128)(2,1)S(1)} collective-permute-done((bf16[48,4096]{1,0:T(8,128)(2,1)S(1)}, bf16[48,4096]{1,0:T(8,128)(2,1)S(1)}, u32[]{:S(2)}, u32[]{:S(2)}) %collective-permute-start.2) | collective-permute-done | bytes 393248 | tf_op jit(solution)/shard_map/ppermute | solution.py:323
  38.4 1.6 %mix.1.a0 = bf16[1024,256]{1,0:T(8,128)(2,1)S(1)} custom-call(s32[4]{0:T(128)S(1)} %pad_add_fusion.at_ref, f32[8,16,256]{2,1,0:T(8,128)S(1)} %all-to-all-done.ends_ref, f32[16,256]{1,0:T(8,128)S(1)} %get-tuple-element.31.rt_ref, bf16[128,256]{1,0:T(8,128)(2,1)S(1)} %get-tuple-element.34.din_ref, bf16[1024,256]{1,0:T(8,128)(2,1)} %get-tuple-element.35.y_ref, ...), custom_call_target="tpu_custom_call" | custom-call | flops 1000000 | bytes 65536 | tf_op jit(solution)/shard_map/mix/pallas_call | solution.py:327
  40.0 3.5 %collective-permute-start.5 = (bf16[1024,256]{1,0:T(8,128)(2,1)S(1)}, bf16[1024,256]{1,0:T(8,128)(2,1)S(1)}, u32[]{:S(2)}, u32[]{:S(2)}) collective-permute-start(bf16[1024,256]{1,0:T(8,128)(2,1)S(1)} %mix.1.a0), channel_id=1, source_target_pairs={{0,2},{2,0},{1,3},{3,1},{4,6},{6,4},{5,7},{7,5},{8,10},{10,8},{9,1... | collective-permute-start | bytes 1572872 | tf_op jit(solution)/shard_map/ppermute | solution.py:337
  43.5 0.1 collective-permute-start.8
  43.6 1.3 constant_dynamic-slice_fusion.5
  44.9 3.1 %collective-permute-start.6 = (bf16[1024,256]{1,0:T(8,128)(2,1)S(1)}, bf16[1024,256]{1,0:T(8,128)(2,1)S(1)}, u32[]{:S(2)}, u32[]{:S(2)}) collective-permute-start(bf16[1024,256]{1,0:T(8,128)(2,1)S(1)} %mix.1.a0), channel_id=1, source_target_pairs={{0,1},{1,0},{2,3},{3,2},{4,5},{5,4},{6,7},{7,6},{8,9},{9,8},{10,11... | collective-permute-start | bytes 1572872 | tf_op jit(solution)/shard_map/ppermute | solution.py:240
  48.0 0.1 collective-permute-start.7
  48.2 0.1 pad_maximum_fusion
  48.3 0.5 collective-permute-start.10
  48.8 0.8 collective-permute-done.6.a1
  49.5 1.5 %collective-permute-done.7.w1 = bf16[256,2048]{1,0:T(8,128)(2,1)S(1)} collective-permute-done((bf16[256,2048]{1,0:T(8,128)(2,1)S(1)}, bf16[256,2048]{1,0:T(8,128)(2,1)S(1)}, u32[]{:S(2)}, u32[]{:S(2)}) %collective-permute-start.7) | collective-permute-done | bytes 1048608 | tf_op jit(solution)/shard_map/ppermute | solution.py:240
  51.0 5.0 %near.1.near_ref = bf16[1024,2048]{1,0:T(8,128)(2,1)S(1)} custom-call(s32[4]{0:T(128)S(1)} %pad_add_fusion.at_ref, bf16[1024,256]{1,0:T(8,128)(2,1)S(1)} %mix.1.a0, bf16[1024,256]{1,0:T(8,128)(2,1)S(1)} %collective-permute-done.6.a1, bf16[256,8192]{1,0:T(8,128)(2,1)} %w0.1, bf16[256,2048]{1,0:T(8,128)(2,1)S(1)} %collective-permute-done.7.w1), custom_call_target="tpu_custom_call" | custom-call | flops 2000000000 | bytes 6291456 | tf_op jit(solution)/shard_map/near/pallas_call | solution.py:360
  56.0 0.0 collective-permute-done.8.f2
  56.0 0.0 collective-permute-done.5.a2
  56.0 0.6 collective-permute-start.9
  56.6 0.3 collective-permute-start.11
  56.9 0.0 collective-permute-done.10.g013
  56.9 1.5 %collective-permute-done.11.g2 = bf16[48,2048]{1,0:T(8,128)(2,1)S(1)} collective-permute-done((bf16[48,2048]{1,0:T(8,128)(2,1)S(1)}, bf16[48,2048]{1,0:T(8,128)(2,1)S(1)}, u32[]{:S(2)}, u32[]{:S(2)}) %collective-permute-start.11) | collective-permute-done | bytes 196640 | tf_op jit(solution)/shard_map/ppermute | solution.py:240
  58.4 0.0 collective-permute-done.9.a3
  58.4 5.5 %far.1 = bf16[1024,2048]{1,0:T(8,128)(2,1)} custom-call(s32[4]{0:T(128)S(1)} %pad_add_fusion.at_ref, bf16[1024,256]{1,0:T(8,128)(2,1)S(1)} %collective-permute-done.5.a2, bf16[1024,256]{1,0:T(8,128)(2,1)S(1)} %collective-permute-done.9.a3, bf16[48,4096]{1,0:T(8,128)(2,1)S(1)} %collective-permute-done.1.f0, bf16[48,4096]{1,0:T(8,128)(2,1)S(1)} %collective-permute-done.2.f1, ...), custom_call_target="tpu_custom_call" | custom-call | flops 2000000000 | bytes 10485760 | tf_op jit(solution)/shard_map/far/pallas_call | solution.py:378
  63.9 0.0 reduce-scatter.2.cloned.1.call-update
  63.9 56.1 %reduce-scatter.2.cloned.1.call-done = bf16[128,2048]{1,0:T(8,128)(2,1)} async-done(((bf16[1024,2048]{1,0:T(8,128)(2,1)}), bf16[128,2048]{1,0:T(8,128)(2,1)}) %reduce-scatter.2.cloned.1.call-update) | async-done | bytes 524304 | tf_op jit(solution)/shard_map/reduce_scatter | solution.py:396
  120.0 1.1 fusion
  121.1 3.3 %collective-permute-start.14 = (bf16[32,2048]{1,0:T(8,128)(2,1)S(1)}, bf16[32,2048]{1,0:T(8,128)(2,1)S(1)}, u32[]{:S(2)}, u32[]{:S(2)}) collective-permute-start(bf16[32,2048]{1,0:T(8,128)(2,1)S(1)} %get-tuple-element.47), channel_id=1, source_target_pairs={{0,3},{1,2},{2,1},{3,0},{4,7},{5,6},{6,5},{7,4},{8,11},{9,10},{10,... | collective-permute-start | bytes 393224 | tf_op jit(solution)/shard_map/ppermute | solution.py:401
  124.4 0.3 collective-permute-start.13
  124.7 0.2 collective-permute-start.12
  124.9 3.8 %collective-permute-done.14.p3 = bf16[32,2048]{1,0:T(8,128)(2,1)S(1)} collective-permute-done((bf16[32,2048]{1,0:T(8,128)(2,1)S(1)}, bf16[32,2048]{1,0:T(8,128)(2,1)S(1)}, u32[]{:S(2)}, u32[]{:S(2)}) %collective-permute-start.14) | collective-permute-done | bytes 131104 | tf_op jit(solution)/shard_map/ppermute | solution.py:401
  128.7 2.6 %collective-permute-done.13.p2 = bf16[32,2048]{1,0:T(8,128)(2,1)S(1)} collective-permute-done((bf16[32,2048]{1,0:T(8,128)(2,1)S(1)}, bf16[32,2048]{1,0:T(8,128)(2,1)S(1)}, u32[]{:S(2)}, u32[]{:S(2)}) %collective-permute-start.13) | collective-permute-done | bytes 131104 | tf_op jit(solution)/shard_map/ppermute | solution.py:401
  131.3 0.0 collective-permute-done.12.p1
  131.3 1.4 join.1
  (9 shorter events, 0.1 us)
Async XLA Ops:
  7.2 9.2 %collective-permute-start = (bf16[3,8,256]{2,1,0:T(8,128)(2,1)S(1)}, bf16[3,8,256]{2,1,0:T(8,128)(2,1)S(1)}, u32[]{:S(2)}, u32[]{:S(2)}) collective-permute-start(bf16[3,8,256]{2,1,0:T(8,128)(2,1)S(1)} %slice.15), channel_id=1, source_target_pairs={{0,32},{32,64},{64,96},{96,128},{128,160},{160,192},{192,224},{1,3... | collective-permute-start | bytes 36872 | tf_op jit(solution)/shard_map/ppermute | solution.py:251
  12.2 13.0 %collective-permute-start.1 = (bf16[48,4096]{1,0:T(8,128)(2,1)S(1)}, bf16[48,4096]{1,0:T(8,128)(2,1)S(1)}, u32[]{:S(2)}, u32[]{:S(2)}) collective-permute-start(bf16[48,4096]{1,0:T(8,128)(2,1)S(1)} %dynamic_slice.24), channel_id=1, source_target_pairs={{0,34},{34,0},{2,32},{32,2},{1,35},{35,1},{3,33},{33,3},{4,38},{38... | collective-permute-start | bytes 1179656 | tf_op jit(solution)/shard_map/ppermute | solution.py:261
  16.2 18.5 %collective-permute-start.4 = (bf16[64,4096]{1,0:T(8,128)(2,1)S(1)}, bf16[64,4096]{1,0:T(8,128)(2,1)S(1)}, u32[]{:S(2)}, u32[]{:S(2)}) collective-permute-start(bf16[64,4096]{1,0:T(8,128)(2,1)S(1)} %constant_dynamic-slice_fusion.6), channel_id=1, source_target_pairs={{0,34},{34,0},{2,32},{32,2},{1,35},{35,1},{3,33},{33,3},{4,38},{38... | collective-permute-start | bytes 1572872 | tf_op jit(solution)/shard_map/ppermute | solution.py:262
  16.4 8.8 %copy-start = (f32[16,16]{1,0:T(8,128)S(1)}, f32[16,16]{1,0:T(8,128)}, u32[]{:S(2)}) copy-start(f32[16,16]{1,0:T(8,128)} %rate_ref.3) | copy-start | bytes 3076
  16.4 8.8 %copy-start.1 = (f32[16,16]{1,0:T(8,128)S(1)}, f32[16,16]{1,0:T(8,128)}, u32[]{:S(2)}) copy-start(f32[16,16]{1,0:T(8,128)} %param.7) | copy-start | bytes 3076
  21.1 11.9 %all-to-all-start = ((f32[8,16,256]{2,1,0:T(8,128)}), f32[8,16,256]{2,1,0:T(8,128)S(1)}, u32[]{:S(2)}, u32[]{:S(2)}) async-start(f32[8,16,256]{2,1,0:T(8,128)} %get-tuple-element.28), calls=%async_computation | async-start | bytes 262144 | tf_op jit(solution)/shard_map/all_to_all | solution.py:300
  25.1 94.9 %reduce-scatter.2.cloned.1.call-start = ((), (), s32[]{:S(2)}) async-start(), calls=%async_computation.2 | async-start | bytes 4718592 | tf_op jit(solution)/shard_map/reduce_scatter | solution.py:396
  25.2 10.7 %collective-permute-start.3 = (bf16[48,4096]{1,0:T(8,128)(2,1)S(1)}, bf16[48,4096]{1,0:T(8,128)(2,1)S(1)}, u32[]{:S(2)}, u32[]{:S(2)}) collective-permute-start(bf16[48,4096]{1,0:T(8,128)(2,1)S(1)} %collective-permute-done.1.f0), channel_id=1, source_target_pairs={{0,192},{64,0},{128,64},{192,128},{1,193},{65,1},{129,65},{193,129... | collective-permute-start | bytes 1179656 | tf_op jit(solution)/shard_map/ppermute | solution.py:324
  27.9 10.5 %collective-permute-start.2 = (bf16[48,4096]{1,0:T(8,128)(2,1)S(1)}, bf16[48,4096]{1,0:T(8,128)(2,1)S(1)}, u32[]{:S(2)}, u32[]{:S(2)}) collective-permute-start(bf16[48,4096]{1,0:T(8,128)(2,1)S(1)} %collective-permute-done.1.f0), channel_id=1, source_target_pairs={{0,64},{64,128},{128,192},{192,0},{1,65},{65,129},{129,193},{193,1... | collective-permute-start | bytes 1179656 | tf_op jit(solution)/shard_map/ppermute | solution.py:323
  40.0 16.0 %collective-permute-start.5 = (bf16[1024,256]{1,0:T(8,128)(2,1)S(1)}, bf16[1024,256]{1,0:T(8,128)(2,1)S(1)}, u32[]{:S(2)}, u32[]{:S(2)}) collective-permute-start(bf16[1024,256]{1,0:T(8,128)(2,1)S(1)} %mix.1.a0), channel_id=1, source_target_pairs={{0,2},{2,0},{1,3},{3,1},{4,6},{6,4},{5,7},{7,5},{8,10},{10,8},{9,1... | collective-permute-start | bytes 1572872 | tf_op jit(solution)/shard_map/ppermute | solution.py:337
  43.5 12.5 %collective-permute-start.8 = (bf16[48,4096]{1,0:T(8,128)(2,1)S(1)}, bf16[48,4096]{1,0:T(8,128)(2,1)S(1)}, u32[]{:S(2)}, u32[]{:S(2)}) collective-permute-start(bf16[48,4096]{1,0:T(8,128)(2,1)S(1)} %collective-permute-done.1.f0), channel_id=1, source_target_pairs={{0,128},{64,192},{128,0},{192,64},{1,129},{65,193},{129,1},{193,65... | collective-permute-start | bytes 1179656 | tf_op jit(solution)/shard_map/ppermute | solution.py:326
  44.9 4.6 %collective-permute-start.6 = (bf16[1024,256]{1,0:T(8,128)(2,1)S(1)}, bf16[1024,256]{1,0:T(8,128)(2,1)S(1)}, u32[]{:S(2)}, u32[]{:S(2)}) collective-permute-start(bf16[1024,256]{1,0:T(8,128)(2,1)S(1)} %mix.1.a0), channel_id=1, source_target_pairs={{0,1},{1,0},{2,3},{3,2},{4,5},{5,4},{6,7},{7,6},{8,9},{9,8},{10,11... | collective-permute-start | bytes 1572872 | tf_op jit(solution)/shard_map/ppermute | solution.py:240
  48.0 3.0 %collective-permute-start.7 = (bf16[256,2048]{1,0:T(8,128)(2,1)S(1)}, bf16[256,2048]{1,0:T(8,128)(2,1)S(1)}, u32[]{:S(2)}, u32[]{:S(2)}) collective-permute-start(bf16[256,2048]{1,0:T(8,128)(2,1)S(1)} %constant_dynamic-slice_fusion.5), channel_id=1, source_target_pairs={{0,1},{1,0},{2,3},{3,2},{4,5},{5,4},{6,7},{7,6},{8,9},{9,8},{10,11... | collective-permute-start | bytes 3145736 | tf_op jit(solution)/shard_map/ppermute | solution.py:240
  48.3 8.6 %collective-permute-start.10 = (bf16[208,2048]{1,0:T(8,128)(2,1)S(1)}, bf16[208,2048]{1,0:T(8,128)(2,1)S(1)}, u32[]{:S(2)}, u32[]{:S(2)}) collective-permute-start(bf16[208,2048]{1,0:T(8,128)(2,1)S(1)} %pad_maximum_fusion), channel_id=1, source_target_pairs={{0,1},{1,0},{2,3},{3,2},{4,5},{5,4},{6,7},{7,6},{8,9},{9,8},{10,11... | collective-permute-start | bytes 2555912 | tf_op jit(solution)/shard_map/ppermute | solution.py:240
  56.0 2.4 %collective-permute-start.9 = (bf16[1024,256]{1,0:T(8,128)(2,1)S(1)}, bf16[1024,256]{1,0:T(8,128)(2,1)S(1)}, u32[]{:S(2)}, u32[]{:S(2)}) collective-permute-start(bf16[1024,256]{1,0:T(8,128)(2,1)S(1)} %collective-permute-done.5.a2), channel_id=1, source_target_pairs={{0,1},{1,0},{2,3},{3,2},{4,5},{5,4},{6,7},{7,6},{8,9},{9,8},{10,11... | collective-permute-start | bytes 1572872 | tf_op jit(solution)/shard_map/ppermute | solution.py:240
  56.6 1.8 %collective-permute-start.11 = (bf16[48,2048]{1,0:T(8,128)(2,1)S(1)}, bf16[48,2048]{1,0:T(8,128)(2,1)S(1)}, u32[]{:S(2)}, u32[]{:S(2)}) collective-permute-start(bf16[48,2048]{1,0:T(8,128)(2,1)S(1)} %constant_dynamic-slice_fusion), channel_id=1, source_target_pairs={{0,1},{1,0},{2,3},{3,2},{4,5},{5,4},{6,7},{7,6},{8,9},{9,8},{10,11... | collective-permute-start | bytes 589832 | tf_op jit(solution)/shard_map/ppermute | solution.py:240
  121.1 7.6 %collective-permute-start.14 = (bf16[32,2048]{1,0:T(8,128)(2,1)S(1)}, bf16[32,2048]{1,0:T(8,128)(2,1)S(1)}, u32[]{:S(2)}, u32[]{:S(2)}) collective-permute-start(bf16[32,2048]{1,0:T(8,128)(2,1)S(1)} %get-tuple-element.47), channel_id=1, source_target_pairs={{0,3},{1,2},{2,1},{3,0},{4,7},{5,6},{6,5},{7,4},{8,11},{9,10},{10,... | collective-permute-start | bytes 393224 | tf_op jit(solution)/shard_map/ppermute | solution.py:401
  124.4 6.8 %collective-permute-start.13 = (bf16[32,2048]{1,0:T(8,128)(2,1)S(1)}, bf16[32,2048]{1,0:T(8,128)(2,1)S(1)}, u32[]{:S(2)}, u32[]{:S(2)}) collective-permute-start(bf16[32,2048]{1,0:T(8,128)(2,1)S(1)} %get-tuple-element.48), channel_id=1, source_target_pairs={{0,2},{1,3},{2,0},{3,1},{4,6},{5,7},{6,4},{7,5},{8,10},{9,11},{10,... | collective-permute-start | bytes 393224 | tf_op jit(solution)/shard_map/ppermute | solution.py:401
  124.7 6.6 %collective-permute-start.12 = (bf16[32,2048]{1,0:T(8,128)(2,1)S(1)}, bf16[32,2048]{1,0:T(8,128)(2,1)S(1)}, u32[]{:S(2)}, u32[]{:S(2)}) collective-permute-start(bf16[32,2048]{1,0:T(8,128)(2,1)S(1)} %get-tuple-element.49), channel_id=1, source_target_pairs={{0,1},{1,0},{2,3},{3,2},{4,5},{5,4},{6,7},{7,6},{8,9},{9,8},{10,11... | collective-permute-start | bytes 393224 | tf_op jit(solution)/shard_map/ppermute | solution.py:401
Sparse Core Ops, SparseCore 0:
  64.0 55.9 reduce-scatter.1

commit v11 on v10

--- a/solution.py
+++ b/solution.py
@@ -347,7 +347,7 @@
     w_other = other_core(w_given)
     g013 = other_core(given((f0_late, f1, f3, rest)))
 
-    tile = 512
+    tile = 1024
     strips = width // tile
 
     def strip(shape):
@@ -368,7 +368,7 @@
             out_specs=strip((rows, width)),
             scratch_shapes=[pltpu.VMEM((rows, 2 * channels), BF), pltpu.VMEM((2 * channels, tile), BF)],
         ),
-        compiler_params=pltpu.CompilerParams(vmem_limit_bytes=16 * 2**20),
+        compiler_params=pltpu.CompilerParams(vmem_limit_bytes=24 * 2**20),
         cost_estimate=pl.CostEstimate(flops=2 * 10**9, bytes_accessed=6 * 2**20, transcendentals=0),
         name="near",
     )(at, mixed, a_other, far(out_weight), w_other)
@@ -388,7 +388,7 @@
             out_specs=strip((rows, width)),
             scratch_shapes=[pltpu.VMEM((rows, 2 * channels), BF), pltpu.VMEM((2 * channels, tile), BF)],
         ),
-        compiler_params=pltpu.CompilerParams(vmem_limit_bytes=20 * 2**20),
+        compiler_params=pltpu.CompilerParams(vmem_limit_bytes=30 * 2**20),
         cost_estimate=pl.CostEstimate(flops=2 * 10**9, bytes_accessed=10 * 2**20, transcendentals=0),
         name="far",
     )(at, a_far, a_far_other, f0_late, f1, f2, f3, rest, g013, g2, near)

time: 140 us -> 139 us (level)
  transfers between devices with their start and end apart: 17 -> 17, of which waited for: 9 -> 9; matrix products, arithmetic and copies ran while one was open for 3% -> 3% of each run, Pallas kernels for 11% -> 10%
where the time goes in v11:
time: 139 us
  waiting for transfers between devices  71.2 us (51%)
  starting transfers between devices  26.1 us (19%)
  Pallas kernels  22.5 us (16%)
  between operations  13.6 us (10%)
  local copies, waits for them, and re-layouts  5.36 us (4%)
    reduce_scatter x1, waiting for transfers between devices, local(): summed = lax.psum_scatter(partial, 'z', scatter_dimension=0, tiled=True)  55.6 us
    ppermute x3, waiting for transfers between devices, traded(): return lax.ppermute(summed[k * size:(k + 1) * size], ('xh', 'c'), pairs)  6.3 us
    pallas_call x1, Pallas kernels, local(): pl.pallas_call(far_kernel, out_shape=pltpu.HBM((rows, width), BF), grid_s...  5.35 us
    pallas_call x1, Pallas kernels, local(): pl.pallas_call(conv_kernel, out_shape=(pltpu.HBM((rows, channels), BF), p...  5.04 us
    ppermute x5, starting transfers between devices, other_core(): return lax.ppermute(value, 'c', [(0, 1), (1, 0)])  4.97 us
    pallas_call x1, Pallas kernels, local(): pl.pallas_call(state_kernel, out_shape=(pltpu.HBM((rows, channels), BF),...  4.68 us
    pallas_call x1, Pallas kernels, local(): pl.pallas_call(near_kernel, out_shape=jax.ShapeDtypeStruct((rows, width),...  4.48 us
    all_to_all x1, starting transfers between devices, local(): ends = lax.all_to_all(end, ('y', 'xl'), 0, 0, tiled=True)  4.01 us
  transfers between devices with their start and end apart: 17, of which 9 were waited for; matrix products, arithmetic and copies ran while one was open for 3% of the time, Pallas kernels for 10%

profile of v11, /device:TPU:1, one launch (start us, length us, event | category | flops | bytes accessed | tf_op | source)
XLA Modules:
  0.0 138.8 jit_solution(3690431985086662551)
XLA Ops:
  6.5 0.7 slice.15
  7.2 3.9 %collective-permute-start = (bf16[3,8,256]{2,1,0:T(8,128)(2,1)S(1)}, bf16[3,8,256]{2,1,0:T(8,128)(2,1)S(1)}, u32[]{:S(2)}, u32[]{:S(2)}) collective-permute-start(bf16[3,8,256]{2,1,0:T(8,128)(2,1)S(1)} %slice.15), channel_id=1, source_target_pairs={{0,32},{32,64},{64,96},{96,128},{128,160},{160,192},{192,224},{1,3... | collective-permute-start | bytes 36872 | tf_op jit(solution)/shard_map/ppermute | solution.py:251
  11.2 1.0 dynamic_slice.24
  12.2 2.9 %collective-permute-start.1 = (bf16[48,4096]{1,0:T(8,128)(2,1)S(1)}, bf16[48,4096]{1,0:T(8,128)(2,1)S(1)}, u32[]{:S(2)}, u32[]{:S(2)}) collective-permute-start(bf16[48,4096]{1,0:T(8,128)(2,1)S(1)} %dynamic_slice.24), channel_id=1, source_target_pairs={{0,34},{34,0},{2,32},{32,2},{1,35},{35,1},{3,33},{33,3},{4,38},{38... | collective-permute-start | bytes 1179656 | tf_op jit(solution)/shard_map/ppermute | solution.py:261
  15.1 1.1 constant_dynamic-slice_fusion.6
  16.2 0.1 collective-permute-start.4
  16.3 0.1 pad_add_fusion.at_ref
  16.4 0.0 collective-permute-done.halo_ref
  16.4 4.7 %state.1 = (bf16[1024,256]{1,0:T(8,128)(2,1)}, f32[8,16,256]{2,1,0:T(8,128)}, f32[16,256]{1,0:T(8,128)S(1)}) custom-call(bf16[3,1024,256]{2,1,0:T(8,128)(2,1)} %p_ref.1, bf16[3,1024,256]{2,1,0:T(8,128)(2,1)} %p_ref.1, bf16[3,8,256]{2,1,0:T(8,128)(2,1)S(1)} %collective-permute-done.halo_ref, f32[3,3,256]{2,1,0:T(4,128)} %sf_ref.3, f32[16,16]{1,0:T(8,128)} %rate_ref.3), custom_call_target="tpu_custom_call" | custom-call | flops 1000000 | bytes 65536 | tf_op jit(solution)/shard_map/state/pallas_call | solution.py:274
  21.1 4.0 %all-to-all-start = ((f32[8,16,256]{2,1,0:T(8,128)}), f32[8,16,256]{2,1,0:T(8,128)S(1)}, u32[]{:S(2)}, u32[]{:S(2)}) async-start(f32[8,16,256]{2,1,0:T(8,128)} %get-tuple-element.28), calls=%async_computation | async-start | bytes 262144 | tf_op jit(solution)/shard_map/all_to_all | solution.py:300
  25.1 0.0 reduce-scatter.2.cloned.1.call-start
  25.2 0.0 collective-permute-done.1.f0
  25.2 2.7 %collective-permute-start.3 = (bf16[48,4096]{1,0:T(8,128)(2,1)S(1)}, bf16[48,4096]{1,0:T(8,128)(2,1)S(1)}, u32[]{:S(2)}, u32[]{:S(2)}) collective-permute-start(bf16[48,4096]{1,0:T(8,128)(2,1)S(1)} %collective-permute-done.1.f0), channel_id=1, source_target_pairs={{0,192},{64,0},{128,64},{192,128},{1,193},{65,1},{129,65},{193,129... | collective-permute-start | bytes 1179656 | tf_op jit(solution)/shard_map/ppermute | solution.py:324
  27.9 0.0 collective-permute-start.2
  27.9 5.0 %conv.1 = (bf16[1024,256]{1,0:T(8,128)(2,1)}, bf16[1024,256]{1,0:T(8,128)(2,1)}, bf16[128,256]{1,0:T(8,128)(2,1)S(1)}) custom-call(bf16[3,1024,256]{2,1,0:T(8,128)(2,1)} %p_ref.1, bf16[1024,256]{1,0:T(8,128)(2,1)} %get-tuple-element.32.x_ref, bf16[3,8,256]{2,1,0:T(8,128)(2,1)S(1)} %collective-permute-done.halo_ref, f32[3,3,256]{2,1,0:T(4,128)} %sf_ref.3, ...), custom_call_target="tpu_custom_call" | custom-call | flops 6000000000 | bytes 65536 | tf_op jit(solution)/shard_map/conv/pallas_call | solution.py:301
  33.0 0.0 all-to-all-done.ends_ref
  33.0 1.8 %collective-permute-done.4.rest = bf16[64,4096]{1,0:T(8,128)(2,1)S(1)} collective-permute-done((bf16[64,4096]{1,0:T(8,128)(2,1)S(1)}, bf16[64,4096]{1,0:T(8,128)(2,1)S(1)}, u32[]{:S(2)}, u32[]{:S(2)}) %collective-permute-start.4) | collective-permute-done | bytes 524320 | tf_op jit(solution)/shard_map/ppermute | solution.py:262
  34.8 1.1 collective-permute-done.3.f3
  35.9 2.5 %collective-permute-done.2.f1 = bf16[48,4096]{1,0:T(8,128)(2,1)S(1)} collective-permute-done((bf16[48,4096]{1,0:T(8,128)(2,1)S(1)}, bf16[48,4096]{1,0:T(8,128)(2,1)S(1)}, u32[]{:S(2)}, u32[]{:S(2)}) %collective-permute-start.2) | collective-permute-done | bytes 393248 | tf_op jit(solution)/shard_map/ppermute | solution.py:323
  38.4 1.6 %mix.1.a0 = bf16[1024,256]{1,0:T(8,128)(2,1)S(1)} custom-call(s32[4]{0:T(128)S(1)} %pad_add_fusion.at_ref, f32[8,16,256]{2,1,0:T(8,128)S(1)} %all-to-all-done.ends_ref, f32[16,256]{1,0:T(8,128)S(1)} %get-tuple-element.31.rt_ref, bf16[128,256]{1,0:T(8,128)(2,1)S(1)} %get-tuple-element.34.din_ref, bf16[1024,256]{1,0:T(8,128)(2,1)} %get-tuple-element.35.y_ref, ...), custom_call_target="tpu_custom_call" | custom-call | flops 1000000 | bytes 65536 | tf_op jit(solution)/shard_map/mix/pallas_call | solution.py:327
  40.0 3.5 %collective-permute-start.5 = (bf16[1024,256]{1,0:T(8,128)(2,1)S(1)}, bf16[1024,256]{1,0:T(8,128)(2,1)S(1)}, u32[]{:S(2)}, u32[]{:S(2)}) collective-permute-start(bf16[1024,256]{1,0:T(8,128)(2,1)S(1)} %mix.1.a0), channel_id=1, source_target_pairs={{0,2},{2,0},{1,3},{3,1},{4,6},{6,4},{5,7},{7,5},{8,10},{10,8},{9,1... | collective-permute-start | bytes 1572872 | tf_op jit(solution)/shard_map/ppermute | solution.py:337
  43.5 0.1 collective-permute-start.8
  43.6 1.3 constant_dynamic-slice_fusion.5
  44.9 3.1 %collective-permute-start.6 = (bf16[1024,256]{1,0:T(8,128)(2,1)S(1)}, bf16[1024,256]{1,0:T(8,128)(2,1)S(1)}, u32[]{:S(2)}, u32[]{:S(2)}) collective-permute-start(bf16[1024,256]{1,0:T(8,128)(2,1)S(1)} %mix.1.a0), channel_id=1, source_target_pairs={{0,1},{1,0},{2,3},{3,2},{4,5},{5,4},{6,7},{7,6},{8,9},{9,8},{10,11... | collective-permute-start | bytes 1572872 | tf_op jit(solution)/shard_map/ppermute | solution.py:240
  48.0 0.1 collective-permute-start.7
  48.2 0.1 pad_maximum_fusion
  48.3 0.5 collective-permute-start.10
  48.8 0.8 collective-permute-done.6.a1
  49.5 1.5 %collective-permute-done.7.w1 = bf16[256,2048]{1,0:T(8,128)(2,1)S(1)} collective-permute-done((bf16[256,2048]{1,0:T(8,128)(2,1)S(1)}, bf16[256,2048]{1,0:T(8,128)(2,1)S(1)}, u32[]{:S(2)}, u32[]{:S(2)}) %collective-permute-start.7) | collective-permute-done | bytes 1048608 | tf_op jit(solution)/shard_map/ppermute | solution.py:240
  51.0 4.5 %near.1.near_ref = bf16[1024,2048]{1,0:T(8,128)(2,1)S(1)} custom-call(s32[4]{0:T(128)S(1)} %pad_add_fusion.at_ref, bf16[1024,256]{1,0:T(8,128)(2,1)S(1)} %mix.1.a0, bf16[1024,256]{1,0:T(8,128)(2,1)S(1)} %collective-permute-done.6.a1, bf16[256,8192]{1,0:T(8,128)(2,1)} %w0.1, bf16[256,2048]{1,0:T(8,128)(2,1)S(1)} %collective-permute-done.7.w1), custom_call_target="tpu_custom_call" | custom-call | flops 2000000000 | bytes 6291456 | tf_op jit(solution)/shard_map/near/pallas_call | solution.py:360
  55.5 0.0 collective-permute-done.8.f2
  55.5 0.0 collective-permute-done.5.a2
  55.5 1.0 collective-permute-start.9
  56.6 0.3 collective-permute-start.11
  56.9 0.0 collective-permute-done.10.g013
  56.9 1.5 %collective-permute-done.11.g2 = bf16[48,2048]{1,0:T(8,128)(2,1)S(1)} collective-permute-done((bf16[48,2048]{1,0:T(8,128)(2,1)S(1)}, bf16[48,2048]{1,0:T(8,128)(2,1)S(1)}, u32[]{:S(2)}, u32[]{:S(2)}) %collective-permute-start.11) | collective-permute-done | bytes 196640 | tf_op jit(solution)/shard_map/ppermute | solution.py:240
  58.4 0.0 collective-permute-done.9.a3
  58.4 5.4 %far.1 = bf16[1024,2048]{1,0:T(8,128)(2,1)} custom-call(s32[4]{0:T(128)S(1)} %pad_add_fusion.at_ref, bf16[1024,256]{1,0:T(8,128)(2,1)S(1)} %collective-permute-done.5.a2, bf16[1024,256]{1,0:T(8,128)(2,1)S(1)} %collective-permute-done.9.a3, bf16[48,4096]{1,0:T(8,128)(2,1)S(1)} %collective-permute-done.1.f0, bf16[48,4096]{1,0:T(8,128)(2,1)S(1)} %collective-permute-done.2.f1, ...), custom_call_target="tpu_custom_call" | custom-call | flops 2000000000 | bytes 10485760 | tf_op jit(solution)/shard_map/far/pallas_call | solution.py:378
  63.8 0.0 reduce-scatter.2.cloned.1.call-update
  63.8 55.6 %reduce-scatter.2.cloned.1.call-done = bf16[128,2048]{1,0:T(8,128)(2,1)} async-done(((bf16[1024,2048]{1,0:T(8,128)(2,1)}), bf16[128,2048]{1,0:T(8,128)(2,1)}) %reduce-scatter.2.cloned.1.call-update) | async-done | bytes 524304 | tf_op jit(solution)/shard_map/reduce_scatter | solution.py:396
  119.4 1.1 fusion
  120.5 3.3 %collective-permute-start.14 = (bf16[32,2048]{1,0:T(8,128)(2,1)S(1)}, bf16[32,2048]{1,0:T(8,128)(2,1)S(1)}, u32[]{:S(2)}, u32[]{:S(2)}) collective-permute-start(bf16[32,2048]{1,0:T(8,128)(2,1)S(1)} %get-tuple-element.47), channel_id=1, source_target_pairs={{0,3},{1,2},{2,1},{3,0},{4,7},{5,6},{6,5},{7,4},{8,11},{9,10},{10,... | collective-permute-start | bytes 393224 | tf_op jit(solution)/shard_map/ppermute | solution.py:401
  123.8 0.3 collective-permute-start.13
  124.1 0.2 collective-permute-start.12
  124.3 3.7 %collective-permute-done.14.p3 = bf16[32,2048]{1,0:T(8,128)(2,1)S(1)} collective-permute-done((bf16[32,2048]{1,0:T(8,128)(2,1)S(1)}, bf16[32,2048]{1,0:T(8,128)(2,1)S(1)}, u32[]{:S(2)}, u32[]{:S(2)}) %collective-permute-start.14) | collective-permute-done | bytes 131104 | tf_op jit(solution)/shard_map/ppermute | solution.py:401
  128.1 2.6 %collective-permute-done.13.p2 = bf16[32,2048]{1,0:T(8,128)(2,1)S(1)} collective-permute-done((bf16[32,2048]{1,0:T(8,128)(2,1)S(1)}, bf16[32,2048]{1,0:T(8,128)(2,1)S(1)}, u32[]{:S(2)}, u32[]{:S(2)}) %collective-permute-start.13) | collective-permute-done | bytes 131104 | tf_op jit(solution)/shard_map/ppermute | solution.py:401
  130.6 0.0 collective-permute-done.12.p1
  130.6 1.4 join.1
  (9 shorter events, 0.1 us)
Async XLA Ops:
  7.2 9.2 %collective-permute-start = (bf16[3,8,256]{2,1,0:T(8,128)(2,1)S(1)}, bf16[3,8,256]{2,1,0:T(8,128)(2,1)S(1)}, u32[]{:S(2)}, u32[]{:S(2)}) collective-permute-start(bf16[3,8,256]{2,1,0:T(8,128)(2,1)S(1)} %slice.15), channel_id=1, source_target_pairs={{0,32},{32,64},{64,96},{96,128},{128,160},{160,192},{192,224},{1,3... | collective-permute-start | bytes 36872 | tf_op jit(solution)/shard_map/ppermute | solution.py:251
  12.2 13.0 %collective-permute-start.1 = (bf16[48,4096]{1,0:T(8,128)(2,1)S(1)}, bf16[48,4096]{1,0:T(8,128)(2,1)S(1)}, u32[]{:S(2)}, u32[]{:S(2)}) collective-permute-start(bf16[48,4096]{1,0:T(8,128)(2,1)S(1)} %dynamic_slice.24), channel_id=1, source_target_pairs={{0,34},{34,0},{2,32},{32,2},{1,35},{35,1},{3,33},{33,3},{4,38},{38... | collective-permute-start | bytes 1179656 | tf_op jit(solution)/shard_map/ppermute | solution.py:261
  16.2 18.5 %collective-permute-start.4 = (bf16[64,4096]{1,0:T(8,128)(2,1)S(1)}, bf16[64,4096]{1,0:T(8,128)(2,1)S(1)}, u32[]{:S(2)}, u32[]{:S(2)}) collective-permute-start(bf16[64,4096]{1,0:T(8,128)(2,1)S(1)} %constant_dynamic-slice_fusion.6), channel_id=1, source_target_pairs={{0,34},{34,0},{2,32},{32,2},{1,35},{35,1},{3,33},{33,3},{4,38},{38... | collective-permute-start | bytes 1572872 | tf_op jit(solution)/shard_map/ppermute | solution.py:262
  16.4 8.8 %copy-start = (f32[16,16]{1,0:T(8,128)S(1)}, f32[16,16]{1,0:T(8,128)}, u32[]{:S(2)}) copy-start(f32[16,16]{1,0:T(8,128)} %rate_ref.3) | copy-start | bytes 3076
  16.4 8.8 %copy-start.1 = (f32[16,16]{1,0:T(8,128)S(1)}, f32[16,16]{1,0:T(8,128)}, u32[]{:S(2)}) copy-start(f32[16,16]{1,0:T(8,128)} %param.7) | copy-start | bytes 3076
  21.1 11.9 %all-to-all-start = ((f32[8,16,256]{2,1,0:T(8,128)}), f32[8,16,256]{2,1,0:T(8,128)S(1)}, u32[]{:S(2)}, u32[]{:S(2)}) async-start(f32[8,16,256]{2,1,0:T(8,128)} %get-tuple-element.28), calls=%async_computation | async-start | bytes 262144 | tf_op jit(solution)/shard_map/all_to_all | solution.py:300
  25.1 94.3 %reduce-scatter.2.cloned.1.call-start = ((), (), s32[]{:S(2)}) async-start(), calls=%async_computation.2 | async-start | bytes 4718592 | tf_op jit(solution)/shard_map/reduce_scatter | solution.py:396
  25.2 10.7 %collective-permute-start.3 = (bf16[48,4096]{1,0:T(8,128)(2,1)S(1)}, bf16[48,4096]{1,0:T(8,128)(2,1)S(1)}, u32[]{:S(2)}, u32[]{:S(2)}) collective-permute-start(bf16[48,4096]{1,0:T(8,128)(2,1)S(1)} %collective-permute-done.1.f0), channel_id=1, source_target_pairs={{0,192},{64,0},{128,64},{192,128},{1,193},{65,1},{129,65},{193,129... | collective-permute-start | bytes 1179656 | tf_op jit(solution)/shard_map/ppermute | solution.py:324
  27.9 10.5 %collective-permute-start.2 = (bf16[48,4096]{1,0:T(8,128)(2,1)S(1)}, bf16[48,4096]{1,0:T(8,128)(2,1)S(1)}, u32[]{:S(2)}, u32[]{:S(2)}) collective-permute-start(bf16[48,4096]{1,0:T(8,128)(2,1)S(1)} %collective-permute-done.1.f0), channel_id=1, source_target_pairs={{0,64},{64,128},{128,192},{192,0},{1,65},{65,129},{129,193},{193,1... | collective-permute-start | bytes 1179656 | tf_op jit(solution)/shard_map/ppermute | solution.py:323
  40.0 15.5 %collective-permute-start.5 = (bf16[1024,256]{1,0:T(8,128)(2,1)S(1)}, bf16[1024,256]{1,0:T(8,128)(2,1)S(1)}, u32[]{:S(2)}, u32[]{:S(2)}) collective-permute-start(bf16[1024,256]{1,0:T(8,128)(2,1)S(1)} %mix.1.a0), channel_id=1, source_target_pairs={{0,2},{2,0},{1,3},{3,1},{4,6},{6,4},{5,7},{7,5},{8,10},{10,8},{9,1... | collective-permute-start | bytes 1572872 | tf_op jit(solution)/shard_map/ppermute | solution.py:337
  43.5 12.0 %collective-permute-start.8 = (bf16[48,4096]{1,0:T(8,128)(2,1)S(1)}, bf16[48,4096]{1,0:T(8,128)(2,1)S(1)}, u32[]{:S(2)}, u32[]{:S(2)}) collective-permute-start(bf16[48,4096]{1,0:T(8,128)(2,1)S(1)} %collective-permute-done.1.f0), channel_id=1, source_target_pairs={{0,128},{64,192},{128,0},{192,64},{1,129},{65,193},{129,1},{193,65... | collective-permute-start | bytes 1179656 | tf_op jit(solution)/shard_map/ppermute | solution.py:326
  44.9 4.6 %collective-permute-start.6 = (bf16[1024,256]{1,0:T(8,128)(2,1)S(1)}, bf16[1024,256]{1,0:T(8,128)(2,1)S(1)}, u32[]{:S(2)}, u32[]{:S(2)}) collective-permute-start(bf16[1024,256]{1,0:T(8,128)(2,1)S(1)} %mix.1.a0), channel_id=1, source_target_pairs={{0,1},{1,0},{2,3},{3,2},{4,5},{5,4},{6,7},{7,6},{8,9},{9,8},{10,11... | collective-permute-start | bytes 1572872 | tf_op jit(solution)/shard_map/ppermute | solution.py:240
  48.0 3.0 %collective-permute-start.7 = (bf16[256,2048]{1,0:T(8,128)(2,1)S(1)}, bf16[256,2048]{1,0:T(8,128)(2,1)S(1)}, u32[]{:S(2)}, u32[]{:S(2)}) collective-permute-start(bf16[256,2048]{1,0:T(8,128)(2,1)S(1)} %constant_dynamic-slice_fusion.5), channel_id=1, source_target_pairs={{0,1},{1,0},{2,3},{3,2},{4,5},{5,4},{6,7},{7,6},{8,9},{9,8},{10,11... | collective-permute-start | bytes 3145736 | tf_op jit(solution)/shard_map/ppermute | solution.py:240
  48.3 8.6 %collective-permute-start.10 = (bf16[208,2048]{1,0:T(8,128)(2,1)S(1)}, bf16[208,2048]{1,0:T(8,128)(2,1)S(1)}, u32[]{:S(2)}, u32[]{:S(2)}) collective-permute-start(bf16[208,2048]{1,0:T(8,128)(2,1)S(1)} %pad_maximum_fusion), channel_id=1, source_target_pairs={{0,1},{1,0},{2,3},{3,2},{4,5},{5,4},{6,7},{7,6},{8,9},{9,8},{10,11... | collective-permute-start | bytes 2555912 | tf_op jit(solution)/shard_map/ppermute | solution.py:240
  55.5 2.9 %collective-permute-start.9 = (bf16[1024,256]{1,0:T(8,128)(2,1)S(1)}, bf16[1024,256]{1,0:T(8,128)(2,1)S(1)}, u32[]{:S(2)}, u32[]{:S(2)}) collective-permute-start(bf16[1024,256]{1,0:T(8,128)(2,1)S(1)} %collective-permute-done.5.a2), channel_id=1, source_target_pairs={{0,1},{1,0},{2,3},{3,2},{4,5},{5,4},{6,7},{7,6},{8,9},{9,8},{10,11... | collective-permute-start | bytes 1572872 | tf_op jit(solution)/shard_map/ppermute | solution.py:240
  56.6 1.8 %collective-permute-start.11 = (bf16[48,2048]{1,0:T(8,128)(2,1)S(1)}, bf16[48,2048]{1,0:T(8,128)(2,1)S(1)}, u32[]{:S(2)}, u32[]{:S(2)}) collective-permute-start(bf16[48,2048]{1,0:T(8,128)(2,1)S(1)} %constant_dynamic-slice_fusion), channel_id=1, source_target_pairs={{0,1},{1,0},{2,3},{3,2},{4,5},{5,4},{6,7},{7,6},{8,9},{9,8},{10,11... | collective-permute-start | bytes 589832 | tf_op jit(solution)/shard_map/ppermute | solution.py:240
  120.5 7.5 %collective-permute-start.14 = (bf16[32,2048]{1,0:T(8,128)(2,1)S(1)}, bf16[32,2048]{1,0:T(8,128)(2,1)S(1)}, u32[]{:S(2)}, u32[]{:S(2)}) collective-permute-start(bf16[32,2048]{1,0:T(8,128)(2,1)S(1)} %get-tuple-element.47), channel_id=1, source_target_pairs={{0,3},{1,2},{2,1},{3,0},{4,7},{5,6},{6,5},{7,4},{8,11},{9,10},{10,... | collective-permute-start | bytes 393224 | tf_op jit(solution)/shard_map/ppermute | solution.py:401
  123.8 6.8 %collective-permute-start.13 = (bf16[32,2048]{1,0:T(8,128)(2,1)S(1)}, bf16[32,2048]{1,0:T(8,128)(2,1)S(1)}, u32[]{:S(2)}, u32[]{:S(2)}) collective-permute-start(bf16[32,2048]{1,0:T(8,128)(2,1)S(1)} %get-tuple-element.48), channel_id=1, source_target_pairs={{0,2},{1,3},{2,0},{3,1},{4,6},{5,7},{6,4},{7,5},{8,10},{9,11},{10,... | collective-permute-start | bytes 393224 | tf_op jit(solution)/shard_map/ppermute | solution.py:401
  124.1 6.5 %collective-permute-start.12 = (bf16[32,2048]{1,0:T(8,128)(2,1)S(1)}, bf16[32,2048]{1,0:T(8,128)(2,1)S(1)}, u32[]{:S(2)}, u32[]{:S(2)}) collective-permute-start(bf16[32,2048]{1,0:T(8,128)(2,1)S(1)} %get-tuple-element.49), channel_id=1, source_target_pairs={{0,1},{1,0},{2,3},{3,2},{4,5},{5,4},{6,7},{7,6},{8,9},{9,8},{10,11... | collective-permute-start | bytes 393224 | tf_op jit(solution)/shard_map/ppermute | solution.py:401
Sparse Core Ops, SparseCore 0:
  63.9 55.4 reduce-scatter.1

commit v12 on v11

--- a/solution.py
+++ b/solution.py
@@ -262,7 +262,7 @@
     rest = lax.ppermute(there(out_weight, 4 * size, tail), ("xl", "xh"), mirror)
 
     flat = groups * MODES
-    span = 256
+    span = 512
     once = {"pipeline_mode": pl.Buffered(1)}
 
     def whole(shape):

time: 139 us -> 139 us (level)
  no operation moved by 1% of the time
where the time goes in v12:
time: 139 us; the launch traced here: 138 us
  waiting for transfers between devices  71.6 us (52%)
  starting transfers between devices  25.9 us (19%)
  Pallas kernels  21.8 us (16%)
  between operations  13.6 us (10%)
  local copies, waits for them, and re-layouts  5.36 us (4%)
    reduce_scatter x1, waiting for transfers between devices, local(): summed = lax.psum_scatter(partial, 'z', scatter_dimension=0, tiled=True)  55.8 us
    ppermute x3, waiting for transfers between devices, traded(): return lax.ppermute(summed[k * size:(k + 1) * size], ('xh', 'c'), pairs)  6.33 us
    pallas_call x1, Pallas kernels, local(): pl.pallas_call(far_kernel, out_shape=pltpu.HBM((rows, width), BF), grid_s...  5.35 us
    pallas_call x1, Pallas kernels, local(): pl.pallas_call(conv_kernel, out_shape=(pltpu.HBM((rows, channels), BF), p...  5.04 us
    ppermute x5, starting transfers between devices, other_core(): return lax.ppermute(value, 'c', [(0, 1), (1, 0)])  4.79 us
    pallas_call x1, Pallas kernels, local(): pl.pallas_call(near_kernel, out_shape=jax.ShapeDtypeStruct((rows, width),...  4.48 us
    pallas_call x1, Pallas kernels, local(): pl.pallas_call(state_kernel, out_shape=(pltpu.HBM((rows, channels), BF),...  4.04 us
    all_to_all x1, starting transfers between devices, local(): ends = lax.all_to_all(end, ('y', 'xl'), 0, 0, tiled=True)  4.01 us
  transfers between devices with their start and end apart: 17, of which 9 were waited for; matrix products, arithmetic and copies ran while one was open for 3% of the time, Pallas kernels for 10%

profile of v12, /device:TPU:1, one launch (start us, length us, event | category | flops | bytes accessed | tf_op | source)
XLA Modules:
  0.0 138.4 jit_solution(16798283813322861213)
XLA Ops:
  6.5 0.7 slice.15
  7.2 3.9 %collective-permute-start = (bf16[3,8,256]{2,1,0:T(8,128)(2,1)S(1)}, bf16[3,8,256]{2,1,0:T(8,128)(2,1)S(1)}, u32[]{:S(2)}, u32[]{:S(2)}) collective-permute-start(bf16[3,8,256]{2,1,0:T(8,128)(2,1)S(1)} %slice.15), channel_id=1, source_target_pairs={{0,32},{32,64},{64,96},{96,128},{128,160},{160,192},{192,224},{1,3... | collective-permute-start | bytes 36872 | tf_op jit(solution)/shard_map/ppermute | solution.py:251
  11.2 1.0 dynamic_slice.24
  12.2 2.9 %collective-permute-start.1 = (bf16[48,4096]{1,0:T(8,128)(2,1)S(1)}, bf16[48,4096]{1,0:T(8,128)(2,1)S(1)}, u32[]{:S(2)}, u32[]{:S(2)}) collective-permute-start(bf16[48,4096]{1,0:T(8,128)(2,1)S(1)} %dynamic_slice.24), channel_id=1, source_target_pairs={{0,34},{34,0},{2,32},{32,2},{1,35},{35,1},{3,33},{33,3},{4,38},{38... | collective-permute-start | bytes 1179656 | tf_op jit(solution)/shard_map/ppermute | solution.py:261
  15.1 1.1 constant_dynamic-slice_fusion.6
  16.2 0.1 collective-permute-start.4
  16.3 0.1 pad_add_fusion.at_ref
  16.4 0.0 collective-permute-done.halo_ref
  16.4 4.0 %state.1 = (bf16[1024,256]{1,0:T(8,128)(2,1)}, f32[8,16,256]{2,1,0:T(8,128)}, f32[16,256]{1,0:T(8,128)S(1)}) custom-call(bf16[3,1024,256]{2,1,0:T(8,128)(2,1)} %p_ref.1, bf16[3,1024,256]{2,1,0:T(8,128)(2,1)} %p_ref.1, bf16[3,8,256]{2,1,0:T(8,128)(2,1)S(1)} %collective-permute-done.halo_ref, f32[3,3,256]{2,1,0:T(4,128)} %sf_ref.3, f32[16,16]{1,0:T(8,128)} %rate_ref.3), custom_call_target="tpu_custom_call" | custom-call | flops 1000000 | bytes 65536 | tf_op jit(solution)/shard_map/state/pallas_call | solution.py:274
  20.5 4.0 %all-to-all-start = ((f32[8,16,256]{2,1,0:T(8,128)}), f32[8,16,256]{2,1,0:T(8,128)S(1)}, u32[]{:S(2)}, u32[]{:S(2)}) async-start(f32[8,16,256]{2,1,0:T(8,128)} %get-tuple-element.28), calls=%async_computation | async-start | bytes 262144 | tf_op jit(solution)/shard_map/all_to_all | solution.py:300
  24.5 0.0 reduce-scatter.2.cloned.1.call-start
  24.6 0.0 collective-permute-done.1.f0
  24.6 2.7 %collective-permute-start.3 = (bf16[48,4096]{1,0:T(8,128)(2,1)S(1)}, bf16[48,4096]{1,0:T(8,128)(2,1)S(1)}, u32[]{:S(2)}, u32[]{:S(2)}) collective-permute-start(bf16[48,4096]{1,0:T(8,128)(2,1)S(1)} %collective-permute-done.1.f0), channel_id=1, source_target_pairs={{0,192},{64,0},{128,64},{192,128},{1,193},{65,1},{129,65},{193,129... | collective-permute-start | bytes 1179656 | tf_op jit(solution)/shard_map/ppermute | solution.py:324
  27.3 0.0 collective-permute-start.2
  27.3 5.0 %conv.1 = (bf16[1024,256]{1,0:T(8,128)(2,1)}, bf16[1024,256]{1,0:T(8,128)(2,1)}, bf16[128,256]{1,0:T(8,128)(2,1)S(1)}) custom-call(bf16[3,1024,256]{2,1,0:T(8,128)(2,1)} %p_ref.1, bf16[1024,256]{1,0:T(8,128)(2,1)} %get-tuple-element.32.x_ref, bf16[3,8,256]{2,1,0:T(8,128)(2,1)S(1)} %collective-permute-done.halo_ref, f32[3,3,256]{2,1,0:T(4,128)} %sf_ref.3, ...), custom_call_target="tpu_custom_call" | custom-call | flops 6000000000 | bytes 65536 | tf_op jit(solution)/shard_map/conv/pallas_call | solution.py:301
  32.3 0.0 all-to-all-done.ends_ref
  32.3 2.4 %collective-permute-done.4.rest = bf16[64,4096]{1,0:T(8,128)(2,1)S(1)} collective-permute-done((bf16[64,4096]{1,0:T(8,128)(2,1)S(1)}, bf16[64,4096]{1,0:T(8,128)(2,1)S(1)}, u32[]{:S(2)}, u32[]{:S(2)}) %collective-permute-start.4) | collective-permute-done | bytes 524320 | tf_op jit(solution)/shard_map/ppermute | solution.py:262
  34.8 0.5 collective-permute-done.3.f3
  35.3 2.5 %collective-permute-done.2.f1 = bf16[48,4096]{1,0:T(8,128)(2,1)S(1)} collective-permute-done((bf16[48,4096]{1,0:T(8,128)(2,1)S(1)}, bf16[48,4096]{1,0:T(8,128)(2,1)S(1)}, u32[]{:S(2)}, u32[]{:S(2)}) %collective-permute-start.2) | collective-permute-done | bytes 393248 | tf_op jit(solution)/shard_map/ppermute | solution.py:323
  37.8 1.6 %mix.1.a0 = bf16[1024,256]{1,0:T(8,128)(2,1)S(1)} custom-call(s32[4]{0:T(128)S(1)} %pad_add_fusion.at_ref, f32[8,16,256]{2,1,0:T(8,128)S(1)} %all-to-all-done.ends_ref, f32[16,256]{1,0:T(8,128)S(1)} %get-tuple-element.31.rt_ref, bf16[128,256]{1,0:T(8,128)(2,1)S(1)} %get-tuple-element.34.din_ref, bf16[1024,256]{1,0:T(8,128)(2,1)} %get-tuple-element.35.y_ref, ...), custom_call_target="tpu_custom_call" | custom-call | flops 1000000 | bytes 65536 | tf_op jit(solution)/shard_map/mix/pallas_call | solution.py:327
  39.4 3.5 %collective-permute-start.5 = (bf16[1024,256]{1,0:T(8,128)(2,1)S(1)}, bf16[1024,256]{1,0:T(8,128)(2,1)S(1)}, u32[]{:S(2)}, u32[]{:S(2)}) collective-permute-start(bf16[1024,256]{1,0:T(8,128)(2,1)S(1)} %mix.1.a0), channel_id=1, source_target_pairs={{0,2},{2,0},{1,3},{3,1},{4,6},{6,4},{5,7},{7,5},{8,10},{10,8},{9,1... | collective-permute-start | bytes 1572872 | tf_op jit(solution)/shard_map/ppermute | solution.py:337
  42.9 0.1 collective-permute-start.8
  43.0 1.3 constant_dynamic-slice_fusion.5
  44.3 3.1 %collective-permute-start.6 = (bf16[1024,256]{1,0:T(8,128)(2,1)S(1)}, bf16[1024,256]{1,0:T(8,128)(2,1)S(1)}, u32[]{:S(2)}, u32[]{:S(2)}) collective-permute-start(bf16[1024,256]{1,0:T(8,128)(2,1)S(1)} %mix.1.a0), channel_id=1, source_target_pairs={{0,1},{1,0},{2,3},{3,2},{4,5},{5,4},{6,7},{7,6},{8,9},{9,8},{10,11... | collective-permute-start | bytes 1572872 | tf_op jit(solution)/shard_map/ppermute | solution.py:240
  47.4 0.1 collective-permute-start.7
  47.6 0.1 pad_maximum_fusion
  47.6 0.5 collective-permute-start.10
  48.1 0.8 collective-permute-done.6.a1
  48.9 1.5 %collective-permute-done.7.w1 = bf16[256,2048]{1,0:T(8,128)(2,1)S(1)} collective-permute-done((bf16[256,2048]{1,0:T(8,128)(2,1)S(1)}, bf16[256,2048]{1,0:T(8,128)(2,1)S(1)}, u32[]{:S(2)}, u32[]{:S(2)}) %collective-permute-start.7) | collective-permute-done | bytes 1048608 | tf_op jit(solution)/shard_map/ppermute | solution.py:240
  50.4 4.5 %near.1.near_ref = bf16[1024,2048]{1,0:T(8,128)(2,1)S(1)} custom-call(s32[4]{0:T(128)S(1)} %pad_add_fusion.at_ref, bf16[1024,256]{1,0:T(8,128)(2,1)S(1)} %mix.1.a0, bf16[1024,256]{1,0:T(8,128)(2,1)S(1)} %collective-permute-done.6.a1, bf16[256,8192]{1,0:T(8,128)(2,1)} %w0.1, bf16[256,2048]{1,0:T(8,128)(2,1)S(1)} %collective-permute-done.7.w1), custom_call_target="tpu_custom_call" | custom-call | flops 2000000000 | bytes 6291456 | tf_op jit(solution)/shard_map/near/pallas_call | solution.py:360
  54.9 0.0 collective-permute-done.8.f2
  54.9 0.0 collective-permute-done.5.a2
  54.9 1.0 collective-permute-start.9
  56.0 0.1 collective-permute-start.11
  56.1 0.0 collective-permute-done.10.g013
  56.1 1.7 %collective-permute-done.11.g2 = bf16[48,2048]{1,0:T(8,128)(2,1)S(1)} collective-permute-done((bf16[48,2048]{1,0:T(8,128)(2,1)S(1)}, bf16[48,2048]{1,0:T(8,128)(2,1)S(1)}, u32[]{:S(2)}, u32[]{:S(2)}) %collective-permute-start.11) | collective-permute-done | bytes 196640 | tf_op jit(solution)/shard_map/ppermute | solution.py:240
  57.8 0.0 collective-permute-done.9.a3
  57.8 5.3 %far.1 = bf16[1024,2048]{1,0:T(8,128)(2,1)} custom-call(s32[4]{0:T(128)S(1)} %pad_add_fusion.at_ref, bf16[1024,256]{1,0:T(8,128)(2,1)S(1)} %collective-permute-done.5.a2, bf16[1024,256]{1,0:T(8,128)(2,1)S(1)} %collective-permute-done.9.a3, bf16[48,4096]{1,0:T(8,128)(2,1)S(1)} %collective-permute-done.1.f0, bf16[48,4096]{1,0:T(8,128)(2,1)S(1)} %collective-permute-done.2.f1, ...), custom_call_target="tpu_custom_call" | custom-call | flops 2000000000 | bytes 10485760 | tf_op jit(solution)/shard_map/far/pallas_call | solution.py:378
  63.1 0.0 reduce-scatter.2.cloned.1.call-update
  63.1 55.8 %reduce-scatter.2.cloned.1.call-done = bf16[128,2048]{1,0:T(8,128)(2,1)} async-done(((bf16[1024,2048]{1,0:T(8,128)(2,1)}), bf16[128,2048]{1,0:T(8,128)(2,1)}) %reduce-scatter.2.cloned.1.call-update) | async-done | bytes 524304 | tf_op jit(solution)/shard_map/reduce_scatter | solution.py:396
  118.9 1.1 fusion
  120.0 3.3 %collective-permute-start.14 = (bf16[32,2048]{1,0:T(8,128)(2,1)S(1)}, bf16[32,2048]{1,0:T(8,128)(2,1)S(1)}, u32[]{:S(2)}, u32[]{:S(2)}) collective-permute-start(bf16[32,2048]{1,0:T(8,128)(2,1)S(1)} %get-tuple-element.47), channel_id=1, source_target_pairs={{0,3},{1,2},{2,1},{3,0},{4,7},{5,6},{6,5},{7,4},{8,11},{9,10},{10,... | collective-permute-start | bytes 393224 | tf_op jit(solution)/shard_map/ppermute | solution.py:401
  123.3 0.3 collective-permute-start.13
  123.6 0.2 collective-permute-start.12
  123.8 3.8 %collective-permute-done.14.p3 = bf16[32,2048]{1,0:T(8,128)(2,1)S(1)} collective-permute-done((bf16[32,2048]{1,0:T(8,128)(2,1)S(1)}, bf16[32,2048]{1,0:T(8,128)(2,1)S(1)}, u32[]{:S(2)}, u32[]{:S(2)}) %collective-permute-start.14) | collective-permute-done | bytes 131104 | tf_op jit(solution)/shard_map/ppermute | solution.py:401
  127.6 2.6 %collective-permute-done.13.p2 = bf16[32,2048]{1,0:T(8,128)(2,1)S(1)} collective-permute-done((bf16[32,2048]{1,0:T(8,128)(2,1)S(1)}, bf16[32,2048]{1,0:T(8,128)(2,1)S(1)}, u32[]{:S(2)}, u32[]{:S(2)}) %collective-permute-start.13) | collective-permute-done | bytes 131104 | tf_op jit(solution)/shard_map/ppermute | solution.py:401
  130.2 0.0 collective-permute-done.12.p1
  130.2 1.4 join.1
  (9 shorter events, 0.1 us)
Async XLA Ops:
  7.2 9.2 %collective-permute-start = (bf16[3,8,256]{2,1,0:T(8,128)(2,1)S(1)}, bf16[3,8,256]{2,1,0:T(8,128)(2,1)S(1)}, u32[]{:S(2)}, u32[]{:S(2)}) collective-permute-start(bf16[3,8,256]{2,1,0:T(8,128)(2,1)S(1)} %slice.15), channel_id=1, source_target_pairs={{0,32},{32,64},{64,96},{96,128},{128,160},{160,192},{192,224},{1,3... | collective-permute-start | bytes 36872 | tf_op jit(solution)/shard_map/ppermute | solution.py:251
  12.2 12.3 %collective-permute-start.1 = (bf16[48,4096]{1,0:T(8,128)(2,1)S(1)}, bf16[48,4096]{1,0:T(8,128)(2,1)S(1)}, u32[]{:S(2)}, u32[]{:S(2)}) collective-permute-start(bf16[48,4096]{1,0:T(8,128)(2,1)S(1)} %dynamic_slice.24), channel_id=1, source_target_pairs={{0,34},{34,0},{2,32},{32,2},{1,35},{35,1},{3,33},{33,3},{4,38},{38... | collective-permute-start | bytes 1179656 | tf_op jit(solution)/shard_map/ppermute | solution.py:261
  16.2 18.5 %collective-permute-start.4 = (bf16[64,4096]{1,0:T(8,128)(2,1)S(1)}, bf16[64,4096]{1,0:T(8,128)(2,1)S(1)}, u32[]{:S(2)}, u32[]{:S(2)}) collective-permute-start(bf16[64,4096]{1,0:T(8,128)(2,1)S(1)} %constant_dynamic-slice_fusion.6), channel_id=1, source_target_pairs={{0,34},{34,0},{2,32},{32,2},{1,35},{35,1},{3,33},{33,3},{4,38},{38... | collective-permute-start | bytes 1572872 | tf_op jit(solution)/shard_map/ppermute | solution.py:262
  16.4 8.1 %copy-start = (f32[16,16]{1,0:T(8,128)S(1)}, f32[16,16]{1,0:T(8,128)}, u32[]{:S(2)}) copy-start(f32[16,16]{1,0:T(8,128)} %rate_ref.3) | copy-start | bytes 3076
  16.4 8.1 %copy-start.1 = (f32[16,16]{1,0:T(8,128)S(1)}, f32[16,16]{1,0:T(8,128)}, u32[]{:S(2)}) copy-start(f32[16,16]{1,0:T(8,128)} %param.7) | copy-start | bytes 3076
  20.5 11.9 %all-to-all-start = ((f32[8,16,256]{2,1,0:T(8,128)}), f32[8,16,256]{2,1,0:T(8,128)S(1)}, u32[]{:S(2)}, u32[]{:S(2)}) async-start(f32[8,16,256]{2,1,0:T(8,128)} %get-tuple-element.28), calls=%async_computation | async-start | bytes 262144 | tf_op jit(solution)/shard_map/all_to_all | solution.py:300
  24.5 94.4 %reduce-scatter.2.cloned.1.call-start = ((), (), s32[]{:S(2)}) async-start(), calls=%async_computation.2 | async-start | bytes 4718592 | tf_op jit(solution)/shard_map/reduce_scatter | solution.py:396
  24.6 10.7 %collective-permute-start.3 = (bf16[48,4096]{1,0:T(8,128)(2,1)S(1)}, bf16[48,4096]{1,0:T(8,128)(2,1)S(1)}, u32[]{:S(2)}, u32[]{:S(2)}) collective-permute-start(bf16[48,4096]{1,0:T(8,128)(2,1)S(1)} %collective-permute-done.1.f0), channel_id=1, source_target_pairs={{0,192},{64,0},{128,64},{192,128},{1,193},{65,1},{129,65},{193,129... | collective-permute-start | bytes 1179656 | tf_op jit(solution)/shard_map/ppermute | solution.py:324
  27.3 10.5 %collective-permute-start.2 = (bf16[48,4096]{1,0:T(8,128)(2,1)S(1)}, bf16[48,4096]{1,0:T(8,128)(2,1)S(1)}, u32[]{:S(2)}, u32[]{:S(2)}) collective-permute-start(bf16[48,4096]{1,0:T(8,128)(2,1)S(1)} %collective-permute-done.1.f0), channel_id=1, source_target_pairs={{0,64},{64,128},{128,192},{192,0},{1,65},{65,129},{129,193},{193,1... | collective-permute-start | bytes 1179656 | tf_op jit(solution)/shard_map/ppermute | solution.py:323
  39.4 15.5 %collective-permute-start.5 = (bf16[1024,256]{1,0:T(8,128)(2,1)S(1)}, bf16[1024,256]{1,0:T(8,128)(2,1)S(1)}, u32[]{:S(2)}, u32[]{:S(2)}) collective-permute-start(bf16[1024,256]{1,0:T(8,128)(2,1)S(1)} %mix.1.a0), channel_id=1, source_target_pairs={{0,2},{2,0},{1,3},{3,1},{4,6},{6,4},{5,7},{7,5},{8,10},{10,8},{9,1... | collective-permute-start | bytes 1572872 | tf_op jit(solution)/shard_map/ppermute | solution.py:337
  42.9 12.0 %collective-permute-start.8 = (bf16[48,4096]{1,0:T(8,128)(2,1)S(1)}, bf16[48,4096]{1,0:T(8,128)(2,1)S(1)}, u32[]{:S(2)}, u32[]{:S(2)}) collective-permute-start(bf16[48,4096]{1,0:T(8,128)(2,1)S(1)} %collective-permute-done.1.f0), channel_id=1, source_target_pairs={{0,128},{64,192},{128,0},{192,64},{1,129},{65,193},{129,1},{193,65... | collective-permute-start | bytes 1179656 | tf_op jit(solution)/shard_map/ppermute | solution.py:326
  44.3 4.6 %collective-permute-start.6 = (bf16[1024,256]{1,0:T(8,128)(2,1)S(1)}, bf16[1024,256]{1,0:T(8,128)(2,1)S(1)}, u32[]{:S(2)}, u32[]{:S(2)}) collective-permute-start(bf16[1024,256]{1,0:T(8,128)(2,1)S(1)} %mix.1.a0), channel_id=1, source_target_pairs={{0,1},{1,0},{2,3},{3,2},{4,5},{5,4},{6,7},{7,6},{8,9},{9,8},{10,11... | collective-permute-start | bytes 1572872 | tf_op jit(solution)/shard_map/ppermute | solution.py:240
  47.4 3.0 %collective-permute-start.7 = (bf16[256,2048]{1,0:T(8,128)(2,1)S(1)}, bf16[256,2048]{1,0:T(8,128)(2,1)S(1)}, u32[]{:S(2)}, u32[]{:S(2)}) collective-permute-start(bf16[256,2048]{1,0:T(8,128)(2,1)S(1)} %constant_dynamic-slice_fusion.5), channel_id=1, source_target_pairs={{0,1},{1,0},{2,3},{3,2},{4,5},{5,4},{6,7},{7,6},{8,9},{9,8},{10,11... | collective-permute-start | bytes 3145736 | tf_op jit(solution)/shard_map/ppermute | solution.py:240
  47.6 8.4 %collective-permute-start.10 = (bf16[208,2048]{1,0:T(8,128)(2,1)S(1)}, bf16[208,2048]{1,0:T(8,128)(2,1)S(1)}, u32[]{:S(2)}, u32[]{:S(2)}) collective-permute-start(bf16[208,2048]{1,0:T(8,128)(2,1)S(1)} %pad_maximum_fusion), channel_id=1, source_target_pairs={{0,1},{1,0},{2,3},{3,2},{4,5},{5,4},{6,7},{7,6},{8,9},{9,8},{10,11... | collective-permute-start | bytes 2555912 | tf_op jit(solution)/shard_map/ppermute | solution.py:240
  54.9 2.9 %collective-permute-start.9 = (bf16[1024,256]{1,0:T(8,128)(2,1)S(1)}, bf16[1024,256]{1,0:T(8,128)(2,1)S(1)}, u32[]{:S(2)}, u32[]{:S(2)}) collective-permute-start(bf16[1024,256]{1,0:T(8,128)(2,1)S(1)} %collective-permute-done.5.a2), channel_id=1, source_target_pairs={{0,1},{1,0},{2,3},{3,2},{4,5},{5,4},{6,7},{7,6},{8,9},{9,8},{10,11... | collective-permute-start | bytes 1572872 | tf_op jit(solution)/shard_map/ppermute | solution.py:240
  56.0 1.8 %collective-permute-start.11 = (bf16[48,2048]{1,0:T(8,128)(2,1)S(1)}, bf16[48,2048]{1,0:T(8,128)(2,1)S(1)}, u32[]{:S(2)}, u32[]{:S(2)}) collective-permute-start(bf16[48,2048]{1,0:T(8,128)(2,1)S(1)} %constant_dynamic-slice_fusion), channel_id=1, source_target_pairs={{0,1},{1,0},{2,3},{3,2},{4,5},{5,4},{6,7},{7,6},{8,9},{9,8},{10,11... | collective-permute-start | bytes 589832 | tf_op jit(solution)/shard_map/ppermute | solution.py:240
  120.0 7.5 %collective-permute-start.14 = (bf16[32,2048]{1,0:T(8,128)(2,1)S(1)}, bf16[32,2048]{1,0:T(8,128)(2,1)S(1)}, u32[]{:S(2)}, u32[]{:S(2)}) collective-permute-start(bf16[32,2048]{1,0:T(8,128)(2,1)S(1)} %get-tuple-element.47), channel_id=1, source_target_pairs={{0,3},{1,2},{2,1},{3,0},{4,7},{5,6},{6,5},{7,4},{8,11},{9,10},{10,... | collective-permute-start | bytes 393224 | tf_op jit(solution)/shard_map/ppermute | solution.py:401
  123.3 6.8 %collective-permute-start.13 = (bf16[32,2048]{1,0:T(8,128)(2,1)S(1)}, bf16[32,2048]{1,0:T(8,128)(2,1)S(1)}, u32[]{:S(2)}, u32[]{:S(2)}) collective-permute-start(bf16[32,2048]{1,0:T(8,128)(2,1)S(1)} %get-tuple-element.48), channel_id=1, source_target_pairs={{0,2},{1,3},{2,0},{3,1},{4,6},{5,7},{6,4},{7,5},{8,10},{9,11},{10,... | collective-permute-start | bytes 393224 | tf_op jit(solution)/shard_map/ppermute | solution.py:401
  123.6 6.6 %collective-permute-start.12 = (bf16[32,2048]{1,0:T(8,128)(2,1)S(1)}, bf16[32,2048]{1,0:T(8,128)(2,1)S(1)}, u32[]{:S(2)}, u32[]{:S(2)}) collective-permute-start(bf16[32,2048]{1,0:T(8,128)(2,1)S(1)} %get-tuple-element.49), channel_id=1, source_target_pairs={{0,1},{1,0},{2,3},{3,2},{4,5},{5,4},{6,7},{7,6},{8,9},{9,8},{10,11... | collective-permute-start | bytes 393224 | tf_op jit(solution)/shard_map/ppermute | solution.py:401
Sparse Core Ops, SparseCore 0:
  63.3 55.6 reduce-scatter.1

commit v13 on v11

--- a/solution.py
+++ b/solution.py
@@ -180,32 +180,20 @@
         state = power * state
 
 
-def side_by_side(left, refs):
-    depth = refs[0].shape[1]
-
-    @pl.when(pl.program_id(0) == 0)
-    def _():
-        for k, ref in enumerate(refs):
-            left[:, k * depth : (k + 1) * depth] = ref[...]
-
-
-def near_kernel(at_ref, a0, a1, w0, w1, c_ref, left, right):
-    depth = w0.shape[0]
-    side_by_side(left, (a0, a1))
-    right[0:depth] = w0[...]
-    right[depth : 2 * depth] = w1[...]
+def near_kernel(at_ref, a0, a1, w0, w1, c_ref):
     block = 256
-    for m in range(left.shape[0] // block):
+    for m in range(a0.shape[0] // block):
         span = slice(m * block, (m + 1) * block)
-        c_ref[span, :] = jnp.dot(left[span, :], right[...], preferred_element_type=F32).astype(BF)
-
-
-def far_kernel(at_ref, a2, a3, f0, f1, f2, f3, rest, g013, g2, near_ref, c_ref, left, right):
+        total = jnp.dot(a0[span, :], w0[...], preferred_element_type=F32)
+        total += jnp.dot(a1[span, :], w1[...], preferred_element_type=F32)
+        c_ref[span, :] = total.astype(BF)
+
+
+def far_kernel(at_ref, a2, a3, f0, f1, f2, f3, rest, g013, g2, near_ref, c_ref, right):
     y, mine = at_ref[1], at_ref[2]
     size = f0.shape[0]
     depth = right.shape[0] // 2
     tail = depth - 4 * size
-    side_by_side(left, (a2, a3))
     for k, ref in enumerate((f0, f1, f2, f3)):
         owner = lax.rem(y - k + 4, 4) * size
         right[pl.ds(pl.multiple_of(owner, 16), size), :] = ref[0:size]
@@ -214,9 +202,10 @@
     right[4 * size : depth] = rest[...]
     right[depth + 4 * size : 2 * depth] = g013[3 * size : 3 * size + tail]
     block = 256
-    for m in range(left.shape[0] // block):
+    for m in range(a2.shape[0] // block):
         span = slice(m * block, (m + 1) * block)
-        total = jnp.dot(left[span, :], right[...], preferred_element_type=F32)
+        total = jnp.dot(a2[span, :], right[0:depth], preferred_element_type=F32)
+        total += jnp.dot(a3[span, :], right[depth : 2 * depth], preferred_element_type=F32)
         total = (total + near_ref[span, :].astype(F32)).astype(BF)
         for b in range(block // 32):
             high, low = m * (block // 128) + b // 4, b % 4
@@ -366,7 +355,6 @@
             in_specs=left_specs
             + [pl.BlockSpec((channels, tile), lambda i, at_ref: (0, at_ref[2] * strips + i)), strip(w_other.shape)],
             out_specs=strip((rows, width)),
-            scratch_shapes=[pltpu.VMEM((rows, 2 * channels), BF), pltpu.VMEM((2 * channels, tile), BF)],
         ),
         compiler_params=pltpu.CompilerParams(vmem_limit_bytes=24 * 2**20),
         cost_estimate=pl.CostEstimate(flops=2 * 10**9, bytes_accessed=6 * 2**20, transcendentals=0),
@@ -386,7 +374,7 @@
             + [strip(g013.shape), strip(g2.shape)]
             + [strip((rows, width))],
             out_specs=strip((rows, width)),
-            scratch_shapes=[pltpu.VMEM((rows, 2 * channels), BF), pltpu.VMEM((2 * channels, tile), BF)],
+            scratch_shapes=[pltpu.VMEM((2 * channels, tile), BF)],
         ),
         compiler_params=pltpu.CompilerParams(vmem_limit_bytes=30 * 2**20),
         cost_estimate=pl.CostEstimate(flops=2 * 10**9, bytes_accessed=10 * 2**20, transcendentals=0),

time: 139 us -> 139 us (level)
  no operation moved by 1% of the time
where the time goes in v13:
time: 139 us
  waiting for transfers between devices  71.2 us (51%)
  starting transfers between devices  26.1 us (19%)
  Pallas kernels  22.3 us (16%)
  between operations  13.6 us (10%)
  local copies, waits for them, and re-layouts  5.36 us (4%)
    reduce_scatter x1, waiting for transfers between devices, local(): summed = lax.psum_scatter(partial, 'z', scatter_dimension=0, tiled=True)  55.6 us
    ppermute x3, waiting for transfers between devices, traded(): return lax.ppermute(summed[k * size:(k + 1) * size], ('xh', 'c'), pairs)  6.34 us
    pallas_call x1, Pallas kernels, local(): pl.pallas_call(far_kernel, out_shape=pltpu.HBM((rows, width), BF), grid_s...  5.26 us
    ppermute x5, starting transfers between devices, other_core(): return lax.ppermute(value, 'c', [(0, 1), (1, 0)])  5.04 us
    pallas_call x1, Pallas kernels, local(): pl.pallas_call(conv_kernel, out_shape=(pltpu.HBM((rows, channels), BF), p...  5.04 us
    pallas_call x1, Pallas kernels, local(): pl.pallas_call(state_kernel, out_shape=(pltpu.HBM((rows, channels), BF),...  4.68 us
    pallas_call x1, Pallas kernels, local(): pl.pallas_call(near_kernel, out_shape=jax.ShapeDtypeStruct((rows, width),...  4.4 us
    all_to_all x1, starting transfers between devices, local(): ends = lax.all_to_all(end, ('y', 'xl'), 0, 0, tiled=True)  4.01 us
  transfers between devices with their start and end apart: 17, of which 9 were waited for; matrix products, arithmetic and copies ran while one was open for 3% of the time, Pallas kernels for 10%

profile of v13, /device:TPU:1, one launch (start us, length us, event | category | flops | bytes accessed | tf_op | source)
XLA Modules:
  0.0 138.8 jit_solution(5124145785609873097)
XLA Ops:
  6.5 0.7 slice.15
  7.2 3.9 %collective-permute-start = (bf16[3,8,256]{2,1,0:T(8,128)(2,1)S(1)}, bf16[3,8,256]{2,1,0:T(8,128)(2,1)S(1)}, u32[]{:S(2)}, u32[]{:S(2)}) collective-permute-start(bf16[3,8,256]{2,1,0:T(8,128)(2,1)S(1)} %slice.15), channel_id=1, source_target_pairs={{0,32},{32,64},{64,96},{96,128},{128,160},{160,192},{192,224},{1,3... | collective-permute-start | bytes 36872 | tf_op jit(solution)/shard_map/ppermute | solution.py:240
  11.2 1.0 dynamic_slice.24
  12.2 2.9 %collective-permute-start.1 = (bf16[48,4096]{1,0:T(8,128)(2,1)S(1)}, bf16[48,4096]{1,0:T(8,128)(2,1)S(1)}, u32[]{:S(2)}, u32[]{:S(2)}) collective-permute-start(bf16[48,4096]{1,0:T(8,128)(2,1)S(1)} %dynamic_slice.24), channel_id=1, source_target_pairs={{0,34},{34,0},{2,32},{32,2},{1,35},{35,1},{3,33},{33,3},{4,38},{38... | collective-permute-start | bytes 1179656 | tf_op jit(solution)/shard_map/ppermute | solution.py:250
  15.1 1.1 constant_dynamic-slice_fusion.6
  16.2 0.1 collective-permute-start.4
  16.3 0.1 pad_add_fusion.at_ref
  16.4 0.0 collective-permute-done.halo_ref
  16.4 4.7 %state.1 = (bf16[1024,256]{1,0:T(8,128)(2,1)}, f32[8,16,256]{2,1,0:T(8,128)}, f32[16,256]{1,0:T(8,128)S(1)}) custom-call(bf16[3,1024,256]{2,1,0:T(8,128)(2,1)} %p_ref.1, bf16[3,1024,256]{2,1,0:T(8,128)(2,1)} %p_ref.1, bf16[3,8,256]{2,1,0:T(8,128)(2,1)S(1)} %collective-permute-done.halo_ref, f32[3,3,256]{2,1,0:T(4,128)} %sf_ref.3, f32[16,16]{1,0:T(8,128)} %rate_ref.3), custom_call_target="tpu_custom_call" | custom-call | flops 1000000 | bytes 65536 | tf_op jit(solution)/shard_map/state/pallas_call | solution.py:263
  21.1 4.0 %all-to-all-start = ((f32[8,16,256]{2,1,0:T(8,128)}), f32[8,16,256]{2,1,0:T(8,128)S(1)}, u32[]{:S(2)}, u32[]{:S(2)}) async-start(f32[8,16,256]{2,1,0:T(8,128)} %get-tuple-element.28), calls=%async_computation | async-start | bytes 262144 | tf_op jit(solution)/shard_map/all_to_all | solution.py:289
  25.1 0.0 reduce-scatter.2.cloned.1.call-start
  25.2 0.0 collective-permute-done.1.f0
  25.2 2.7 %collective-permute-start.3 = (bf16[48,4096]{1,0:T(8,128)(2,1)S(1)}, bf16[48,4096]{1,0:T(8,128)(2,1)S(1)}, u32[]{:S(2)}, u32[]{:S(2)}) collective-permute-start(bf16[48,4096]{1,0:T(8,128)(2,1)S(1)} %collective-permute-done.1.f0), channel_id=1, source_target_pairs={{0,192},{64,0},{128,64},{192,128},{1,193},{65,1},{129,65},{193,129... | collective-permute-start | bytes 1179656 | tf_op jit(solution)/shard_map/ppermute | solution.py:313
  27.9 0.0 collective-permute-start.2
  27.9 5.0 %conv.1 = (bf16[1024,256]{1,0:T(8,128)(2,1)}, bf16[1024,256]{1,0:T(8,128)(2,1)}, bf16[128,256]{1,0:T(8,128)(2,1)S(1)}) custom-call(bf16[3,1024,256]{2,1,0:T(8,128)(2,1)} %p_ref.1, bf16[1024,256]{1,0:T(8,128)(2,1)} %get-tuple-element.32.x_ref, bf16[3,8,256]{2,1,0:T(8,128)(2,1)S(1)} %collective-permute-done.halo_ref, f32[3,3,256]{2,1,0:T(4,128)} %sf_ref.3, ...), custom_call_target="tpu_custom_call" | custom-call | flops 6000000000 | bytes 65536 | tf_op jit(solution)/shard_map/conv/pallas_call | solution.py:290
  33.0 0.0 all-to-all-done.ends_ref
  33.0 1.8 %collective-permute-done.4.rest = bf16[64,4096]{1,0:T(8,128)(2,1)S(1)} collective-permute-done((bf16[64,4096]{1,0:T(8,128)(2,1)S(1)}, bf16[64,4096]{1,0:T(8,128)(2,1)S(1)}, u32[]{:S(2)}, u32[]{:S(2)}) %collective-permute-start.4) | collective-permute-done | bytes 524320 | tf_op jit(solution)/shard_map/ppermute | solution.py:251
  34.8 1.1 collective-permute-done.3.f3
  35.9 2.5 %collective-permute-done.2.f1 = bf16[48,4096]{1,0:T(8,128)(2,1)S(1)} collective-permute-done((bf16[48,4096]{1,0:T(8,128)(2,1)S(1)}, bf16[48,4096]{1,0:T(8,128)(2,1)S(1)}, u32[]{:S(2)}, u32[]{:S(2)}) %collective-permute-start.2) | collective-permute-done | bytes 393248 | tf_op jit(solution)/shard_map/ppermute | solution.py:312
  38.4 1.6 %mix.1.a0 = bf16[1024,256]{1,0:T(8,128)(2,1)S(1)} custom-call(s32[4]{0:T(128)S(1)} %pad_add_fusion.at_ref, f32[8,16,256]{2,1,0:T(8,128)S(1)} %all-to-all-done.ends_ref, f32[16,256]{1,0:T(8,128)S(1)} %get-tuple-element.31.rt_ref, bf16[128,256]{1,0:T(8,128)(2,1)S(1)} %get-tuple-element.34.din_ref, bf16[1024,256]{1,0:T(8,128)(2,1)} %get-tuple-element.35.y_ref, ...), custom_call_target="tpu_custom_call" | custom-call | flops 1000000 | bytes 65536 | tf_op jit(solution)/shard_map/mix/pallas_call | solution.py:316
  40.0 3.5 %collective-permute-start.5 = (bf16[1024,256]{1,0:T(8,128)(2,1)S(1)}, bf16[1024,256]{1,0:T(8,128)(2,1)S(1)}, u32[]{:S(2)}, u32[]{:S(2)}) collective-permute-start(bf16[1024,256]{1,0:T(8,128)(2,1)S(1)} %mix.1.a0), channel_id=1, source_target_pairs={{0,2},{2,0},{1,3},{3,1},{4,6},{6,4},{5,7},{7,5},{8,10},{10,8},{9,1... | collective-permute-start | bytes 1572872 | tf_op jit(solution)/shard_map/ppermute | solution.py:326
  43.5 0.1 collective-permute-start.8
  43.6 1.3 constant_dynamic-slice_fusion.5
  44.9 3.1 %collective-permute-start.6 = (bf16[1024,256]{1,0:T(8,128)(2,1)S(1)}, bf16[1024,256]{1,0:T(8,128)(2,1)S(1)}, u32[]{:S(2)}, u32[]{:S(2)}) collective-permute-start(bf16[1024,256]{1,0:T(8,128)(2,1)S(1)} %mix.1.a0), channel_id=1, source_target_pairs={{0,1},{1,0},{2,3},{3,2},{4,5},{5,4},{6,7},{7,6},{8,9},{9,8},{10,11... | collective-permute-start | bytes 1572872 | tf_op jit(solution)/shard_map/ppermute | solution.py:229
  48.0 0.1 collective-permute-start.7
  48.2 0.1 pad_maximum_fusion
  48.3 0.5 collective-permute-start.10
  48.8 0.8 collective-permute-done.6.a1
  49.5 1.5 %collective-permute-done.7.w1 = bf16[256,2048]{1,0:T(8,128)(2,1)S(1)} collective-permute-done((bf16[256,2048]{1,0:T(8,128)(2,1)S(1)}, bf16[256,2048]{1,0:T(8,128)(2,1)S(1)}, u32[]{:S(2)}, u32[]{:S(2)}) %collective-permute-start.7) | collective-permute-done | bytes 1048608 | tf_op jit(solution)/shard_map/ppermute | solution.py:229
  51.0 4.4 %near.1.near_ref = bf16[1024,2048]{1,0:T(8,128)(2,1)S(1)} custom-call(s32[4]{0:T(128)S(1)} %pad_add_fusion.at_ref, bf16[1024,256]{1,0:T(8,128)(2,1)S(1)} %mix.1.a0, bf16[1024,256]{1,0:T(8,128)(2,1)S(1)} %collective-permute-done.6.a1, bf16[256,8192]{1,0:T(8,128)(2,1)} %w0.1, bf16[256,2048]{1,0:T(8,128)(2,1)S(1)} %collective-permute-done.7.w1), custom_call_target="tpu_custom_call" | custom-call | flops 2000000000 | bytes 6291456 | tf_op jit(solution)/shard_map/near/pallas_call | solution.py:349
  55.4 0.0 collective-permute-done.8.f2
  55.5 0.0 collective-permute-done.5.a2
  55.5 1.1 collective-permute-start.9
  56.6 0.3 collective-permute-start.11
  56.9 0.0 collective-permute-done.10.g013
  56.9 1.5 %collective-permute-done.11.g2 = bf16[48,2048]{1,0:T(8,128)(2,1)S(1)} collective-permute-done((bf16[48,2048]{1,0:T(8,128)(2,1)S(1)}, bf16[48,2048]{1,0:T(8,128)(2,1)S(1)}, u32[]{:S(2)}, u32[]{:S(2)}) %collective-permute-start.11) | collective-permute-done | bytes 196640 | tf_op jit(solution)/shard_map/ppermute | solution.py:229
  58.4 0.0 collective-permute-done.9.a3
  58.4 5.3 %far.1 = bf16[1024,2048]{1,0:T(8,128)(2,1)} custom-call(s32[4]{0:T(128)S(1)} %pad_add_fusion.at_ref, bf16[1024,256]{1,0:T(8,128)(2,1)S(1)} %collective-permute-done.5.a2, bf16[1024,256]{1,0:T(8,128)(2,1)S(1)} %collective-permute-done.9.a3, bf16[48,4096]{1,0:T(8,128)(2,1)S(1)} %collective-permute-done.1.f0, bf16[48,4096]{1,0:T(8,128)(2,1)S(1)} %collective-permute-done.2.f1, ...), custom_call_target="tpu_custom_call" | custom-call | flops 2000000000 | bytes 10485760 | tf_op jit(solution)/shard_map/far/pallas_call | solution.py:366
  63.7 0.0 reduce-scatter.2.cloned.1.call-update
  63.7 55.6 %reduce-scatter.2.cloned.1.call-done = bf16[128,2048]{1,0:T(8,128)(2,1)} async-done(((bf16[1024,2048]{1,0:T(8,128)(2,1)}), bf16[128,2048]{1,0:T(8,128)(2,1)}) %reduce-scatter.2.cloned.1.call-update) | async-done | bytes 524304 | tf_op jit(solution)/shard_map/reduce_scatter | solution.py:384
  119.3 1.1 fusion
  120.4 3.3 %collective-permute-start.14 = (bf16[32,2048]{1,0:T(8,128)(2,1)S(1)}, bf16[32,2048]{1,0:T(8,128)(2,1)S(1)}, u32[]{:S(2)}, u32[]{:S(2)}) collective-permute-start(bf16[32,2048]{1,0:T(8,128)(2,1)S(1)} %get-tuple-element.47), channel_id=1, source_target_pairs={{0,3},{1,2},{2,1},{3,0},{4,7},{5,6},{6,5},{7,4},{8,11},{9,10},{10,... | collective-permute-start | bytes 393224 | tf_op jit(solution)/shard_map/ppermute | solution.py:389
  123.7 0.3 collective-permute-start.13
  124.0 0.2 collective-permute-start.12
  124.2 3.8 %collective-permute-done.14.p3 = bf16[32,2048]{1,0:T(8,128)(2,1)S(1)} collective-permute-done((bf16[32,2048]{1,0:T(8,128)(2,1)S(1)}, bf16[32,2048]{1,0:T(8,128)(2,1)S(1)}, u32[]{:S(2)}, u32[]{:S(2)}) %collective-permute-start.14) | collective-permute-done | bytes 131104 | tf_op jit(solution)/shard_map/ppermute | solution.py:389
  128.0 2.6 %collective-permute-done.13.p2 = bf16[32,2048]{1,0:T(8,128)(2,1)S(1)} collective-permute-done((bf16[32,2048]{1,0:T(8,128)(2,1)S(1)}, bf16[32,2048]{1,0:T(8,128)(2,1)S(1)}, u32[]{:S(2)}, u32[]{:S(2)}) %collective-permute-start.13) | collective-permute-done | bytes 131104 | tf_op jit(solution)/shard_map/ppermute | solution.py:389
  130.6 0.0 collective-permute-done.12.p1
  130.6 1.4 join.1
  (9 shorter events, 0.1 us)
Async XLA Ops:
  7.2 9.2 %collective-permute-start = (bf16[3,8,256]{2,1,0:T(8,128)(2,1)S(1)}, bf16[3,8,256]{2,1,0:T(8,128)(2,1)S(1)}, u32[]{:S(2)}, u32[]{:S(2)}) collective-permute-start(bf16[3,8,256]{2,1,0:T(8,128)(2,1)S(1)} %slice.15), channel_id=1, source_target_pairs={{0,32},{32,64},{64,96},{96,128},{128,160},{160,192},{192,224},{1,3... | collective-permute-start | bytes 36872 | tf_op jit(solution)/shard_map/ppermute | solution.py:240
  12.2 13.0 %collective-permute-start.1 = (bf16[48,4096]{1,0:T(8,128)(2,1)S(1)}, bf16[48,4096]{1,0:T(8,128)(2,1)S(1)}, u32[]{:S(2)}, u32[]{:S(2)}) collective-permute-start(bf16[48,4096]{1,0:T(8,128)(2,1)S(1)} %dynamic_slice.24), channel_id=1, source_target_pairs={{0,34},{34,0},{2,32},{32,2},{1,35},{35,1},{3,33},{33,3},{4,38},{38... | collective-permute-start | bytes 1179656 | tf_op jit(solution)/shard_map/ppermute | solution.py:250
  16.2 18.5 %collective-permute-start.4 = (bf16[64,4096]{1,0:T(8,128)(2,1)S(1)}, bf16[64,4096]{1,0:T(8,128)(2,1)S(1)}, u32[]{:S(2)}, u32[]{:S(2)}) collective-permute-start(bf16[64,4096]{1,0:T(8,128)(2,1)S(1)} %constant_dynamic-slice_fusion.6), channel_id=1, source_target_pairs={{0,34},{34,0},{2,32},{32,2},{1,35},{35,1},{3,33},{33,3},{4,38},{38... | collective-permute-start | bytes 1572872 | tf_op jit(solution)/shard_map/ppermute | solution.py:251
  16.4 8.8 %copy-start = (f32[16,16]{1,0:T(8,128)S(1)}, f32[16,16]{1,0:T(8,128)}, u32[]{:S(2)}) copy-start(f32[16,16]{1,0:T(8,128)} %rate_ref.3) | copy-start | bytes 3076
  16.4 8.8 %copy-start.1 = (f32[16,16]{1,0:T(8,128)S(1)}, f32[16,16]{1,0:T(8,128)}, u32[]{:S(2)}) copy-start(f32[16,16]{1,0:T(8,128)} %param.7) | copy-start | bytes 3076
  21.1 11.9 %all-to-all-start = ((f32[8,16,256]{2,1,0:T(8,128)}), f32[8,16,256]{2,1,0:T(8,128)S(1)}, u32[]{:S(2)}, u32[]{:S(2)}) async-start(f32[8,16,256]{2,1,0:T(8,128)} %get-tuple-element.28), calls=%async_computation | async-start | bytes 262144 | tf_op jit(solution)/shard_map/all_to_all | solution.py:289
  25.1 94.2 %reduce-scatter.2.cloned.1.call-start = ((), (), s32[]{:S(2)}) async-start(), calls=%async_computation.2 | async-start | bytes 4718592 | tf_op jit(solution)/shard_map/reduce_scatter | solution.py:384
  25.2 10.7 %collective-permute-start.3 = (bf16[48,4096]{1,0:T(8,128)(2,1)S(1)}, bf16[48,4096]{1,0:T(8,128)(2,1)S(1)}, u32[]{:S(2)}, u32[]{:S(2)}) collective-permute-start(bf16[48,4096]{1,0:T(8,128)(2,1)S(1)} %collective-permute-done.1.f0), channel_id=1, source_target_pairs={{0,192},{64,0},{128,64},{192,128},{1,193},{65,1},{129,65},{193,129... | collective-permute-start | bytes 1179656 | tf_op jit(solution)/shard_map/ppermute | solution.py:313
  27.9 10.5 %collective-permute-start.2 = (bf16[48,4096]{1,0:T(8,128)(2,1)S(1)}, bf16[48,4096]{1,0:T(8,128)(2,1)S(1)}, u32[]{:S(2)}, u32[]{:S(2)}) collective-permute-start(bf16[48,4096]{1,0:T(8,128)(2,1)S(1)} %collective-permute-done.1.f0), channel_id=1, source_target_pairs={{0,64},{64,128},{128,192},{192,0},{1,65},{65,129},{129,193},{193,1... | collective-permute-start | bytes 1179656 | tf_op jit(solution)/shard_map/ppermute | solution.py:312
  40.0 15.4 %collective-permute-start.5 = (bf16[1024,256]{1,0:T(8,128)(2,1)S(1)}, bf16[1024,256]{1,0:T(8,128)(2,1)S(1)}, u32[]{:S(2)}, u32[]{:S(2)}) collective-permute-start(bf16[1024,256]{1,0:T(8,128)(2,1)S(1)} %mix.1.a0), channel_id=1, source_target_pairs={{0,2},{2,0},{1,3},{3,1},{4,6},{6,4},{5,7},{7,5},{8,10},{10,8},{9,1... | collective-permute-start | bytes 1572872 | tf_op jit(solution)/shard_map/ppermute | solution.py:326
  43.5 11.9 %collective-permute-start.8 = (bf16[48,4096]{1,0:T(8,128)(2,1)S(1)}, bf16[48,4096]{1,0:T(8,128)(2,1)S(1)}, u32[]{:S(2)}, u32[]{:S(2)}) collective-permute-start(bf16[48,4096]{1,0:T(8,128)(2,1)S(1)} %collective-permute-done.1.f0), channel_id=1, source_target_pairs={{0,128},{64,192},{128,0},{192,64},{1,129},{65,193},{129,1},{193,65... | collective-permute-start | bytes 1179656 | tf_op jit(solution)/shard_map/ppermute | solution.py:315
  44.9 4.6 %collective-permute-start.6 = (bf16[1024,256]{1,0:T(8,128)(2,1)S(1)}, bf16[1024,256]{1,0:T(8,128)(2,1)S(1)}, u32[]{:S(2)}, u32[]{:S(2)}) collective-permute-start(bf16[1024,256]{1,0:T(8,128)(2,1)S(1)} %mix.1.a0), channel_id=1, source_target_pairs={{0,1},{1,0},{2,3},{3,2},{4,5},{5,4},{6,7},{7,6},{8,9},{9,8},{10,11... | collective-permute-start | bytes 1572872 | tf_op jit(solution)/shard_map/ppermute | solution.py:229
  48.0 3.0 %collective-permute-start.7 = (bf16[256,2048]{1,0:T(8,128)(2,1)S(1)}, bf16[256,2048]{1,0:T(8,128)(2,1)S(1)}, u32[]{:S(2)}, u32[]{:S(2)}) collective-permute-start(bf16[256,2048]{1,0:T(8,128)(2,1)S(1)} %constant_dynamic-slice_fusion.5), channel_id=1, source_target_pairs={{0,1},{1,0},{2,3},{3,2},{4,5},{5,4},{6,7},{7,6},{8,9},{9,8},{10,11... | collective-permute-start | bytes 3145736 | tf_op jit(solution)/shard_map/ppermute | solution.py:229
  48.3 8.6 %collective-permute-start.10 = (bf16[208,2048]{1,0:T(8,128)(2,1)S(1)}, bf16[208,2048]{1,0:T(8,128)(2,1)S(1)}, u32[]{:S(2)}, u32[]{:S(2)}) collective-permute-start(bf16[208,2048]{1,0:T(8,128)(2,1)S(1)} %pad_maximum_fusion), channel_id=1, source_target_pairs={{0,1},{1,0},{2,3},{3,2},{4,5},{5,4},{6,7},{7,6},{8,9},{9,8},{10,11... | collective-permute-start | bytes 2555912 | tf_op jit(solution)/shard_map/ppermute | solution.py:229
  55.5 2.9 %collective-permute-start.9 = (bf16[1024,256]{1,0:T(8,128)(2,1)S(1)}, bf16[1024,256]{1,0:T(8,128)(2,1)S(1)}, u32[]{:S(2)}, u32[]{:S(2)}) collective-permute-start(bf16[1024,256]{1,0:T(8,128)(2,1)S(1)} %collective-permute-done.5.a2), channel_id=1, source_target_pairs={{0,1},{1,0},{2,3},{3,2},{4,5},{5,4},{6,7},{7,6},{8,9},{9,8},{10,11... | collective-permute-start | bytes 1572872 | tf_op jit(solution)/shard_map/ppermute | solution.py:229
  56.6 1.8 %collective-permute-start.11 = (bf16[48,2048]{1,0:T(8,128)(2,1)S(1)}, bf16[48,2048]{1,0:T(8,128)(2,1)S(1)}, u32[]{:S(2)}, u32[]{:S(2)}) collective-permute-start(bf16[48,2048]{1,0:T(8,128)(2,1)S(1)} %constant_dynamic-slice_fusion), channel_id=1, source_target_pairs={{0,1},{1,0},{2,3},{3,2},{4,5},{5,4},{6,7},{7,6},{8,9},{9,8},{10,11... | collective-permute-start | bytes 589832 | tf_op jit(solution)/shard_map/ppermute | solution.py:229
  120.4 7.6 %collective-permute-start.14 = (bf16[32,2048]{1,0:T(8,128)(2,1)S(1)}, bf16[32,2048]{1,0:T(8,128)(2,1)S(1)}, u32[]{:S(2)}, u32[]{:S(2)}) collective-permute-start(bf16[32,2048]{1,0:T(8,128)(2,1)S(1)} %get-tuple-element.47), channel_id=1, source_target_pairs={{0,3},{1,2},{2,1},{3,0},{4,7},{5,6},{6,5},{7,4},{8,11},{9,10},{10,... | collective-permute-start | bytes 393224 | tf_op jit(solution)/shard_map/ppermute | solution.py:389
  123.7 6.8 %collective-permute-start.13 = (bf16[32,2048]{1,0:T(8,128)(2,1)S(1)}, bf16[32,2048]{1,0:T(8,128)(2,1)S(1)}, u32[]{:S(2)}, u32[]{:S(2)}) collective-permute-start(bf16[32,2048]{1,0:T(8,128)(2,1)S(1)} %get-tuple-element.48), channel_id=1, source_target_pairs={{0,2},{1,3},{2,0},{3,1},{4,6},{5,7},{6,4},{7,5},{8,10},{9,11},{10,... | collective-permute-start | bytes 393224 | tf_op jit(solution)/shard_map/ppermute | solution.py:389
  124.0 6.6 %collective-permute-start.12 = (bf16[32,2048]{1,0:T(8,128)(2,1)S(1)}, bf16[32,2048]{1,0:T(8,128)(2,1)S(1)}, u32[]{:S(2)}, u32[]{:S(2)}) collective-permute-start(bf16[32,2048]{1,0:T(8,128)(2,1)S(1)} %get-tuple-element.49), channel_id=1, source_target_pairs={{0,1},{1,0},{2,3},{3,2},{4,5},{5,4},{6,7},{7,6},{8,9},{9,8},{10,11... | collective-permute-start | bytes 393224 | tf_op jit(solution)/shard_map/ppermute | solution.py:389
Sparse Core Ops, SparseCore 0:
  63.8 55.4 reduce-scatter.1
